TPU v7x, 256 devices: a whole 4x4x8 slice. The times are simulated.
256 devices in a mesh: section: 8 (over z_hi, x), dp: 32 (over z_lo, y, core).
Axes of the slice: x: 4, y: 4, z: 8 (z_hi: 2, z_lo: 4; z = z_hi * 4 + z_lo), core: 2. Of those that a mesh axis runs over, the one named last changes fastest.
Arguments:
- states: bfloat16 [128, 128, 2048], P('dp'), may hold values from -6 to 6
- outage: int32 [128, 128], P('dp'), may hold values 0 or 1
- targets: float32 [128, 128], P('dp'), may hold values from -6 to 6
- pattern: int32 [8, 2], replicated, may hold values from 0 to 3, as said below
- weights: bfloat16 [8, 2048, 2048], P('section'), may hold values from -0.75 to 0.75
- readout: float32 [2048], replicated, may hold values from -0.125 to 0.125
Outputs:
- grad_weights: float32 [8, 2048, 2048], P('section', 'dp')
Inputs may be any that keep to these rules, and one draw needn't show every extreme that they name: `pattern`: rows 0 to 3 are the pairs (k, k); row 4 + k pairs block k with a block other than k.
All inputs are finite; a program needn't handle non-finite values. No bound on the sum of `outage` on one device may be relied on, other than what follows from the above.
Results may differ from a plain program's by a relative error of at most 0.006.
Values may be sent and summed in bfloat16 or wider, within the bound.
A program may use at most 128 MiB of HBM per device.

v0:
```python
import jax
import jax.numpy as jnp
from jax import lax
from jax.sharding import PartitionSpec as P

HEADS = 16
BLOCK = 32


epsilon = 1e-05


def passed_along(block, axis, distance):
    devices = range(lax.axis_size(axis))
    route = [(i - distance, i) for i in devices if i - distance in devices]
    return lax.ppermute(block, axis, route)


def allowed_pairs(pattern, outage):
    buses = outage.shape[-1]
    block_count = buses // BLOCK
    block_ids = jnp.arange(block_count, dtype=jnp.int32)
    pair_hits = (pattern[:, 0][None, None, :] == block_ids[:, None, None]) & (
        pattern[:, 1][None, None, :] == block_ids[None, :, None]
    )
    block_table = jnp.max(pair_hits.astype(jnp.float32), axis=2)
    member = ((jnp.arange(buses, dtype=jnp.int32) // BLOCK)[:, None] == block_ids[None, :]).astype(
        jnp.float32
    )
    pair_mask = jnp.dot(
        jnp.dot(member, block_table, precision=lax.Precision.HIGHEST),
        member.T,
        precision=lax.Precision.HIGHEST,
    )
    in_service = outage.astype(jnp.float32)
    self_mask = jnp.eye(buses, dtype=jnp.float32)
    return pair_mask[None] * jnp.maximum(in_service[:, None, :], self_mask[None])


def layer_forward(hidden, weight, allowed):
    num_states, buses, width = hidden.shape
    split_shape = (num_states, buses, HEADS, width // HEADS)
    hidden_f = hidden.astype(jnp.float32)
    centred = hidden_f - jnp.mean(hidden_f, axis=-1, keepdims=True)
    inverse_std = lax.rsqrt(jnp.mean(centred * centred, axis=-1, keepdims=True) + epsilon)
    scaled = centred * inverse_std
    normed = scaled.astype(jnp.bfloat16)
    values_b = (
        jnp.dot(normed.reshape(-1, width), weight, preferred_element_type=jnp.float32)
        .astype(jnp.bfloat16)
        .reshape(split_shape)
    )
    features = (jax.nn.elu(values_b.astype(jnp.float32)) + 1.0).astype(jnp.bfloat16)
    kernel = (
        jnp.einsum("nihc,njhc->nhij", features, features, preferred_element_type=jnp.float32)
        * allowed[:, None]
    )
    totals = jnp.sum(kernel, axis=-1, keepdims=True)
    attention = kernel / totals
    attention_b = attention.astype(jnp.bfloat16)
    gathered = jnp.einsum(
        "nhij,njhc->nihc", attention_b, values_b, preferred_element_type=jnp.float32
    )
    output = (hidden_f + gathered.reshape(num_states, buses, width)).astype(jnp.bfloat16)
    return (output, (scaled, inverse_std, values_b, attention, totals))


def layer_backward(upstream, weight, allowed, kept_parts):
    scaled, inverse_std, values_b, attention, totals = kept_parts
    num_states, buses, width = upstream.shape
    grad_f = upstream.astype(jnp.float32)
    grad_heads = upstream.reshape(values_b.shape)
    values_f = values_b.astype(jnp.float32)
    features = (jax.nn.elu(values_f) + 1.0).astype(jnp.bfloat16)
    attention_b = attention.astype(jnp.bfloat16)
    value_grad = jnp.einsum(
        "nhij,nihc->njhc", attention_b, grad_heads, preferred_element_type=jnp.float32
    )
    attention_grad = jnp.einsum(
        "nihc,njhc->nhij", grad_heads, values_b, preferred_element_type=jnp.float32
    )
    row_terms = jnp.sum(attention_grad * attention, axis=-1, keepdims=True)
    kernel_grad = ((attention_grad - row_terms) / totals * allowed[:, None]).astype(jnp.bfloat16)
    feature_grad = jnp.einsum(
        "nhij,njhc->nihc", kernel_grad, features, preferred_element_type=jnp.float32
    )
    feature_grad = feature_grad + jnp.einsum(
        "nhji,njhc->nihc", kernel_grad, features, preferred_element_type=jnp.float32
    )
    slope = jnp.where(values_f > 0.0, 1.0, jnp.exp(jnp.minimum(values_f, 0.0)))
    value_total = (
        (value_grad + feature_grad * slope).astype(jnp.bfloat16).reshape(num_states, buses, width)
    )
    normed_grad = lax.dot_general(
        value_total.reshape(-1, width),
        weight,
        (((1,), (1,)), ((), ())),
        preferred_element_type=jnp.float32,
    ).reshape(num_states, buses, width)
    mean_grad = jnp.mean(normed_grad, axis=-1, keepdims=True)
    mean_cross = jnp.mean(normed_grad * scaled, axis=-1, keepdims=True)
    lower = (grad_f + inverse_std * (normed_grad - mean_grad - scaled * mean_cross)).astype(
        jnp.bfloat16
    )
    return (lower, value_total)


def per_device(states, outage, targets, pattern, weights, readout):
    sections = lax.axis_size("section")
    rank = lax.axis_index("section")
    micro, buses, width = states.shape
    weight = weights[0]
    allowed = allowed_pairs(pattern, outage)
    head_size = width // HEADS
    steps_total = sections + micro - 1
    zero_rows = jnp.zeros((buses, width), jnp.bfloat16)
    stash_init = (
        jnp.zeros((micro, buses, width), jnp.float32),
        jnp.zeros((micro, buses, 1), jnp.float32),
        jnp.zeros((micro, buses, HEADS, head_size), jnp.bfloat16),
        jnp.zeros((micro, HEADS, buses, buses), jnp.float32),
        jnp.zeros((micro, HEADS, buses, 1), jnp.float32),
    )
    upstream_init = jnp.zeros((micro, buses, width), jnp.bfloat16)

    def forward_step(step, carry):
        incoming, stashed, upstream_stash = carry
        slot_raw = step - rank
        active = (slot_raw >= 0) & (slot_raw < micro)
        slot = jnp.clip(slot_raw, 0, micro - 1)
        first_state = lax.dynamic_index_in_dim(states, slot, 0, keepdims=True)
        source = jnp.where(rank == 0, first_state, incoming[None])
        allowed_slot = lax.dynamic_index_in_dim(allowed, slot, 0, keepdims=True)

        def forward_do_work(stash_in, upstream_in):
            output, kept_parts = layer_forward(source, weight, allowed_slot)
            stash_out = tuple(
                (
                    lax.dynamic_update_index_in_dim(whole_array, new_piece, slot, 0)
                    for whole_array, new_piece in zip(stash_in, kept_parts)
                )
            )
            predicted = jnp.sum(output.astype(jnp.float32) * readout, axis=-1)
            misfit = predicted - lax.dynamic_index_in_dim(targets, slot, 0, keepdims=True)
            cotangent = (misfit[..., None] * readout).astype(jnp.bfloat16)
            upstream_out = lax.dynamic_update_index_in_dim(upstream_in, cotangent, slot, 0)
            return (output[0], stash_out, upstream_out)

        def forward_no_work(stash_in, upstream_in):
            return (zero_rows, stash_in, upstream_in)

        output, stashed, upstream_stash = lax.cond(
            active, forward_do_work, forward_no_work, stashed, upstream_stash
        )
        passed = passed_along(output, "section", 1)
        return (passed, stashed, upstream_stash)

    unused_rows, stashed, upstream_stash = lax.fori_loop(
        0, steps_total, forward_step, (zero_rows, stash_init, upstream_init)
    )
    grad_init = jnp.zeros((width, width), jnp.float32)

    def backward_step(step, carry):
        incoming, collected = carry
        slot_raw = step - (sections - 1 - rank)
        active = (slot_raw >= 0) & (slot_raw < micro)
        slot = jnp.clip(slot_raw, 0, micro - 1)
        last_grad = lax.dynamic_index_in_dim(upstream_stash, slot, 0, keepdims=True)
        upstream = jnp.where(rank == sections - 1, last_grad, incoming[None])
        allowed_slot = lax.dynamic_index_in_dim(allowed, slot, 0, keepdims=True)

        def backward_do_work(collected_in):
            kept_parts = tuple(
                (
                    lax.dynamic_index_in_dim(whole_array, slot, 0, keepdims=True)
                    for whole_array in stashed
                )
            )
            lower, value_total = layer_backward(upstream, weight, allowed_slot, kept_parts)
            normed = kept_parts[0].astype(jnp.bfloat16).reshape(buses, width)
            product = lax.dot_general(
                normed,
                value_total.reshape(buses, width),
                (((0,), (0,)), ((), ())),
                preferred_element_type=jnp.float32,
            )
            collected_out = collected_in + product
            return (lower[0], collected_out)

        def backward_no_work(collected_in):
            return (zero_rows, collected_in)

        lower, collected = lax.cond(active, backward_do_work, backward_no_work, collected)
        passed = passed_along(lower, "section", -1)
        return (passed, collected)

    unused_rows, collected = lax.fori_loop(0, steps_total, backward_step, (zero_rows, grad_init))
    summed = lax.psum_scatter(collected, "dp", scatter_dimension=0, tiled=True)
    return summed[None]


def solution(mesh):
    in_specs = (
        P("dp", None, None),
        P("dp", None),
        P("dp", None),
        P(),
        P("section", None, None),
        P(),
    )
    out_specs = P("section", "dp", None)
    return jax.shard_map(
        per_device, mesh=mesh, in_specs=in_specs, out_specs=out_specs, check_vma=False
    )
```

profile of v0, /device:TPU:6, one launch (start us, length us, event | category | flops | bytes accessed | tf_op | source)
XLA Modules:
  0.0 1086.8 jit_solution(2609769477839571578)
XLA Ops:
  19.7 266.6 %while.48 = (s32[]{:T(128)}, bf16[128,2048]{0,1:T(8,128)(2,1)S(1)}, f32[4,128,2048]{1,2,0:T(8,128)}, f32[4,128,1]{1,2,0:T(1,128)S(1)}, bf16[4,128,16,128]{3,2,1,...) while((s32[]{:T(128)}, bf16[128,2048]{0,1:T(8,128)(2,1)S(1)}, ...), condition=%wide.region_8.9_spmd.clone, body=%wide.region_1.8_spmd.clone.sunk | while | flops 1216641408 | bytes 26020904 | solution.py:158
  19.8 9.0 collective-permute-start
  28.8 11.2 %collective-permute-done = bf16[128,2048]{0,1:T(8,128)(2,1)S(1)} collective-permute-done((bf16[128,2048]{0,1:T(8,128)(2,1)S(1)}, bf16[128,2048]{0,1:T(8,128)(2,1)S(1)}, u32[]{:S(2)}, u32[]{:S(2)}) %collective-permute-start) | collective-permute-done | bytes 524320 | tf_op jit(solution)/shard_map/while/body/eval_jaxpr/ppermute | solution.py:16
  40.1 10.5 collective-permute-start
  50.6 10.2 collective-permute-done
  60.9 10.5 collective-permute-start
  71.4 19.4 %collective-permute-done = bf16[128,2048]{0,1:T(8,128)(2,1)S(1)} collective-permute-done((bf16[128,2048]{0,1:T(8,128)(2,1)S(1)}, bf16[128,2048]{0,1:T(8,128)(2,1)S(1)}, u32[]{:S(2)}, u32[]{:S(2)}) %collective-permute-start) | collective-permute-done | bytes 524320 | tf_op jit(solution)/shard_map/while/body/eval_jaxpr/ppermute | solution.py:16
  90.8 12.1 %conditional.6 = (bf16[128,2048]{0,1:T(8,128)(2,1)S(1)}, f32[4,128,2048]{1,2,0:T(8,128)}, f32[4,128,1]{1,2,0:T(1,128)S(1)}, bf16[4,128,16,128]{3,2,1,0:T(8,128)(...) conditional(s32[]{:T(128)} %convert_element_type.260, ...), branch_computations={%region_2.2_spmd, %region_3.7_spmd} | conditional | flops 1216641408 | bytes 23923316 | solution.py:152
  104.8 9.1 collective-permute-done
  114.0 12.2 %conditional.6 = (bf16[128,2048]{0,1:T(8,128)(2,1)S(1)}, f32[4,128,2048]{1,2,0:T(8,128)}, f32[4,128,1]{1,2,0:T(1,128)S(1)}, bf16[4,128,16,128]{3,2,1,0:T(8,128)(...) conditional(s32[]{:T(128)} %convert_element_type.260, ...), branch_computations={%region_2.2_spmd, %region_3.7_spmd} | conditional | flops 1216641408 | bytes 23923316 | solution.py:152
  126.2 8.2 collective-permute-start
  134.4 6.7 collective-permute-done
  141.1 12.0 %conditional.6 = (bf16[128,2048]{0,1:T(8,128)(2,1)S(1)}, f32[4,128,2048]{1,2,0:T(8,128)}, f32[4,128,1]{1,2,0:T(1,128)S(1)}, bf16[4,128,16,128]{3,2,1,0:T(8,128)(...) conditional(s32[]{:T(128)} %convert_element_type.260, ...), branch_computations={%region_2.2_spmd, %region_3.7_spmd} | conditional | flops 1216641408 | bytes 23923316 | solution.py:152
  153.1 10.7 collective-permute-start
  163.7 6.7 collective-permute-done
  170.4 12.0 %conditional.6 = (bf16[128,2048]{0,1:T(8,128)(2,1)S(1)}, f32[4,128,2048]{1,2,0:T(8,128)}, f32[4,128,1]{1,2,0:T(1,128)S(1)}, bf16[4,128,16,128]{3,2,1,0:T(8,128)(...) conditional(s32[]{:T(128)} %convert_element_type.260, ...), branch_computations={%region_2.2_spmd, %region_3.7_spmd} | conditional | flops 1216641408 | bytes 23923316 | solution.py:152
  182.4 10.4 collective-permute-start
  192.9 6.7 collective-permute-done
  199.6 22.3 %collective-permute-start = (bf16[128,2048]{0,1:T(8,128)(2,1)S(1)}, bf16[128,2048]{0,1:T(8,128)(2,1)S(1)}, u32[]{:S(2)}, u32[]{:S(2)}) collective-permute-start(bf16[128,2048]{0,1:T(8,128)(2,1)S(1)} %get-tuple-element.1371), channel_id=1, source_target_pairs={{0,32},{32,64},{64,96},{96,128},{128,160},{160,192},{192,224},{1,3... | collective-permute-start | bytes 1572872 | tf_op jit(solution)/shard_map/while/body/eval_jaxpr/ppermute | solution.py:16
  228.7 10.4 collective-permute-start
  239.1 7.2 collective-permute-done
  246.4 12.4 %collective-permute-start = (bf16[128,2048]{0,1:T(8,128)(2,1)S(1)}, bf16[128,2048]{0,1:T(8,128)(2,1)S(1)}, u32[]{:S(2)}, u32[]{:S(2)}) collective-permute-start(bf16[128,2048]{0,1:T(8,128)(2,1)S(1)} %get-tuple-element.1371), channel_id=1, source_target_pairs={{0,32},{32,64},{64,96},{96,128},{128,160},{160,192},{192,224},{1,3... | collective-permute-start | bytes 1572872 | tf_op jit(solution)/shard_map/while/body/eval_jaxpr/ppermute | solution.py:16
  258.8 10.1 collective-permute-done
  269.0 10.5 collective-permute-start
  304.1 7.8 broadcast_in_dim.86
  312.0 449.9 %while.49 = (s32[]{:T(128)}, bf16[128,2048]{1,0:T(8,128)(2,1)S(1)}, f32[2048,2048]{1,0:T(8,128)}, s32[]{:T(128)}, pred[]{:T(512)}, /*index=5*/bf16[4,128,2048]{2...) while((s32[]{:T(128)}, bf16[128,2048]{1,0:T(8,128)(2,1)S(1)}, ...), condition=%wide.region_15.16_spmd.clone, body=%wide.region_9.15_spmd.clone.sunk | while | flops 2431154176 | bytes 104727040 | solution.py:197
  315.0 20.6 %collective-permute-done.1 = bf16[128,2048]{1,0:T(8,128)(2,1)S(1)} collective-permute-done((bf16[128,2048]{1,0:T(8,128)(2,1)}, bf16[128,2048]{1,0:T(8,128)(2,1)S(1)}, u32[]{:S(2)}, u32[]{:S(2)}) %collective-permute-start.1) | collective-permute-done | bytes 524320 | tf_op jit(solution)/shard_map/while/body/eval_jaxpr/ppermute | solution.py:16
  338.3 20.9 %collective-permute-done.1 = bf16[128,2048]{1,0:T(8,128)(2,1)S(1)} collective-permute-done((bf16[128,2048]{1,0:T(8,128)(2,1)}, bf16[128,2048]{1,0:T(8,128)(2,1)S(1)}, u32[]{:S(2)}, u32[]{:S(2)}) %collective-permute-start.1) | collective-permute-done | bytes 524320 | tf_op jit(solution)/shard_map/while/body/eval_jaxpr/ppermute | solution.py:16
  362.0 15.5 %collective-permute-done.1 = bf16[128,2048]{1,0:T(8,128)(2,1)S(1)} collective-permute-done((bf16[128,2048]{1,0:T(8,128)(2,1)}, bf16[128,2048]{1,0:T(8,128)(2,1)S(1)}, u32[]{:S(2)}, u32[]{:S(2)}) %collective-permute-start.1) | collective-permute-done | bytes 524320 | tf_op jit(solution)/shard_map/while/body/eval_jaxpr/ppermute | solution.py:16
  380.2 105.0 %collective-permute-done.1 = bf16[128,2048]{1,0:T(8,128)(2,1)S(1)} collective-permute-done((bf16[128,2048]{1,0:T(8,128)(2,1)}, bf16[128,2048]{1,0:T(8,128)(2,1)S(1)}, u32[]{:S(2)}, u32[]{:S(2)}) %collective-permute-start.1) | collective-permute-done | bytes 524320 | tf_op jit(solution)/shard_map/while/body/eval_jaxpr/ppermute | solution.py:16
  485.2 30.6 %conditional.7 = (bf16[128,2048]{1,0:T(8,128)(2,1)}, f32[2048,2048]{1,0:T(8,128)}) conditional(s32[]{:T(128)} %convert_element_type.261, f32[2048,2048]{1,0:T(8,128)} %get-tuple-element.1493, (pred[]{:T(512)}, s32[]{:T(128)}, bf16[4,128,2048]{2,1,0:T(8,128)(2,1)}, bf16[128,2048]{1,0:T(8,128)(2,1)S(1)}, f32[4,128,1]{1,2,0:T(1,128)S(1)}, ...), branch_computations={%region_10.10_spmd, %region_11.14_spmd} | conditional | flops 2431154176 | bytes 102629536 | solution.py:193
  494.6 14.3 %convolution_add_fusion = f32[2048,2048]{1,0:T(8,128)} fusion(f32[2048,2048]{1,0:T(8,128)} %get-tuple-element.880, bf16[128,2048]{0,1:T(8,128)(2,1)S(1)} %bitcast.126, f32[4,128,2048]{2,1,0:T(8,128)} %get-tuple-element.879, s32[]{:T(128)S(6)} %min.26), kind=kOutput, calls=%fused_computation.48 | convolution fusion | flops 1077936128 | bytes 34603012 | tf_op jit(solution)/shard_map/while/body/eval_jaxpr/cond/branch_1_fun/dot_general | solution.py:181
  517.7 15.4 %collective-permute-done.1 = bf16[128,2048]{1,0:T(8,128)(2,1)S(1)} collective-permute-done((bf16[128,2048]{1,0:T(8,128)(2,1)}, bf16[128,2048]{1,0:T(8,128)(2,1)S(1)}, u32[]{:S(2)}, u32[]{:S(2)}) %collective-permute-start.1) | collective-permute-done | bytes 524320 | tf_op jit(solution)/shard_map/while/body/eval_jaxpr/ppermute | solution.py:16
  533.1 30.6 %conditional.7 = (bf16[128,2048]{1,0:T(8,128)(2,1)}, f32[2048,2048]{1,0:T(8,128)}) conditional(s32[]{:T(128)} %convert_element_type.261, f32[2048,2048]{1,0:T(8,128)} %get-tuple-element.1493, (pred[]{:T(512)}, s32[]{:T(128)}, bf16[4,128,2048]{2,1,0:T(8,128)(2,1)}, bf16[128,2048]{1,0:T(8,128)(2,1)S(1)}, f32[4,128,1]{1,2,0:T(1,128)S(1)}, ...), branch_computations={%region_10.10_spmd, %region_11.14_spmd} | conditional | flops 2431154176 | bytes 102629536 | solution.py:193
  542.5 14.3 %convolution_add_fusion = f32[2048,2048]{1,0:T(8,128)} fusion(f32[2048,2048]{1,0:T(8,128)} %get-tuple-element.880, bf16[128,2048]{0,1:T(8,128)(2,1)S(1)} %bitcast.126, f32[4,128,2048]{2,1,0:T(8,128)} %get-tuple-element.879, s32[]{:T(128)S(6)} %min.26), kind=kOutput, calls=%fused_computation.48 | convolution fusion | flops 1077936128 | bytes 34603012 | tf_op jit(solution)/shard_map/while/body/eval_jaxpr/cond/branch_1_fun/dot_general | solution.py:181
  565.6 15.4 %collective-permute-done.1 = bf16[128,2048]{1,0:T(8,128)(2,1)S(1)} collective-permute-done((bf16[128,2048]{1,0:T(8,128)(2,1)}, bf16[128,2048]{1,0:T(8,128)(2,1)S(1)}, u32[]{:S(2)}, u32[]{:S(2)}) %collective-permute-start.1) | collective-permute-done | bytes 524320 | tf_op jit(solution)/shard_map/while/body/eval_jaxpr/ppermute | solution.py:16
  581.0 30.6 %conditional.7 = (bf16[128,2048]{1,0:T(8,128)(2,1)}, f32[2048,2048]{1,0:T(8,128)}) conditional(s32[]{:T(128)} %convert_element_type.261, f32[2048,2048]{1,0:T(8,128)} %get-tuple-element.1493, (pred[]{:T(512)}, s32[]{:T(128)}, bf16[4,128,2048]{2,1,0:T(8,128)(2,1)}, bf16[128,2048]{1,0:T(8,128)(2,1)S(1)}, f32[4,128,1]{1,2,0:T(1,128)S(1)}, ...), branch_computations={%region_10.10_spmd, %region_11.14_spmd} | conditional | flops 2431154176 | bytes 102629536 | solution.py:193
  590.4 14.3 %convolution_add_fusion = f32[2048,2048]{1,0:T(8,128)} fusion(f32[2048,2048]{1,0:T(8,128)} %get-tuple-element.880, bf16[128,2048]{0,1:T(8,128)(2,1)S(1)} %bitcast.126, f32[4,128,2048]{2,1,0:T(8,128)} %get-tuple-element.879, s32[]{:T(128)S(6)} %min.26), kind=kOutput, calls=%fused_computation.48 | convolution fusion | flops 1077936128 | bytes 34603012 | tf_op jit(solution)/shard_map/while/body/eval_jaxpr/cond/branch_1_fun/dot_general | solution.py:181
  613.5 15.4 %collective-permute-done.1 = bf16[128,2048]{1,0:T(8,128)(2,1)S(1)} collective-permute-done((bf16[128,2048]{1,0:T(8,128)(2,1)}, bf16[128,2048]{1,0:T(8,128)(2,1)S(1)}, u32[]{:S(2)}, u32[]{:S(2)}) %collective-permute-start.1) | collective-permute-done | bytes 524320 | tf_op jit(solution)/shard_map/while/body/eval_jaxpr/ppermute | solution.py:16
  628.9 30.6 %conditional.7 = (bf16[128,2048]{1,0:T(8,128)(2,1)}, f32[2048,2048]{1,0:T(8,128)}) conditional(s32[]{:T(128)} %convert_element_type.261, f32[2048,2048]{1,0:T(8,128)} %get-tuple-element.1493, (pred[]{:T(512)}, s32[]{:T(128)}, bf16[4,128,2048]{2,1,0:T(8,128)(2,1)}, bf16[128,2048]{1,0:T(8,128)(2,1)S(1)}, f32[4,128,1]{1,2,0:T(1,128)S(1)}, ...), branch_computations={%region_10.10_spmd, %region_11.14_spmd} | conditional | flops 2431154176 | bytes 102629536 | solution.py:193
  638.3 14.3 %convolution_add_fusion = f32[2048,2048]{1,0:T(8,128)} fusion(f32[2048,2048]{1,0:T(8,128)} %get-tuple-element.880, bf16[128,2048]{0,1:T(8,128)(2,1)S(1)} %bitcast.126, f32[4,128,2048]{2,1,0:T(8,128)} %get-tuple-element.879, s32[]{:T(128)S(6)} %min.26), kind=kOutput, calls=%fused_computation.48 | convolution fusion | flops 1077936128 | bytes 34603012 | tf_op jit(solution)/shard_map/while/body/eval_jaxpr/cond/branch_1_fun/dot_general | solution.py:181
  661.4 17.7 %collective-permute-done.1 = bf16[128,2048]{1,0:T(8,128)(2,1)S(1)} collective-permute-done((bf16[128,2048]{1,0:T(8,128)(2,1)}, bf16[128,2048]{1,0:T(8,128)(2,1)S(1)}, u32[]{:S(2)}, u32[]{:S(2)}) %collective-permute-start.1) | collective-permute-done | bytes 524320 | tf_op jit(solution)/shard_map/while/body/eval_jaxpr/ppermute | solution.py:16
  679.9 23.4 %collective-permute-start.1 = (bf16[128,2048]{1,0:T(8,128)(2,1)}, bf16[128,2048]{1,0:T(8,128)(2,1)S(1)}, u32[]{:S(2)}, u32[]{:S(2)}) collective-permute-start(bf16[128,2048]{1,0:T(8,128)(2,1)} %get-tuple-element.1393), channel_id=1, source_target_pairs={{32,0},{64,32},{96,64},{128,96},{160,128},{192,160},{224,192},{33,... | collective-permute-start | bytes 1572872 | tf_op jit(solution)/shard_map/while/body/eval_jaxpr/ppermute | solution.py:16
  703.3 7.0 collective-permute-done.1
  715.4 13.6 %collective-permute-done.1 = bf16[128,2048]{1,0:T(8,128)(2,1)S(1)} collective-permute-done((bf16[128,2048]{1,0:T(8,128)(2,1)}, bf16[128,2048]{1,0:T(8,128)(2,1)S(1)}, u32[]{:S(2)}, u32[]{:S(2)}) %collective-permute-start.1) | collective-permute-done | bytes 524320 | tf_op jit(solution)/shard_map/while/body/eval_jaxpr/ppermute | solution.py:16
  729.9 25.1 %collective-permute-start.1 = (bf16[128,2048]{1,0:T(8,128)(2,1)}, bf16[128,2048]{1,0:T(8,128)(2,1)S(1)}, u32[]{:S(2)}, u32[]{:S(2)}) collective-permute-start(bf16[128,2048]{1,0:T(8,128)(2,1)} %get-tuple-element.1393), channel_id=1, source_target_pairs={{32,0},{64,32},{96,64},{128,96},{160,128},{192,160},{224,192},{33,... | collective-permute-start | bytes 1572872 | tf_op jit(solution)/shard_map/while/body/eval_jaxpr/ppermute | solution.py:16
  754.9 7.0 collective-permute-done.1
  762.0 318.0 %reduce-scatter.2.cloned.1.call-done = f32[64,2048]{1,0:T(8,128)} async-done(((f32[2048,2048]{1,0:T(8,128)}), f32[64,2048]{1,0:T(8,128)}) %reduce-scatter.2.cloned.1.call-update) | async-done | bytes 524304 | tf_op jit(solution)/shard_map/reduce_scatter | solution.py:198
  (227 shorter events, 191.6 us)
Async XLA Ops:
  6.5 1073.5 %reduce-scatter.2.cloned.1.call-start = ((), (), s32[]{:S(2)}) async-start(), calls=%async_computation.1 | async-start | bytes 17301504 | tf_op jit(solution)/shard_map/reduce_scatter | solution.py:198
  13.8 5.8 copy-start.2
  19.8 20.2 %collective-permute-start = (bf16[128,2048]{0,1:T(8,128)(2,1)S(1)}, bf16[128,2048]{0,1:T(8,128)(2,1)S(1)}, u32[]{:S(2)}, u32[]{:S(2)}) collective-permute-start(bf16[128,2048]{0,1:T(8,128)(2,1)S(1)} %get-tuple-element.1371), channel_id=1, source_target_pairs={{0,32},{32,64},{64,96},{96,128},{128,160},{160,192},{192,224},{1,3... | collective-permute-start | bytes 1572872 | tf_op jit(solution)/shard_map/while/body/eval_jaxpr/ppermute | solution.py:16
  40.1 20.7 %collective-permute-start = (bf16[128,2048]{0,1:T(8,128)(2,1)S(1)}, bf16[128,2048]{0,1:T(8,128)(2,1)S(1)}, u32[]{:S(2)}, u32[]{:S(2)}) collective-permute-start(bf16[128,2048]{0,1:T(8,128)(2,1)S(1)} %get-tuple-element.1371), channel_id=1, source_target_pairs={{0,32},{32,64},{64,96},{96,128},{128,160},{160,192},{192,224},{1,3... | collective-permute-start | bytes 1572872 | tf_op jit(solution)/shard_map/while/body/eval_jaxpr/ppermute | solution.py:16
  60.9 29.9 %collective-permute-start = (bf16[128,2048]{0,1:T(8,128)(2,1)S(1)}, bf16[128,2048]{0,1:T(8,128)(2,1)S(1)}, u32[]{:S(2)}, u32[]{:S(2)}) collective-permute-start(bf16[128,2048]{0,1:T(8,128)(2,1)S(1)} %get-tuple-element.1371), channel_id=1, source_target_pairs={{0,32},{32,64},{64,96},{96,128},{128,160},{160,192},{192,224},{1,3... | collective-permute-start | bytes 1572872 | tf_op jit(solution)/shard_map/while/body/eval_jaxpr/ppermute | solution.py:16
  102.9 11.1 %collective-permute-start = (bf16[128,2048]{0,1:T(8,128)(2,1)S(1)}, bf16[128,2048]{0,1:T(8,128)(2,1)S(1)}, u32[]{:S(2)}, u32[]{:S(2)}) collective-permute-start(bf16[128,2048]{0,1:T(8,128)(2,1)S(1)} %get-tuple-element.1371), channel_id=1, source_target_pairs={{0,32},{32,64},{64,96},{96,128},{128,160},{160,192},{192,224},{1,3... | collective-permute-start | bytes 1572872 | tf_op jit(solution)/shard_map/while/body/eval_jaxpr/ppermute | solution.py:16
  126.2 14.9 %collective-permute-start = (bf16[128,2048]{0,1:T(8,128)(2,1)S(1)}, bf16[128,2048]{0,1:T(8,128)(2,1)S(1)}, u32[]{:S(2)}, u32[]{:S(2)}) collective-permute-start(bf16[128,2048]{0,1:T(8,128)(2,1)S(1)} %get-tuple-element.1371), channel_id=1, source_target_pairs={{0,32},{32,64},{64,96},{96,128},{128,160},{160,192},{192,224},{1,3... | collective-permute-start | bytes 1572872 | tf_op jit(solution)/shard_map/while/body/eval_jaxpr/ppermute | solution.py:16
  153.1 17.3 %collective-permute-start = (bf16[128,2048]{0,1:T(8,128)(2,1)S(1)}, bf16[128,2048]{0,1:T(8,128)(2,1)S(1)}, u32[]{:S(2)}, u32[]{:S(2)}) collective-permute-start(bf16[128,2048]{0,1:T(8,128)(2,1)S(1)} %get-tuple-element.1371), channel_id=1, source_target_pairs={{0,32},{32,64},{64,96},{96,128},{128,160},{160,192},{192,224},{1,3... | collective-permute-start | bytes 1572872 | tf_op jit(solution)/shard_map/while/body/eval_jaxpr/ppermute | solution.py:16
  182.4 17.1 %collective-permute-start = (bf16[128,2048]{0,1:T(8,128)(2,1)S(1)}, bf16[128,2048]{0,1:T(8,128)(2,1)S(1)}, u32[]{:S(2)}, u32[]{:S(2)}) collective-permute-start(bf16[128,2048]{0,1:T(8,128)(2,1)S(1)} %get-tuple-element.1371), channel_id=1, source_target_pairs={{0,32},{32,64},{64,96},{96,128},{128,160},{160,192},{192,224},{1,3... | collective-permute-start | bytes 1572872 | tf_op jit(solution)/shard_map/while/body/eval_jaxpr/ppermute | solution.py:16
  199.6 29.0 %collective-permute-start = (bf16[128,2048]{0,1:T(8,128)(2,1)S(1)}, bf16[128,2048]{0,1:T(8,128)(2,1)S(1)}, u32[]{:S(2)}, u32[]{:S(2)}) collective-permute-start(bf16[128,2048]{0,1:T(8,128)(2,1)S(1)} %get-tuple-element.1371), channel_id=1, source_target_pairs={{0,32},{32,64},{64,96},{96,128},{128,160},{160,192},{192,224},{1,3... | collective-permute-start | bytes 1572872 | tf_op jit(solution)/shard_map/while/body/eval_jaxpr/ppermute | solution.py:16
  228.7 17.6 %collective-permute-start = (bf16[128,2048]{0,1:T(8,128)(2,1)S(1)}, bf16[128,2048]{0,1:T(8,128)(2,1)S(1)}, u32[]{:S(2)}, u32[]{:S(2)}) collective-permute-start(bf16[128,2048]{0,1:T(8,128)(2,1)S(1)} %get-tuple-element.1371), channel_id=1, source_target_pairs={{0,32},{32,64},{64,96},{96,128},{128,160},{160,192},{192,224},{1,3... | collective-permute-start | bytes 1572872 | tf_op jit(solution)/shard_map/while/body/eval_jaxpr/ppermute | solution.py:16
  246.4 22.6 %collective-permute-start = (bf16[128,2048]{0,1:T(8,128)(2,1)S(1)}, bf16[128,2048]{0,1:T(8,128)(2,1)S(1)}, u32[]{:S(2)}, u32[]{:S(2)}) collective-permute-start(bf16[128,2048]{0,1:T(8,128)(2,1)S(1)} %get-tuple-element.1371), channel_id=1, source_target_pairs={{0,32},{32,64},{64,96},{96,128},{128,160},{160,192},{192,224},{1,3... | collective-permute-start | bytes 1572872 | tf_op jit(solution)/shard_map/while/body/eval_jaxpr/ppermute | solution.py:16
  269.0 17.2 %collective-permute-start = (bf16[128,2048]{0,1:T(8,128)(2,1)S(1)}, bf16[128,2048]{0,1:T(8,128)(2,1)S(1)}, u32[]{:S(2)}, u32[]{:S(2)}) collective-permute-start(bf16[128,2048]{0,1:T(8,128)(2,1)S(1)} %get-tuple-element.1371), channel_id=1, source_target_pairs={{0,32},{32,64},{64,96},{96,128},{128,160},{160,192},{192,224},{1,3... | collective-permute-start | bytes 1572872 | tf_op jit(solution)/shard_map/while/body/eval_jaxpr/ppermute | solution.py:16
  297.0 4.1 copy-start.1
  313.0 22.5 %collective-permute-start.1 = (bf16[128,2048]{1,0:T(8,128)(2,1)}, bf16[128,2048]{1,0:T(8,128)(2,1)S(1)}, u32[]{:S(2)}, u32[]{:S(2)}) collective-permute-start(bf16[128,2048]{1,0:T(8,128)(2,1)} %get-tuple-element.1393), channel_id=1, source_target_pairs={{32,0},{64,32},{96,64},{128,96},{160,128},{192,160},{224,192},{33,... | collective-permute-start | bytes 1572872 | tf_op jit(solution)/shard_map/while/body/eval_jaxpr/ppermute | solution.py:16
  336.4 22.8 %collective-permute-start.1 = (bf16[128,2048]{1,0:T(8,128)(2,1)}, bf16[128,2048]{1,0:T(8,128)(2,1)S(1)}, u32[]{:S(2)}, u32[]{:S(2)}) collective-permute-start(bf16[128,2048]{1,0:T(8,128)(2,1)} %get-tuple-element.1393), channel_id=1, source_target_pairs={{32,0},{64,32},{96,64},{128,96},{160,128},{192,160},{224,192},{33,... | collective-permute-start | bytes 1572872 | tf_op jit(solution)/shard_map/while/body/eval_jaxpr/ppermute | solution.py:16
  360.1 17.4 %collective-permute-start.1 = (bf16[128,2048]{1,0:T(8,128)(2,1)}, bf16[128,2048]{1,0:T(8,128)(2,1)S(1)}, u32[]{:S(2)}, u32[]{:S(2)}) collective-permute-start(bf16[128,2048]{1,0:T(8,128)(2,1)} %get-tuple-element.1393), channel_id=1, source_target_pairs={{32,0},{64,32},{96,64},{128,96},{160,128},{192,160},{224,192},{33,... | collective-permute-start | bytes 1572872 | tf_op jit(solution)/shard_map/while/body/eval_jaxpr/ppermute | solution.py:16
  378.3 106.9 %collective-permute-start.1 = (bf16[128,2048]{1,0:T(8,128)(2,1)}, bf16[128,2048]{1,0:T(8,128)(2,1)S(1)}, u32[]{:S(2)}, u32[]{:S(2)}) collective-permute-start(bf16[128,2048]{1,0:T(8,128)(2,1)} %get-tuple-element.1393), channel_id=1, source_target_pairs={{32,0},{64,32},{96,64},{128,96},{160,128},{192,160},{224,192},{33,... | collective-permute-start | bytes 1572872 | tf_op jit(solution)/shard_map/while/body/eval_jaxpr/ppermute | solution.py:16
  488.3 3.6 copy-start
  492.8 16.1 %slice-start = ((s8[8388608]{0:T(1024)(128)(4,1)}), s8[4194304]{0:T(1024)(128)(4,1)S(1)}, s32[]{:S(2)}) async-start(s8[8388608]{0:T(1024)(128)(4,1)} %bitcast.124), calls=%async_computation.2 | async-start | bytes 8388608 | tf_op jit(solution)/shard_map/while/body/eval_jaxpr/cond
  494.6 14.4 %slice-start.1 = ((s8[8388608]{0:T(1024)(128)(4,1)}), s8[4194304]{0:T(1024)(128)(4,1)S(1)}, s32[]{:S(2)}) async-start(s8[8388608]{0:T(1024)(128)(4,1)} %bitcast.124), calls=%async_computation.3 | async-start | bytes 8388608 | tf_op jit(solution)/shard_map/while/body/eval_jaxpr/cond
  515.8 17.3 %collective-permute-start.1 = (bf16[128,2048]{1,0:T(8,128)(2,1)}, bf16[128,2048]{1,0:T(8,128)(2,1)S(1)}, u32[]{:S(2)}, u32[]{:S(2)}) collective-permute-start(bf16[128,2048]{1,0:T(8,128)(2,1)} %get-tuple-element.1393), channel_id=1, source_target_pairs={{32,0},{64,32},{96,64},{128,96},{160,128},{192,160},{224,192},{33,... | collective-permute-start | bytes 1572872 | tf_op jit(solution)/shard_map/while/body/eval_jaxpr/ppermute | solution.py:16
  536.2 3.6 copy-start
  540.7 16.1 %slice-start = ((s8[8388608]{0:T(1024)(128)(4,1)}), s8[4194304]{0:T(1024)(128)(4,1)S(1)}, s32[]{:S(2)}) async-start(s8[8388608]{0:T(1024)(128)(4,1)} %bitcast.124), calls=%async_computation.2 | async-start | bytes 8388608 | tf_op jit(solution)/shard_map/while/body/eval_jaxpr/cond
  542.5 14.4 %slice-start.1 = ((s8[8388608]{0:T(1024)(128)(4,1)}), s8[4194304]{0:T(1024)(128)(4,1)S(1)}, s32[]{:S(2)}) async-start(s8[8388608]{0:T(1024)(128)(4,1)} %bitcast.124), calls=%async_computation.3 | async-start | bytes 8388608 | tf_op jit(solution)/shard_map/while/body/eval_jaxpr/cond
  563.7 17.3 %collective-permute-start.1 = (bf16[128,2048]{1,0:T(8,128)(2,1)}, bf16[128,2048]{1,0:T(8,128)(2,1)S(1)}, u32[]{:S(2)}, u32[]{:S(2)}) collective-permute-start(bf16[128,2048]{1,0:T(8,128)(2,1)} %get-tuple-element.1393), channel_id=1, source_target_pairs={{32,0},{64,32},{96,64},{128,96},{160,128},{192,160},{224,192},{33,... | collective-permute-start | bytes 1572872 | tf_op jit(solution)/shard_map/while/body/eval_jaxpr/ppermute | solution.py:16
  584.1 3.6 copy-start
  588.6 16.1 %slice-start = ((s8[8388608]{0:T(1024)(128)(4,1)}), s8[4194304]{0:T(1024)(128)(4,1)S(1)}, s32[]{:S(2)}) async-start(s8[8388608]{0:T(1024)(128)(4,1)} %bitcast.124), calls=%async_computation.2 | async-start | bytes 8388608 | tf_op jit(solution)/shard_map/while/body/eval_jaxpr/cond
  590.4 14.4 %slice-start.1 = ((s8[8388608]{0:T(1024)(128)(4,1)}), s8[4194304]{0:T(1024)(128)(4,1)S(1)}, s32[]{:S(2)}) async-start(s8[8388608]{0:T(1024)(128)(4,1)} %bitcast.124), calls=%async_computation.3 | async-start | bytes 8388608 | tf_op jit(solution)/shard_map/while/body/eval_jaxpr/cond
  611.6 17.3 %collective-permute-start.1 = (bf16[128,2048]{1,0:T(8,128)(2,1)}, bf16[128,2048]{1,0:T(8,128)(2,1)S(1)}, u32[]{:S(2)}, u32[]{:S(2)}) collective-permute-start(bf16[128,2048]{1,0:T(8,128)(2,1)} %get-tuple-element.1393), channel_id=1, source_target_pairs={{32,0},{64,32},{96,64},{128,96},{160,128},{192,160},{224,192},{33,... | collective-permute-start | bytes 1572872 | tf_op jit(solution)/shard_map/while/body/eval_jaxpr/ppermute | solution.py:16
  632.0 3.6 copy-start
  636.5 16.1 %slice-start = ((s8[8388608]{0:T(1024)(128)(4,1)}), s8[4194304]{0:T(1024)(128)(4,1)S(1)}, s32[]{:S(2)}) async-start(s8[8388608]{0:T(1024)(128)(4,1)} %bitcast.124), calls=%async_computation.2 | async-start | bytes 8388608 | tf_op jit(solution)/shard_map/while/body/eval_jaxpr/cond
  638.3 14.4 %slice-start.1 = ((s8[8388608]{0:T(1024)(128)(4,1)}), s8[4194304]{0:T(1024)(128)(4,1)S(1)}, s32[]{:S(2)}) async-start(s8[8388608]{0:T(1024)(128)(4,1)} %bitcast.124), calls=%async_computation.3 | async-start | bytes 8388608 | tf_op jit(solution)/shard_map/while/body/eval_jaxpr/cond
  659.5 19.6 %collective-permute-start.1 = (bf16[128,2048]{1,0:T(8,128)(2,1)}, bf16[128,2048]{1,0:T(8,128)(2,1)S(1)}, u32[]{:S(2)}, u32[]{:S(2)}) collective-permute-start(bf16[128,2048]{1,0:T(8,128)(2,1)} %get-tuple-element.1393), channel_id=1, source_target_pairs={{32,0},{64,32},{96,64},{128,96},{160,128},{192,160},{224,192},{33,... | collective-permute-start | bytes 1572872 | tf_op jit(solution)/shard_map/while/body/eval_jaxpr/ppermute | solution.py:16
  679.9 30.4 %collective-permute-start.1 = (bf16[128,2048]{1,0:T(8,128)(2,1)}, bf16[128,2048]{1,0:T(8,128)(2,1)S(1)}, u32[]{:S(2)}, u32[]{:S(2)}) collective-permute-start(bf16[128,2048]{1,0:T(8,128)(2,1)} %get-tuple-element.1393), channel_id=1, source_target_pairs={{32,0},{64,32},{96,64},{128,96},{160,128},{192,160},{224,192},{33,... | collective-permute-start | bytes 1572872 | tf_op jit(solution)/shard_map/while/body/eval_jaxpr/ppermute | solution.py:16
  711.1 17.9 %collective-permute-start.1 = (bf16[128,2048]{1,0:T(8,128)(2,1)}, bf16[128,2048]{1,0:T(8,128)(2,1)S(1)}, u32[]{:S(2)}, u32[]{:S(2)}) collective-permute-start(bf16[128,2048]{1,0:T(8,128)(2,1)} %get-tuple-element.1393), channel_id=1, source_target_pairs={{32,0},{64,32},{96,64},{128,96},{160,128},{192,160},{224,192},{33,... | collective-permute-start | bytes 1572872 | tf_op jit(solution)/shard_map/while/body/eval_jaxpr/ppermute | solution.py:16
  729.9 32.1 %collective-permute-start.1 = (bf16[128,2048]{1,0:T(8,128)(2,1)}, bf16[128,2048]{1,0:T(8,128)(2,1)S(1)}, u32[]{:S(2)}, u32[]{:S(2)}) collective-permute-start(bf16[128,2048]{1,0:T(8,128)(2,1)} %get-tuple-element.1393), channel_id=1, source_target_pairs={{32,0},{64,32},{96,64},{128,96},{160,128},{192,160},{224,192},{33,... | collective-permute-start | bytes 1572872 | tf_op jit(solution)/shard_map/while/body/eval_jaxpr/ppermute | solution.py:16
Sparse Core Ops, SparseCore 0:
  762.1 317.8 reduce-scatter.1
where the time goes:
time: 1090 us
  waiting for transfers between devices  672 us (62%)
  starting transfers between devices  185 us (17%)
  matrix products  123 us (11%)
  local copies, waits for them, and re-layouts  49.8 us (5%)
  other arithmetic  42.8 us (4%)
  between operations  13.5 us (1%)
    ppermute x22, waiting for transfers between devices, passed_along(): return lax.ppermute(block, axis, route)  354 us
    reduce_scatter x1, waiting for transfers between devices, per_device(): summed = lax.psum_scatter(collected, 'dp', scatter_dimension=0, tiled=True)  318 us
    ppermute x22, starting transfers between devices, passed_along(): return lax.ppermute(block, axis, route)  185 us
    dot_general x4, matrix products, backward_do_work(): lax.dot_general(normed, value_total.reshape(buses, width), (((0,), (0,)),...  57.4 us
  transfers between devices with their start and end apart: 23, of which 23 were waited for; matrix products, arithmetic and copies ran while one was open for 0% of the time, Pallas kernels for 0%

commit v1 on v0

--- a/solution.py
+++ b/solution.py
@@ -1,7 +1,7 @@
 import jax
 import jax.numpy as jnp
 from jax import lax
-from jax.sharding import PartitionSpec as P
+from jax.sharding import Mesh, PartitionSpec as P
 
 HEADS = 16
 BLOCK = 32
@@ -158,7 +158,7 @@
     unused_rows, stashed, upstream_stash = lax.fori_loop(
         0, steps_total, forward_step, (zero_rows, stash_init, upstream_init)
     )
-    grad_init = jnp.zeros((width, width), jnp.float32)
+    totals_init = jnp.zeros((micro, buses, width), jnp.bfloat16)
 
     def backward_step(step, carry):
         incoming, collected = carry
@@ -177,14 +177,7 @@
                 )
             )
             lower, value_total = layer_backward(upstream, weight, allowed_slot, kept_parts)
-            normed = kept_parts[0].astype(jnp.bfloat16).reshape(buses, width)
-            product = lax.dot_general(
-                normed,
-                value_total.reshape(buses, width),
-                (((0,), (0,)), ((), ())),
-                preferred_element_type=jnp.float32,
-            )
-            collected_out = collected_in + product
+            collected_out = lax.dynamic_update_index_in_dim(collected_in, value_total, slot, 0)
             return (lower[0], collected_out)
 
         def backward_no_work(collected_in):
@@ -194,21 +187,36 @@
         passed = passed_along(lower, "section", -1)
         return (passed, collected)
 
-    unused_rows, collected = lax.fori_loop(0, steps_total, backward_step, (zero_rows, grad_init))
-    summed = lax.psum_scatter(collected, "dp", scatter_dimension=0, tiled=True)
+    unused_rows, collected = lax.fori_loop(0, steps_total, backward_step, (zero_rows, totals_init))
+    cores = lax.axis_size("core")
+    groups = lax.axis_size("dp_hi")
+    rows_each = width // (groups * cores)
+    normed_all = stashed[0].astype(jnp.bfloat16).reshape(micro * buses, groups, cores, rows_each)
+    normed_all = jnp.swapaxes(normed_all, 1, 2).reshape(micro * buses, width)
+    grad = lax.dot_general(
+        normed_all,
+        collected.reshape(micro * buses, width),
+        (((0,), (0,)), ((), ())),
+        preferred_element_type=jnp.float32,
+    )
+    half = lax.psum_scatter(grad, "core", scatter_dimension=0, tiled=True)
+    summed = lax.psum_scatter(half, "dp_hi", scatter_dimension=0, tiled=True)
     return summed[None]
 
 
 def solution(mesh):
+    sections, dp = mesh.devices.shape
+    split = Mesh(mesh.devices.reshape(sections, dp // 2, 2), ("section", "dp_hi", "core"))
+    rows = ("dp_hi", "core")
     in_specs = (
-        P("dp", None, None),
-        P("dp", None),
-        P("dp", None),
+        P(rows, None, None),
+        P(rows, None),
+        P(rows, None),
         P(),
         P("section", None, None),
         P(),
     )
-    out_specs = P("section", "dp", None)
+    out_specs = P("section", rows, None)
     return jax.shard_map(
-        per_device, mesh=mesh, in_specs=in_specs, out_specs=out_specs, check_vma=False
-    )
+        per_device, mesh=split, in_specs=in_specs, out_specs=out_specs, check_vma=False
+    )

time: 1090 us -> 946 us (0.87)
  the two profiles are of different devices: /device:TPU:6 before, /device:TPU:96 now
where the time goes in v1:
time: 946 us; the launch traced here: 935 us
  waiting for transfers between devices  599 us (63%)
  starting transfers between devices  132 us (14%)
  matrix products  71.7 us (8%)
  local copies, waits for them, and re-layouts  67.5 us (7%)
  other arithmetic  50.6 us (5%)
  between operations  13.5 us (1%)
    ppermute x22, waiting for transfers between devices, passed_along(): return lax.ppermute(block, axis, route)  362 us
    reduce_scatter x1, waiting for transfers between devices, per_device(): half = lax.psum_scatter(grad, 'core', scatter_dimension=0, tiled=True)  134 us
    ppermute x22, starting transfers between devices, passed_along(): return lax.ppermute(block, axis, route)  132 us
    reduce_scatter x1, waiting for transfers between devices, per_device(): summed = lax.psum_scatter(half, 'dp_hi', scatter_dimension=0, tiled=True)  104 us
    unnamed x13, local copies, waits for them, and re-layouts  23.6 us
  transfers between devices with their start and end apart: 24, of which 24 were waited for; matrix products, arithmetic and copies ran while one was open for 0% of the time, Pallas kernels for 0%

profile of v1, /device:TPU:96, one launch (start us, length us, event | category | flops | bytes accessed | tf_op | source)
XLA Modules:
  0.0 935.2 jit_solution(14030761050844992930)
XLA Ops:
  20.6 259.0 %while.48 = (s32[]{:T(128)}, bf16[128,2048]{0,1:T(8,128)(2,1)S(1)}, f32[4,128,2048]{1,2,0:T(8,128)}, f32[4,128,1]{1,2,0:T(1,128)S(1)}, bf16[4,128,16,128]{3,2,1,...) while((s32[]{:T(128)}, bf16[128,2048]{0,1:T(8,128)(2,1)S(1)}, ...), condition=%wide.region_8.9_spmd.clone, body=%wide.region_1.8_spmd.clone.sunk | while | flops 1216641408 | bytes 26020904 | solution.py:158
  20.6 13.1 %conditional.6 = (bf16[128,2048]{0,1:T(8,128)(2,1)S(1)}, f32[4,128,2048]{1,2,0:T(8,128)}, f32[4,128,1]{1,2,0:T(1,128)S(1)}, bf16[4,128,16,128]{3,2,1,0:T(8,128)(...) conditional(s32[]{:T(128)} %convert_element_type.254, ...), branch_computations={%region_2.2_spmd, %region_3.7_spmd} | conditional | flops 1216641408 | bytes 23923316 | solution.py:152
  22.3 4.7 convolution_convert_fusion
  35.1 11.4 %collective-permute-done = bf16[128,2048]{0,1:T(8,128)(2,1)S(1)} collective-permute-done((bf16[128,2048]{0,1:T(8,128)(2,1)S(1)}, bf16[128,2048]{0,1:T(8,128)(2,1)S(1)}, u32[]{:S(2)}, u32[]{:S(2)}) %collective-permute-start) | collective-permute-done | bytes 524320 | tf_op jit(solution)/shard_map/while/body/eval_jaxpr/ppermute | solution.py:16
  46.5 13.1 %conditional.6 = (bf16[128,2048]{0,1:T(8,128)(2,1)S(1)}, f32[4,128,2048]{1,2,0:T(8,128)}, f32[4,128,1]{1,2,0:T(1,128)S(1)}, bf16[4,128,16,128]{3,2,1,0:T(8,128)(...) conditional(s32[]{:T(128)} %convert_element_type.254, ...), branch_computations={%region_2.2_spmd, %region_3.7_spmd} | conditional | flops 1216641408 | bytes 23923316 | solution.py:152
  48.1 4.7 convolution_convert_fusion
  64.0 10.6 %collective-permute-done = bf16[128,2048]{0,1:T(8,128)(2,1)S(1)} collective-permute-done((bf16[128,2048]{0,1:T(8,128)(2,1)S(1)}, bf16[128,2048]{0,1:T(8,128)(2,1)S(1)}, u32[]{:S(2)}, u32[]{:S(2)}) %collective-permute-start) | collective-permute-done | bytes 524320 | tf_op jit(solution)/shard_map/while/body/eval_jaxpr/ppermute | solution.py:16
  74.6 13.1 %conditional.6 = (bf16[128,2048]{0,1:T(8,128)(2,1)S(1)}, f32[4,128,2048]{1,2,0:T(8,128)}, f32[4,128,1]{1,2,0:T(1,128)S(1)}, bf16[4,128,16,128]{3,2,1,0:T(8,128)(...) conditional(s32[]{:T(128)} %convert_element_type.254, ...), branch_computations={%region_2.2_spmd, %region_3.7_spmd} | conditional | flops 1216641408 | bytes 23923316 | solution.py:152
  76.2 4.7 convolution_convert_fusion
  92.1 9.6 %collective-permute-done = bf16[128,2048]{0,1:T(8,128)(2,1)S(1)} collective-permute-done((bf16[128,2048]{0,1:T(8,128)(2,1)S(1)}, bf16[128,2048]{0,1:T(8,128)(2,1)S(1)}, u32[]{:S(2)}, u32[]{:S(2)}) %collective-permute-start) | collective-permute-done | bytes 524320 | tf_op jit(solution)/shard_map/while/body/eval_jaxpr/ppermute | solution.py:16
  101.7 13.1 %conditional.6 = (bf16[128,2048]{0,1:T(8,128)(2,1)S(1)}, f32[4,128,2048]{1,2,0:T(8,128)}, f32[4,128,1]{1,2,0:T(1,128)S(1)}, bf16[4,128,16,128]{3,2,1,0:T(8,128)(...) conditional(s32[]{:T(128)} %convert_element_type.254, ...), branch_computations={%region_2.2_spmd, %region_3.7_spmd} | conditional | flops 1216641408 | bytes 23923316 | solution.py:152
  103.3 4.7 convolution_convert_fusion
  119.2 8.7 collective-permute-done
  128.0 17.4 %collective-permute-start = (bf16[128,2048]{0,1:T(8,128)(2,1)S(1)}, bf16[128,2048]{0,1:T(8,128)(2,1)S(1)}, u32[]{:S(2)}, u32[]{:S(2)}) collective-permute-start(bf16[128,2048]{0,1:T(8,128)(2,1)S(1)} %get-tuple-element.1371), channel_id=1, source_target_pairs={{0,32},{32,64},{64,96},{96,128},{128,160},{160,192},{192,224},{1,3... | collective-permute-start | bytes 1572872 | tf_op jit(solution)/shard_map/while/body/eval_jaxpr/ppermute | solution.py:16
  145.4 7.8 collective-permute-done
  157.7 6.9 collective-permute-done
  164.7 16.4 %collective-permute-start = (bf16[128,2048]{0,1:T(8,128)(2,1)S(1)}, bf16[128,2048]{0,1:T(8,128)(2,1)S(1)}, u32[]{:S(2)}, u32[]{:S(2)}) collective-permute-start(bf16[128,2048]{0,1:T(8,128)(2,1)S(1)} %get-tuple-element.1371), channel_id=1, source_target_pairs={{0,32},{32,64},{64,96},{96,128},{128,160},{160,192},{192,224},{1,3... | collective-permute-start | bytes 1572872 | tf_op jit(solution)/shard_map/while/body/eval_jaxpr/ppermute | solution.py:16
  181.1 6.6 collective-permute-done
  187.8 7.5 collective-permute-start
  195.3 6.6 collective-permute-done
  202.1 23.4 %collective-permute-start = (bf16[128,2048]{0,1:T(8,128)(2,1)S(1)}, bf16[128,2048]{0,1:T(8,128)(2,1)S(1)}, u32[]{:S(2)}, u32[]{:S(2)}) collective-permute-start(bf16[128,2048]{0,1:T(8,128)(2,1)S(1)} %get-tuple-element.1371), channel_id=1, source_target_pairs={{0,32},{32,64},{64,96},{96,128},{128,160},{160,192},{192,224},{1,3... | collective-permute-start | bytes 1572872 | tf_op jit(solution)/shard_map/while/body/eval_jaxpr/ppermute | solution.py:16
  225.5 6.6 collective-permute-done
  232.2 10.5 %collective-permute-start = (bf16[128,2048]{0,1:T(8,128)(2,1)S(1)}, bf16[128,2048]{0,1:T(8,128)(2,1)S(1)}, u32[]{:S(2)}, u32[]{:S(2)}) collective-permute-start(bf16[128,2048]{0,1:T(8,128)(2,1)S(1)} %get-tuple-element.1371), channel_id=1, source_target_pairs={{0,32},{32,64},{64,96},{96,128},{128,160},{160,192},{192,224},{1,3... | collective-permute-start | bytes 1572872 | tf_op jit(solution)/shard_map/while/body/eval_jaxpr/ppermute | solution.py:16
  242.7 6.6 collective-permute-done
  249.5 23.4 %collective-permute-start = (bf16[128,2048]{0,1:T(8,128)(2,1)S(1)}, bf16[128,2048]{0,1:T(8,128)(2,1)S(1)}, u32[]{:S(2)}, u32[]{:S(2)}) collective-permute-start(bf16[128,2048]{0,1:T(8,128)(2,1)S(1)} %get-tuple-element.1371), channel_id=1, source_target_pairs={{0,32},{32,64},{64,96},{96,128},{128,160},{160,192},{192,224},{1,3... | collective-permute-start | bytes 1572872 | tf_op jit(solution)/shard_map/while/body/eval_jaxpr/ppermute | solution.py:16
  272.9 6.6 collective-permute-done
  279.5 5.5 copy.62
  288.8 5.5 copy.60
  303.2 360.5 %while.49 = (s32[]{:T(128)}, bf16[128,2048]{1,0:T(8,128)(2,1)S(1)}, bf16[4,128,2048]{1,2,0:T(8,128)(2,1)}, s32[]{:T(128)}, pred[]{:T(512)}, /*index=5*/bf16[4,12...) while((s32[]{:T(128)}, bf16[128,2048]{1,0:T(8,128)(2,1)S(1)}, ...), condition=%wide.region_15.16_spmd.clone, body=%wide.region_9.15_spmd.clone.sunk | while | flops 1353218048 | bytes 71172608 | solution.py:190
  305.5 16.6 %collective-permute-done.1 = bf16[128,2048]{1,0:T(8,128)(2,1)S(1)} collective-permute-done((bf16[128,2048]{1,0:T(8,128)(2,1)}, bf16[128,2048]{1,0:T(8,128)(2,1)S(1)}, u32[]{:S(2)}, u32[]{:S(2)}) %collective-permute-start.1) | collective-permute-done | bytes 524320 | tf_op jit(solution)/shard_map/while/body/eval_jaxpr/ppermute | solution.py:16
  324.2 19.4 %collective-permute-done.1 = bf16[128,2048]{1,0:T(8,128)(2,1)S(1)} collective-permute-done((bf16[128,2048]{1,0:T(8,128)(2,1)}, bf16[128,2048]{1,0:T(8,128)(2,1)S(1)}, u32[]{:S(2)}, u32[]{:S(2)}) %collective-permute-start.1) | collective-permute-done | bytes 524320 | tf_op jit(solution)/shard_map/while/body/eval_jaxpr/ppermute | solution.py:16
  345.8 19.2 %collective-permute-done.1 = bf16[128,2048]{1,0:T(8,128)(2,1)S(1)} collective-permute-done((bf16[128,2048]{1,0:T(8,128)(2,1)}, bf16[128,2048]{1,0:T(8,128)(2,1)S(1)}, u32[]{:S(2)}, u32[]{:S(2)}) %collective-permute-start.1) | collective-permute-done | bytes 524320 | tf_op jit(solution)/shard_map/while/body/eval_jaxpr/ppermute | solution.py:16
  367.1 22.8 %collective-permute-done.1 = bf16[128,2048]{1,0:T(8,128)(2,1)S(1)} collective-permute-done((bf16[128,2048]{1,0:T(8,128)(2,1)}, bf16[128,2048]{1,0:T(8,128)(2,1)S(1)}, u32[]{:S(2)}, u32[]{:S(2)}) %collective-permute-start.1) | collective-permute-done | bytes 524320 | tf_op jit(solution)/shard_map/while/body/eval_jaxpr/ppermute | solution.py:16
  392.1 21.8 %collective-permute-done.1 = bf16[128,2048]{1,0:T(8,128)(2,1)S(1)} collective-permute-done((bf16[128,2048]{1,0:T(8,128)(2,1)}, bf16[128,2048]{1,0:T(8,128)(2,1)S(1)}, u32[]{:S(2)}, u32[]{:S(2)}) %collective-permute-start.1) | collective-permute-done | bytes 524320 | tf_op jit(solution)/shard_map/while/body/eval_jaxpr/ppermute | solution.py:16
  416.1 10.0 %collective-permute-done.1 = bf16[128,2048]{1,0:T(8,128)(2,1)S(1)} collective-permute-done((bf16[128,2048]{1,0:T(8,128)(2,1)}, bf16[128,2048]{1,0:T(8,128)(2,1)S(1)}, u32[]{:S(2)}, u32[]{:S(2)}) %collective-permute-start.1) | collective-permute-done | bytes 524320 | tf_op jit(solution)/shard_map/while/body/eval_jaxpr/ppermute | solution.py:16
  428.2 105.3 %collective-permute-done.1 = bf16[128,2048]{1,0:T(8,128)(2,1)S(1)} collective-permute-done((bf16[128,2048]{1,0:T(8,128)(2,1)}, bf16[128,2048]{1,0:T(8,128)(2,1)S(1)}, u32[]{:S(2)}, u32[]{:S(2)}) %collective-permute-start.1) | collective-permute-done | bytes 524320 | tf_op jit(solution)/shard_map/while/body/eval_jaxpr/ppermute | solution.py:16
  533.5 16.7 %conditional.7 = (bf16[128,2048]{1,0:T(8,128)(2,1)}, bf16[4,128,2048]{1,2,0:T(8,128)(2,1)}) conditional(s32[]{:T(128)} %convert_element_type.255, bf16[4,128,2048]{1,2,0:T(8,128)(2,1)} %get-tuple-element.1493, (pred[]{:T(512)}, s32[]{:T(128)}, bf16[4,128,2048]{2,1,0:T(8,128)(2,1)}, bf16[128,2048]{1,0:T(8,128)(2,1)S(1)}, ...), branch_computations={%region_10.10_spmd, %region_11.14_spmd} | conditional | flops 1353218048 | bytes 69075104 | solution.py:186
  551.5 16.1 %collective-permute-done.1 = bf16[128,2048]{1,0:T(8,128)(2,1)S(1)} collective-permute-done((bf16[128,2048]{1,0:T(8,128)(2,1)}, bf16[128,2048]{1,0:T(8,128)(2,1)S(1)}, u32[]{:S(2)}, u32[]{:S(2)}) %collective-permute-start.1) | collective-permute-done | bytes 524320 | tf_op jit(solution)/shard_map/while/body/eval_jaxpr/ppermute | solution.py:16
  567.6 16.7 %conditional.7 = (bf16[128,2048]{1,0:T(8,128)(2,1)}, bf16[4,128,2048]{1,2,0:T(8,128)(2,1)}) conditional(s32[]{:T(128)} %convert_element_type.255, bf16[4,128,2048]{1,2,0:T(8,128)(2,1)} %get-tuple-element.1493, (pred[]{:T(512)}, s32[]{:T(128)}, bf16[4,128,2048]{2,1,0:T(8,128)(2,1)}, bf16[128,2048]{1,0:T(8,128)(2,1)S(1)}, ...), branch_computations={%region_10.10_spmd, %region_11.14_spmd} | conditional | flops 1353218048 | bytes 69075104 | solution.py:186
  585.5 16.0 %collective-permute-done.1 = bf16[128,2048]{1,0:T(8,128)(2,1)S(1)} collective-permute-done((bf16[128,2048]{1,0:T(8,128)(2,1)}, bf16[128,2048]{1,0:T(8,128)(2,1)S(1)}, u32[]{:S(2)}, u32[]{:S(2)}) %collective-permute-start.1) | collective-permute-done | bytes 524320 | tf_op jit(solution)/shard_map/while/body/eval_jaxpr/ppermute | solution.py:16
  601.6 16.7 %conditional.7 = (bf16[128,2048]{1,0:T(8,128)(2,1)}, bf16[4,128,2048]{1,2,0:T(8,128)(2,1)}) conditional(s32[]{:T(128)} %convert_element_type.255, bf16[4,128,2048]{1,2,0:T(8,128)(2,1)} %get-tuple-element.1493, (pred[]{:T(512)}, s32[]{:T(128)}, bf16[4,128,2048]{2,1,0:T(8,128)(2,1)}, bf16[128,2048]{1,0:T(8,128)(2,1)S(1)}, ...), branch_computations={%region_10.10_spmd, %region_11.14_spmd} | conditional | flops 1353218048 | bytes 69075104 | solution.py:186
  619.5 16.1 %collective-permute-done.1 = bf16[128,2048]{1,0:T(8,128)(2,1)S(1)} collective-permute-done((bf16[128,2048]{1,0:T(8,128)(2,1)}, bf16[128,2048]{1,0:T(8,128)(2,1)S(1)}, u32[]{:S(2)}, u32[]{:S(2)}) %collective-permute-start.1) | collective-permute-done | bytes 524320 | tf_op jit(solution)/shard_map/while/body/eval_jaxpr/ppermute | solution.py:16
  635.7 16.7 %conditional.7 = (bf16[128,2048]{1,0:T(8,128)(2,1)}, bf16[4,128,2048]{1,2,0:T(8,128)(2,1)}) conditional(s32[]{:T(128)} %convert_element_type.255, bf16[4,128,2048]{1,2,0:T(8,128)(2,1)} %get-tuple-element.1493, (pred[]{:T(512)}, s32[]{:T(128)}, bf16[4,128,2048]{2,1,0:T(8,128)(2,1)}, bf16[128,2048]{1,0:T(8,128)(2,1)S(1)}, ...), branch_computations={%region_10.10_spmd, %region_11.14_spmd} | conditional | flops 1353218048 | bytes 69075104 | solution.py:186
  653.7 10.0 %collective-permute-done.1 = bf16[128,2048]{1,0:T(8,128)(2,1)S(1)} collective-permute-done((bf16[128,2048]{1,0:T(8,128)(2,1)}, bf16[128,2048]{1,0:T(8,128)(2,1)S(1)}, u32[]{:S(2)}, u32[]{:S(2)}) %collective-permute-start.1) | collective-permute-done | bytes 524320 | tf_op jit(solution)/shard_map/while/body/eval_jaxpr/ppermute | solution.py:16
  667.8 10.7 %copy.57 = bf16[4,128,2048]{1,0,2:T(4,128)(2,1)} copy(bf16[4,128,2048]{1,2,0:T(8,128)(2,1)S(1)} %copy-done.1) | data formatting | bytes 4194304 | tf_op jit(solution)/shard_map/convert_element_type | solution.py:194
  682.8 8.2 fusion.78
  691.1 133.6 %reduce-scatter.3.cloned.1.call-done = f32[1024,2048]{1,0:T(8,128)} async-done(((f32[2048,2048]{1,0:T(8,128)}), f32[1024,2048]{1,0:T(8,128)}) %reduce-scatter.3.cloned.1.call-update) | async-done | bytes 8388624 | tf_op jit(solution)/shard_map/reduce_scatter | solution.py:202
  824.7 103.6 %reduce-scatter.5.cloned.1.call-done = f32[64,2048]{1,0:T(8,128)} async-done(((f32[1024,2048]{1,0:T(8,128)}), f32[64,2048]{1,0:T(8,128)}) %reduce-scatter.5.cloned.1.call-update) | async-done | bytes 524304 | tf_op jit(solution)/shard_map/reduce_scatter | solution.py:203
  (240 shorter events, 181.0 us)
Async XLA Ops:
  6.5 818.2 %reduce-scatter.3.cloned.1.call-start = ((), (), s32[]{:S(2)}) async-start(), calls=%async_computation.2 | async-start | bytes 25165824 | tf_op jit(solution)/shard_map/reduce_scatter | solution.py:202
  17.2 3.3 copy-start.4
  33.7 12.7 %collective-permute-start = (bf16[128,2048]{0,1:T(8,128)(2,1)S(1)}, bf16[128,2048]{0,1:T(8,128)(2,1)S(1)}, u32[]{:S(2)}, u32[]{:S(2)}) collective-permute-start(bf16[128,2048]{0,1:T(8,128)(2,1)S(1)} %get-tuple-element.1371), channel_id=1, source_target_pairs={{0,32},{32,64},{64,96},{96,128},{128,160},{160,192},{192,224},{1,3... | collective-permute-start | bytes 1572872 | tf_op jit(solution)/shard_map/while/body/eval_jaxpr/ppermute | solution.py:16
  59.5 15.0 %collective-permute-start = (bf16[128,2048]{0,1:T(8,128)(2,1)S(1)}, bf16[128,2048]{0,1:T(8,128)(2,1)S(1)}, u32[]{:S(2)}, u32[]{:S(2)}) collective-permute-start(bf16[128,2048]{0,1:T(8,128)(2,1)S(1)} %get-tuple-element.1371), channel_id=1, source_target_pairs={{0,32},{32,64},{64,96},{96,128},{128,160},{160,192},{192,224},{1,3... | collective-permute-start | bytes 1572872 | tf_op jit(solution)/shard_map/while/body/eval_jaxpr/ppermute | solution.py:16
  87.6 14.1 %collective-permute-start = (bf16[128,2048]{0,1:T(8,128)(2,1)S(1)}, bf16[128,2048]{0,1:T(8,128)(2,1)S(1)}, u32[]{:S(2)}, u32[]{:S(2)}) collective-permute-start(bf16[128,2048]{0,1:T(8,128)(2,1)S(1)} %get-tuple-element.1371), channel_id=1, source_target_pairs={{0,32},{32,64},{64,96},{96,128},{128,160},{160,192},{192,224},{1,3... | collective-permute-start | bytes 1572872 | tf_op jit(solution)/shard_map/while/body/eval_jaxpr/ppermute | solution.py:16
  114.8 13.1 %collective-permute-start = (bf16[128,2048]{0,1:T(8,128)(2,1)S(1)}, bf16[128,2048]{0,1:T(8,128)(2,1)S(1)}, u32[]{:S(2)}, u32[]{:S(2)}) collective-permute-start(bf16[128,2048]{0,1:T(8,128)(2,1)S(1)} %get-tuple-element.1371), channel_id=1, source_target_pairs={{0,32},{32,64},{64,96},{96,128},{128,160},{160,192},{192,224},{1,3... | collective-permute-start | bytes 1572872 | tf_op jit(solution)/shard_map/while/body/eval_jaxpr/ppermute | solution.py:16
  128.0 25.2 %collective-permute-start = (bf16[128,2048]{0,1:T(8,128)(2,1)S(1)}, bf16[128,2048]{0,1:T(8,128)(2,1)S(1)}, u32[]{:S(2)}, u32[]{:S(2)}) collective-permute-start(bf16[128,2048]{0,1:T(8,128)(2,1)S(1)} %get-tuple-element.1371), channel_id=1, source_target_pairs={{0,32},{32,64},{64,96},{96,128},{128,160},{160,192},{192,224},{1,3... | collective-permute-start | bytes 1572872 | tf_op jit(solution)/shard_map/while/body/eval_jaxpr/ppermute | solution.py:16
  153.3 11.3 %collective-permute-start = (bf16[128,2048]{0,1:T(8,128)(2,1)S(1)}, bf16[128,2048]{0,1:T(8,128)(2,1)S(1)}, u32[]{:S(2)}, u32[]{:S(2)}) collective-permute-start(bf16[128,2048]{0,1:T(8,128)(2,1)S(1)} %get-tuple-element.1371), channel_id=1, source_target_pairs={{0,32},{32,64},{64,96},{96,128},{128,160},{160,192},{192,224},{1,3... | collective-permute-start | bytes 1572872 | tf_op jit(solution)/shard_map/while/body/eval_jaxpr/ppermute | solution.py:16
  164.7 23.1 %collective-permute-start = (bf16[128,2048]{0,1:T(8,128)(2,1)S(1)}, bf16[128,2048]{0,1:T(8,128)(2,1)S(1)}, u32[]{:S(2)}, u32[]{:S(2)}) collective-permute-start(bf16[128,2048]{0,1:T(8,128)(2,1)S(1)} %get-tuple-element.1371), channel_id=1, source_target_pairs={{0,32},{32,64},{64,96},{96,128},{128,160},{160,192},{192,224},{1,3... | collective-permute-start | bytes 1572872 | tf_op jit(solution)/shard_map/while/body/eval_jaxpr/ppermute | solution.py:16
  187.8 14.1 %collective-permute-start = (bf16[128,2048]{0,1:T(8,128)(2,1)S(1)}, bf16[128,2048]{0,1:T(8,128)(2,1)S(1)}, u32[]{:S(2)}, u32[]{:S(2)}) collective-permute-start(bf16[128,2048]{0,1:T(8,128)(2,1)S(1)} %get-tuple-element.1371), channel_id=1, source_target_pairs={{0,32},{32,64},{64,96},{96,128},{128,160},{160,192},{192,224},{1,3... | collective-permute-start | bytes 1572872 | tf_op jit(solution)/shard_map/while/body/eval_jaxpr/ppermute | solution.py:16
  202.1 30.0 %collective-permute-start = (bf16[128,2048]{0,1:T(8,128)(2,1)S(1)}, bf16[128,2048]{0,1:T(8,128)(2,1)S(1)}, u32[]{:S(2)}, u32[]{:S(2)}) collective-permute-start(bf16[128,2048]{0,1:T(8,128)(2,1)S(1)} %get-tuple-element.1371), channel_id=1, source_target_pairs={{0,32},{32,64},{64,96},{96,128},{128,160},{160,192},{192,224},{1,3... | collective-permute-start | bytes 1572872 | tf_op jit(solution)/shard_map/while/body/eval_jaxpr/ppermute | solution.py:16
  232.2 17.2 %collective-permute-start = (bf16[128,2048]{0,1:T(8,128)(2,1)S(1)}, bf16[128,2048]{0,1:T(8,128)(2,1)S(1)}, u32[]{:S(2)}, u32[]{:S(2)}) collective-permute-start(bf16[128,2048]{0,1:T(8,128)(2,1)S(1)} %get-tuple-element.1371), channel_id=1, source_target_pairs={{0,32},{32,64},{64,96},{96,128},{128,160},{160,192},{192,224},{1,3... | collective-permute-start | bytes 1572872 | tf_op jit(solution)/shard_map/while/body/eval_jaxpr/ppermute | solution.py:16
  249.5 30.1 %collective-permute-start = (bf16[128,2048]{0,1:T(8,128)(2,1)S(1)}, bf16[128,2048]{0,1:T(8,128)(2,1)S(1)}, u32[]{:S(2)}, u32[]{:S(2)}) collective-permute-start(bf16[128,2048]{0,1:T(8,128)(2,1)S(1)} %get-tuple-element.1371), channel_id=1, source_target_pairs={{0,32},{32,64},{64,96},{96,128},{128,160},{160,192},{192,224},{1,3... | collective-permute-start | bytes 1572872 | tf_op jit(solution)/shard_map/while/body/eval_jaxpr/ppermute | solution.py:16
  288.8 5.5 copy-start.2
  304.2 17.9 %collective-permute-start.1 = (bf16[128,2048]{1,0:T(8,128)(2,1)}, bf16[128,2048]{1,0:T(8,128)(2,1)S(1)}, u32[]{:S(2)}, u32[]{:S(2)}) collective-permute-start(bf16[128,2048]{1,0:T(8,128)(2,1)} %get-tuple-element.1393), channel_id=1, source_target_pairs={{32,0},{64,32},{96,64},{128,96},{160,128},{192,160},{224,192},{33,... | collective-permute-start | bytes 1572872 | tf_op jit(solution)/shard_map/while/body/eval_jaxpr/ppermute | solution.py:16
  323.0 20.7 %collective-permute-start.1 = (bf16[128,2048]{1,0:T(8,128)(2,1)}, bf16[128,2048]{1,0:T(8,128)(2,1)S(1)}, u32[]{:S(2)}, u32[]{:S(2)}) collective-permute-start(bf16[128,2048]{1,0:T(8,128)(2,1)} %get-tuple-element.1393), channel_id=1, source_target_pairs={{32,0},{64,32},{96,64},{128,96},{160,128},{192,160},{224,192},{33,... | collective-permute-start | bytes 1572872 | tf_op jit(solution)/shard_map/while/body/eval_jaxpr/ppermute | solution.py:16
  344.5 20.5 %collective-permute-start.1 = (bf16[128,2048]{1,0:T(8,128)(2,1)}, bf16[128,2048]{1,0:T(8,128)(2,1)S(1)}, u32[]{:S(2)}, u32[]{:S(2)}) collective-permute-start(bf16[128,2048]{1,0:T(8,128)(2,1)} %get-tuple-element.1393), channel_id=1, source_target_pairs={{32,0},{64,32},{96,64},{128,96},{160,128},{192,160},{224,192},{33,... | collective-permute-start | bytes 1572872 | tf_op jit(solution)/shard_map/while/body/eval_jaxpr/ppermute | solution.py:16
  365.9 24.1 %collective-permute-start.1 = (bf16[128,2048]{1,0:T(8,128)(2,1)}, bf16[128,2048]{1,0:T(8,128)(2,1)S(1)}, u32[]{:S(2)}, u32[]{:S(2)}) collective-permute-start(bf16[128,2048]{1,0:T(8,128)(2,1)} %get-tuple-element.1393), channel_id=1, source_target_pairs={{32,0},{64,32},{96,64},{128,96},{160,128},{192,160},{224,192},{33,... | collective-permute-start | bytes 1572872 | tf_op jit(solution)/shard_map/while/body/eval_jaxpr/ppermute | solution.py:16
  390.8 23.1 %collective-permute-start.1 = (bf16[128,2048]{1,0:T(8,128)(2,1)}, bf16[128,2048]{1,0:T(8,128)(2,1)S(1)}, u32[]{:S(2)}, u32[]{:S(2)}) collective-permute-start(bf16[128,2048]{1,0:T(8,128)(2,1)} %get-tuple-element.1393), channel_id=1, source_target_pairs={{32,0},{64,32},{96,64},{128,96},{160,128},{192,160},{224,192},{33,... | collective-permute-start | bytes 1572872 | tf_op jit(solution)/shard_map/while/body/eval_jaxpr/ppermute | solution.py:16
  414.8 11.3 %collective-permute-start.1 = (bf16[128,2048]{1,0:T(8,128)(2,1)}, bf16[128,2048]{1,0:T(8,128)(2,1)S(1)}, u32[]{:S(2)}, u32[]{:S(2)}) collective-permute-start(bf16[128,2048]{1,0:T(8,128)(2,1)} %get-tuple-element.1393), channel_id=1, source_target_pairs={{32,0},{64,32},{96,64},{128,96},{160,128},{192,160},{224,192},{33,... | collective-permute-start | bytes 1572872 | tf_op jit(solution)/shard_map/while/body/eval_jaxpr/ppermute | solution.py:16
  426.9 106.6 %collective-permute-start.1 = (bf16[128,2048]{1,0:T(8,128)(2,1)}, bf16[128,2048]{1,0:T(8,128)(2,1)S(1)}, u32[]{:S(2)}, u32[]{:S(2)}) collective-permute-start(bf16[128,2048]{1,0:T(8,128)(2,1)} %get-tuple-element.1393), channel_id=1, source_target_pairs={{32,0},{64,32},{96,64},{128,96},{160,128},{192,160},{224,192},{33,... | collective-permute-start | bytes 1572872 | tf_op jit(solution)/shard_map/while/body/eval_jaxpr/ppermute | solution.py:16
  536.6 1.9 copy-start
  538.5 4.8 slice-start
  539.2 4.1 slice-start.1
  550.2 17.4 %collective-permute-start.1 = (bf16[128,2048]{1,0:T(8,128)(2,1)}, bf16[128,2048]{1,0:T(8,128)(2,1)S(1)}, u32[]{:S(2)}, u32[]{:S(2)}) collective-permute-start(bf16[128,2048]{1,0:T(8,128)(2,1)} %get-tuple-element.1393), channel_id=1, source_target_pairs={{32,0},{64,32},{96,64},{128,96},{160,128},{192,160},{224,192},{33,... | collective-permute-start | bytes 1572872 | tf_op jit(solution)/shard_map/while/body/eval_jaxpr/ppermute | solution.py:16
  570.7 1.9 copy-start
  572.6 4.8 slice-start
  573.3 4.1 slice-start.1
  584.3 17.3 %collective-permute-start.1 = (bf16[128,2048]{1,0:T(8,128)(2,1)}, bf16[128,2048]{1,0:T(8,128)(2,1)S(1)}, u32[]{:S(2)}, u32[]{:S(2)}) collective-permute-start(bf16[128,2048]{1,0:T(8,128)(2,1)} %get-tuple-element.1393), channel_id=1, source_target_pairs={{32,0},{64,32},{96,64},{128,96},{160,128},{192,160},{224,192},{33,... | collective-permute-start | bytes 1572872 | tf_op jit(solution)/shard_map/while/body/eval_jaxpr/ppermute | solution.py:16
  604.7 1.9 copy-start
  606.6 4.8 slice-start
  607.3 4.1 slice-start.1
  618.2 17.4 %collective-permute-start.1 = (bf16[128,2048]{1,0:T(8,128)(2,1)}, bf16[128,2048]{1,0:T(8,128)(2,1)S(1)}, u32[]{:S(2)}, u32[]{:S(2)}) collective-permute-start(bf16[128,2048]{1,0:T(8,128)(2,1)} %get-tuple-element.1393), channel_id=1, source_target_pairs={{32,0},{64,32},{96,64},{128,96},{160,128},{192,160},{224,192},{33,... | collective-permute-start | bytes 1572872 | tf_op jit(solution)/shard_map/while/body/eval_jaxpr/ppermute | solution.py:16
  638.8 1.9 copy-start
  640.7 4.8 slice-start
  641.4 4.1 slice-start.1
  652.4 11.3 %collective-permute-start.1 = (bf16[128,2048]{1,0:T(8,128)(2,1)}, bf16[128,2048]{1,0:T(8,128)(2,1)S(1)}, u32[]{:S(2)}, u32[]{:S(2)}) collective-permute-start(bf16[128,2048]{1,0:T(8,128)(2,1)} %get-tuple-element.1393), channel_id=1, source_target_pairs={{32,0},{64,32},{96,64},{128,96},{160,128},{192,160},{224,192},{33,... | collective-permute-start | bytes 1572872 | tf_op jit(solution)/shard_map/while/body/eval_jaxpr/ppermute | solution.py:16
  663.6 4.2 copy-start.1
  681.2 1.6 copy-start.3
  691.0 237.3 %reduce-scatter.5.cloned.1.call-start = ((), (), s32[]{:S(2)}) async-start(), calls=%async_computation.3 | async-start | bytes 8912896 | tf_op jit(solution)/shard_map/reduce_scatter | solution.py:203
Sparse Core Ops, SparseCore 0:
  691.1 133.5 reduce-scatter.2
  827.4 100.8 reduce-scatter.4

commit v2 on v1

--- a/solution.py
+++ b/solution.py
@@ -199,7 +199,11 @@
         (((0,), (0,)), ((), ())),
         preferred_element_type=jnp.float32,
     )
-    half = lax.psum_scatter(grad, "core", scatter_dimension=0, tiled=True)
+    core = lax.axis_index("core")
+    pieces = grad.reshape(cores, width // cores, width)
+    kept = lax.dynamic_index_in_dim(pieces, core, 0, keepdims=False)
+    sent = lax.dynamic_index_in_dim(pieces, 1 - core, 0, keepdims=False)
+    half = kept + lax.ppermute(sent, "core", [(0, 1), (1, 0)])
     summed = lax.psum_scatter(half, "dp_hi", scatter_dimension=0, tiled=True)
     return summed[None]
 

time: 946 us -> 928 us (0.981)
  waiting for transfers between devices: 599 us -> 572 us
    reduce_scatter x1 -> x0, waiting for transfers between devices: 134 us -> none  [per_device(): half = lax.psum_scatter(grad, 'core', scatter_dimension=0, tiled=True)]
    reduce_scatter x1, waiting for transfers between devices: 104 us -> 199 us  [per_device(): summed = lax.psum_scatter(half, 'dp_hi', scatter_dimension=0, tiled=True)]
    ppermute x0 -> x1, waiting for transfers between devices: none -> 13.5 us  [per_device(): half = kept + lax.ppermute(sent, 'core', [(0, 1), (1, 0)])]
    add x0 -> x1, other arithmetic: none -> 11.7 us  [per_device(): half = kept + lax.ppermute(sent, 'core', [(0, 1), (1, 0)])]
    unnamed x13 -> x11, local copies, waits for them, and re-layouts: 23.6 us -> 26.4 us
where the time goes in v2:
time: 928 us; the launch traced here: 917 us
  waiting for transfers between devices  572 us (62%)
  starting transfers between devices  127 us (14%)
  local copies, waits for them, and re-layouts  76.4 us (8%)
  matrix products  70 us (8%)
  other arithmetic  56.7 us (6%)
  between operations  13.5 us (1%)
    ppermute x22, waiting for transfers between devices, passed_along(): return lax.ppermute(block, axis, route)  359 us
    reduce_scatter x1, waiting for transfers between devices, per_device(): summed = lax.psum_scatter(half, 'dp_hi', scatter_dimension=0, tiled=True)  199 us
    ppermute x22, starting transfers between devices, passed_along(): return lax.ppermute(block, axis, route)  127 us
    unnamed x11, local copies, waits for them, and re-layouts  26.4 us
    dot_general x4, matrix products, layer_forward(): jnp.dot(normed.reshape(-1, width), weight, preferred_element_type=jnp.flo...  18.8 us
  transfers between devices with their start and end apart: 24, of which 24 were waited for; matrix products, arithmetic and copies ran while one was open for 0% of the time, Pallas kernels for 0%

profile of v2, /device:TPU:96, one launch (start us, length us, event | category | flops | bytes accessed | tf_op | source)
XLA Modules:
  0.0 916.8 jit_solution(7897613277135439699)
XLA Ops:
  19.7 250.4 %while.48 = (s32[]{:T(128)}, bf16[128,2048]{0,1:T(8,128)(2,1)S(1)}, f32[4,128,2048]{1,2,0:T(8,128)}, f32[4,128,1]{1,2,0:T(1,128)S(1)}, bf16[4,128,16,128]{3,2,1,...) while((s32[]{:T(128)}, bf16[128,2048]{0,1:T(8,128)(2,1)S(1)}, ...), condition=%wide.region_8.9_spmd.clone, body=%wide.region_1.8_spmd.clone.sunk | while | flops 1216641408 | bytes 26020904 | solution.py:158
  19.7 12.1 %conditional.6 = (bf16[128,2048]{0,1:T(8,128)(2,1)S(1)}, f32[4,128,2048]{1,2,0:T(8,128)}, f32[4,128,1]{1,2,0:T(1,128)S(1)}, bf16[4,128,16,128]{3,2,1,0:T(8,128)(...) conditional(s32[]{:T(128)} %convert_element_type.254, ...), branch_computations={%region_2.2_spmd, %region_3.7_spmd} | conditional | flops 1216641408 | bytes 23923316 | solution.py:152
  20.4 4.7 convolution_convert_fusion
  33.1 11.4 %collective-permute-done = bf16[128,2048]{0,1:T(8,128)(2,1)S(1)} collective-permute-done((bf16[128,2048]{0,1:T(8,128)(2,1)S(1)}, bf16[128,2048]{0,1:T(8,128)(2,1)S(1)}, u32[]{:S(2)}, u32[]{:S(2)}) %collective-permute-start) | collective-permute-done | bytes 524320 | tf_op jit(solution)/shard_map/while/body/eval_jaxpr/ppermute | solution.py:16
  44.5 12.0 %conditional.6 = (bf16[128,2048]{0,1:T(8,128)(2,1)S(1)}, f32[4,128,2048]{1,2,0:T(8,128)}, f32[4,128,1]{1,2,0:T(1,128)S(1)}, bf16[4,128,16,128]{3,2,1,0:T(8,128)(...) conditional(s32[]{:T(128)} %convert_element_type.254, ...), branch_computations={%region_2.2_spmd, %region_3.7_spmd} | conditional | flops 1216641408 | bytes 23923316 | solution.py:152
  45.2 4.7 convolution_convert_fusion
  61.0 10.6 %collective-permute-done = bf16[128,2048]{0,1:T(8,128)(2,1)S(1)} collective-permute-done((bf16[128,2048]{0,1:T(8,128)(2,1)S(1)}, bf16[128,2048]{0,1:T(8,128)(2,1)S(1)}, u32[]{:S(2)}, u32[]{:S(2)}) %collective-permute-start) | collective-permute-done | bytes 524320 | tf_op jit(solution)/shard_map/while/body/eval_jaxpr/ppermute | solution.py:16
  71.5 12.0 %conditional.6 = (bf16[128,2048]{0,1:T(8,128)(2,1)S(1)}, f32[4,128,2048]{1,2,0:T(8,128)}, f32[4,128,1]{1,2,0:T(1,128)S(1)}, bf16[4,128,16,128]{3,2,1,0:T(8,128)(...) conditional(s32[]{:T(128)} %convert_element_type.254, ...), branch_computations={%region_2.2_spmd, %region_3.7_spmd} | conditional | flops 1216641408 | bytes 23923316 | solution.py:152
  88.0 9.6 %collective-permute-done = bf16[128,2048]{0,1:T(8,128)(2,1)S(1)} collective-permute-done((bf16[128,2048]{0,1:T(8,128)(2,1)S(1)}, bf16[128,2048]{0,1:T(8,128)(2,1)S(1)}, u32[]{:S(2)}, u32[]{:S(2)}) %collective-permute-start) | collective-permute-done | bytes 524320 | tf_op jit(solution)/shard_map/while/body/eval_jaxpr/ppermute | solution.py:16
  97.6 12.0 %conditional.6 = (bf16[128,2048]{0,1:T(8,128)(2,1)S(1)}, f32[4,128,2048]{1,2,0:T(8,128)}, f32[4,128,1]{1,2,0:T(1,128)S(1)}, bf16[4,128,16,128]{3,2,1,0:T(8,128)(...) conditional(s32[]{:T(128)} %convert_element_type.254, ...), branch_computations={%region_2.2_spmd, %region_3.7_spmd} | conditional | flops 1216641408 | bytes 23923316 | solution.py:152
  98.4 4.7 convolution_convert_fusion
  114.1 8.7 collective-permute-done
  122.9 16.3 %collective-permute-start = (bf16[128,2048]{0,1:T(8,128)(2,1)S(1)}, bf16[128,2048]{0,1:T(8,128)(2,1)S(1)}, u32[]{:S(2)}, u32[]{:S(2)}) collective-permute-start(bf16[128,2048]{0,1:T(8,128)(2,1)S(1)} %get-tuple-element.1403), channel_id=1, source_target_pairs={{0,32},{32,64},{64,96},{96,128},{128,160},{160,192},{192,224},{1,3... | collective-permute-start | bytes 1572872 | tf_op jit(solution)/shard_map/while/body/eval_jaxpr/ppermute | solution.py:16
  139.2 7.8 collective-permute-done
  151.5 6.9 collective-permute-done
  158.5 15.3 %collective-permute-start = (bf16[128,2048]{0,1:T(8,128)(2,1)S(1)}, bf16[128,2048]{0,1:T(8,128)(2,1)S(1)}, u32[]{:S(2)}, u32[]{:S(2)}) collective-permute-start(bf16[128,2048]{0,1:T(8,128)(2,1)S(1)} %get-tuple-element.1403), channel_id=1, source_target_pairs={{0,32},{32,64},{64,96},{96,128},{128,160},{160,192},{192,224},{1,3... | collective-permute-start | bytes 1572872 | tf_op jit(solution)/shard_map/while/body/eval_jaxpr/ppermute | solution.py:16
  173.9 6.6 collective-permute-done
  180.6 7.5 collective-permute-start
  188.1 6.6 collective-permute-done
  194.9 22.3 %collective-permute-start = (bf16[128,2048]{0,1:T(8,128)(2,1)S(1)}, bf16[128,2048]{0,1:T(8,128)(2,1)S(1)}, u32[]{:S(2)}, u32[]{:S(2)}) collective-permute-start(bf16[128,2048]{0,1:T(8,128)(2,1)S(1)} %get-tuple-element.1403), channel_id=1, source_target_pairs={{0,32},{32,64},{64,96},{96,128},{128,160},{160,192},{192,224},{1,3... | collective-permute-start | bytes 1572872 | tf_op jit(solution)/shard_map/while/body/eval_jaxpr/ppermute | solution.py:16
  217.2 6.6 collective-permute-done
  223.9 10.4 %collective-permute-start = (bf16[128,2048]{0,1:T(8,128)(2,1)S(1)}, bf16[128,2048]{0,1:T(8,128)(2,1)S(1)}, u32[]{:S(2)}, u32[]{:S(2)}) collective-permute-start(bf16[128,2048]{0,1:T(8,128)(2,1)S(1)} %get-tuple-element.1403), channel_id=1, source_target_pairs={{0,32},{32,64},{64,96},{96,128},{128,160},{160,192},{192,224},{1,3... | collective-permute-start | bytes 1572872 | tf_op jit(solution)/shard_map/while/body/eval_jaxpr/ppermute | solution.py:16
  234.4 6.6 collective-permute-done
  241.1 22.3 %collective-permute-start = (bf16[128,2048]{0,1:T(8,128)(2,1)S(1)}, bf16[128,2048]{0,1:T(8,128)(2,1)S(1)}, u32[]{:S(2)}, u32[]{:S(2)}) collective-permute-start(bf16[128,2048]{0,1:T(8,128)(2,1)S(1)} %get-tuple-element.1403), channel_id=1, source_target_pairs={{0,32},{32,64},{64,96},{96,128},{128,160},{160,192},{192,224},{1,3... | collective-permute-start | bytes 1572872 | tf_op jit(solution)/shard_map/while/body/eval_jaxpr/ppermute | solution.py:16
  263.5 6.6 collective-permute-done
  272.6 5.5 copy.82
  286.5 10.7 %copy.77 = bf16[4,128,2048]{1,0,2:T(4,128)(2,1)} copy(bf16[4,128,2048]{1,2,0:T(8,128)(2,1)S(1)} %convert_element_type.151) | data formatting | bytes 4194304 | tf_op jit(solution)/shard_map/convert_element_type | solution.py:194
  301.4 5.4 copy.80
  308.5 358.3 %while.49 = (s32[]{:T(128)}, bf16[128,2048]{1,0:T(8,128)(2,1)S(1)}, bf16[4,128,2048]{1,2,0:T(8,128)(2,1)}, s32[]{:T(128)}, pred[]{:T(512)}, /*index=5*/bf16[4,12...) while((s32[]{:T(128)}, bf16[128,2048]{1,0:T(8,128)(2,1)S(1)}, ...), condition=%wide.region_15.16_spmd.clone, body=%wide.region_9.15_spmd.clone.sunk | while | flops 1353218048 | bytes 71172608 | solution.py:190
  310.7 16.5 %collective-permute-done.1 = bf16[128,2048]{1,0:T(8,128)(2,1)S(1)} collective-permute-done((bf16[128,2048]{1,0:T(8,128)(2,1)}, bf16[128,2048]{1,0:T(8,128)(2,1)S(1)}, u32[]{:S(2)}, u32[]{:S(2)}) %collective-permute-start.1) | collective-permute-done | bytes 524320 | tf_op jit(solution)/shard_map/while/body/eval_jaxpr/ppermute | solution.py:16
  329.3 16.8 %collective-permute-done.1 = bf16[128,2048]{1,0:T(8,128)(2,1)S(1)} collective-permute-done((bf16[128,2048]{1,0:T(8,128)(2,1)}, bf16[128,2048]{1,0:T(8,128)(2,1)S(1)}, u32[]{:S(2)}, u32[]{:S(2)}) %collective-permute-start.1) | collective-permute-done | bytes 524320 | tf_op jit(solution)/shard_map/while/body/eval_jaxpr/ppermute | solution.py:16
  348.2 17.4 %collective-permute-done.1 = bf16[128,2048]{1,0:T(8,128)(2,1)S(1)} collective-permute-done((bf16[128,2048]{1,0:T(8,128)(2,1)}, bf16[128,2048]{1,0:T(8,128)(2,1)S(1)}, u32[]{:S(2)}, u32[]{:S(2)}) %collective-permute-start.1) | collective-permute-done | bytes 524320 | tf_op jit(solution)/shard_map/while/body/eval_jaxpr/ppermute | solution.py:16
  367.7 20.6 %collective-permute-done.1 = bf16[128,2048]{1,0:T(8,128)(2,1)S(1)} collective-permute-done((bf16[128,2048]{1,0:T(8,128)(2,1)}, bf16[128,2048]{1,0:T(8,128)(2,1)S(1)}, u32[]{:S(2)}, u32[]{:S(2)}) %collective-permute-start.1) | collective-permute-done | bytes 524320 | tf_op jit(solution)/shard_map/while/body/eval_jaxpr/ppermute | solution.py:16
  390.5 20.3 %collective-permute-done.1 = bf16[128,2048]{1,0:T(8,128)(2,1)S(1)} collective-permute-done((bf16[128,2048]{1,0:T(8,128)(2,1)}, bf16[128,2048]{1,0:T(8,128)(2,1)S(1)}, u32[]{:S(2)}, u32[]{:S(2)}) %collective-permute-start.1) | collective-permute-done | bytes 524320 | tf_op jit(solution)/shard_map/while/body/eval_jaxpr/ppermute | solution.py:16
  412.9 10.0 %collective-permute-done.1 = bf16[128,2048]{1,0:T(8,128)(2,1)S(1)} collective-permute-done((bf16[128,2048]{1,0:T(8,128)(2,1)}, bf16[128,2048]{1,0:T(8,128)(2,1)S(1)}, u32[]{:S(2)}, u32[]{:S(2)}) %collective-permute-start.1) | collective-permute-done | bytes 524320 | tf_op jit(solution)/shard_map/while/body/eval_jaxpr/ppermute | solution.py:16
  425.0 111.4 %collective-permute-done.1 = bf16[128,2048]{1,0:T(8,128)(2,1)S(1)} collective-permute-done((bf16[128,2048]{1,0:T(8,128)(2,1)}, bf16[128,2048]{1,0:T(8,128)(2,1)S(1)}, u32[]{:S(2)}, u32[]{:S(2)}) %collective-permute-start.1) | collective-permute-done | bytes 524320 | tf_op jit(solution)/shard_map/while/body/eval_jaxpr/ppermute | solution.py:16
  536.5 16.9 %conditional.7 = (bf16[128,2048]{1,0:T(8,128)(2,1)}, bf16[4,128,2048]{1,2,0:T(8,128)(2,1)}) conditional(s32[]{:T(128)} %convert_element_type.255, bf16[4,128,2048]{1,2,0:T(8,128)(2,1)} %get-tuple-element.1525, (pred[]{:T(512)}, s32[]{:T(128)}, bf16[4,128,2048]{2,1,0:T(8,128)(2,1)}, bf16[128,2048]{1,0:T(8,128)(2,1)S(1)}, ...), branch_computations={%region_10.10_spmd, %region_11.14_spmd} | conditional | flops 1353218048 | bytes 69075104 | solution.py:186
  554.6 16.0 %collective-permute-done.1 = bf16[128,2048]{1,0:T(8,128)(2,1)S(1)} collective-permute-done((bf16[128,2048]{1,0:T(8,128)(2,1)}, bf16[128,2048]{1,0:T(8,128)(2,1)S(1)}, u32[]{:S(2)}, u32[]{:S(2)}) %collective-permute-start.1) | collective-permute-done | bytes 524320 | tf_op jit(solution)/shard_map/while/body/eval_jaxpr/ppermute | solution.py:16
  570.6 16.9 %conditional.7 = (bf16[128,2048]{1,0:T(8,128)(2,1)}, bf16[4,128,2048]{1,2,0:T(8,128)(2,1)}) conditional(s32[]{:T(128)} %convert_element_type.255, bf16[4,128,2048]{1,2,0:T(8,128)(2,1)} %get-tuple-element.1525, (pred[]{:T(512)}, s32[]{:T(128)}, bf16[4,128,2048]{2,1,0:T(8,128)(2,1)}, bf16[128,2048]{1,0:T(8,128)(2,1)S(1)}, ...), branch_computations={%region_10.10_spmd, %region_11.14_spmd} | conditional | flops 1353218048 | bytes 69075104 | solution.py:186
  588.8 15.8 %collective-permute-done.1 = bf16[128,2048]{1,0:T(8,128)(2,1)S(1)} collective-permute-done((bf16[128,2048]{1,0:T(8,128)(2,1)}, bf16[128,2048]{1,0:T(8,128)(2,1)S(1)}, u32[]{:S(2)}, u32[]{:S(2)}) %collective-permute-start.1) | collective-permute-done | bytes 524320 | tf_op jit(solution)/shard_map/while/body/eval_jaxpr/ppermute | solution.py:16
  604.6 16.8 %conditional.7 = (bf16[128,2048]{1,0:T(8,128)(2,1)}, bf16[4,128,2048]{1,2,0:T(8,128)(2,1)}) conditional(s32[]{:T(128)} %convert_element_type.255, bf16[4,128,2048]{1,2,0:T(8,128)(2,1)} %get-tuple-element.1525, (pred[]{:T(512)}, s32[]{:T(128)}, bf16[4,128,2048]{2,1,0:T(8,128)(2,1)}, bf16[128,2048]{1,0:T(8,128)(2,1)S(1)}, ...), branch_computations={%region_10.10_spmd, %region_11.14_spmd} | conditional | flops 1353218048 | bytes 69075104 | solution.py:186
  622.8 15.9 %collective-permute-done.1 = bf16[128,2048]{1,0:T(8,128)(2,1)S(1)} collective-permute-done((bf16[128,2048]{1,0:T(8,128)(2,1)}, bf16[128,2048]{1,0:T(8,128)(2,1)S(1)}, u32[]{:S(2)}, u32[]{:S(2)}) %collective-permute-start.1) | collective-permute-done | bytes 524320 | tf_op jit(solution)/shard_map/while/body/eval_jaxpr/ppermute | solution.py:16
  638.7 16.8 %conditional.7 = (bf16[128,2048]{1,0:T(8,128)(2,1)}, bf16[4,128,2048]{1,2,0:T(8,128)(2,1)}) conditional(s32[]{:T(128)} %convert_element_type.255, bf16[4,128,2048]{1,2,0:T(8,128)(2,1)} %get-tuple-element.1525, (pred[]{:T(512)}, s32[]{:T(128)}, bf16[4,128,2048]{2,1,0:T(8,128)(2,1)}, bf16[128,2048]{1,0:T(8,128)(2,1)S(1)}, ...), branch_computations={%region_10.10_spmd, %region_11.14_spmd} | conditional | flops 1353218048 | bytes 69075104 | solution.py:186
  656.8 10.0 %collective-permute-done.1 = bf16[128,2048]{1,0:T(8,128)(2,1)S(1)} collective-permute-done((bf16[128,2048]{1,0:T(8,128)(2,1)}, bf16[128,2048]{1,0:T(8,128)(2,1)S(1)}, u32[]{:S(2)}, u32[]{:S(2)}) %collective-permute-start.1) | collective-permute-done | bytes 524320 | tf_op jit(solution)/shard_map/while/body/eval_jaxpr/ppermute | solution.py:16
  670.9 6.3 fusion.78
  685.4 13.5 %collective-permute-done.2 = f32[1024,2048]{1,0:T(8,128)} collective-permute-done((f32[1024,2048]{1,0:T(8,128)}, f32[1024,2048]{1,0:T(8,128)}, u32[]{:S(2)}, u32[]{:S(2)}) %collective-permute-start.2) | collective-permute-done | bytes 8388640 | tf_op jit(solution)/shard_map/ppermute | solution.py:206
  698.9 11.7 %bitcast_add_fusion = f32[1024,2048]{1,0:T(8,128)} fusion(f32[1024,2048]{1,0:T(8,128)} %collective-permute-done.2, f32[2,1024,2048]{2,1,0:T(8,128)} %copy-done, s32[]{:T(128)S(6)} %select_n.156), kind=kLoop, calls=%fused_computation.103 | loop fusion | flops 2097152 | bytes 25165828 | tf_op jit(solution)/shard_map/add | solution.py:206
  710.6 199.3 %reduce-scatter.2.cloned.1.call-done = f32[64,2048]{1,0:T(8,128)} async-done(((f32[1024,2048]{1,0:T(8,128)}), f32[64,2048]{1,0:T(8,128)}) %reduce-scatter.2.cloned.1.call-update) | async-done | bytes 524304 | tf_op jit(solution)/shard_map/reduce_scatter | solution.py:207
  (239 shorter events, 189.2 us)
Async XLA Ops:
  6.5 903.4 %reduce-scatter.2.cloned.1.call-start = ((), (), s32[]{:S(2)}) async-start(), calls=%async_computation.1 | async-start | bytes 8912896 | tf_op jit(solution)/shard_map/reduce_scatter | solution.py:207
  17.4 2.2 copy-start.3
  31.7 12.7 %collective-permute-start = (bf16[128,2048]{0,1:T(8,128)(2,1)S(1)}, bf16[128,2048]{0,1:T(8,128)(2,1)S(1)}, u32[]{:S(2)}, u32[]{:S(2)}) collective-permute-start(bf16[128,2048]{0,1:T(8,128)(2,1)S(1)} %get-tuple-element.1403), channel_id=1, source_target_pairs={{0,32},{32,64},{64,96},{96,128},{128,160},{160,192},{192,224},{1,3... | collective-permute-start | bytes 1572872 | tf_op jit(solution)/shard_map/while/body/eval_jaxpr/ppermute | solution.py:16
  56.5 15.0 %collective-permute-start = (bf16[128,2048]{0,1:T(8,128)(2,1)S(1)}, bf16[128,2048]{0,1:T(8,128)(2,1)S(1)}, u32[]{:S(2)}, u32[]{:S(2)}) collective-permute-start(bf16[128,2048]{0,1:T(8,128)(2,1)S(1)} %get-tuple-element.1403), channel_id=1, source_target_pairs={{0,32},{32,64},{64,96},{96,128},{128,160},{160,192},{192,224},{1,3... | collective-permute-start | bytes 1572872 | tf_op jit(solution)/shard_map/while/body/eval_jaxpr/ppermute | solution.py:16
  83.5 14.1 %collective-permute-start = (bf16[128,2048]{0,1:T(8,128)(2,1)S(1)}, bf16[128,2048]{0,1:T(8,128)(2,1)S(1)}, u32[]{:S(2)}, u32[]{:S(2)}) collective-permute-start(bf16[128,2048]{0,1:T(8,128)(2,1)S(1)} %get-tuple-element.1403), channel_id=1, source_target_pairs={{0,32},{32,64},{64,96},{96,128},{128,160},{160,192},{192,224},{1,3... | collective-permute-start | bytes 1572872 | tf_op jit(solution)/shard_map/while/body/eval_jaxpr/ppermute | solution.py:16
  109.6 13.1 %collective-permute-start = (bf16[128,2048]{0,1:T(8,128)(2,1)S(1)}, bf16[128,2048]{0,1:T(8,128)(2,1)S(1)}, u32[]{:S(2)}, u32[]{:S(2)}) collective-permute-start(bf16[128,2048]{0,1:T(8,128)(2,1)S(1)} %get-tuple-element.1403), channel_id=1, source_target_pairs={{0,32},{32,64},{64,96},{96,128},{128,160},{160,192},{192,224},{1,3... | collective-permute-start | bytes 1572872 | tf_op jit(solution)/shard_map/while/body/eval_jaxpr/ppermute | solution.py:16
  122.9 24.1 %collective-permute-start = (bf16[128,2048]{0,1:T(8,128)(2,1)S(1)}, bf16[128,2048]{0,1:T(8,128)(2,1)S(1)}, u32[]{:S(2)}, u32[]{:S(2)}) collective-permute-start(bf16[128,2048]{0,1:T(8,128)(2,1)S(1)} %get-tuple-element.1403), channel_id=1, source_target_pairs={{0,32},{32,64},{64,96},{96,128},{128,160},{160,192},{192,224},{1,3... | collective-permute-start | bytes 1572872 | tf_op jit(solution)/shard_map/while/body/eval_jaxpr/ppermute | solution.py:16
  147.1 11.3 %collective-permute-start = (bf16[128,2048]{0,1:T(8,128)(2,1)S(1)}, bf16[128,2048]{0,1:T(8,128)(2,1)S(1)}, u32[]{:S(2)}, u32[]{:S(2)}) collective-permute-start(bf16[128,2048]{0,1:T(8,128)(2,1)S(1)} %get-tuple-element.1403), channel_id=1, source_target_pairs={{0,32},{32,64},{64,96},{96,128},{128,160},{160,192},{192,224},{1,3... | collective-permute-start | bytes 1572872 | tf_op jit(solution)/shard_map/while/body/eval_jaxpr/ppermute | solution.py:16
  158.5 22.0 %collective-permute-start = (bf16[128,2048]{0,1:T(8,128)(2,1)S(1)}, bf16[128,2048]{0,1:T(8,128)(2,1)S(1)}, u32[]{:S(2)}, u32[]{:S(2)}) collective-permute-start(bf16[128,2048]{0,1:T(8,128)(2,1)S(1)} %get-tuple-element.1403), channel_id=1, source_target_pairs={{0,32},{32,64},{64,96},{96,128},{128,160},{160,192},{192,224},{1,3... | collective-permute-start | bytes 1572872 | tf_op jit(solution)/shard_map/while/body/eval_jaxpr/ppermute | solution.py:16
  180.6 14.2 %collective-permute-start = (bf16[128,2048]{0,1:T(8,128)(2,1)S(1)}, bf16[128,2048]{0,1:T(8,128)(2,1)S(1)}, u32[]{:S(2)}, u32[]{:S(2)}) collective-permute-start(bf16[128,2048]{0,1:T(8,128)(2,1)S(1)} %get-tuple-element.1403), channel_id=1, source_target_pairs={{0,32},{32,64},{64,96},{96,128},{128,160},{160,192},{192,224},{1,3... | collective-permute-start | bytes 1572872 | tf_op jit(solution)/shard_map/while/body/eval_jaxpr/ppermute | solution.py:16
  194.9 29.0 %collective-permute-start = (bf16[128,2048]{0,1:T(8,128)(2,1)S(1)}, bf16[128,2048]{0,1:T(8,128)(2,1)S(1)}, u32[]{:S(2)}, u32[]{:S(2)}) collective-permute-start(bf16[128,2048]{0,1:T(8,128)(2,1)S(1)} %get-tuple-element.1403), channel_id=1, source_target_pairs={{0,32},{32,64},{64,96},{96,128},{128,160},{160,192},{192,224},{1,3... | collective-permute-start | bytes 1572872 | tf_op jit(solution)/shard_map/while/body/eval_jaxpr/ppermute | solution.py:16
  223.9 17.1 %collective-permute-start = (bf16[128,2048]{0,1:T(8,128)(2,1)S(1)}, bf16[128,2048]{0,1:T(8,128)(2,1)S(1)}, u32[]{:S(2)}, u32[]{:S(2)}) collective-permute-start(bf16[128,2048]{0,1:T(8,128)(2,1)S(1)} %get-tuple-element.1403), channel_id=1, source_target_pairs={{0,32},{32,64},{64,96},{96,128},{128,160},{160,192},{192,224},{1,3... | collective-permute-start | bytes 1572872 | tf_op jit(solution)/shard_map/while/body/eval_jaxpr/ppermute | solution.py:16
  241.1 29.0 %collective-permute-start = (bf16[128,2048]{0,1:T(8,128)(2,1)S(1)}, bf16[128,2048]{0,1:T(8,128)(2,1)S(1)}, u32[]{:S(2)}, u32[]{:S(2)}) collective-permute-start(bf16[128,2048]{0,1:T(8,128)(2,1)S(1)} %get-tuple-element.1403), channel_id=1, source_target_pairs={{0,32},{32,64},{64,96},{96,128},{128,160},{160,192},{192,224},{1,3... | collective-permute-start | bytes 1572872 | tf_op jit(solution)/shard_map/while/body/eval_jaxpr/ppermute | solution.py:16
  309.4 17.8 %collective-permute-start.1 = (bf16[128,2048]{1,0:T(8,128)(2,1)}, bf16[128,2048]{1,0:T(8,128)(2,1)S(1)}, u32[]{:S(2)}, u32[]{:S(2)}) collective-permute-start(bf16[128,2048]{1,0:T(8,128)(2,1)} %get-tuple-element.1425), channel_id=1, source_target_pairs={{32,0},{64,32},{96,64},{128,96},{160,128},{192,160},{224,192},{33,... | collective-permute-start | bytes 1572872 | tf_op jit(solution)/shard_map/while/body/eval_jaxpr/ppermute | solution.py:16
  328.0 18.1 %collective-permute-start.1 = (bf16[128,2048]{1,0:T(8,128)(2,1)}, bf16[128,2048]{1,0:T(8,128)(2,1)S(1)}, u32[]{:S(2)}, u32[]{:S(2)}) collective-permute-start(bf16[128,2048]{1,0:T(8,128)(2,1)} %get-tuple-element.1425), channel_id=1, source_target_pairs={{32,0},{64,32},{96,64},{128,96},{160,128},{192,160},{224,192},{33,... | collective-permute-start | bytes 1572872 | tf_op jit(solution)/shard_map/while/body/eval_jaxpr/ppermute | solution.py:16
  346.9 18.7 %collective-permute-start.1 = (bf16[128,2048]{1,0:T(8,128)(2,1)}, bf16[128,2048]{1,0:T(8,128)(2,1)S(1)}, u32[]{:S(2)}, u32[]{:S(2)}) collective-permute-start(bf16[128,2048]{1,0:T(8,128)(2,1)} %get-tuple-element.1425), channel_id=1, source_target_pairs={{32,0},{64,32},{96,64},{128,96},{160,128},{192,160},{224,192},{33,... | collective-permute-start | bytes 1572872 | tf_op jit(solution)/shard_map/while/body/eval_jaxpr/ppermute | solution.py:16
  366.5 21.9 %collective-permute-start.1 = (bf16[128,2048]{1,0:T(8,128)(2,1)}, bf16[128,2048]{1,0:T(8,128)(2,1)S(1)}, u32[]{:S(2)}, u32[]{:S(2)}) collective-permute-start(bf16[128,2048]{1,0:T(8,128)(2,1)} %get-tuple-element.1425), channel_id=1, source_target_pairs={{32,0},{64,32},{96,64},{128,96},{160,128},{192,160},{224,192},{33,... | collective-permute-start | bytes 1572872 | tf_op jit(solution)/shard_map/while/body/eval_jaxpr/ppermute | solution.py:16
  389.2 21.6 %collective-permute-start.1 = (bf16[128,2048]{1,0:T(8,128)(2,1)}, bf16[128,2048]{1,0:T(8,128)(2,1)S(1)}, u32[]{:S(2)}, u32[]{:S(2)}) collective-permute-start(bf16[128,2048]{1,0:T(8,128)(2,1)} %get-tuple-element.1425), channel_id=1, source_target_pairs={{32,0},{64,32},{96,64},{128,96},{160,128},{192,160},{224,192},{33,... | collective-permute-start | bytes 1572872 | tf_op jit(solution)/shard_map/while/body/eval_jaxpr/ppermute | solution.py:16
  411.6 11.3 %collective-permute-start.1 = (bf16[128,2048]{1,0:T(8,128)(2,1)}, bf16[128,2048]{1,0:T(8,128)(2,1)S(1)}, u32[]{:S(2)}, u32[]{:S(2)}) collective-permute-start(bf16[128,2048]{1,0:T(8,128)(2,1)} %get-tuple-element.1425), channel_id=1, source_target_pairs={{32,0},{64,32},{96,64},{128,96},{160,128},{192,160},{224,192},{33,... | collective-permute-start | bytes 1572872 | tf_op jit(solution)/shard_map/while/body/eval_jaxpr/ppermute | solution.py:16
  423.7 112.7 %collective-permute-start.1 = (bf16[128,2048]{1,0:T(8,128)(2,1)}, bf16[128,2048]{1,0:T(8,128)(2,1)S(1)}, u32[]{:S(2)}, u32[]{:S(2)}) collective-permute-start(bf16[128,2048]{1,0:T(8,128)(2,1)} %get-tuple-element.1425), channel_id=1, source_target_pairs={{32,0},{64,32},{96,64},{128,96},{160,128},{192,160},{224,192},{33,... | collective-permute-start | bytes 1572872 | tf_op jit(solution)/shard_map/while/body/eval_jaxpr/ppermute | solution.py:16
  539.7 1.9 copy-start.1
  541.6 3.9 slice-start
  542.3 3.2 slice-start.1
  553.3 17.3 %collective-permute-start.1 = (bf16[128,2048]{1,0:T(8,128)(2,1)}, bf16[128,2048]{1,0:T(8,128)(2,1)S(1)}, u32[]{:S(2)}, u32[]{:S(2)}) collective-permute-start(bf16[128,2048]{1,0:T(8,128)(2,1)} %get-tuple-element.1425), channel_id=1, source_target_pairs={{32,0},{64,32},{96,64},{128,96},{160,128},{192,160},{224,192},{33,... | collective-permute-start | bytes 1572872 | tf_op jit(solution)/shard_map/while/body/eval_jaxpr/ppermute | solution.py:16
  573.9 1.9 copy-start.1
  575.8 3.9 slice-start
  576.5 3.2 slice-start.1
  587.5 17.1 %collective-permute-start.1 = (bf16[128,2048]{1,0:T(8,128)(2,1)}, bf16[128,2048]{1,0:T(8,128)(2,1)S(1)}, u32[]{:S(2)}, u32[]{:S(2)}) collective-permute-start(bf16[128,2048]{1,0:T(8,128)(2,1)} %get-tuple-element.1425), channel_id=1, source_target_pairs={{32,0},{64,32},{96,64},{128,96},{160,128},{192,160},{224,192},{33,... | collective-permute-start | bytes 1572872 | tf_op jit(solution)/shard_map/while/body/eval_jaxpr/ppermute | solution.py:16
  607.9 1.9 copy-start.1
  609.8 3.9 slice-start
  610.5 3.2 slice-start.1
  621.5 17.2 %collective-permute-start.1 = (bf16[128,2048]{1,0:T(8,128)(2,1)}, bf16[128,2048]{1,0:T(8,128)(2,1)S(1)}, u32[]{:S(2)}, u32[]{:S(2)}) collective-permute-start(bf16[128,2048]{1,0:T(8,128)(2,1)} %get-tuple-element.1425), channel_id=1, source_target_pairs={{32,0},{64,32},{96,64},{128,96},{160,128},{192,160},{224,192},{33,... | collective-permute-start | bytes 1572872 | tf_op jit(solution)/shard_map/while/body/eval_jaxpr/ppermute | solution.py:16
  642.0 1.9 copy-start.1
  643.9 3.9 slice-start
  644.6 3.2 slice-start.1
  655.5 11.3 %collective-permute-start.1 = (bf16[128,2048]{1,0:T(8,128)(2,1)}, bf16[128,2048]{1,0:T(8,128)(2,1)S(1)}, u32[]{:S(2)}, u32[]{:S(2)}) collective-permute-start(bf16[128,2048]{1,0:T(8,128)(2,1)} %get-tuple-element.1425), channel_id=1, source_target_pairs={{32,0},{64,32},{96,64},{128,96},{160,128},{192,160},{224,192},{33,... | collective-permute-start | bytes 1572872 | tf_op jit(solution)/shard_map/while/body/eval_jaxpr/ppermute | solution.py:16
  666.8 4.1 copy-start.2
  677.2 8.2 copy-start
  685.4 13.5 %collective-permute-start.2 = (f32[1024,2048]{1,0:T(8,128)}, f32[1024,2048]{1,0:T(8,128)}, u32[]{:S(2)}, u32[]{:S(2)}) collective-permute-start(f32[1024,2048]{1,0:T(8,128)} %dynamic-slice_bitcast_fusion.1), channel_id=1, source_target_pairs={{0,1},{1,0},{2,3},{3,2},{4,5},{5,4},{6,7},{7,6},{8,9},{9,8},{10,11... | collective-permute-start | bytes 25165832 | tf_op jit(solution)/shard_map/ppermute | solution.py:206
Sparse Core Ops, SparseCore 0:
  710.8 199.1 reduce-scatter.1

commit v3 on v1

--- a/solution.py
+++ b/solution.py
@@ -14,6 +14,18 @@
     devices = range(lax.axis_size(axis))
     route = [(i - distance, i) for i in devices if i - distance in devices]
     return lax.ppermute(block, axis, route)
+
+
+def scatter_sum(block, axis):
+    count = lax.axis_size(axis)
+    me = lax.axis_index(axis)
+    pieces = block.reshape(count, block.shape[0] // count, block.shape[1])
+    total = lax.dynamic_index_in_dim(pieces, me, 0, keepdims=False)
+    for shift in range(1, count):
+        sent = lax.dynamic_index_in_dim(pieces, (me + shift) % count, 0, keepdims=False)
+        route = [(i, (i + shift) % count) for i in range(count)]
+        total = total + lax.ppermute(sent, axis, route)
+    return total
 
 
 def allowed_pairs(pattern, outage):
@@ -189,25 +201,27 @@
 
     unused_rows, collected = lax.fori_loop(0, steps_total, backward_step, (zero_rows, totals_init))
     cores = lax.axis_size("core")
-    groups = lax.axis_size("dp_hi")
-    rows_each = width // (groups * cores)
-    normed_all = stashed[0].astype(jnp.bfloat16).reshape(micro * buses, groups, cores, rows_each)
-    normed_all = jnp.swapaxes(normed_all, 1, 2).reshape(micro * buses, width)
+    ys = lax.axis_size("y")
+    zs = lax.axis_size("z")
+    rows_each = width // (zs * ys * cores)
+    normed_all = stashed[0].astype(jnp.bfloat16).reshape(micro * buses, zs, ys, cores, rows_each)
+    normed_all = jnp.transpose(normed_all, (0, 3, 2, 1, 4)).reshape(micro * buses, width)
     grad = lax.dot_general(
         normed_all,
         collected.reshape(micro * buses, width),
         (((0,), (0,)), ((), ())),
         preferred_element_type=jnp.float32,
     )
-    half = lax.psum_scatter(grad, "core", scatter_dimension=0, tiled=True)
-    summed = lax.psum_scatter(half, "dp_hi", scatter_dimension=0, tiled=True)
+    summed = grad
+    for axis in ("core", "y", "z"):
+        summed = scatter_sum(summed, axis)
     return summed[None]
 
 
 def solution(mesh):
     sections, dp = mesh.devices.shape
-    split = Mesh(mesh.devices.reshape(sections, dp // 2, 2), ("section", "dp_hi", "core"))
-    rows = ("dp_hi", "core")
+    split = Mesh(mesh.devices.reshape(sections, 4, dp // 8, 2), ("section", "z", "y", "core"))
+    rows = ("z", "y", "core")
     in_specs = (
         P(rows, None, None),
         P(rows, None),

time: 946 us -> 978 us (1.034)
  starting transfers between devices: 132 us -> 251 us
  waiting for transfers between devices: 599 us -> 506 us
  other arithmetic: 50.6 us -> 64.8 us
  between operations: 13.5 us -> 0.11 us
  local copies, waits for them, and re-layouts: 67.5 us -> 80.7 us
    reduce_scatter x2 -> x0, waiting for transfers between devices: 237 us -> none  [the longest x1 134 us: per_device(): half = lax.psum_scatter(grad, 'core', scatter_dimension=0, tiled=True)]
    ppermute x0 -> x7, waiting for transfers between devices: none -> 148 us  [scatter_sum(): total = total + lax.ppermute(sent, axis, route)]
    ppermute x0 -> x7, starting transfers between devices: none -> 124 us  [scatter_sum(): total = total + lax.ppermute(sent, axis, route)]
    add x0 -> x2, other arithmetic: none -> 16 us  [scatter_sum(): total = total + lax.ppermute(sent, axis, route)]
    squeeze x0 -> x3, local copies, waits for them, and re-layouts: none -> 14.2 us  [scatter_sum(): lax.dynamic_index_in_dim(pieces, (me + shift) % count, 0, keepdims=False)]
  transfers between devices with their start and end apart: 24 -> 29, of which waited for: 24 -> 27; matrix products, arithmetic and copies ran while one was open for 0% -> 0% of each run, Pallas kernels for 0% -> 0%
where the time goes in v3:
time: 978 us; the launch traced here: 976 us
  waiting for transfers between devices  506 us (52%)
  starting transfers between devices  251 us (26%)
  local copies, waits for them, and re-layouts  80.7 us (8%)
  matrix products  71.9 us (7%)
  other arithmetic  64.8 us (7%)
    ppermute x22, waiting for transfers between devices, passed_along(): return lax.ppermute(block, axis, route)  358 us
    ppermute x7, waiting for transfers between devices, scatter_sum(): total = total + lax.ppermute(sent, axis, route)  148 us
    ppermute x22, starting transfers between devices, passed_along(): return lax.ppermute(block, axis, route)  127 us
    ppermute x7, starting transfers between devices, scatter_sum(): total = total + lax.ppermute(sent, axis, route)  124 us
    unnamed x13, local copies, waits for them, and re-layouts  22.6 us
  transfers between devices with their start and end apart: 29, of which 27 were waited for; matrix products, arithmetic and copies ran while one was open for 0% of the time, Pallas kernels for 0%

profile of v3, /device:TPU:96, one launch (start us, length us, event | category | flops | bytes accessed | tf_op | source)
XLA Modules:
  0.0 976.2 jit_solution(8120245949372155426)
XLA Ops:
  13.1 250.8 %while.48 = (s32[]{:T(128)}, bf16[128,2048]{0,1:T(8,128)(2,1)S(1)}, f32[4,128,2048]{1,2,0:T(8,128)}, f32[4,128,1]{1,2,0:T(1,128)S(1)}, bf16[4,128,16,128]{3,2,1,...) while((s32[]{:T(128)}, bf16[128,2048]{0,1:T(8,128)(2,1)S(1)}, ...), condition=%wide.region_8.9_spmd.clone, body=%wide.region_1.8_spmd.clone.sunk | while | flops 1216641408 | bytes 26020904 | solution.py:170
  13.2 12.1 %conditional.6 = (bf16[128,2048]{0,1:T(8,128)(2,1)S(1)}, f32[4,128,2048]{1,2,0:T(8,128)}, f32[4,128,1]{1,2,0:T(1,128)S(1)}, bf16[4,128,16,128]{3,2,1,0:T(8,128)(...) conditional(s32[]{:T(128)} %convert_element_type.254, ...), branch_computations={%region_2.2_spmd, %region_3.7_spmd} | conditional | flops 1216641408 | bytes 23923316 | solution.py:164
  26.6 11.4 %collective-permute-done = bf16[128,2048]{0,1:T(8,128)(2,1)S(1)} collective-permute-done((bf16[128,2048]{0,1:T(8,128)(2,1)S(1)}, bf16[128,2048]{0,1:T(8,128)(2,1)S(1)}, u32[]{:S(2)}, u32[]{:S(2)}) %collective-permute-start) | collective-permute-done | bytes 524320 | tf_op jit(solution)/shard_map/while/body/eval_jaxpr/ppermute | solution.py:16
  38.0 12.0 %conditional.6 = (bf16[128,2048]{0,1:T(8,128)(2,1)S(1)}, f32[4,128,2048]{1,2,0:T(8,128)}, f32[4,128,1]{1,2,0:T(1,128)S(1)}, bf16[4,128,16,128]{3,2,1,0:T(8,128)(...) conditional(s32[]{:T(128)} %convert_element_type.254, ...), branch_computations={%region_2.2_spmd, %region_3.7_spmd} | conditional | flops 1216641408 | bytes 23923316 | solution.py:164
  54.5 10.6 %collective-permute-done = bf16[128,2048]{0,1:T(8,128)(2,1)S(1)} collective-permute-done((bf16[128,2048]{0,1:T(8,128)(2,1)S(1)}, bf16[128,2048]{0,1:T(8,128)(2,1)S(1)}, u32[]{:S(2)}, u32[]{:S(2)}) %collective-permute-start) | collective-permute-done | bytes 524320 | tf_op jit(solution)/shard_map/while/body/eval_jaxpr/ppermute | solution.py:16
  65.1 12.1 %conditional.6 = (bf16[128,2048]{0,1:T(8,128)(2,1)S(1)}, f32[4,128,2048]{1,2,0:T(8,128)}, f32[4,128,1]{1,2,0:T(1,128)S(1)}, bf16[4,128,16,128]{3,2,1,0:T(8,128)(...) conditional(s32[]{:T(128)} %convert_element_type.254, ...), branch_computations={%region_2.2_spmd, %region_3.7_spmd} | conditional | flops 1216641408 | bytes 23923316 | solution.py:164
  81.5 9.7 collective-permute-done
  91.2 12.1 %conditional.6 = (bf16[128,2048]{0,1:T(8,128)(2,1)S(1)}, f32[4,128,2048]{1,2,0:T(8,128)}, f32[4,128,1]{1,2,0:T(1,128)S(1)}, bf16[4,128,16,128]{3,2,1,0:T(8,128)(...) conditional(s32[]{:T(128)} %convert_element_type.254, ...), branch_computations={%region_2.2_spmd, %region_3.7_spmd} | conditional | flops 1216641408 | bytes 23923316 | solution.py:164
  107.7 8.7 collective-permute-done
  116.5 16.4 %collective-permute-start = (bf16[128,2048]{0,1:T(8,128)(2,1)S(1)}, bf16[128,2048]{0,1:T(8,128)(2,1)S(1)}, u32[]{:S(2)}, u32[]{:S(2)}) collective-permute-start(bf16[128,2048]{0,1:T(8,128)(2,1)S(1)} %get-tuple-element.1409), channel_id=1, source_target_pairs={{0,32},{32,64},{64,96},{96,128},{128,160},{160,192},{192,224},{1,3... | collective-permute-start | bytes 1572872 | tf_op jit(solution)/shard_map/while/body/eval_jaxpr/ppermute | solution.py:16
  132.9 7.8 collective-permute-done
  145.2 6.9 collective-permute-done
  152.2 15.4 %collective-permute-start = (bf16[128,2048]{0,1:T(8,128)(2,1)S(1)}, bf16[128,2048]{0,1:T(8,128)(2,1)S(1)}, u32[]{:S(2)}, u32[]{:S(2)}) collective-permute-start(bf16[128,2048]{0,1:T(8,128)(2,1)S(1)} %get-tuple-element.1409), channel_id=1, source_target_pairs={{0,32},{32,64},{64,96},{96,128},{128,160},{160,192},{192,224},{1,3... | collective-permute-start | bytes 1572872 | tf_op jit(solution)/shard_map/while/body/eval_jaxpr/ppermute | solution.py:16
  167.6 6.6 collective-permute-done
  174.4 7.5 collective-permute-start
  181.9 6.6 collective-permute-done
  188.7 22.2 %collective-permute-start = (bf16[128,2048]{0,1:T(8,128)(2,1)S(1)}, bf16[128,2048]{0,1:T(8,128)(2,1)S(1)}, u32[]{:S(2)}, u32[]{:S(2)}) collective-permute-start(bf16[128,2048]{0,1:T(8,128)(2,1)S(1)} %get-tuple-element.1409), channel_id=1, source_target_pairs={{0,32},{32,64},{64,96},{96,128},{128,160},{160,192},{192,224},{1,3... | collective-permute-start | bytes 1572872 | tf_op jit(solution)/shard_map/while/body/eval_jaxpr/ppermute | solution.py:16
  210.9 6.6 collective-permute-done
  217.6 10.5 %collective-permute-start = (bf16[128,2048]{0,1:T(8,128)(2,1)S(1)}, bf16[128,2048]{0,1:T(8,128)(2,1)S(1)}, u32[]{:S(2)}, u32[]{:S(2)}) collective-permute-start(bf16[128,2048]{0,1:T(8,128)(2,1)S(1)} %get-tuple-element.1409), channel_id=1, source_target_pairs={{0,32},{32,64},{64,96},{96,128},{128,160},{160,192},{192,224},{1,3... | collective-permute-start | bytes 1572872 | tf_op jit(solution)/shard_map/while/body/eval_jaxpr/ppermute | solution.py:16
  228.1 6.6 collective-permute-done
  234.8 22.4 %collective-permute-start = (bf16[128,2048]{0,1:T(8,128)(2,1)S(1)}, bf16[128,2048]{0,1:T(8,128)(2,1)S(1)}, u32[]{:S(2)}, u32[]{:S(2)}) collective-permute-start(bf16[128,2048]{0,1:T(8,128)(2,1)S(1)} %get-tuple-element.1409), channel_id=1, source_target_pairs={{0,32},{32,64},{64,96},{96,128},{128,160},{160,192},{192,224},{1,3... | collective-permute-start | bytes 1572872 | tf_op jit(solution)/shard_map/while/body/eval_jaxpr/ppermute | solution.py:16
  257.3 6.6 collective-permute-done
  287.5 357.0 %while.49 = (s32[]{:T(128)}, bf16[128,2048]{1,0:T(8,128)(2,1)S(1)}, bf16[4,128,2048]{1,2,0:T(8,128)(2,1)}, s32[]{:T(128)}, pred[]{:T(512)}, /*index=5*/bf16[4,12...) while((s32[]{:T(128)}, bf16[128,2048]{1,0:T(8,128)(2,1)S(1)}, ...), condition=%wide.region_15.16_spmd.clone, body=%wide.region_9.15_spmd.clone.sunk | while | flops 1353218048 | bytes 71172608 | solution.py:202
  289.8 16.5 %collective-permute-done.1 = bf16[128,2048]{1,0:T(8,128)(2,1)S(1)} collective-permute-done((bf16[128,2048]{1,0:T(8,128)(2,1)}, bf16[128,2048]{1,0:T(8,128)(2,1)S(1)}, u32[]{:S(2)}, u32[]{:S(2)}) %collective-permute-start.1) | collective-permute-done | bytes 524320 | tf_op jit(solution)/shard_map/while/body/eval_jaxpr/ppermute | solution.py:16
  308.4 17.0 %collective-permute-done.1 = bf16[128,2048]{1,0:T(8,128)(2,1)S(1)} collective-permute-done((bf16[128,2048]{1,0:T(8,128)(2,1)}, bf16[128,2048]{1,0:T(8,128)(2,1)S(1)}, u32[]{:S(2)}, u32[]{:S(2)}) %collective-permute-start.1) | collective-permute-done | bytes 524320 | tf_op jit(solution)/shard_map/while/body/eval_jaxpr/ppermute | solution.py:16
  327.5 17.6 %collective-permute-done.1 = bf16[128,2048]{1,0:T(8,128)(2,1)S(1)} collective-permute-done((bf16[128,2048]{1,0:T(8,128)(2,1)}, bf16[128,2048]{1,0:T(8,128)(2,1)S(1)}, u32[]{:S(2)}, u32[]{:S(2)}) %collective-permute-start.1) | collective-permute-done | bytes 524320 | tf_op jit(solution)/shard_map/while/body/eval_jaxpr/ppermute | solution.py:16
  347.2 20.7 %collective-permute-done.1 = bf16[128,2048]{1,0:T(8,128)(2,1)S(1)} collective-permute-done((bf16[128,2048]{1,0:T(8,128)(2,1)}, bf16[128,2048]{1,0:T(8,128)(2,1)S(1)}, u32[]{:S(2)}, u32[]{:S(2)}) %collective-permute-start.1) | collective-permute-done | bytes 524320 | tf_op jit(solution)/shard_map/while/body/eval_jaxpr/ppermute | solution.py:16
  370.0 20.4 %collective-permute-done.1 = bf16[128,2048]{1,0:T(8,128)(2,1)S(1)} collective-permute-done((bf16[128,2048]{1,0:T(8,128)(2,1)}, bf16[128,2048]{1,0:T(8,128)(2,1)S(1)}, u32[]{:S(2)}, u32[]{:S(2)}) %collective-permute-start.1) | collective-permute-done | bytes 524320 | tf_op jit(solution)/shard_map/while/body/eval_jaxpr/ppermute | solution.py:16
  392.6 10.0 %collective-permute-done.1 = bf16[128,2048]{1,0:T(8,128)(2,1)S(1)} collective-permute-done((bf16[128,2048]{1,0:T(8,128)(2,1)}, bf16[128,2048]{1,0:T(8,128)(2,1)S(1)}, u32[]{:S(2)}, u32[]{:S(2)}) %collective-permute-start.1) | collective-permute-done | bytes 524320 | tf_op jit(solution)/shard_map/while/body/eval_jaxpr/ppermute | solution.py:16
  404.7 109.8 %collective-permute-done.1 = bf16[128,2048]{1,0:T(8,128)(2,1)S(1)} collective-permute-done((bf16[128,2048]{1,0:T(8,128)(2,1)}, bf16[128,2048]{1,0:T(8,128)(2,1)S(1)}, u32[]{:S(2)}, u32[]{:S(2)}) %collective-permute-start.1) | collective-permute-done | bytes 524320 | tf_op jit(solution)/shard_map/while/body/eval_jaxpr/ppermute | solution.py:16
  514.5 16.7 %conditional.7 = (bf16[128,2048]{1,0:T(8,128)(2,1)}, bf16[4,128,2048]{1,2,0:T(8,128)(2,1)}) conditional(s32[]{:T(128)} %convert_element_type.255, bf16[4,128,2048]{1,2,0:T(8,128)(2,1)} %get-tuple-element.1531, (pred[]{:T(512)}, s32[]{:T(128)}, bf16[4,128,2048]{2,1,0:T(8,128)(2,1)}, bf16[128,2048]{1,0:T(8,128)(2,1)S(1)}, ...), branch_computations={%region_10.10_spmd, %region_11.14_spmd} | conditional | flops 1353218048 | bytes 69075104 | solution.py:198
  532.5 16.0 %collective-permute-done.1 = bf16[128,2048]{1,0:T(8,128)(2,1)S(1)} collective-permute-done((bf16[128,2048]{1,0:T(8,128)(2,1)}, bf16[128,2048]{1,0:T(8,128)(2,1)S(1)}, u32[]{:S(2)}, u32[]{:S(2)}) %collective-permute-start.1) | collective-permute-done | bytes 524320 | tf_op jit(solution)/shard_map/while/body/eval_jaxpr/ppermute | solution.py:16
  548.5 16.7 %conditional.7 = (bf16[128,2048]{1,0:T(8,128)(2,1)}, bf16[4,128,2048]{1,2,0:T(8,128)(2,1)}) conditional(s32[]{:T(128)} %convert_element_type.255, bf16[4,128,2048]{1,2,0:T(8,128)(2,1)} %get-tuple-element.1531, (pred[]{:T(512)}, s32[]{:T(128)}, bf16[4,128,2048]{2,1,0:T(8,128)(2,1)}, bf16[128,2048]{1,0:T(8,128)(2,1)S(1)}, ...), branch_computations={%region_10.10_spmd, %region_11.14_spmd} | conditional | flops 1353218048 | bytes 69075104 | solution.py:198
  566.4 16.1 %collective-permute-done.1 = bf16[128,2048]{1,0:T(8,128)(2,1)S(1)} collective-permute-done((bf16[128,2048]{1,0:T(8,128)(2,1)}, bf16[128,2048]{1,0:T(8,128)(2,1)S(1)}, u32[]{:S(2)}, u32[]{:S(2)}) %collective-permute-start.1) | collective-permute-done | bytes 524320 | tf_op jit(solution)/shard_map/while/body/eval_jaxpr/ppermute | solution.py:16
  582.5 16.7 %conditional.7 = (bf16[128,2048]{1,0:T(8,128)(2,1)}, bf16[4,128,2048]{1,2,0:T(8,128)(2,1)}) conditional(s32[]{:T(128)} %convert_element_type.255, bf16[4,128,2048]{1,2,0:T(8,128)(2,1)} %get-tuple-element.1531, (pred[]{:T(512)}, s32[]{:T(128)}, bf16[4,128,2048]{2,1,0:T(8,128)(2,1)}, bf16[128,2048]{1,0:T(8,128)(2,1)S(1)}, ...), branch_computations={%region_10.10_spmd, %region_11.14_spmd} | conditional | flops 1353218048 | bytes 69075104 | solution.py:198
  600.5 16.0 %collective-permute-done.1 = bf16[128,2048]{1,0:T(8,128)(2,1)S(1)} collective-permute-done((bf16[128,2048]{1,0:T(8,128)(2,1)}, bf16[128,2048]{1,0:T(8,128)(2,1)S(1)}, u32[]{:S(2)}, u32[]{:S(2)}) %collective-permute-start.1) | collective-permute-done | bytes 524320 | tf_op jit(solution)/shard_map/while/body/eval_jaxpr/ppermute | solution.py:16
  616.5 16.7 %conditional.7 = (bf16[128,2048]{1,0:T(8,128)(2,1)}, bf16[4,128,2048]{1,2,0:T(8,128)(2,1)}) conditional(s32[]{:T(128)} %convert_element_type.255, bf16[4,128,2048]{1,2,0:T(8,128)(2,1)} %get-tuple-element.1531, (pred[]{:T(512)}, s32[]{:T(128)}, bf16[4,128,2048]{2,1,0:T(8,128)(2,1)}, bf16[128,2048]{1,0:T(8,128)(2,1)S(1)}, ...), branch_computations={%region_10.10_spmd, %region_11.14_spmd} | conditional | flops 1353218048 | bytes 69075104 | solution.py:198
  634.4 10.0 %collective-permute-done.1 = bf16[128,2048]{1,0:T(8,128)(2,1)S(1)} collective-permute-done((bf16[128,2048]{1,0:T(8,128)(2,1)}, bf16[128,2048]{1,0:T(8,128)(2,1)S(1)}, u32[]{:S(2)}, u32[]{:S(2)}) %collective-permute-start.1) | collective-permute-done | bytes 524320 | tf_op jit(solution)/shard_map/while/body/eval_jaxpr/ppermute | solution.py:16
  648.5 10.7 %copy.77 = bf16[4,128,2048]{1,0,2:T(4,128)(2,1)} copy(bf16[4,128,2048]{1,2,0:T(8,128)(2,1)S(1)} %copy-done.1) | data formatting | bytes 4194304 | tf_op jit(solution)/shard_map/convert_element_type | solution.py:207
  663.6 8.3 fusion.83
  671.9 7.7 dynamic-slice_bitcast_fusion.1
  679.6 13.5 %collective-permute-done.2 = f32[1024,2048]{1,0:T(8,128)} collective-permute-done((f32[1024,2048]{1,0:T(8,128)}, f32[1024,2048]{1,0:T(8,128)}, u32[]{:S(2)}, u32[]{:S(2)}) %collective-permute-start.2) | collective-permute-done | bytes 8388640 | tf_op jit(solution)/shard_map/ppermute | solution.py:27
  693.1 11.7 %bitcast_add_fusion = f32[1024,2048]{1,0:T(8,128)} fusion(f32[1024,2048]{1,0:T(8,128)} %collective-permute-done.2, f32[2,1024,2048]{2,1,0:T(8,128)} %fusion.83, s32[]{:T(128)S(6)} %select_n.213), kind=kLoop, calls=%fused_computation.103 | loop fusion | flops 2097152 | bytes 25165828 | tf_op jit(solution)/shard_map/add | solution.py:27
  716.0 43.5 %collective-permute-done.3 = f32[256,2048]{1,0:T(8,128)} collective-permute-done((f32[256,2048]{1,0:T(8,128)}, f32[256,2048]{1,0:T(8,128)}, u32[]{:S(2)}, u32[]{:S(2)}) %collective-permute-start.3) | collective-permute-done | bytes 2097184 | tf_op jit(solution)/shard_map/ppermute | solution.py:27
  759.5 46.1 %collective-permute-done.4 = f32[256,2048]{1,0:T(8,128)} collective-permute-done((f32[256,2048]{1,0:T(8,128)}, f32[256,2048]{1,0:T(8,128)}, u32[]{:S(2)}, u32[]{:S(2)}) %collective-permute-start.4) | collective-permute-done | bytes 2097184 | tf_op jit(solution)/shard_map/ppermute | solution.py:27
  810.8 118.0 %collective-permute-start.7 = (f32[64,2048]{1,0:T(8,128)S(1)}, f32[64,2048]{1,0:T(8,128)}, u32[]{:S(2)}, u32[]{:S(2)}) collective-permute-start(f32[64,2048]{1,0:T(8,128)S(1)} %get-tuple-element.1216), channel_id=1, source_target_pairs={{0,16},{8,24},{16,0},{24,8},{1,17},{9,25},{17,1},{25,9},{2,18},{10... | collective-permute-start | bytes 1572872 | tf_op jit(solution)/shard_map/ppermute | solution.py:27
  928.8 10.2 %collective-permute-done.6 = f32[64,2048]{1,0:T(8,128)} collective-permute-done((f32[64,2048]{1,0:T(8,128)}, f32[64,2048]{1,0:T(8,128)}, u32[]{:S(2)}, u32[]{:S(2)}) %collective-permute-start.6) | collective-permute-done | bytes 524320 | tf_op jit(solution)/shard_map/ppermute | solution.py:27
  939.0 34.9 %collective-permute-done.7 = f32[64,2048]{1,0:T(8,128)} collective-permute-done((f32[64,2048]{1,0:T(8,128)S(1)}, f32[64,2048]{1,0:T(8,128)}, u32[]{:S(2)}, u32[]{:S(2)}) %collective-permute-start.7) | collective-permute-done | bytes 524320 | tf_op jit(solution)/shard_map/ppermute | solution.py:27
  (254 shorter events, 224.3 us)
Async XLA Ops:
  9.8 3.3 copy-start.4
  25.3 12.7 %collective-permute-start = (bf16[128,2048]{0,1:T(8,128)(2,1)S(1)}, bf16[128,2048]{0,1:T(8,128)(2,1)S(1)}, u32[]{:S(2)}, u32[]{:S(2)}) collective-permute-start(bf16[128,2048]{0,1:T(8,128)(2,1)S(1)} %get-tuple-element.1409), channel_id=1, source_target_pairs={{0,32},{32,64},{64,96},{96,128},{128,160},{160,192},{192,224},{1,3... | collective-permute-start | bytes 1572872 | tf_op jit(solution)/shard_map/while/body/eval_jaxpr/ppermute | solution.py:16
  50.0 15.1 %collective-permute-start = (bf16[128,2048]{0,1:T(8,128)(2,1)S(1)}, bf16[128,2048]{0,1:T(8,128)(2,1)S(1)}, u32[]{:S(2)}, u32[]{:S(2)}) collective-permute-start(bf16[128,2048]{0,1:T(8,128)(2,1)S(1)} %get-tuple-element.1409), channel_id=1, source_target_pairs={{0,32},{32,64},{64,96},{96,128},{128,160},{160,192},{192,224},{1,3... | collective-permute-start | bytes 1572872 | tf_op jit(solution)/shard_map/while/body/eval_jaxpr/ppermute | solution.py:16
  77.2 14.0 %collective-permute-start = (bf16[128,2048]{0,1:T(8,128)(2,1)S(1)}, bf16[128,2048]{0,1:T(8,128)(2,1)S(1)}, u32[]{:S(2)}, u32[]{:S(2)}) collective-permute-start(bf16[128,2048]{0,1:T(8,128)(2,1)S(1)} %get-tuple-element.1409), channel_id=1, source_target_pairs={{0,32},{32,64},{64,96},{96,128},{128,160},{160,192},{192,224},{1,3... | collective-permute-start | bytes 1572872 | tf_op jit(solution)/shard_map/while/body/eval_jaxpr/ppermute | solution.py:16
  103.2 13.2 %collective-permute-start = (bf16[128,2048]{0,1:T(8,128)(2,1)S(1)}, bf16[128,2048]{0,1:T(8,128)(2,1)S(1)}, u32[]{:S(2)}, u32[]{:S(2)}) collective-permute-start(bf16[128,2048]{0,1:T(8,128)(2,1)S(1)} %get-tuple-element.1409), channel_id=1, source_target_pairs={{0,32},{32,64},{64,96},{96,128},{128,160},{160,192},{192,224},{1,3... | collective-permute-start | bytes 1572872 | tf_op jit(solution)/shard_map/while/body/eval_jaxpr/ppermute | solution.py:16
  116.5 24.2 %collective-permute-start = (bf16[128,2048]{0,1:T(8,128)(2,1)S(1)}, bf16[128,2048]{0,1:T(8,128)(2,1)S(1)}, u32[]{:S(2)}, u32[]{:S(2)}) collective-permute-start(bf16[128,2048]{0,1:T(8,128)(2,1)S(1)} %get-tuple-element.1409), channel_id=1, source_target_pairs={{0,32},{32,64},{64,96},{96,128},{128,160},{160,192},{192,224},{1,3... | collective-permute-start | bytes 1572872 | tf_op jit(solution)/shard_map/while/body/eval_jaxpr/ppermute | solution.py:16
  140.8 11.3 %collective-permute-start = (bf16[128,2048]{0,1:T(8,128)(2,1)S(1)}, bf16[128,2048]{0,1:T(8,128)(2,1)S(1)}, u32[]{:S(2)}, u32[]{:S(2)}) collective-permute-start(bf16[128,2048]{0,1:T(8,128)(2,1)S(1)} %get-tuple-element.1409), channel_id=1, source_target_pairs={{0,32},{32,64},{64,96},{96,128},{128,160},{160,192},{192,224},{1,3... | collective-permute-start | bytes 1572872 | tf_op jit(solution)/shard_map/while/body/eval_jaxpr/ppermute | solution.py:16
  152.2 22.1 %collective-permute-start = (bf16[128,2048]{0,1:T(8,128)(2,1)S(1)}, bf16[128,2048]{0,1:T(8,128)(2,1)S(1)}, u32[]{:S(2)}, u32[]{:S(2)}) collective-permute-start(bf16[128,2048]{0,1:T(8,128)(2,1)S(1)} %get-tuple-element.1409), channel_id=1, source_target_pairs={{0,32},{32,64},{64,96},{96,128},{128,160},{160,192},{192,224},{1,3... | collective-permute-start | bytes 1572872 | tf_op jit(solution)/shard_map/while/body/eval_jaxpr/ppermute | solution.py:16
  174.4 14.2 %collective-permute-start = (bf16[128,2048]{0,1:T(8,128)(2,1)S(1)}, bf16[128,2048]{0,1:T(8,128)(2,1)S(1)}, u32[]{:S(2)}, u32[]{:S(2)}) collective-permute-start(bf16[128,2048]{0,1:T(8,128)(2,1)S(1)} %get-tuple-element.1409), channel_id=1, source_target_pairs={{0,32},{32,64},{64,96},{96,128},{128,160},{160,192},{192,224},{1,3... | collective-permute-start | bytes 1572872 | tf_op jit(solution)/shard_map/while/body/eval_jaxpr/ppermute | solution.py:16
  188.7 28.9 %collective-permute-start = (bf16[128,2048]{0,1:T(8,128)(2,1)S(1)}, bf16[128,2048]{0,1:T(8,128)(2,1)S(1)}, u32[]{:S(2)}, u32[]{:S(2)}) collective-permute-start(bf16[128,2048]{0,1:T(8,128)(2,1)S(1)} %get-tuple-element.1409), channel_id=1, source_target_pairs={{0,32},{32,64},{64,96},{96,128},{128,160},{160,192},{192,224},{1,3... | collective-permute-start | bytes 1572872 | tf_op jit(solution)/shard_map/while/body/eval_jaxpr/ppermute | solution.py:16
  217.6 17.1 %collective-permute-start = (bf16[128,2048]{0,1:T(8,128)(2,1)S(1)}, bf16[128,2048]{0,1:T(8,128)(2,1)S(1)}, u32[]{:S(2)}, u32[]{:S(2)}) collective-permute-start(bf16[128,2048]{0,1:T(8,128)(2,1)S(1)} %get-tuple-element.1409), channel_id=1, source_target_pairs={{0,32},{32,64},{64,96},{96,128},{128,160},{160,192},{192,224},{1,3... | collective-permute-start | bytes 1572872 | tf_op jit(solution)/shard_map/while/body/eval_jaxpr/ppermute | solution.py:16
  234.8 29.1 %collective-permute-start = (bf16[128,2048]{0,1:T(8,128)(2,1)S(1)}, bf16[128,2048]{0,1:T(8,128)(2,1)S(1)}, u32[]{:S(2)}, u32[]{:S(2)}) collective-permute-start(bf16[128,2048]{0,1:T(8,128)(2,1)S(1)} %get-tuple-element.1409), channel_id=1, source_target_pairs={{0,32},{32,64},{64,96},{96,128},{128,160},{160,192},{192,224},{1,3... | collective-permute-start | bytes 1572872 | tf_op jit(solution)/shard_map/while/body/eval_jaxpr/ppermute | solution.py:16
  273.1 5.5 copy-start.2
  288.5 17.8 %collective-permute-start.1 = (bf16[128,2048]{1,0:T(8,128)(2,1)}, bf16[128,2048]{1,0:T(8,128)(2,1)S(1)}, u32[]{:S(2)}, u32[]{:S(2)}) collective-permute-start(bf16[128,2048]{1,0:T(8,128)(2,1)} %get-tuple-element.1431), channel_id=1, source_target_pairs={{32,0},{64,32},{96,64},{128,96},{160,128},{192,160},{224,192},{33,... | collective-permute-start | bytes 1572872 | tf_op jit(solution)/shard_map/while/body/eval_jaxpr/ppermute | solution.py:16
  307.1 18.3 %collective-permute-start.1 = (bf16[128,2048]{1,0:T(8,128)(2,1)}, bf16[128,2048]{1,0:T(8,128)(2,1)S(1)}, u32[]{:S(2)}, u32[]{:S(2)}) collective-permute-start(bf16[128,2048]{1,0:T(8,128)(2,1)} %get-tuple-element.1431), channel_id=1, source_target_pairs={{32,0},{64,32},{96,64},{128,96},{160,128},{192,160},{224,192},{33,... | collective-permute-start | bytes 1572872 | tf_op jit(solution)/shard_map/while/body/eval_jaxpr/ppermute | solution.py:16
  326.2 18.8 %collective-permute-start.1 = (bf16[128,2048]{1,0:T(8,128)(2,1)}, bf16[128,2048]{1,0:T(8,128)(2,1)S(1)}, u32[]{:S(2)}, u32[]{:S(2)}) collective-permute-start(bf16[128,2048]{1,0:T(8,128)(2,1)} %get-tuple-element.1431), channel_id=1, source_target_pairs={{32,0},{64,32},{96,64},{128,96},{160,128},{192,160},{224,192},{33,... | collective-permute-start | bytes 1572872 | tf_op jit(solution)/shard_map/while/body/eval_jaxpr/ppermute | solution.py:16
  345.9 22.0 %collective-permute-start.1 = (bf16[128,2048]{1,0:T(8,128)(2,1)}, bf16[128,2048]{1,0:T(8,128)(2,1)S(1)}, u32[]{:S(2)}, u32[]{:S(2)}) collective-permute-start(bf16[128,2048]{1,0:T(8,128)(2,1)} %get-tuple-element.1431), channel_id=1, source_target_pairs={{32,0},{64,32},{96,64},{128,96},{160,128},{192,160},{224,192},{33,... | collective-permute-start | bytes 1572872 | tf_op jit(solution)/shard_map/while/body/eval_jaxpr/ppermute | solution.py:16
  368.7 21.7 %collective-permute-start.1 = (bf16[128,2048]{1,0:T(8,128)(2,1)}, bf16[128,2048]{1,0:T(8,128)(2,1)S(1)}, u32[]{:S(2)}, u32[]{:S(2)}) collective-permute-start(bf16[128,2048]{1,0:T(8,128)(2,1)} %get-tuple-element.1431), channel_id=1, source_target_pairs={{32,0},{64,32},{96,64},{128,96},{160,128},{192,160},{224,192},{33,... | collective-permute-start | bytes 1572872 | tf_op jit(solution)/shard_map/while/body/eval_jaxpr/ppermute | solution.py:16
  391.3 11.3 %collective-permute-start.1 = (bf16[128,2048]{1,0:T(8,128)(2,1)}, bf16[128,2048]{1,0:T(8,128)(2,1)S(1)}, u32[]{:S(2)}, u32[]{:S(2)}) collective-permute-start(bf16[128,2048]{1,0:T(8,128)(2,1)} %get-tuple-element.1431), channel_id=1, source_target_pairs={{32,0},{64,32},{96,64},{128,96},{160,128},{192,160},{224,192},{33,... | collective-permute-start | bytes 1572872 | tf_op jit(solution)/shard_map/while/body/eval_jaxpr/ppermute | solution.py:16
  403.4 111.1 %collective-permute-start.1 = (bf16[128,2048]{1,0:T(8,128)(2,1)}, bf16[128,2048]{1,0:T(8,128)(2,1)S(1)}, u32[]{:S(2)}, u32[]{:S(2)}) collective-permute-start(bf16[128,2048]{1,0:T(8,128)(2,1)} %get-tuple-element.1431), channel_id=1, source_target_pairs={{32,0},{64,32},{96,64},{128,96},{160,128},{192,160},{224,192},{33,... | collective-permute-start | bytes 1572872 | tf_op jit(solution)/shard_map/while/body/eval_jaxpr/ppermute | solution.py:16
  517.6 1.9 copy-start
  519.5 4.8 slice-start
  520.3 4.1 slice-start.1
  531.2 17.3 %collective-permute-start.1 = (bf16[128,2048]{1,0:T(8,128)(2,1)}, bf16[128,2048]{1,0:T(8,128)(2,1)S(1)}, u32[]{:S(2)}, u32[]{:S(2)}) collective-permute-start(bf16[128,2048]{1,0:T(8,128)(2,1)} %get-tuple-element.1431), channel_id=1, source_target_pairs={{32,0},{64,32},{96,64},{128,96},{160,128},{192,160},{224,192},{33,... | collective-permute-start | bytes 1572872 | tf_op jit(solution)/shard_map/while/body/eval_jaxpr/ppermute | solution.py:16
  551.6 1.9 copy-start
  553.5 4.8 slice-start
  554.2 4.1 slice-start.1
  565.2 17.3 %collective-permute-start.1 = (bf16[128,2048]{1,0:T(8,128)(2,1)}, bf16[128,2048]{1,0:T(8,128)(2,1)S(1)}, u32[]{:S(2)}, u32[]{:S(2)}) collective-permute-start(bf16[128,2048]{1,0:T(8,128)(2,1)} %get-tuple-element.1431), channel_id=1, source_target_pairs={{32,0},{64,32},{96,64},{128,96},{160,128},{192,160},{224,192},{33,... | collective-permute-start | bytes 1572872 | tf_op jit(solution)/shard_map/while/body/eval_jaxpr/ppermute | solution.py:16
  585.6 1.9 copy-start
  587.5 4.8 slice-start
  588.2 4.1 slice-start.1
  599.2 17.3 %collective-permute-start.1 = (bf16[128,2048]{1,0:T(8,128)(2,1)}, bf16[128,2048]{1,0:T(8,128)(2,1)S(1)}, u32[]{:S(2)}, u32[]{:S(2)}) collective-permute-start(bf16[128,2048]{1,0:T(8,128)(2,1)} %get-tuple-element.1431), channel_id=1, source_target_pairs={{32,0},{64,32},{96,64},{128,96},{160,128},{192,160},{224,192},{33,... | collective-permute-start | bytes 1572872 | tf_op jit(solution)/shard_map/while/body/eval_jaxpr/ppermute | solution.py:16
  619.6 1.9 copy-start
  621.5 4.8 slice-start
  622.2 4.1 slice-start.1
  633.1 11.3 %collective-permute-start.1 = (bf16[128,2048]{1,0:T(8,128)(2,1)}, bf16[128,2048]{1,0:T(8,128)(2,1)S(1)}, u32[]{:S(2)}, u32[]{:S(2)}) collective-permute-start(bf16[128,2048]{1,0:T(8,128)(2,1)} %get-tuple-element.1431), channel_id=1, source_target_pairs={{32,0},{64,32},{96,64},{128,96},{160,128},{192,160},{224,192},{33,... | collective-permute-start | bytes 1572872 | tf_op jit(solution)/shard_map/while/body/eval_jaxpr/ppermute | solution.py:16
  644.4 4.1 copy-start.1
  662.0 1.6 copy-start.3
  679.6 13.5 %collective-permute-start.2 = (f32[1024,2048]{1,0:T(8,128)}, f32[1024,2048]{1,0:T(8,128)}, u32[]{:S(2)}, u32[]{:S(2)}) collective-permute-start(f32[1024,2048]{1,0:T(8,128)} %dynamic-slice_bitcast_fusion.1), channel_id=1, source_target_pairs={{0,1},{1,0},{2,3},{3,2},{4,5},{5,4},{6,7},{7,6},{8,9},{9,8},{10,11... | collective-permute-start | bytes 25165832 | tf_op jit(solution)/shard_map/ppermute | solution.py:27
  710.3 49.2 %collective-permute-start.3 = (f32[256,2048]{1,0:T(8,128)}, f32[256,2048]{1,0:T(8,128)}, u32[]{:S(2)}, u32[]{:S(2)}) collective-permute-start(f32[256,2048]{1,0:T(8,128)} %get-tuple-element.1211), channel_id=1, source_target_pairs={{0,2},{2,4},{4,6},{6,0},{1,3},{3,5},{5,7},{7,1},{8,10},{10,12},{12... | collective-permute-start | bytes 6291464 | tf_op jit(solution)/shard_map/ppermute | solution.py:27
  711.9 93.7 %collective-permute-start.4 = (f32[256,2048]{1,0:T(8,128)}, f32[256,2048]{1,0:T(8,128)}, u32[]{:S(2)}, u32[]{:S(2)}) collective-permute-start(f32[256,2048]{1,0:T(8,128)} %get-tuple-element.1213), channel_id=1, source_target_pairs={{0,4},{2,6},{4,0},{6,2},{1,5},{3,7},{5,1},{7,3},{8,12},{10,14},{12... | collective-permute-start | bytes 6291464 | tf_op jit(solution)/shard_map/ppermute | solution.py:27
  714.7 90.9 %collective-permute-start.5 = (f32[256,2048]{1,0:T(8,128)S(1)}, f32[256,2048]{1,0:T(8,128)}, u32[]{:S(2)}, u32[]{:S(2)}) collective-permute-start(f32[256,2048]{1,0:T(8,128)S(1)} %get-tuple-element.1212), channel_id=1, source_target_pairs={{0,6},{2,0},{4,2},{6,4},{1,7},{3,1},{5,3},{7,5},{8,14},{10,8},{12,... | collective-permute-start | bytes 6291464 | tf_op jit(solution)/shard_map/ppermute | solution.py:27
  810.8 128.2 %collective-permute-start.6 = (f32[64,2048]{1,0:T(8,128)}, f32[64,2048]{1,0:T(8,128)}, u32[]{:S(2)}, u32[]{:S(2)}) collective-permute-start(f32[64,2048]{1,0:T(8,128)} %get-tuple-element.1214), channel_id=1, source_target_pairs={{0,8},{8,16},{16,24},{24,0},{1,9},{9,17},{17,25},{25,1},{2,10},{10... | collective-permute-start | bytes 1572872 | tf_op jit(solution)/shard_map/ppermute | solution.py:27
  810.8 163.1 %collective-permute-start.7 = (f32[64,2048]{1,0:T(8,128)S(1)}, f32[64,2048]{1,0:T(8,128)}, u32[]{:S(2)}, u32[]{:S(2)}) collective-permute-start(f32[64,2048]{1,0:T(8,128)S(1)} %get-tuple-element.1216), channel_id=1, source_target_pairs={{0,16},{8,24},{16,0},{24,8},{1,17},{9,25},{17,1},{25,9},{2,18},{10... | collective-permute-start | bytes 1572872 | tf_op jit(solution)/shard_map/ppermute | solution.py:27
  928.8 45.1 %collective-permute-start.8 = (f32[64,2048]{1,0:T(8,128)S(1)}, f32[64,2048]{1,0:T(8,128)}, u32[]{:S(2)}, u32[]{:S(2)}) collective-permute-start(f32[64,2048]{1,0:T(8,128)S(1)} %get-tuple-element.1215), channel_id=1, source_target_pairs={{0,24},{8,0},{16,8},{24,16},{1,25},{9,1},{17,9},{25,17},{2,26},{10... | collective-permute-start | bytes 1572872 | tf_op jit(solution)/shard_map/ppermute | solution.py:27

commit v4 on v1

--- a/solution.py
+++ b/solution.py
@@ -190,17 +190,25 @@
     unused_rows, collected = lax.fori_loop(0, steps_total, backward_step, (zero_rows, totals_init))
     cores = lax.axis_size("core")
     groups = lax.axis_size("dp_hi")
+    core = lax.axis_index("core")
     rows_each = width // (groups * cores)
     normed_all = stashed[0].astype(jnp.bfloat16).reshape(micro * buses, groups, cores, rows_each)
-    normed_all = jnp.swapaxes(normed_all, 1, 2).reshape(micro * buses, width)
-    grad = lax.dot_general(
-        normed_all,
-        collected.reshape(micro * buses, width),
-        (((0,), (0,)), ((), ())),
-        preferred_element_type=jnp.float32,
-    )
-    half = lax.psum_scatter(grad, "core", scatter_dimension=0, tiled=True)
-    summed = lax.psum_scatter(half, "dp_hi", scatter_dimension=0, tiled=True)
+    totals_all = collected.reshape(micro * buses, width)
+
+    def partial_grad(which):
+        chosen = lax.dynamic_index_in_dim(normed_all, which, 2, keepdims=False)
+        return lax.dot_general(
+            chosen.reshape(micro * buses, groups * rows_each),
+            totals_all,
+            (((0,), (0,)), ((), ())),
+            preferred_element_type=jnp.float32,
+        )
+
+    received = lax.ppermute(partial_grad(1 - core), "core", [(0, 1), (1, 0)])
+    half = lax.optimization_barrier(partial_grad(core)) + received
+    summed = lax.psum_scatter(
+        half.astype(jnp.bfloat16), "dp_hi", scatter_dimension=0, tiled=True
+    ).astype(jnp.float32)
     return summed[None]
 
 

time: 946 us -> 916 us (0.968)
  waiting for transfers between devices: 599 us -> 557 us
  other arithmetic: 50.6 us -> 61.6 us
    reduce_scatter x2 -> x1, waiting for transfers between devices: 237 us -> 188 us  [per_device(): lax.psum_scatter(half.astype(jnp.bfloat16), 'dp_hi', scatter_dimension=0,...]
  transfers between devices with their start and end apart: 24 -> 24, of which waited for: 24 -> 24; matrix products, arithmetic and copies ran while one was open for 0% -> 1% of each run, Pallas kernels for 0% -> 0%
where the time goes in v4:
time: 916 us; the launch traced here: 905 us
  waiting for transfers between devices  557 us (61%)
  starting transfers between devices  132 us (14%)
  matrix products  71.5 us (8%)
  local copies, waits for them, and re-layouts  67.6 us (7%)
  other arithmetic  61.6 us (7%)
  between operations  13.5 us (1%)
    ppermute x22, waiting for transfers between devices, passed_along(): return lax.ppermute(block, axis, route)  362 us
    reduce_scatter x1, waiting for transfers between devices, per_device(): lax.psum_scatter(half.astype(jnp.bfloat16), 'dp_hi', scatter_dimension=0,...  188 us
    ppermute x22, starting transfers between devices, passed_along(): return lax.ppermute(block, axis, route)  132 us
    unnamed x13, local copies, waits for them, and re-layouts  23.4 us
    dot_general x4, matrix products, layer_forward(): jnp.dot(normed.reshape(-1, width), weight, preferred_element_type=jnp.flo...  18.7 us
  transfers between devices with their start and end apart: 24, of which 24 were waited for; matrix products, arithmetic and copies ran while one was open for 1% of the time, Pallas kernels for 0%

profile of v4, /device:TPU:96, one launch (start us, length us, event | category | flops | bytes accessed | tf_op | source)
XLA Modules:
  0.0 904.6 jit_solution(6192704213205864034)
XLA Ops:
  20.5 259.0 %while.48 = (s32[]{:T(128)}, bf16[128,2048]{0,1:T(8,128)(2,1)S(1)}, f32[4,128,2048]{1,2,0:T(8,128)}, f32[4,128,1]{1,2,0:T(1,128)S(1)}, bf16[4,128,16,128]{3,2,1,...) while((s32[]{:T(128)}, bf16[128,2048]{0,1:T(8,128)(2,1)S(1)}, ...), condition=%wide.region_8.9_spmd.clone, body=%wide.region_1.8_spmd.clone.sunk | while | flops 1216641408 | bytes 26020904 | solution.py:158
  20.6 13.2 %conditional.6 = (bf16[128,2048]{0,1:T(8,128)(2,1)S(1)}, f32[4,128,2048]{1,2,0:T(8,128)}, f32[4,128,1]{1,2,0:T(1,128)S(1)}, bf16[4,128,16,128]{3,2,1,0:T(8,128)(...) conditional(s32[]{:T(128)} %convert_element_type.260, ...), branch_computations={%region_2.2_spmd, %region_3.7_spmd} | conditional | flops 1216641408 | bytes 23923316 | solution.py:152
  22.2 4.7 convolution_convert_fusion
  35.0 11.4 %collective-permute-done = bf16[128,2048]{0,1:T(8,128)(2,1)S(1)} collective-permute-done((bf16[128,2048]{0,1:T(8,128)(2,1)S(1)}, bf16[128,2048]{0,1:T(8,128)(2,1)S(1)}, u32[]{:S(2)}, u32[]{:S(2)}) %collective-permute-start) | collective-permute-done | bytes 524320 | tf_op jit(solution)/shard_map/while/body/eval_jaxpr/ppermute | solution.py:16
  46.4 13.0 %conditional.6 = (bf16[128,2048]{0,1:T(8,128)(2,1)S(1)}, f32[4,128,2048]{1,2,0:T(8,128)}, f32[4,128,1]{1,2,0:T(1,128)S(1)}, bf16[4,128,16,128]{3,2,1,0:T(8,128)(...) conditional(s32[]{:T(128)} %convert_element_type.260, ...), branch_computations={%region_2.2_spmd, %region_3.7_spmd} | conditional | flops 1216641408 | bytes 23923316 | solution.py:152
  48.1 4.7 convolution_convert_fusion
  64.0 10.6 %collective-permute-done = bf16[128,2048]{0,1:T(8,128)(2,1)S(1)} collective-permute-done((bf16[128,2048]{0,1:T(8,128)(2,1)S(1)}, bf16[128,2048]{0,1:T(8,128)(2,1)S(1)}, u32[]{:S(2)}, u32[]{:S(2)}) %collective-permute-start) | collective-permute-done | bytes 524320 | tf_op jit(solution)/shard_map/while/body/eval_jaxpr/ppermute | solution.py:16
  74.6 13.1 %conditional.6 = (bf16[128,2048]{0,1:T(8,128)(2,1)S(1)}, f32[4,128,2048]{1,2,0:T(8,128)}, f32[4,128,1]{1,2,0:T(1,128)S(1)}, bf16[4,128,16,128]{3,2,1,0:T(8,128)(...) conditional(s32[]{:T(128)} %convert_element_type.260, ...), branch_computations={%region_2.2_spmd, %region_3.7_spmd} | conditional | flops 1216641408 | bytes 23923316 | solution.py:152
  76.2 4.7 convolution_convert_fusion
  92.0 9.6 %collective-permute-done = bf16[128,2048]{0,1:T(8,128)(2,1)S(1)} collective-permute-done((bf16[128,2048]{0,1:T(8,128)(2,1)S(1)}, bf16[128,2048]{0,1:T(8,128)(2,1)S(1)}, u32[]{:S(2)}, u32[]{:S(2)}) %collective-permute-start) | collective-permute-done | bytes 524320 | tf_op jit(solution)/shard_map/while/body/eval_jaxpr/ppermute | solution.py:16
  101.7 13.1 %conditional.6 = (bf16[128,2048]{0,1:T(8,128)(2,1)S(1)}, f32[4,128,2048]{1,2,0:T(8,128)}, f32[4,128,1]{1,2,0:T(1,128)S(1)}, bf16[4,128,16,128]{3,2,1,0:T(8,128)(...) conditional(s32[]{:T(128)} %convert_element_type.260, ...), branch_computations={%region_2.2_spmd, %region_3.7_spmd} | conditional | flops 1216641408 | bytes 23923316 | solution.py:152
  119.2 8.7 collective-permute-done
  128.0 17.4 %collective-permute-start = (bf16[128,2048]{0,1:T(8,128)(2,1)S(1)}, bf16[128,2048]{0,1:T(8,128)(2,1)S(1)}, u32[]{:S(2)}, u32[]{:S(2)}) collective-permute-start(bf16[128,2048]{0,1:T(8,128)(2,1)S(1)} %get-tuple-element.1373), channel_id=1, source_target_pairs={{0,32},{32,64},{64,96},{96,128},{128,160},{160,192},{192,224},{1,3... | collective-permute-start | bytes 1572872 | tf_op jit(solution)/shard_map/while/body/eval_jaxpr/ppermute | solution.py:16
  145.4 7.8 collective-permute-done
  157.7 6.9 collective-permute-done
  164.6 16.5 %collective-permute-start = (bf16[128,2048]{0,1:T(8,128)(2,1)S(1)}, bf16[128,2048]{0,1:T(8,128)(2,1)S(1)}, u32[]{:S(2)}, u32[]{:S(2)}) collective-permute-start(bf16[128,2048]{0,1:T(8,128)(2,1)S(1)} %get-tuple-element.1373), channel_id=1, source_target_pairs={{0,32},{32,64},{64,96},{96,128},{128,160},{160,192},{192,224},{1,3... | collective-permute-start | bytes 1572872 | tf_op jit(solution)/shard_map/while/body/eval_jaxpr/ppermute | solution.py:16
  181.1 6.6 collective-permute-done
  187.9 7.5 collective-permute-start
  195.4 6.6 collective-permute-done
  202.1 23.3 %collective-permute-start = (bf16[128,2048]{0,1:T(8,128)(2,1)S(1)}, bf16[128,2048]{0,1:T(8,128)(2,1)S(1)}, u32[]{:S(2)}, u32[]{:S(2)}) collective-permute-start(bf16[128,2048]{0,1:T(8,128)(2,1)S(1)} %get-tuple-element.1373), channel_id=1, source_target_pairs={{0,32},{32,64},{64,96},{96,128},{128,160},{160,192},{192,224},{1,3... | collective-permute-start | bytes 1572872 | tf_op jit(solution)/shard_map/while/body/eval_jaxpr/ppermute | solution.py:16
  225.4 6.6 collective-permute-done
  232.2 10.5 %collective-permute-start = (bf16[128,2048]{0,1:T(8,128)(2,1)S(1)}, bf16[128,2048]{0,1:T(8,128)(2,1)S(1)}, u32[]{:S(2)}, u32[]{:S(2)}) collective-permute-start(bf16[128,2048]{0,1:T(8,128)(2,1)S(1)} %get-tuple-element.1373), channel_id=1, source_target_pairs={{0,32},{32,64},{64,96},{96,128},{128,160},{160,192},{192,224},{1,3... | collective-permute-start | bytes 1572872 | tf_op jit(solution)/shard_map/while/body/eval_jaxpr/ppermute | solution.py:16
  242.7 6.6 collective-permute-done
  249.5 23.4 %collective-permute-start = (bf16[128,2048]{0,1:T(8,128)(2,1)S(1)}, bf16[128,2048]{0,1:T(8,128)(2,1)S(1)}, u32[]{:S(2)}, u32[]{:S(2)}) collective-permute-start(bf16[128,2048]{0,1:T(8,128)(2,1)S(1)} %get-tuple-element.1373), channel_id=1, source_target_pairs={{0,32},{32,64},{64,96},{96,128},{128,160},{160,192},{192,224},{1,3... | collective-permute-start | bytes 1572872 | tf_op jit(solution)/shard_map/while/body/eval_jaxpr/ppermute | solution.py:16
  272.9 6.6 collective-permute-done
  279.6 5.4 copy.60
  288.7 5.5 copy.58
  303.1 360.5 %while.49 = (s32[]{:T(128)}, bf16[128,2048]{1,0:T(8,128)(2,1)S(1)}, bf16[4,128,2048]{1,2,0:T(8,128)(2,1)}, s32[]{:T(128)}, pred[]{:T(512)}, /*index=5*/bf16[4,12...) while((s32[]{:T(128)}, bf16[128,2048]{1,0:T(8,128)(2,1)S(1)}, ...), condition=%wide.region_15.16_spmd.clone, body=%wide.region_9.15_spmd.clone.sunk | while | flops 1353218048 | bytes 71172608 | solution.py:190
  305.4 16.6 %collective-permute-done.1 = bf16[128,2048]{1,0:T(8,128)(2,1)S(1)} collective-permute-done((bf16[128,2048]{1,0:T(8,128)(2,1)}, bf16[128,2048]{1,0:T(8,128)(2,1)S(1)}, u32[]{:S(2)}, u32[]{:S(2)}) %collective-permute-start.1) | collective-permute-done | bytes 524320 | tf_op jit(solution)/shard_map/while/body/eval_jaxpr/ppermute | solution.py:16
  324.1 19.4 %collective-permute-done.1 = bf16[128,2048]{1,0:T(8,128)(2,1)S(1)} collective-permute-done((bf16[128,2048]{1,0:T(8,128)(2,1)}, bf16[128,2048]{1,0:T(8,128)(2,1)S(1)}, u32[]{:S(2)}, u32[]{:S(2)}) %collective-permute-start.1) | collective-permute-done | bytes 524320 | tf_op jit(solution)/shard_map/while/body/eval_jaxpr/ppermute | solution.py:16
  345.7 19.2 %collective-permute-done.1 = bf16[128,2048]{1,0:T(8,128)(2,1)S(1)} collective-permute-done((bf16[128,2048]{1,0:T(8,128)(2,1)}, bf16[128,2048]{1,0:T(8,128)(2,1)S(1)}, u32[]{:S(2)}, u32[]{:S(2)}) %collective-permute-start.1) | collective-permute-done | bytes 524320 | tf_op jit(solution)/shard_map/while/body/eval_jaxpr/ppermute | solution.py:16
  367.0 22.8 %collective-permute-done.1 = bf16[128,2048]{1,0:T(8,128)(2,1)S(1)} collective-permute-done((bf16[128,2048]{1,0:T(8,128)(2,1)}, bf16[128,2048]{1,0:T(8,128)(2,1)S(1)}, u32[]{:S(2)}, u32[]{:S(2)}) %collective-permute-start.1) | collective-permute-done | bytes 524320 | tf_op jit(solution)/shard_map/while/body/eval_jaxpr/ppermute | solution.py:16
  392.0 21.8 %collective-permute-done.1 = bf16[128,2048]{1,0:T(8,128)(2,1)S(1)} collective-permute-done((bf16[128,2048]{1,0:T(8,128)(2,1)}, bf16[128,2048]{1,0:T(8,128)(2,1)S(1)}, u32[]{:S(2)}, u32[]{:S(2)}) %collective-permute-start.1) | collective-permute-done | bytes 524320 | tf_op jit(solution)/shard_map/while/body/eval_jaxpr/ppermute | solution.py:16
  415.9 10.0 %collective-permute-done.1 = bf16[128,2048]{1,0:T(8,128)(2,1)S(1)} collective-permute-done((bf16[128,2048]{1,0:T(8,128)(2,1)}, bf16[128,2048]{1,0:T(8,128)(2,1)S(1)}, u32[]{:S(2)}, u32[]{:S(2)}) %collective-permute-start.1) | collective-permute-done | bytes 524320 | tf_op jit(solution)/shard_map/while/body/eval_jaxpr/ppermute | solution.py:16
  428.0 105.3 %collective-permute-done.1 = bf16[128,2048]{1,0:T(8,128)(2,1)S(1)} collective-permute-done((bf16[128,2048]{1,0:T(8,128)(2,1)}, bf16[128,2048]{1,0:T(8,128)(2,1)S(1)}, u32[]{:S(2)}, u32[]{:S(2)}) %collective-permute-start.1) | collective-permute-done | bytes 524320 | tf_op jit(solution)/shard_map/while/body/eval_jaxpr/ppermute | solution.py:16
  533.3 16.7 %conditional.7 = (bf16[128,2048]{1,0:T(8,128)(2,1)}, bf16[4,128,2048]{1,2,0:T(8,128)(2,1)}) conditional(s32[]{:T(128)} %convert_element_type.261, bf16[4,128,2048]{1,2,0:T(8,128)(2,1)} %get-tuple-element.1495, (pred[]{:T(512)}, s32[]{:T(128)}, bf16[4,128,2048]{2,1,0:T(8,128)(2,1)}, bf16[128,2048]{1,0:T(8,128)(2,1)S(1)}, ...), branch_computations={%region_10.10_spmd, %region_11.14_spmd} | conditional | flops 1353218048 | bytes 69075104 | solution.py:186
  551.3 16.1 %collective-permute-done.1 = bf16[128,2048]{1,0:T(8,128)(2,1)S(1)} collective-permute-done((bf16[128,2048]{1,0:T(8,128)(2,1)}, bf16[128,2048]{1,0:T(8,128)(2,1)S(1)}, u32[]{:S(2)}, u32[]{:S(2)}) %collective-permute-start.1) | collective-permute-done | bytes 524320 | tf_op jit(solution)/shard_map/while/body/eval_jaxpr/ppermute | solution.py:16
  567.4 16.7 %conditional.7 = (bf16[128,2048]{1,0:T(8,128)(2,1)}, bf16[4,128,2048]{1,2,0:T(8,128)(2,1)}) conditional(s32[]{:T(128)} %convert_element_type.261, bf16[4,128,2048]{1,2,0:T(8,128)(2,1)} %get-tuple-element.1495, (pred[]{:T(512)}, s32[]{:T(128)}, bf16[4,128,2048]{2,1,0:T(8,128)(2,1)}, bf16[128,2048]{1,0:T(8,128)(2,1)S(1)}, ...), branch_computations={%region_10.10_spmd, %region_11.14_spmd} | conditional | flops 1353218048 | bytes 69075104 | solution.py:186
  585.4 16.0 %collective-permute-done.1 = bf16[128,2048]{1,0:T(8,128)(2,1)S(1)} collective-permute-done((bf16[128,2048]{1,0:T(8,128)(2,1)}, bf16[128,2048]{1,0:T(8,128)(2,1)S(1)}, u32[]{:S(2)}, u32[]{:S(2)}) %collective-permute-start.1) | collective-permute-done | bytes 524320 | tf_op jit(solution)/shard_map/while/body/eval_jaxpr/ppermute | solution.py:16
  601.5 16.7 %conditional.7 = (bf16[128,2048]{1,0:T(8,128)(2,1)}, bf16[4,128,2048]{1,2,0:T(8,128)(2,1)}) conditional(s32[]{:T(128)} %convert_element_type.261, bf16[4,128,2048]{1,2,0:T(8,128)(2,1)} %get-tuple-element.1495, (pred[]{:T(512)}, s32[]{:T(128)}, bf16[4,128,2048]{2,1,0:T(8,128)(2,1)}, bf16[128,2048]{1,0:T(8,128)(2,1)S(1)}, ...), branch_computations={%region_10.10_spmd, %region_11.14_spmd} | conditional | flops 1353218048 | bytes 69075104 | solution.py:186
  619.4 16.1 %collective-permute-done.1 = bf16[128,2048]{1,0:T(8,128)(2,1)S(1)} collective-permute-done((bf16[128,2048]{1,0:T(8,128)(2,1)}, bf16[128,2048]{1,0:T(8,128)(2,1)S(1)}, u32[]{:S(2)}, u32[]{:S(2)}) %collective-permute-start.1) | collective-permute-done | bytes 524320 | tf_op jit(solution)/shard_map/while/body/eval_jaxpr/ppermute | solution.py:16
  635.6 16.7 %conditional.7 = (bf16[128,2048]{1,0:T(8,128)(2,1)}, bf16[4,128,2048]{1,2,0:T(8,128)(2,1)}) conditional(s32[]{:T(128)} %convert_element_type.261, bf16[4,128,2048]{1,2,0:T(8,128)(2,1)} %get-tuple-element.1495, (pred[]{:T(512)}, s32[]{:T(128)}, bf16[4,128,2048]{2,1,0:T(8,128)(2,1)}, bf16[128,2048]{1,0:T(8,128)(2,1)S(1)}, ...), branch_computations={%region_10.10_spmd, %region_11.14_spmd} | conditional | flops 1353218048 | bytes 69075104 | solution.py:186
  653.6 10.0 %collective-permute-done.1 = bf16[128,2048]{1,0:T(8,128)(2,1)S(1)} collective-permute-done((bf16[128,2048]{1,0:T(8,128)(2,1)}, bf16[128,2048]{1,0:T(8,128)(2,1)S(1)}, u32[]{:S(2)}, u32[]{:S(2)}) %collective-permute-start.1) | collective-permute-done | bytes 524320 | tf_op jit(solution)/shard_map/while/body/eval_jaxpr/ppermute | solution.py:16
  667.7 10.7 %copy.56 = bf16[4,128,2048]{1,0,2:T(4,128)(2,1)} copy(bf16[4,128,2048]{1,2,0:T(8,128)(2,1)S(1)} %copy-done.1) | data formatting | bytes 4194304 | tf_op jit(solution)/shard_map/convert_element_type | solution.py:195
  685.4 5.6 fusion.78
  691.0 7.7 collective-permute-done.2
  698.7 9.2 %add_convert_fusion = bf16[1024,2048]{1,0:T(8,128)(2,1)} fusion(f32[1024,2048]{1,0:T(8,128)} %fusion.78, f32[1024,2048]{1,0:T(8,128)} %collective-permute-done.2), kind=kLoop, calls=%fused_computation.103 | loop fusion | flops 4194304 | bytes 20971520 | tf_op jit(solution)/shard_map/convert_element_type | solution.py:210
  707.9 188.1 %reduce-scatter.2.cloned.1.call-done = bf16[64,2048]{1,0:T(8,128)(2,1)} async-done(((bf16[1024,2048]{1,0:T(8,128)(2,1)}), bf16[64,2048]{1,0:T(8,128)(2,1)}) %reduce-scatter.2.cloned.1.call-update) | async-done | bytes 262160 | tf_op jit(solution)/shard_map/reduce_scatter | solution.py:209
  (242 shorter events, 190.0 us)
Async XLA Ops:
  6.5 889.4 %reduce-scatter.2.cloned.1.call-start = ((), (), s32[]{:S(2)}) async-start(), calls=%async_computation.1 | async-start | bytes 4456448 | tf_op jit(solution)/shard_map/reduce_scatter | solution.py:209
  17.2 3.3 copy-start.4
  33.7 12.7 %collective-permute-start = (bf16[128,2048]{0,1:T(8,128)(2,1)S(1)}, bf16[128,2048]{0,1:T(8,128)(2,1)S(1)}, u32[]{:S(2)}, u32[]{:S(2)}) collective-permute-start(bf16[128,2048]{0,1:T(8,128)(2,1)S(1)} %get-tuple-element.1373), channel_id=1, source_target_pairs={{0,32},{32,64},{64,96},{96,128},{128,160},{160,192},{192,224},{1,3... | collective-permute-start | bytes 1572872 | tf_op jit(solution)/shard_map/while/body/eval_jaxpr/ppermute | solution.py:16
  59.5 15.1 %collective-permute-start = (bf16[128,2048]{0,1:T(8,128)(2,1)S(1)}, bf16[128,2048]{0,1:T(8,128)(2,1)S(1)}, u32[]{:S(2)}, u32[]{:S(2)}) collective-permute-start(bf16[128,2048]{0,1:T(8,128)(2,1)S(1)} %get-tuple-element.1373), channel_id=1, source_target_pairs={{0,32},{32,64},{64,96},{96,128},{128,160},{160,192},{192,224},{1,3... | collective-permute-start | bytes 1572872 | tf_op jit(solution)/shard_map/while/body/eval_jaxpr/ppermute | solution.py:16
  87.6 14.0 %collective-permute-start = (bf16[128,2048]{0,1:T(8,128)(2,1)S(1)}, bf16[128,2048]{0,1:T(8,128)(2,1)S(1)}, u32[]{:S(2)}, u32[]{:S(2)}) collective-permute-start(bf16[128,2048]{0,1:T(8,128)(2,1)S(1)} %get-tuple-element.1373), channel_id=1, source_target_pairs={{0,32},{32,64},{64,96},{96,128},{128,160},{160,192},{192,224},{1,3... | collective-permute-start | bytes 1572872 | tf_op jit(solution)/shard_map/while/body/eval_jaxpr/ppermute | solution.py:16
  114.7 13.1 %collective-permute-start = (bf16[128,2048]{0,1:T(8,128)(2,1)S(1)}, bf16[128,2048]{0,1:T(8,128)(2,1)S(1)}, u32[]{:S(2)}, u32[]{:S(2)}) collective-permute-start(bf16[128,2048]{0,1:T(8,128)(2,1)S(1)} %get-tuple-element.1373), channel_id=1, source_target_pairs={{0,32},{32,64},{64,96},{96,128},{128,160},{160,192},{192,224},{1,3... | collective-permute-start | bytes 1572872 | tf_op jit(solution)/shard_map/while/body/eval_jaxpr/ppermute | solution.py:16
  128.0 25.2 %collective-permute-start = (bf16[128,2048]{0,1:T(8,128)(2,1)S(1)}, bf16[128,2048]{0,1:T(8,128)(2,1)S(1)}, u32[]{:S(2)}, u32[]{:S(2)}) collective-permute-start(bf16[128,2048]{0,1:T(8,128)(2,1)S(1)} %get-tuple-element.1373), channel_id=1, source_target_pairs={{0,32},{32,64},{64,96},{96,128},{128,160},{160,192},{192,224},{1,3... | collective-permute-start | bytes 1572872 | tf_op jit(solution)/shard_map/while/body/eval_jaxpr/ppermute | solution.py:16
  153.3 11.3 %collective-permute-start = (bf16[128,2048]{0,1:T(8,128)(2,1)S(1)}, bf16[128,2048]{0,1:T(8,128)(2,1)S(1)}, u32[]{:S(2)}, u32[]{:S(2)}) collective-permute-start(bf16[128,2048]{0,1:T(8,128)(2,1)S(1)} %get-tuple-element.1373), channel_id=1, source_target_pairs={{0,32},{32,64},{64,96},{96,128},{128,160},{160,192},{192,224},{1,3... | collective-permute-start | bytes 1572872 | tf_op jit(solution)/shard_map/while/body/eval_jaxpr/ppermute | solution.py:16
  164.6 23.1 %collective-permute-start = (bf16[128,2048]{0,1:T(8,128)(2,1)S(1)}, bf16[128,2048]{0,1:T(8,128)(2,1)S(1)}, u32[]{:S(2)}, u32[]{:S(2)}) collective-permute-start(bf16[128,2048]{0,1:T(8,128)(2,1)S(1)} %get-tuple-element.1373), channel_id=1, source_target_pairs={{0,32},{32,64},{64,96},{96,128},{128,160},{160,192},{192,224},{1,3... | collective-permute-start | bytes 1572872 | tf_op jit(solution)/shard_map/while/body/eval_jaxpr/ppermute | solution.py:16
  187.9 14.2 %collective-permute-start = (bf16[128,2048]{0,1:T(8,128)(2,1)S(1)}, bf16[128,2048]{0,1:T(8,128)(2,1)S(1)}, u32[]{:S(2)}, u32[]{:S(2)}) collective-permute-start(bf16[128,2048]{0,1:T(8,128)(2,1)S(1)} %get-tuple-element.1373), channel_id=1, source_target_pairs={{0,32},{32,64},{64,96},{96,128},{128,160},{160,192},{192,224},{1,3... | collective-permute-start | bytes 1572872 | tf_op jit(solution)/shard_map/while/body/eval_jaxpr/ppermute | solution.py:16
  202.1 30.0 %collective-permute-start = (bf16[128,2048]{0,1:T(8,128)(2,1)S(1)}, bf16[128,2048]{0,1:T(8,128)(2,1)S(1)}, u32[]{:S(2)}, u32[]{:S(2)}) collective-permute-start(bf16[128,2048]{0,1:T(8,128)(2,1)S(1)} %get-tuple-element.1373), channel_id=1, source_target_pairs={{0,32},{32,64},{64,96},{96,128},{128,160},{160,192},{192,224},{1,3... | collective-permute-start | bytes 1572872 | tf_op jit(solution)/shard_map/while/body/eval_jaxpr/ppermute | solution.py:16
  232.2 17.2 %collective-permute-start = (bf16[128,2048]{0,1:T(8,128)(2,1)S(1)}, bf16[128,2048]{0,1:T(8,128)(2,1)S(1)}, u32[]{:S(2)}, u32[]{:S(2)}) collective-permute-start(bf16[128,2048]{0,1:T(8,128)(2,1)S(1)} %get-tuple-element.1373), channel_id=1, source_target_pairs={{0,32},{32,64},{64,96},{96,128},{128,160},{160,192},{192,224},{1,3... | collective-permute-start | bytes 1572872 | tf_op jit(solution)/shard_map/while/body/eval_jaxpr/ppermute | solution.py:16
  249.5 30.1 %collective-permute-start = (bf16[128,2048]{0,1:T(8,128)(2,1)S(1)}, bf16[128,2048]{0,1:T(8,128)(2,1)S(1)}, u32[]{:S(2)}, u32[]{:S(2)}) collective-permute-start(bf16[128,2048]{0,1:T(8,128)(2,1)S(1)} %get-tuple-element.1373), channel_id=1, source_target_pairs={{0,32},{32,64},{64,96},{96,128},{128,160},{160,192},{192,224},{1,3... | collective-permute-start | bytes 1572872 | tf_op jit(solution)/shard_map/while/body/eval_jaxpr/ppermute | solution.py:16
  288.7 5.5 copy-start.2
  304.1 17.9 %collective-permute-start.1 = (bf16[128,2048]{1,0:T(8,128)(2,1)}, bf16[128,2048]{1,0:T(8,128)(2,1)S(1)}, u32[]{:S(2)}, u32[]{:S(2)}) collective-permute-start(bf16[128,2048]{1,0:T(8,128)(2,1)} %get-tuple-element.1395), channel_id=1, source_target_pairs={{32,0},{64,32},{96,64},{128,96},{160,128},{192,160},{224,192},{33,... | collective-permute-start | bytes 1572872 | tf_op jit(solution)/shard_map/while/body/eval_jaxpr/ppermute | solution.py:16
  322.8 20.7 %collective-permute-start.1 = (bf16[128,2048]{1,0:T(8,128)(2,1)}, bf16[128,2048]{1,0:T(8,128)(2,1)S(1)}, u32[]{:S(2)}, u32[]{:S(2)}) collective-permute-start(bf16[128,2048]{1,0:T(8,128)(2,1)} %get-tuple-element.1395), channel_id=1, source_target_pairs={{32,0},{64,32},{96,64},{128,96},{160,128},{192,160},{224,192},{33,... | collective-permute-start | bytes 1572872 | tf_op jit(solution)/shard_map/while/body/eval_jaxpr/ppermute | solution.py:16
  344.4 20.5 %collective-permute-start.1 = (bf16[128,2048]{1,0:T(8,128)(2,1)}, bf16[128,2048]{1,0:T(8,128)(2,1)S(1)}, u32[]{:S(2)}, u32[]{:S(2)}) collective-permute-start(bf16[128,2048]{1,0:T(8,128)(2,1)} %get-tuple-element.1395), channel_id=1, source_target_pairs={{32,0},{64,32},{96,64},{128,96},{160,128},{192,160},{224,192},{33,... | collective-permute-start | bytes 1572872 | tf_op jit(solution)/shard_map/while/body/eval_jaxpr/ppermute | solution.py:16
  365.7 24.1 %collective-permute-start.1 = (bf16[128,2048]{1,0:T(8,128)(2,1)}, bf16[128,2048]{1,0:T(8,128)(2,1)S(1)}, u32[]{:S(2)}, u32[]{:S(2)}) collective-permute-start(bf16[128,2048]{1,0:T(8,128)(2,1)} %get-tuple-element.1395), channel_id=1, source_target_pairs={{32,0},{64,32},{96,64},{128,96},{160,128},{192,160},{224,192},{33,... | collective-permute-start | bytes 1572872 | tf_op jit(solution)/shard_map/while/body/eval_jaxpr/ppermute | solution.py:16
  390.7 23.1 %collective-permute-start.1 = (bf16[128,2048]{1,0:T(8,128)(2,1)}, bf16[128,2048]{1,0:T(8,128)(2,1)S(1)}, u32[]{:S(2)}, u32[]{:S(2)}) collective-permute-start(bf16[128,2048]{1,0:T(8,128)(2,1)} %get-tuple-element.1395), channel_id=1, source_target_pairs={{32,0},{64,32},{96,64},{128,96},{160,128},{192,160},{224,192},{33,... | collective-permute-start | bytes 1572872 | tf_op jit(solution)/shard_map/while/body/eval_jaxpr/ppermute | solution.py:16
  414.6 11.3 %collective-permute-start.1 = (bf16[128,2048]{1,0:T(8,128)(2,1)}, bf16[128,2048]{1,0:T(8,128)(2,1)S(1)}, u32[]{:S(2)}, u32[]{:S(2)}) collective-permute-start(bf16[128,2048]{1,0:T(8,128)(2,1)} %get-tuple-element.1395), channel_id=1, source_target_pairs={{32,0},{64,32},{96,64},{128,96},{160,128},{192,160},{224,192},{33,... | collective-permute-start | bytes 1572872 | tf_op jit(solution)/shard_map/while/body/eval_jaxpr/ppermute | solution.py:16
  426.8 106.6 %collective-permute-start.1 = (bf16[128,2048]{1,0:T(8,128)(2,1)}, bf16[128,2048]{1,0:T(8,128)(2,1)S(1)}, u32[]{:S(2)}, u32[]{:S(2)}) collective-permute-start(bf16[128,2048]{1,0:T(8,128)(2,1)} %get-tuple-element.1395), channel_id=1, source_target_pairs={{32,0},{64,32},{96,64},{128,96},{160,128},{192,160},{224,192},{33,... | collective-permute-start | bytes 1572872 | tf_op jit(solution)/shard_map/while/body/eval_jaxpr/ppermute | solution.py:16
  536.5 1.9 copy-start
  538.4 4.8 slice-start
  539.1 4.1 slice-start.1
  550.0 17.4 %collective-permute-start.1 = (bf16[128,2048]{1,0:T(8,128)(2,1)}, bf16[128,2048]{1,0:T(8,128)(2,1)S(1)}, u32[]{:S(2)}, u32[]{:S(2)}) collective-permute-start(bf16[128,2048]{1,0:T(8,128)(2,1)} %get-tuple-element.1395), channel_id=1, source_target_pairs={{32,0},{64,32},{96,64},{128,96},{160,128},{192,160},{224,192},{33,... | collective-permute-start | bytes 1572872 | tf_op jit(solution)/shard_map/while/body/eval_jaxpr/ppermute | solution.py:16
  570.6 1.9 copy-start
  572.5 4.8 slice-start
  573.2 4.1 slice-start.1
  584.1 17.3 %collective-permute-start.1 = (bf16[128,2048]{1,0:T(8,128)(2,1)}, bf16[128,2048]{1,0:T(8,128)(2,1)S(1)}, u32[]{:S(2)}, u32[]{:S(2)}) collective-permute-start(bf16[128,2048]{1,0:T(8,128)(2,1)} %get-tuple-element.1395), channel_id=1, source_target_pairs={{32,0},{64,32},{96,64},{128,96},{160,128},{192,160},{224,192},{33,... | collective-permute-start | bytes 1572872 | tf_op jit(solution)/shard_map/while/body/eval_jaxpr/ppermute | solution.py:16
  604.6 1.9 copy-start
  606.5 4.8 slice-start
  607.2 4.1 slice-start.1
  618.1 17.4 %collective-permute-start.1 = (bf16[128,2048]{1,0:T(8,128)(2,1)}, bf16[128,2048]{1,0:T(8,128)(2,1)S(1)}, u32[]{:S(2)}, u32[]{:S(2)}) collective-permute-start(bf16[128,2048]{1,0:T(8,128)(2,1)} %get-tuple-element.1395), channel_id=1, source_target_pairs={{32,0},{64,32},{96,64},{128,96},{160,128},{192,160},{224,192},{33,... | collective-permute-start | bytes 1572872 | tf_op jit(solution)/shard_map/while/body/eval_jaxpr/ppermute | solution.py:16
  638.7 1.9 copy-start
  640.6 4.8 slice-start
  641.3 4.1 slice-start.1
  652.3 11.3 %collective-permute-start.1 = (bf16[128,2048]{1,0:T(8,128)(2,1)}, bf16[128,2048]{1,0:T(8,128)(2,1)S(1)}, u32[]{:S(2)}, u32[]{:S(2)}) collective-permute-start(bf16[128,2048]{1,0:T(8,128)(2,1)} %get-tuple-element.1395), channel_id=1, source_target_pairs={{32,0},{64,32},{96,64},{128,96},{160,128},{192,160},{224,192},{33,... | collective-permute-start | bytes 1572872 | tf_op jit(solution)/shard_map/while/body/eval_jaxpr/ppermute | solution.py:16
  663.5 4.2 copy-start.1
  681.4 1.6 copy-start.3
  685.3 13.4 %collective-permute-start.2 = (f32[1024,2048]{1,0:T(8,128)S(1)}, f32[1024,2048]{1,0:T(8,128)}, u32[]{:S(2)}, u32[]{:S(2)}) collective-permute-start(f32[1024,2048]{1,0:T(8,128)S(1)} %fusion.79), channel_id=1, source_target_pairs={{0,1},{1,0},{2,3},{3,2},{4,5},{5,4},{6,7},{7,6},{8,9},{9,8},{10,11... | collective-permute-start | bytes 25165832 | tf_op jit(solution)/shard_map/ppermute | solution.py:207
Sparse Core Ops, SparseCore 0:
  708.0 187.9 reduce-scatter.1

commit v5 on v4

--- a/solution.py
+++ b/solution.py
@@ -206,9 +206,8 @@
 
     received = lax.ppermute(partial_grad(1 - core), "core", [(0, 1), (1, 0)])
     half = lax.optimization_barrier(partial_grad(core)) + received
-    summed = lax.psum_scatter(
-        half.astype(jnp.bfloat16), "dp_hi", scatter_dimension=0, tiled=True
-    ).astype(jnp.float32)
+    swapped = lax.all_to_all(half.astype(jnp.bfloat16), "dp_hi", 0, 0, tiled=True)
+    summed = jnp.sum(swapped.reshape(groups, rows_each, width).astype(jnp.float32), axis=0)
     return summed[None]
 
 

time: 916 us -> 908 us (level)
  blocking collectives: 0 us -> 214 us
  waiting for transfers between devices: 557 us -> 366 us
  between operations: 13.5 us -> 0.12 us
    all_to_all x0 -> x1, blocking collectives: none -> 214 us  [per_device(): lax.all_to_all(half.astype(jnp.bfloat16), 'dp_hi', 0, 0, tiled=True)]
    reduce_scatter x1 -> x0, waiting for transfers between devices: 188 us -> none  [per_device(): lax.psum_scatter(half.astype(jnp.bfloat16), 'dp_hi', scatter_dimension=0,...]
  transfers between devices with their start and end apart: 24 -> 23, of which waited for: 24 -> 23; matrix products, arithmetic and copies ran while one was open for 1% -> 1% of each run, Pallas kernels for 0% -> 0%
where the time goes in v5:
time: 908 us; the launch traced here: 903 us
  waiting for transfers between devices  366 us (40%)
  blocking collectives  214 us (24%)
  starting transfers between devices  128 us (14%)
  matrix products  71.5 us (8%)
  local copies, waits for them, and re-layouts  66.9 us (7%)
  other arithmetic  55.3 us (6%)
    ppermute x22, waiting for transfers between devices, passed_along(): return lax.ppermute(block, axis, route)  358 us
    all_to_all x1, blocking collectives, per_device(): lax.all_to_all(half.astype(jnp.bfloat16), 'dp_hi', 0, 0, tiled=True)  214 us
    ppermute x22, starting transfers between devices, passed_along(): return lax.ppermute(block, axis, route)  128 us
    unnamed x13, local copies, waits for them, and re-layouts  22.6 us
    dot_general x4, matrix products, layer_forward(): jnp.dot(normed.reshape(-1, width), weight, preferred_element_type=jnp.flo...  18.8 us
  transfers between devices with their start and end apart: 23, of which 23 were waited for; matrix products, arithmetic and copies ran while one was open for 1% of the time, Pallas kernels for 0%

profile of v5, /device:TPU:96, one launch (start us, length us, event | category | flops | bytes accessed | tf_op | source)
XLA Modules:
  0.0 903.1 jit_solution(332467495329231139)
XLA Ops:
  13.2 250.9 %while.48 = (s32[]{:T(128)}, bf16[128,2048]{0,1:T(8,128)(2,1)S(1)}, f32[4,128,2048]{1,2,0:T(8,128)}, f32[4,128,1]{1,2,0:T(1,128)S(1)}, bf16[4,128,16,128]{3,2,1,...) while((s32[]{:T(128)}, bf16[128,2048]{0,1:T(8,128)(2,1)S(1)}, ...), condition=%wide.region_8.9_spmd.clone, body=%wide.region_1.8_spmd.clone.sunk | while | flops 1216641408 | bytes 26020904 | solution.py:158
  13.2 12.1 %conditional.6 = (bf16[128,2048]{0,1:T(8,128)(2,1)S(1)}, f32[4,128,2048]{1,2,0:T(8,128)}, f32[4,128,1]{1,2,0:T(1,128)S(1)}, bf16[4,128,16,128]{3,2,1,0:T(8,128)(...) conditional(s32[]{:T(128)} %convert_element_type.264, ...), branch_computations={%region_2.2_spmd, %region_3.7_spmd} | conditional | flops 1216641408 | bytes 23923316 | solution.py:152
  13.8 4.7 convolution_convert_fusion
  26.7 11.4 %collective-permute-done = bf16[128,2048]{0,1:T(8,128)(2,1)S(1)} collective-permute-done((bf16[128,2048]{0,1:T(8,128)(2,1)S(1)}, bf16[128,2048]{0,1:T(8,128)(2,1)S(1)}, u32[]{:S(2)}, u32[]{:S(2)}) %collective-permute-start) | collective-permute-done | bytes 524320 | tf_op jit(solution)/shard_map/while/body/eval_jaxpr/ppermute | solution.py:16
  38.1 12.1 %conditional.6 = (bf16[128,2048]{0,1:T(8,128)(2,1)S(1)}, f32[4,128,2048]{1,2,0:T(8,128)}, f32[4,128,1]{1,2,0:T(1,128)S(1)}, bf16[4,128,16,128]{3,2,1,0:T(8,128)(...) conditional(s32[]{:T(128)} %convert_element_type.264, ...), branch_computations={%region_2.2_spmd, %region_3.7_spmd} | conditional | flops 1216641408 | bytes 23923316 | solution.py:152
  54.6 10.6 %collective-permute-done = bf16[128,2048]{0,1:T(8,128)(2,1)S(1)} collective-permute-done((bf16[128,2048]{0,1:T(8,128)(2,1)S(1)}, bf16[128,2048]{0,1:T(8,128)(2,1)S(1)}, u32[]{:S(2)}, u32[]{:S(2)}) %collective-permute-start) | collective-permute-done | bytes 524320 | tf_op jit(solution)/shard_map/while/body/eval_jaxpr/ppermute | solution.py:16
  65.2 12.0 %conditional.6 = (bf16[128,2048]{0,1:T(8,128)(2,1)S(1)}, f32[4,128,2048]{1,2,0:T(8,128)}, f32[4,128,1]{1,2,0:T(1,128)S(1)}, bf16[4,128,16,128]{3,2,1,0:T(8,128)(...) conditional(s32[]{:T(128)} %convert_element_type.264, ...), branch_computations={%region_2.2_spmd, %region_3.7_spmd} | conditional | flops 1216641408 | bytes 23923316 | solution.py:152
  65.8 4.7 convolution_convert_fusion
  81.7 9.7 %collective-permute-done = bf16[128,2048]{0,1:T(8,128)(2,1)S(1)} collective-permute-done((bf16[128,2048]{0,1:T(8,128)(2,1)S(1)}, bf16[128,2048]{0,1:T(8,128)(2,1)S(1)}, u32[]{:S(2)}, u32[]{:S(2)}) %collective-permute-start) | collective-permute-done | bytes 524320 | tf_op jit(solution)/shard_map/while/body/eval_jaxpr/ppermute | solution.py:16
  91.3 12.0 %conditional.6 = (bf16[128,2048]{0,1:T(8,128)(2,1)S(1)}, f32[4,128,2048]{1,2,0:T(8,128)}, f32[4,128,1]{1,2,0:T(1,128)S(1)}, bf16[4,128,16,128]{3,2,1,0:T(8,128)(...) conditional(s32[]{:T(128)} %convert_element_type.264, ...), branch_computations={%region_2.2_spmd, %region_3.7_spmd} | conditional | flops 1216641408 | bytes 23923316 | solution.py:152
  91.9 4.7 convolution_convert_fusion
  107.8 8.7 collective-permute-done
  116.6 16.4 %collective-permute-start = (bf16[128,2048]{0,1:T(8,128)(2,1)S(1)}, bf16[128,2048]{0,1:T(8,128)(2,1)S(1)}, u32[]{:S(2)}, u32[]{:S(2)}) collective-permute-start(bf16[128,2048]{0,1:T(8,128)(2,1)S(1)} %get-tuple-element.1373), channel_id=1, source_target_pairs={{0,32},{32,64},{64,96},{96,128},{128,160},{160,192},{192,224},{1,3... | collective-permute-start | bytes 1572872 | tf_op jit(solution)/shard_map/while/body/eval_jaxpr/ppermute | solution.py:16
  133.0 7.8 collective-permute-done
  145.3 6.9 collective-permute-done
  152.3 15.4 %collective-permute-start = (bf16[128,2048]{0,1:T(8,128)(2,1)S(1)}, bf16[128,2048]{0,1:T(8,128)(2,1)S(1)}, u32[]{:S(2)}, u32[]{:S(2)}) collective-permute-start(bf16[128,2048]{0,1:T(8,128)(2,1)S(1)} %get-tuple-element.1373), channel_id=1, source_target_pairs={{0,32},{32,64},{64,96},{96,128},{128,160},{160,192},{192,224},{1,3... | collective-permute-start | bytes 1572872 | tf_op jit(solution)/shard_map/while/body/eval_jaxpr/ppermute | solution.py:16
  167.7 6.6 collective-permute-done
  174.4 7.5 collective-permute-start
  182.0 6.6 collective-permute-done
  188.7 22.3 %collective-permute-start = (bf16[128,2048]{0,1:T(8,128)(2,1)S(1)}, bf16[128,2048]{0,1:T(8,128)(2,1)S(1)}, u32[]{:S(2)}, u32[]{:S(2)}) collective-permute-start(bf16[128,2048]{0,1:T(8,128)(2,1)S(1)} %get-tuple-element.1373), channel_id=1, source_target_pairs={{0,32},{32,64},{64,96},{96,128},{128,160},{160,192},{192,224},{1,3... | collective-permute-start | bytes 1572872 | tf_op jit(solution)/shard_map/while/body/eval_jaxpr/ppermute | solution.py:16
  211.1 6.6 collective-permute-done
  217.8 10.4 %collective-permute-start = (bf16[128,2048]{0,1:T(8,128)(2,1)S(1)}, bf16[128,2048]{0,1:T(8,128)(2,1)S(1)}, u32[]{:S(2)}, u32[]{:S(2)}) collective-permute-start(bf16[128,2048]{0,1:T(8,128)(2,1)S(1)} %get-tuple-element.1373), channel_id=1, source_target_pairs={{0,32},{32,64},{64,96},{96,128},{128,160},{160,192},{192,224},{1,3... | collective-permute-start | bytes 1572872 | tf_op jit(solution)/shard_map/while/body/eval_jaxpr/ppermute | solution.py:16
  228.2 6.6 collective-permute-done
  235.0 22.4 %collective-permute-start = (bf16[128,2048]{0,1:T(8,128)(2,1)S(1)}, bf16[128,2048]{0,1:T(8,128)(2,1)S(1)}, u32[]{:S(2)}, u32[]{:S(2)}) collective-permute-start(bf16[128,2048]{0,1:T(8,128)(2,1)S(1)} %get-tuple-element.1373), channel_id=1, source_target_pairs={{0,32},{32,64},{64,96},{96,128},{128,160},{160,192},{192,224},{1,3... | collective-permute-start | bytes 1572872 | tf_op jit(solution)/shard_map/while/body/eval_jaxpr/ppermute | solution.py:16
  257.4 6.6 collective-permute-done
  264.0 5.4 copy.60
  273.2 5.5 copy.58
  287.7 357.0 %while.49 = (s32[]{:T(128)}, bf16[128,2048]{1,0:T(8,128)(2,1)S(1)}, bf16[4,128,2048]{1,2,0:T(8,128)(2,1)}, s32[]{:T(128)}, pred[]{:T(512)}, /*index=5*/bf16[4,12...) while((s32[]{:T(128)}, bf16[128,2048]{1,0:T(8,128)(2,1)S(1)}, ...), condition=%wide.region_15.16_spmd.clone, body=%wide.region_9.15_spmd.clone.sunk | while | flops 1353218048 | bytes 71172608 | solution.py:190
  290.0 16.5 %collective-permute-done.1 = bf16[128,2048]{1,0:T(8,128)(2,1)S(1)} collective-permute-done((bf16[128,2048]{1,0:T(8,128)(2,1)}, bf16[128,2048]{1,0:T(8,128)(2,1)S(1)}, u32[]{:S(2)}, u32[]{:S(2)}) %collective-permute-start.1) | collective-permute-done | bytes 524320 | tf_op jit(solution)/shard_map/while/body/eval_jaxpr/ppermute | solution.py:16
  308.6 16.9 %collective-permute-done.1 = bf16[128,2048]{1,0:T(8,128)(2,1)S(1)} collective-permute-done((bf16[128,2048]{1,0:T(8,128)(2,1)}, bf16[128,2048]{1,0:T(8,128)(2,1)S(1)}, u32[]{:S(2)}, u32[]{:S(2)}) %collective-permute-start.1) | collective-permute-done | bytes 524320 | tf_op jit(solution)/shard_map/while/body/eval_jaxpr/ppermute | solution.py:16
  327.7 17.4 %collective-permute-done.1 = bf16[128,2048]{1,0:T(8,128)(2,1)S(1)} collective-permute-done((bf16[128,2048]{1,0:T(8,128)(2,1)}, bf16[128,2048]{1,0:T(8,128)(2,1)S(1)}, u32[]{:S(2)}, u32[]{:S(2)}) %collective-permute-start.1) | collective-permute-done | bytes 524320 | tf_op jit(solution)/shard_map/while/body/eval_jaxpr/ppermute | solution.py:16
  347.3 20.6 %collective-permute-done.1 = bf16[128,2048]{1,0:T(8,128)(2,1)S(1)} collective-permute-done((bf16[128,2048]{1,0:T(8,128)(2,1)}, bf16[128,2048]{1,0:T(8,128)(2,1)S(1)}, u32[]{:S(2)}, u32[]{:S(2)}) %collective-permute-start.1) | collective-permute-done | bytes 524320 | tf_op jit(solution)/shard_map/while/body/eval_jaxpr/ppermute | solution.py:16
  370.0 20.3 %collective-permute-done.1 = bf16[128,2048]{1,0:T(8,128)(2,1)S(1)} collective-permute-done((bf16[128,2048]{1,0:T(8,128)(2,1)}, bf16[128,2048]{1,0:T(8,128)(2,1)S(1)}, u32[]{:S(2)}, u32[]{:S(2)}) %collective-permute-start.1) | collective-permute-done | bytes 524320 | tf_op jit(solution)/shard_map/while/body/eval_jaxpr/ppermute | solution.py:16
  392.4 10.0 %collective-permute-done.1 = bf16[128,2048]{1,0:T(8,128)(2,1)S(1)} collective-permute-done((bf16[128,2048]{1,0:T(8,128)(2,1)}, bf16[128,2048]{1,0:T(8,128)(2,1)S(1)}, u32[]{:S(2)}, u32[]{:S(2)}) %collective-permute-start.1) | collective-permute-done | bytes 524320 | tf_op jit(solution)/shard_map/while/body/eval_jaxpr/ppermute | solution.py:16
  404.6 110.3 %collective-permute-done.1 = bf16[128,2048]{1,0:T(8,128)(2,1)S(1)} collective-permute-done((bf16[128,2048]{1,0:T(8,128)(2,1)}, bf16[128,2048]{1,0:T(8,128)(2,1)S(1)}, u32[]{:S(2)}, u32[]{:S(2)}) %collective-permute-start.1) | collective-permute-done | bytes 524320 | tf_op jit(solution)/shard_map/while/body/eval_jaxpr/ppermute | solution.py:16
  514.8 16.7 %conditional.7 = (bf16[128,2048]{1,0:T(8,128)(2,1)}, bf16[4,128,2048]{1,2,0:T(8,128)(2,1)}) conditional(s32[]{:T(128)} %convert_element_type.265, bf16[4,128,2048]{1,2,0:T(8,128)(2,1)} %get-tuple-element.1495, (pred[]{:T(512)}, s32[]{:T(128)}, bf16[4,128,2048]{2,1,0:T(8,128)(2,1)}, bf16[128,2048]{1,0:T(8,128)(2,1)S(1)}, ...), branch_computations={%region_10.10_spmd, %region_11.14_spmd} | conditional | flops 1353218048 | bytes 69075104 | solution.py:186
  532.8 16.0 %collective-permute-done.1 = bf16[128,2048]{1,0:T(8,128)(2,1)S(1)} collective-permute-done((bf16[128,2048]{1,0:T(8,128)(2,1)}, bf16[128,2048]{1,0:T(8,128)(2,1)S(1)}, u32[]{:S(2)}, u32[]{:S(2)}) %collective-permute-start.1) | collective-permute-done | bytes 524320 | tf_op jit(solution)/shard_map/while/body/eval_jaxpr/ppermute | solution.py:16
  548.8 16.7 %conditional.7 = (bf16[128,2048]{1,0:T(8,128)(2,1)}, bf16[4,128,2048]{1,2,0:T(8,128)(2,1)}) conditional(s32[]{:T(128)} %convert_element_type.265, bf16[4,128,2048]{1,2,0:T(8,128)(2,1)} %get-tuple-element.1495, (pred[]{:T(512)}, s32[]{:T(128)}, bf16[4,128,2048]{2,1,0:T(8,128)(2,1)}, bf16[128,2048]{1,0:T(8,128)(2,1)S(1)}, ...), branch_computations={%region_10.10_spmd, %region_11.14_spmd} | conditional | flops 1353218048 | bytes 69075104 | solution.py:186
  566.8 15.9 %collective-permute-done.1 = bf16[128,2048]{1,0:T(8,128)(2,1)S(1)} collective-permute-done((bf16[128,2048]{1,0:T(8,128)(2,1)}, bf16[128,2048]{1,0:T(8,128)(2,1)S(1)}, u32[]{:S(2)}, u32[]{:S(2)}) %collective-permute-start.1) | collective-permute-done | bytes 524320 | tf_op jit(solution)/shard_map/while/body/eval_jaxpr/ppermute | solution.py:16
  582.7 16.7 %conditional.7 = (bf16[128,2048]{1,0:T(8,128)(2,1)}, bf16[4,128,2048]{1,2,0:T(8,128)(2,1)}) conditional(s32[]{:T(128)} %convert_element_type.265, bf16[4,128,2048]{1,2,0:T(8,128)(2,1)} %get-tuple-element.1495, (pred[]{:T(512)}, s32[]{:T(128)}, bf16[4,128,2048]{2,1,0:T(8,128)(2,1)}, bf16[128,2048]{1,0:T(8,128)(2,1)S(1)}, ...), branch_computations={%region_10.10_spmd, %region_11.14_spmd} | conditional | flops 1353218048 | bytes 69075104 | solution.py:186
  600.7 16.0 %collective-permute-done.1 = bf16[128,2048]{1,0:T(8,128)(2,1)S(1)} collective-permute-done((bf16[128,2048]{1,0:T(8,128)(2,1)}, bf16[128,2048]{1,0:T(8,128)(2,1)S(1)}, u32[]{:S(2)}, u32[]{:S(2)}) %collective-permute-start.1) | collective-permute-done | bytes 524320 | tf_op jit(solution)/shard_map/while/body/eval_jaxpr/ppermute | solution.py:16
  616.7 16.7 %conditional.7 = (bf16[128,2048]{1,0:T(8,128)(2,1)}, bf16[4,128,2048]{1,2,0:T(8,128)(2,1)}) conditional(s32[]{:T(128)} %convert_element_type.265, bf16[4,128,2048]{1,2,0:T(8,128)(2,1)} %get-tuple-element.1495, (pred[]{:T(512)}, s32[]{:T(128)}, bf16[4,128,2048]{2,1,0:T(8,128)(2,1)}, bf16[128,2048]{1,0:T(8,128)(2,1)S(1)}, ...), branch_computations={%region_10.10_spmd, %region_11.14_spmd} | conditional | flops 1353218048 | bytes 69075104 | solution.py:186
  634.7 10.0 %collective-permute-done.1 = bf16[128,2048]{1,0:T(8,128)(2,1)S(1)} collective-permute-done((bf16[128,2048]{1,0:T(8,128)(2,1)}, bf16[128,2048]{1,0:T(8,128)(2,1)S(1)}, u32[]{:S(2)}, u32[]{:S(2)}) %collective-permute-start.1) | collective-permute-done | bytes 524320 | tf_op jit(solution)/shard_map/while/body/eval_jaxpr/ppermute | solution.py:16
  648.8 10.7 %copy.56 = bf16[4,128,2048]{1,0,2:T(4,128)(2,1)} copy(bf16[4,128,2048]{1,2,0:T(8,128)(2,1)S(1)} %copy-done.1) | data formatting | bytes 4194304 | tf_op jit(solution)/shard_map/convert_element_type | solution.py:195
  666.5 5.6 fusion.78
  672.1 7.7 collective-permute-done.2
  679.8 7.2 add_convert_fusion
  687.0 214.5 %all_to_all.9 = bf16[16,64,2048]{2,1,0:T(8,128)(2,1)S(1)} all-to-all(bf16[16,64,2048]{2,1,0:T(8,128)(2,1)S(1)} %bitcast.139), channel_id=1, replica_groups=mesh['section'=8,'dp_hi'=16,'core'=2] {'dp_hi'}, dimensions={0} | all-to-all | bytes 8388608 | tf_op jit(solution)/shard_map/all_to_all | solution.py:209
  (240 shorter events, 185.0 us)
Async XLA Ops:
  9.8 3.3 copy-start.4
  25.3 12.7 %collective-permute-start = (bf16[128,2048]{0,1:T(8,128)(2,1)S(1)}, bf16[128,2048]{0,1:T(8,128)(2,1)S(1)}, u32[]{:S(2)}, u32[]{:S(2)}) collective-permute-start(bf16[128,2048]{0,1:T(8,128)(2,1)S(1)} %get-tuple-element.1373), channel_id=1, source_target_pairs={{0,32},{32,64},{64,96},{96,128},{128,160},{160,192},{192,224},{1,3... | collective-permute-start | bytes 1572872 | tf_op jit(solution)/shard_map/while/body/eval_jaxpr/ppermute | solution.py:16
  50.1 15.0 %collective-permute-start = (bf16[128,2048]{0,1:T(8,128)(2,1)S(1)}, bf16[128,2048]{0,1:T(8,128)(2,1)S(1)}, u32[]{:S(2)}, u32[]{:S(2)}) collective-permute-start(bf16[128,2048]{0,1:T(8,128)(2,1)S(1)} %get-tuple-element.1373), channel_id=1, source_target_pairs={{0,32},{32,64},{64,96},{96,128},{128,160},{160,192},{192,224},{1,3... | collective-permute-start | bytes 1572872 | tf_op jit(solution)/shard_map/while/body/eval_jaxpr/ppermute | solution.py:16
  77.2 14.1 %collective-permute-start = (bf16[128,2048]{0,1:T(8,128)(2,1)S(1)}, bf16[128,2048]{0,1:T(8,128)(2,1)S(1)}, u32[]{:S(2)}, u32[]{:S(2)}) collective-permute-start(bf16[128,2048]{0,1:T(8,128)(2,1)S(1)} %get-tuple-element.1373), channel_id=1, source_target_pairs={{0,32},{32,64},{64,96},{96,128},{128,160},{160,192},{192,224},{1,3... | collective-permute-start | bytes 1572872 | tf_op jit(solution)/shard_map/while/body/eval_jaxpr/ppermute | solution.py:16
  103.4 13.1 %collective-permute-start = (bf16[128,2048]{0,1:T(8,128)(2,1)S(1)}, bf16[128,2048]{0,1:T(8,128)(2,1)S(1)}, u32[]{:S(2)}, u32[]{:S(2)}) collective-permute-start(bf16[128,2048]{0,1:T(8,128)(2,1)S(1)} %get-tuple-element.1373), channel_id=1, source_target_pairs={{0,32},{32,64},{64,96},{96,128},{128,160},{160,192},{192,224},{1,3... | collective-permute-start | bytes 1572872 | tf_op jit(solution)/shard_map/while/body/eval_jaxpr/ppermute | solution.py:16
  116.6 24.2 %collective-permute-start = (bf16[128,2048]{0,1:T(8,128)(2,1)S(1)}, bf16[128,2048]{0,1:T(8,128)(2,1)S(1)}, u32[]{:S(2)}, u32[]{:S(2)}) collective-permute-start(bf16[128,2048]{0,1:T(8,128)(2,1)S(1)} %get-tuple-element.1373), channel_id=1, source_target_pairs={{0,32},{32,64},{64,96},{96,128},{128,160},{160,192},{192,224},{1,3... | collective-permute-start | bytes 1572872 | tf_op jit(solution)/shard_map/while/body/eval_jaxpr/ppermute | solution.py:16
  140.9 11.3 %collective-permute-start = (bf16[128,2048]{0,1:T(8,128)(2,1)S(1)}, bf16[128,2048]{0,1:T(8,128)(2,1)S(1)}, u32[]{:S(2)}, u32[]{:S(2)}) collective-permute-start(bf16[128,2048]{0,1:T(8,128)(2,1)S(1)} %get-tuple-element.1373), channel_id=1, source_target_pairs={{0,32},{32,64},{64,96},{96,128},{128,160},{160,192},{192,224},{1,3... | collective-permute-start | bytes 1572872 | tf_op jit(solution)/shard_map/while/body/eval_jaxpr/ppermute | solution.py:16
  152.3 22.1 %collective-permute-start = (bf16[128,2048]{0,1:T(8,128)(2,1)S(1)}, bf16[128,2048]{0,1:T(8,128)(2,1)S(1)}, u32[]{:S(2)}, u32[]{:S(2)}) collective-permute-start(bf16[128,2048]{0,1:T(8,128)(2,1)S(1)} %get-tuple-element.1373), channel_id=1, source_target_pairs={{0,32},{32,64},{64,96},{96,128},{128,160},{160,192},{192,224},{1,3... | collective-permute-start | bytes 1572872 | tf_op jit(solution)/shard_map/while/body/eval_jaxpr/ppermute | solution.py:16
  174.4 14.2 %collective-permute-start = (bf16[128,2048]{0,1:T(8,128)(2,1)S(1)}, bf16[128,2048]{0,1:T(8,128)(2,1)S(1)}, u32[]{:S(2)}, u32[]{:S(2)}) collective-permute-start(bf16[128,2048]{0,1:T(8,128)(2,1)S(1)} %get-tuple-element.1373), channel_id=1, source_target_pairs={{0,32},{32,64},{64,96},{96,128},{128,160},{160,192},{192,224},{1,3... | collective-permute-start | bytes 1572872 | tf_op jit(solution)/shard_map/while/body/eval_jaxpr/ppermute | solution.py:16
  188.7 29.0 %collective-permute-start = (bf16[128,2048]{0,1:T(8,128)(2,1)S(1)}, bf16[128,2048]{0,1:T(8,128)(2,1)S(1)}, u32[]{:S(2)}, u32[]{:S(2)}) collective-permute-start(bf16[128,2048]{0,1:T(8,128)(2,1)S(1)} %get-tuple-element.1373), channel_id=1, source_target_pairs={{0,32},{32,64},{64,96},{96,128},{128,160},{160,192},{192,224},{1,3... | collective-permute-start | bytes 1572872 | tf_op jit(solution)/shard_map/while/body/eval_jaxpr/ppermute | solution.py:16
  217.8 17.1 %collective-permute-start = (bf16[128,2048]{0,1:T(8,128)(2,1)S(1)}, bf16[128,2048]{0,1:T(8,128)(2,1)S(1)}, u32[]{:S(2)}, u32[]{:S(2)}) collective-permute-start(bf16[128,2048]{0,1:T(8,128)(2,1)S(1)} %get-tuple-element.1373), channel_id=1, source_target_pairs={{0,32},{32,64},{64,96},{96,128},{128,160},{160,192},{192,224},{1,3... | collective-permute-start | bytes 1572872 | tf_op jit(solution)/shard_map/while/body/eval_jaxpr/ppermute | solution.py:16
  235.0 29.0 %collective-permute-start = (bf16[128,2048]{0,1:T(8,128)(2,1)S(1)}, bf16[128,2048]{0,1:T(8,128)(2,1)S(1)}, u32[]{:S(2)}, u32[]{:S(2)}) collective-permute-start(bf16[128,2048]{0,1:T(8,128)(2,1)S(1)} %get-tuple-element.1373), channel_id=1, source_target_pairs={{0,32},{32,64},{64,96},{96,128},{128,160},{160,192},{192,224},{1,3... | collective-permute-start | bytes 1572872 | tf_op jit(solution)/shard_map/while/body/eval_jaxpr/ppermute | solution.py:16
  273.2 5.5 copy-start.2
  288.7 17.8 %collective-permute-start.1 = (bf16[128,2048]{1,0:T(8,128)(2,1)}, bf16[128,2048]{1,0:T(8,128)(2,1)S(1)}, u32[]{:S(2)}, u32[]{:S(2)}) collective-permute-start(bf16[128,2048]{1,0:T(8,128)(2,1)} %get-tuple-element.1395), channel_id=1, source_target_pairs={{32,0},{64,32},{96,64},{128,96},{160,128},{192,160},{224,192},{33,... | collective-permute-start | bytes 1572872 | tf_op jit(solution)/shard_map/while/body/eval_jaxpr/ppermute | solution.py:16
  307.3 18.2 %collective-permute-start.1 = (bf16[128,2048]{1,0:T(8,128)(2,1)}, bf16[128,2048]{1,0:T(8,128)(2,1)S(1)}, u32[]{:S(2)}, u32[]{:S(2)}) collective-permute-start(bf16[128,2048]{1,0:T(8,128)(2,1)} %get-tuple-element.1395), channel_id=1, source_target_pairs={{32,0},{64,32},{96,64},{128,96},{160,128},{192,160},{224,192},{33,... | collective-permute-start | bytes 1572872 | tf_op jit(solution)/shard_map/while/body/eval_jaxpr/ppermute | solution.py:16
  326.4 18.7 %collective-permute-start.1 = (bf16[128,2048]{1,0:T(8,128)(2,1)}, bf16[128,2048]{1,0:T(8,128)(2,1)S(1)}, u32[]{:S(2)}, u32[]{:S(2)}) collective-permute-start(bf16[128,2048]{1,0:T(8,128)(2,1)} %get-tuple-element.1395), channel_id=1, source_target_pairs={{32,0},{64,32},{96,64},{128,96},{160,128},{192,160},{224,192},{33,... | collective-permute-start | bytes 1572872 | tf_op jit(solution)/shard_map/while/body/eval_jaxpr/ppermute | solution.py:16
  346.0 21.9 %collective-permute-start.1 = (bf16[128,2048]{1,0:T(8,128)(2,1)}, bf16[128,2048]{1,0:T(8,128)(2,1)S(1)}, u32[]{:S(2)}, u32[]{:S(2)}) collective-permute-start(bf16[128,2048]{1,0:T(8,128)(2,1)} %get-tuple-element.1395), channel_id=1, source_target_pairs={{32,0},{64,32},{96,64},{128,96},{160,128},{192,160},{224,192},{33,... | collective-permute-start | bytes 1572872 | tf_op jit(solution)/shard_map/while/body/eval_jaxpr/ppermute | solution.py:16
  368.7 21.6 %collective-permute-start.1 = (bf16[128,2048]{1,0:T(8,128)(2,1)}, bf16[128,2048]{1,0:T(8,128)(2,1)S(1)}, u32[]{:S(2)}, u32[]{:S(2)}) collective-permute-start(bf16[128,2048]{1,0:T(8,128)(2,1)} %get-tuple-element.1395), channel_id=1, source_target_pairs={{32,0},{64,32},{96,64},{128,96},{160,128},{192,160},{224,192},{33,... | collective-permute-start | bytes 1572872 | tf_op jit(solution)/shard_map/while/body/eval_jaxpr/ppermute | solution.py:16
  391.2 11.3 %collective-permute-start.1 = (bf16[128,2048]{1,0:T(8,128)(2,1)}, bf16[128,2048]{1,0:T(8,128)(2,1)S(1)}, u32[]{:S(2)}, u32[]{:S(2)}) collective-permute-start(bf16[128,2048]{1,0:T(8,128)(2,1)} %get-tuple-element.1395), channel_id=1, source_target_pairs={{32,0},{64,32},{96,64},{128,96},{160,128},{192,160},{224,192},{33,... | collective-permute-start | bytes 1572872 | tf_op jit(solution)/shard_map/while/body/eval_jaxpr/ppermute | solution.py:16
  403.3 111.6 %collective-permute-start.1 = (bf16[128,2048]{1,0:T(8,128)(2,1)}, bf16[128,2048]{1,0:T(8,128)(2,1)S(1)}, u32[]{:S(2)}, u32[]{:S(2)}) collective-permute-start(bf16[128,2048]{1,0:T(8,128)(2,1)} %get-tuple-element.1395), channel_id=1, source_target_pairs={{32,0},{64,32},{96,64},{128,96},{160,128},{192,160},{224,192},{33,... | collective-permute-start | bytes 1572872 | tf_op jit(solution)/shard_map/while/body/eval_jaxpr/ppermute | solution.py:16
  518.0 1.9 copy-start
  519.9 4.8 slice-start
  520.6 4.1 slice-start.1
  531.5 17.3 %collective-permute-start.1 = (bf16[128,2048]{1,0:T(8,128)(2,1)}, bf16[128,2048]{1,0:T(8,128)(2,1)S(1)}, u32[]{:S(2)}, u32[]{:S(2)}) collective-permute-start(bf16[128,2048]{1,0:T(8,128)(2,1)} %get-tuple-element.1395), channel_id=1, source_target_pairs={{32,0},{64,32},{96,64},{128,96},{160,128},{192,160},{224,192},{33,... | collective-permute-start | bytes 1572872 | tf_op jit(solution)/shard_map/while/body/eval_jaxpr/ppermute | solution.py:16
  552.0 1.9 copy-start
  553.9 4.8 slice-start
  554.6 4.1 slice-start.1
  565.5 17.2 %collective-permute-start.1 = (bf16[128,2048]{1,0:T(8,128)(2,1)}, bf16[128,2048]{1,0:T(8,128)(2,1)S(1)}, u32[]{:S(2)}, u32[]{:S(2)}) collective-permute-start(bf16[128,2048]{1,0:T(8,128)(2,1)} %get-tuple-element.1395), channel_id=1, source_target_pairs={{32,0},{64,32},{96,64},{128,96},{160,128},{192,160},{224,192},{33,... | collective-permute-start | bytes 1572872 | tf_op jit(solution)/shard_map/while/body/eval_jaxpr/ppermute | solution.py:16
  585.8 1.9 copy-start
  587.8 4.8 slice-start
  588.5 4.1 slice-start.1
  599.4 17.3 %collective-permute-start.1 = (bf16[128,2048]{1,0:T(8,128)(2,1)}, bf16[128,2048]{1,0:T(8,128)(2,1)S(1)}, u32[]{:S(2)}, u32[]{:S(2)}) collective-permute-start(bf16[128,2048]{1,0:T(8,128)(2,1)} %get-tuple-element.1395), channel_id=1, source_target_pairs={{32,0},{64,32},{96,64},{128,96},{160,128},{192,160},{224,192},{33,... | collective-permute-start | bytes 1572872 | tf_op jit(solution)/shard_map/while/body/eval_jaxpr/ppermute | solution.py:16
  619.8 1.9 copy-start
  621.7 4.8 slice-start
  622.5 4.1 slice-start.1
  633.4 11.3 %collective-permute-start.1 = (bf16[128,2048]{1,0:T(8,128)(2,1)}, bf16[128,2048]{1,0:T(8,128)(2,1)S(1)}, u32[]{:S(2)}, u32[]{:S(2)}) collective-permute-start(bf16[128,2048]{1,0:T(8,128)(2,1)} %get-tuple-element.1395), channel_id=1, source_target_pairs={{32,0},{64,32},{96,64},{128,96},{160,128},{192,160},{224,192},{33,... | collective-permute-start | bytes 1572872 | tf_op jit(solution)/shard_map/while/body/eval_jaxpr/ppermute | solution.py:16
  644.7 4.1 copy-start.1
  662.5 1.6 copy-start.3
  666.4 13.4 %collective-permute-start.2 = (f32[1024,2048]{1,0:T(8,128)S(1)}, f32[1024,2048]{1,0:T(8,128)}, u32[]{:S(2)}, u32[]{:S(2)}) collective-permute-start(f32[1024,2048]{1,0:T(8,128)S(1)} %fusion.79), channel_id=1, source_target_pairs={{0,1},{1,0},{2,3},{3,2},{4,5},{5,4},{6,7},{7,6},{8,9},{9,8},{10,11... | collective-permute-start | bytes 25165832 | tf_op jit(solution)/shard_map/ppermute | solution.py:207

commit v6 on v5

--- a/solution.py
+++ b/solution.py
@@ -14,6 +14,19 @@
     devices = range(lax.axis_size(axis))
     route = [(i - distance, i) for i in devices if i - distance in devices]
     return lax.ppermute(block, axis, route)
+
+
+def scatter_sum(block, axis):
+    count = lax.axis_size(axis)
+    me = lax.axis_index(axis)
+    pieces = block.reshape(count, block.shape[0] // count, block.shape[1])
+    total = lax.dynamic_index_in_dim(pieces, me, 0, keepdims=False)
+    for shift in range(1, count):
+        sent = lax.dynamic_index_in_dim(pieces, (me + shift) % count, 0, keepdims=False)
+        route = [(i, (i + shift) % count) for i in range(count)]
+        received = lax.ppermute(sent.astype(jnp.bfloat16), axis, route)
+        total = total + received.astype(jnp.float32)
+    return total
 
 
 def allowed_pairs(pattern, outage):
@@ -206,8 +219,7 @@
 
     received = lax.ppermute(partial_grad(1 - core), "core", [(0, 1), (1, 0)])
     half = lax.optimization_barrier(partial_grad(core)) + received
-    swapped = lax.all_to_all(half.astype(jnp.bfloat16), "dp_hi", 0, 0, tiled=True)
-    summed = jnp.sum(swapped.reshape(groups, rows_each, width).astype(jnp.float32), axis=0)
+    summed = scatter_sum(half, "dp_hi")
     return summed[None]
 
 

time: 908 us -> 934 us (1.029)
  the two profiles are of different devices: /device:TPU:96 before, /device:TPU:17 now
where the time goes in v6:
time: 934 us; the launch traced here: 926 us
  waiting for transfers between devices  424 us (45%)
  starting transfers between devices  292 us (31%)
  matrix products  74.7 us (8%)
  local copies, waits for them, and re-layouts  71.9 us (8%)
  other arithmetic  61.3 us (7%)
    ppermute x22, waiting for transfers between devices, passed_along(): return lax.ppermute(block, axis, route)  341 us
    ppermute x15, starting transfers between devices, scatter_sum(): received = lax.ppermute(sent.astype(jnp.bfloat16), axis, route)  146 us
    ppermute x22, starting transfers between devices, passed_along(): return lax.ppermute(block, axis, route)  125 us
    ppermute x15, waiting for transfers between devices, scatter_sum(): received = lax.ppermute(sent.astype(jnp.bfloat16), axis, route)  75.7 us
    unnamed x19, local copies, waits for them, and re-layouts  24 us
    ppermute x1, starting transfers between devices, per_device(): received = lax.ppermute(partial_grad(1 - core), 'core', [(0, 1), (1, 0)])  21.1 us
    dot_general x4, matrix products, layer_forward(): jnp.dot(normed.reshape(-1, width), weight, preferred_element_type=jnp.flo...  18.8 us
  transfers between devices with their start and end apart: 38, of which 32 were waited for; matrix products, arithmetic and copies ran while one was open for 1% of the time, Pallas kernels for 0%

profile of v6, /device:TPU:17, one launch (start us, length us, event | category | flops | bytes accessed | tf_op | source)
XLA Modules:
  0.0 925.7 jit_solution(14362860415011295816)
XLA Ops:
  13.2 241.8 %while.48 = (s32[]{:T(128)}, bf16[128,2048]{0,1:T(8,128)(2,1)S(1)}, f32[4,128,2048]{1,2,0:T(8,128)}, f32[4,128,1]{1,2,0:T(1,128)S(1)}, bf16[4,128,16,128]{3,2,1,...) while((s32[]{:T(128)}, bf16[128,2048]{0,1:T(8,128)(2,1)S(1)}, ...), condition=%wide.region_8.9_spmd.clone, body=%wide.region_1.8_spmd.clone.sunk | while | flops 1216641408 | bytes 26020904 | solution.py:171
  13.2 12.1 %conditional.6 = (bf16[128,2048]{0,1:T(8,128)(2,1)S(1)}, f32[4,128,2048]{1,2,0:T(8,128)}, f32[4,128,1]{1,2,0:T(1,128)S(1)}, bf16[4,128,16,128]{3,2,1,0:T(8,128)(...) conditional(s32[]{:T(128)} %convert_element_type.494, ...), branch_computations={%region_2.2_spmd, %region_3.7_spmd} | conditional | flops 1216641408 | bytes 23923316 | solution.py:165
  26.7 10.9 %collective-permute-done = bf16[128,2048]{0,1:T(8,128)(2,1)S(1)} collective-permute-done((bf16[128,2048]{0,1:T(8,128)(2,1)S(1)}, bf16[128,2048]{0,1:T(8,128)(2,1)S(1)}, u32[]{:S(2)}, u32[]{:S(2)}) %collective-permute-start) | collective-permute-done | bytes 524320 | tf_op jit(solution)/shard_map/while/body/eval_jaxpr/ppermute | solution.py:16
  37.5 12.1 %conditional.6 = (bf16[128,2048]{0,1:T(8,128)(2,1)S(1)}, f32[4,128,2048]{1,2,0:T(8,128)}, f32[4,128,1]{1,2,0:T(1,128)S(1)}, bf16[4,128,16,128]{3,2,1,0:T(8,128)(...) conditional(s32[]{:T(128)} %convert_element_type.494, ...), branch_computations={%region_2.2_spmd, %region_3.7_spmd} | conditional | flops 1216641408 | bytes 23923316 | solution.py:165
  53.8 9.9 %collective-permute-done = bf16[128,2048]{0,1:T(8,128)(2,1)S(1)} collective-permute-done((bf16[128,2048]{0,1:T(8,128)(2,1)S(1)}, bf16[128,2048]{0,1:T(8,128)(2,1)S(1)}, u32[]{:S(2)}, u32[]{:S(2)}) %collective-permute-start) | collective-permute-done | bytes 524320 | tf_op jit(solution)/shard_map/while/body/eval_jaxpr/ppermute | solution.py:16
  63.7 12.0 %conditional.6 = (bf16[128,2048]{0,1:T(8,128)(2,1)S(1)}, f32[4,128,2048]{1,2,0:T(8,128)}, f32[4,128,1]{1,2,0:T(1,128)S(1)}, bf16[4,128,16,128]{3,2,1,0:T(8,128)(...) conditional(s32[]{:T(128)} %convert_element_type.494, ...), branch_computations={%region_2.2_spmd, %region_3.7_spmd} | conditional | flops 1216641408 | bytes 23923316 | solution.py:165
  79.9 9.0 collective-permute-done
  88.9 12.1 %conditional.6 = (bf16[128,2048]{0,1:T(8,128)(2,1)S(1)}, f32[4,128,2048]{1,2,0:T(8,128)}, f32[4,128,1]{1,2,0:T(1,128)S(1)}, bf16[4,128,16,128]{3,2,1,0:T(8,128)(...) conditional(s32[]{:T(128)} %convert_element_type.494, ...), branch_computations={%region_2.2_spmd, %region_3.7_spmd} | conditional | flops 1216641408 | bytes 23923316 | solution.py:165
  105.1 8.1 collective-permute-done
  113.2 16.1 %collective-permute-start = (bf16[128,2048]{0,1:T(8,128)(2,1)S(1)}, bf16[128,2048]{0,1:T(8,128)(2,1)S(1)}, u32[]{:S(2)}, u32[]{:S(2)}) collective-permute-start(bf16[128,2048]{0,1:T(8,128)(2,1)S(1)} %get-tuple-element.1388), channel_id=1, source_target_pairs={{0,32},{32,64},{64,96},{96,128},{128,160},{160,192},{192,224},{1,3... | collective-permute-start | bytes 1572872 | tf_op jit(solution)/shard_map/while/body/eval_jaxpr/ppermute | solution.py:16
  129.4 7.2 collective-permute-done
  140.8 6.1 collective-permute-done
  147.0 15.6 %collective-permute-start = (bf16[128,2048]{0,1:T(8,128)(2,1)S(1)}, bf16[128,2048]{0,1:T(8,128)(2,1)S(1)}, u32[]{:S(2)}, u32[]{:S(2)}) collective-permute-start(bf16[128,2048]{0,1:T(8,128)(2,1)S(1)} %get-tuple-element.1388), channel_id=1, source_target_pairs={{0,32},{32,64},{64,96},{96,128},{128,160},{160,192},{192,224},{1,3... | collective-permute-start | bytes 1572872 | tf_op jit(solution)/shard_map/while/body/eval_jaxpr/ppermute | solution.py:16
  162.6 6.1 collective-permute-done
  168.7 7.6 collective-permute-start
  176.3 6.1 collective-permute-done
  182.5 22.1 %collective-permute-start = (bf16[128,2048]{0,1:T(8,128)(2,1)S(1)}, bf16[128,2048]{0,1:T(8,128)(2,1)S(1)}, u32[]{:S(2)}, u32[]{:S(2)}) collective-permute-start(bf16[128,2048]{0,1:T(8,128)(2,1)S(1)} %get-tuple-element.1388), channel_id=1, source_target_pairs={{0,32},{32,64},{64,96},{96,128},{128,160},{160,192},{192,224},{1,3... | collective-permute-start | bytes 1572872 | tf_op jit(solution)/shard_map/while/body/eval_jaxpr/ppermute | solution.py:16
  204.6 6.1 collective-permute-done
  210.8 10.0 %collective-permute-start = (bf16[128,2048]{0,1:T(8,128)(2,1)S(1)}, bf16[128,2048]{0,1:T(8,128)(2,1)S(1)}, u32[]{:S(2)}, u32[]{:S(2)}) collective-permute-start(bf16[128,2048]{0,1:T(8,128)(2,1)S(1)} %get-tuple-element.1388), channel_id=1, source_target_pairs={{0,32},{32,64},{64,96},{96,128},{128,160},{160,192},{192,224},{1,3... | collective-permute-start | bytes 1572872 | tf_op jit(solution)/shard_map/while/body/eval_jaxpr/ppermute | solution.py:16
  220.8 6.1 collective-permute-done
  227.0 21.9 %collective-permute-start = (bf16[128,2048]{0,1:T(8,128)(2,1)S(1)}, bf16[128,2048]{0,1:T(8,128)(2,1)S(1)}, u32[]{:S(2)}, u32[]{:S(2)}) collective-permute-start(bf16[128,2048]{0,1:T(8,128)(2,1)S(1)} %get-tuple-element.1388), channel_id=1, source_target_pairs={{0,32},{32,64},{64,96},{96,128},{128,160},{160,192},{192,224},{1,3... | collective-permute-start | bytes 1572872 | tf_op jit(solution)/shard_map/while/body/eval_jaxpr/ppermute | solution.py:16
  248.9 6.1 collective-permute-done
  278.6 346.4 %while.49 = (s32[]{:T(128)}, bf16[128,2048]{1,0:T(8,128)(2,1)S(1)}, bf16[4,128,2048]{1,2,0:T(8,128)(2,1)}, s32[]{:T(128)}, pred[]{:T(512)}, /*index=5*/bf16[4,12...) while((s32[]{:T(128)}, bf16[128,2048]{1,0:T(8,128)(2,1)S(1)}, ...), condition=%wide.region_15.16_spmd.clone, body=%wide.region_9.15_spmd.clone.sunk | while | flops 1353218048 | bytes 71172608 | solution.py:203
  281.2 15.3 %collective-permute-done.1 = bf16[128,2048]{1,0:T(8,128)(2,1)S(1)} collective-permute-done((bf16[128,2048]{1,0:T(8,128)(2,1)}, bf16[128,2048]{1,0:T(8,128)(2,1)S(1)}, u32[]{:S(2)}, u32[]{:S(2)}) %collective-permute-start.1) | collective-permute-done | bytes 524320 | tf_op jit(solution)/shard_map/while/body/eval_jaxpr/ppermute | solution.py:16
  298.6 15.4 %collective-permute-done.1 = bf16[128,2048]{1,0:T(8,128)(2,1)S(1)} collective-permute-done((bf16[128,2048]{1,0:T(8,128)(2,1)}, bf16[128,2048]{1,0:T(8,128)(2,1)S(1)}, u32[]{:S(2)}, u32[]{:S(2)}) %collective-permute-start.1) | collective-permute-done | bytes 524320 | tf_op jit(solution)/shard_map/while/body/eval_jaxpr/ppermute | solution.py:16
  316.2 15.6 %collective-permute-done.1 = bf16[128,2048]{1,0:T(8,128)(2,1)S(1)} collective-permute-done((bf16[128,2048]{1,0:T(8,128)(2,1)}, bf16[128,2048]{1,0:T(8,128)(2,1)S(1)}, u32[]{:S(2)}, u32[]{:S(2)}) %collective-permute-start.1) | collective-permute-done | bytes 524320 | tf_op jit(solution)/shard_map/while/body/eval_jaxpr/ppermute | solution.py:16
  333.9 17.0 %collective-permute-done.1 = bf16[128,2048]{1,0:T(8,128)(2,1)S(1)} collective-permute-done((bf16[128,2048]{1,0:T(8,128)(2,1)}, bf16[128,2048]{1,0:T(8,128)(2,1)S(1)}, u32[]{:S(2)}, u32[]{:S(2)}) %collective-permute-start.1) | collective-permute-done | bytes 524320 | tf_op jit(solution)/shard_map/while/body/eval_jaxpr/ppermute | solution.py:16
  353.0 19.3 %collective-permute-done.1 = bf16[128,2048]{1,0:T(8,128)(2,1)S(1)} collective-permute-done((bf16[128,2048]{1,0:T(8,128)(2,1)}, bf16[128,2048]{1,0:T(8,128)(2,1)S(1)}, u32[]{:S(2)}, u32[]{:S(2)}) %collective-permute-start.1) | collective-permute-done | bytes 524320 | tf_op jit(solution)/shard_map/while/body/eval_jaxpr/ppermute | solution.py:16
  374.4 19.5 %collective-permute-done.1 = bf16[128,2048]{1,0:T(8,128)(2,1)S(1)} collective-permute-done((bf16[128,2048]{1,0:T(8,128)(2,1)}, bf16[128,2048]{1,0:T(8,128)(2,1)S(1)}, u32[]{:S(2)}, u32[]{:S(2)}) %collective-permute-start.1) | collective-permute-done | bytes 524320 | tf_op jit(solution)/shard_map/while/body/eval_jaxpr/ppermute | solution.py:16
  396.0 103.5 %collective-permute-done.1 = bf16[128,2048]{1,0:T(8,128)(2,1)S(1)} collective-permute-done((bf16[128,2048]{1,0:T(8,128)(2,1)}, bf16[128,2048]{1,0:T(8,128)(2,1)S(1)}, u32[]{:S(2)}, u32[]{:S(2)}) %collective-permute-start.1) | collective-permute-done | bytes 524320 | tf_op jit(solution)/shard_map/while/body/eval_jaxpr/ppermute | solution.py:16
  499.5 16.7 %conditional.7 = (bf16[128,2048]{1,0:T(8,128)(2,1)}, bf16[4,128,2048]{1,2,0:T(8,128)(2,1)}) conditional(s32[]{:T(128)} %convert_element_type.495, bf16[4,128,2048]{1,2,0:T(8,128)(2,1)} %get-tuple-element.1510, (pred[]{:T(512)}, s32[]{:T(128)}, bf16[4,128,2048]{2,1,0:T(8,128)(2,1)}, bf16[128,2048]{1,0:T(8,128)(2,1)S(1)}, ...), branch_computations={%region_10.10_spmd, %region_11.14_spmd} | conditional | flops 1353218048 | bytes 69075104 | solution.py:199
  517.5 15.0 %collective-permute-done.1 = bf16[128,2048]{1,0:T(8,128)(2,1)S(1)} collective-permute-done((bf16[128,2048]{1,0:T(8,128)(2,1)}, bf16[128,2048]{1,0:T(8,128)(2,1)S(1)}, u32[]{:S(2)}, u32[]{:S(2)}) %collective-permute-start.1) | collective-permute-done | bytes 524320 | tf_op jit(solution)/shard_map/while/body/eval_jaxpr/ppermute | solution.py:16
  532.5 16.7 %conditional.7 = (bf16[128,2048]{1,0:T(8,128)(2,1)}, bf16[4,128,2048]{1,2,0:T(8,128)(2,1)}) conditional(s32[]{:T(128)} %convert_element_type.495, bf16[4,128,2048]{1,2,0:T(8,128)(2,1)} %get-tuple-element.1510, (pred[]{:T(512)}, s32[]{:T(128)}, bf16[4,128,2048]{2,1,0:T(8,128)(2,1)}, bf16[128,2048]{1,0:T(8,128)(2,1)S(1)}, ...), branch_computations={%region_10.10_spmd, %region_11.14_spmd} | conditional | flops 1353218048 | bytes 69075104 | solution.py:199
  550.5 14.7 %collective-permute-done.1 = bf16[128,2048]{1,0:T(8,128)(2,1)S(1)} collective-permute-done((bf16[128,2048]{1,0:T(8,128)(2,1)}, bf16[128,2048]{1,0:T(8,128)(2,1)S(1)}, u32[]{:S(2)}, u32[]{:S(2)}) %collective-permute-start.1) | collective-permute-done | bytes 524320 | tf_op jit(solution)/shard_map/while/body/eval_jaxpr/ppermute | solution.py:16
  565.2 16.7 %conditional.7 = (bf16[128,2048]{1,0:T(8,128)(2,1)}, bf16[4,128,2048]{1,2,0:T(8,128)(2,1)}) conditional(s32[]{:T(128)} %convert_element_type.495, bf16[4,128,2048]{1,2,0:T(8,128)(2,1)} %get-tuple-element.1510, (pred[]{:T(512)}, s32[]{:T(128)}, bf16[4,128,2048]{2,1,0:T(8,128)(2,1)}, bf16[128,2048]{1,0:T(8,128)(2,1)S(1)}, ...), branch_computations={%region_10.10_spmd, %region_11.14_spmd} | conditional | flops 1353218048 | bytes 69075104 | solution.py:199
  583.2 15.0 %collective-permute-done.1 = bf16[128,2048]{1,0:T(8,128)(2,1)S(1)} collective-permute-done((bf16[128,2048]{1,0:T(8,128)(2,1)}, bf16[128,2048]{1,0:T(8,128)(2,1)S(1)}, u32[]{:S(2)}, u32[]{:S(2)}) %collective-permute-start.1) | collective-permute-done | bytes 524320 | tf_op jit(solution)/shard_map/while/body/eval_jaxpr/ppermute | solution.py:16
  598.2 16.7 %conditional.7 = (bf16[128,2048]{1,0:T(8,128)(2,1)}, bf16[4,128,2048]{1,2,0:T(8,128)(2,1)}) conditional(s32[]{:T(128)} %convert_element_type.495, bf16[4,128,2048]{1,2,0:T(8,128)(2,1)} %get-tuple-element.1510, (pred[]{:T(512)}, s32[]{:T(128)}, bf16[4,128,2048]{2,1,0:T(8,128)(2,1)}, bf16[128,2048]{1,0:T(8,128)(2,1)S(1)}, ...), branch_computations={%region_10.10_spmd, %region_11.14_spmd} | conditional | flops 1353218048 | bytes 69075104 | solution.py:199
  616.1 8.8 collective-permute-done.1
  629.1 10.7 %copy.56 = bf16[4,128,2048]{1,0,2:T(4,128)(2,1)} copy(bf16[4,128,2048]{1,2,0:T(8,128)(2,1)S(1)} %copy-done.1) | data formatting | bytes 4194304 | tf_op jit(solution)/shard_map/convert_element_type | solution.py:208
  649.9 21.1 %collective-permute-start.2 = (f32[1024,2048]{1,0:T(8,128)}, f32[1024,2048]{1,0:T(8,128)}, u32[]{:S(2)}, u32[]{:S(2)}) collective-permute-start(f32[1024,2048]{1,0:T(8,128)} %fusion.109), channel_id=1, source_target_pairs={{0,1},{1,0},{2,3},{3,2},{4,5},{5,4},{6,7},{7,6},{8,9},{9,8},{10,11... | collective-permute-start | bytes 25165832 | tf_op jit(solution)/shard_map/ppermute | solution.py:220
  676.6 7.5 collective-permute-done.2
  684.1 11.7 %add.349 = f32[1024,2048]{1,0:T(8,128)} add(f32[1024,2048]{1,0:T(8,128)} %fusion.108, f32[1024,2048]{1,0:T(8,128)} %collective-permute-done.2) | non-fusion elementwise | flops 2097152 | bytes 25165824 | tf_op jit(solution)/shard_map/add | solution.py:221
  699.7 118.6 %collective-permute-start.10 = (bf16[64,2048]{1,0:T(8,128)(2,1)S(1)}, bf16[64,2048]{1,0:T(8,128)(2,1)S(1)}, u32[]{:S(2)}, u32[]{:S(2)}) collective-permute-start(bf16[64,2048]{1,0:T(8,128)(2,1)S(1)} %get-tuple-element.1187), channel_id=1, source_target_pairs={{0,16},{2,18},{4,20},{6,22},{8,24},{10,26},{12,28},{14,30},{16,0},... | collective-permute-start | bytes 786440 | tf_op jit(solution)/shard_map/ppermute | solution.py:27
  824.7 6.7 collective-permute-done.11
  831.3 7.3 collective-permute-done.12
  845.2 6.3 collective-permute-done.14
  861.5 9.5 %collective-permute-start.7 = (bf16[64,2048]{1,0:T(8,128)(2,1)S(1)}, bf16[64,2048]{1,0:T(8,128)(2,1)}, u32[]{:S(2)}, u32[]{:S(2)}) collective-permute-start(bf16[64,2048]{1,0:T(8,128)(2,1)S(1)} %get-tuple-element.1190), channel_id=1, source_target_pairs={{0,10},{2,12},{4,14},{6,16},{8,18},{10,20},{12,22},{14,24},{16,26}... | collective-permute-start | bytes 786440 | tf_op jit(solution)/shard_map/ppermute | solution.py:27
  880.5 42.0 %collective-permute-done.9 = bf16[64,2048]{1,0:T(8,128)(2,1)} collective-permute-done((bf16[64,2048]{1,0:T(8,128)(2,1)S(1)}, bf16[64,2048]{1,0:T(8,128)(2,1)}, u32[]{:S(2)}, u32[]{:S(2)}) %collective-permute-start.9) | collective-permute-done | bytes 262176 | tf_op jit(solution)/shard_map/ppermute | solution.py:27
  (276 shorter events, 255.2 us)
Async XLA Ops:
  25.3 12.2 %collective-permute-start = (bf16[128,2048]{0,1:T(8,128)(2,1)S(1)}, bf16[128,2048]{0,1:T(8,128)(2,1)S(1)}, u32[]{:S(2)}, u32[]{:S(2)}) collective-permute-start(bf16[128,2048]{0,1:T(8,128)(2,1)S(1)} %get-tuple-element.1388), channel_id=1, source_target_pairs={{0,32},{32,64},{64,96},{96,128},{128,160},{160,192},{192,224},{1,3... | collective-permute-start | bytes 1572872 | tf_op jit(solution)/shard_map/while/body/eval_jaxpr/ppermute | solution.py:16
  49.6 14.1 %collective-permute-start = (bf16[128,2048]{0,1:T(8,128)(2,1)S(1)}, bf16[128,2048]{0,1:T(8,128)(2,1)S(1)}, u32[]{:S(2)}, u32[]{:S(2)}) collective-permute-start(bf16[128,2048]{0,1:T(8,128)(2,1)S(1)} %get-tuple-element.1388), channel_id=1, source_target_pairs={{0,32},{32,64},{64,96},{96,128},{128,160},{160,192},{192,224},{1,3... | collective-permute-start | bytes 1572872 | tf_op jit(solution)/shard_map/while/body/eval_jaxpr/ppermute | solution.py:16
  75.7 13.2 %collective-permute-start = (bf16[128,2048]{0,1:T(8,128)(2,1)S(1)}, bf16[128,2048]{0,1:T(8,128)(2,1)S(1)}, u32[]{:S(2)}, u32[]{:S(2)}) collective-permute-start(bf16[128,2048]{0,1:T(8,128)(2,1)S(1)} %get-tuple-element.1388), channel_id=1, source_target_pairs={{0,32},{32,64},{64,96},{96,128},{128,160},{160,192},{192,224},{1,3... | collective-permute-start | bytes 1572872 | tf_op jit(solution)/shard_map/while/body/eval_jaxpr/ppermute | solution.py:16
  101.0 12.1 %collective-permute-start = (bf16[128,2048]{0,1:T(8,128)(2,1)S(1)}, bf16[128,2048]{0,1:T(8,128)(2,1)S(1)}, u32[]{:S(2)}, u32[]{:S(2)}) collective-permute-start(bf16[128,2048]{0,1:T(8,128)(2,1)S(1)} %get-tuple-element.1388), channel_id=1, source_target_pairs={{0,32},{32,64},{64,96},{96,128},{128,160},{160,192},{192,224},{1,3... | collective-permute-start | bytes 1572872 | tf_op jit(solution)/shard_map/while/body/eval_jaxpr/ppermute | solution.py:16
  113.2 23.3 %collective-permute-start = (bf16[128,2048]{0,1:T(8,128)(2,1)S(1)}, bf16[128,2048]{0,1:T(8,128)(2,1)S(1)}, u32[]{:S(2)}, u32[]{:S(2)}) collective-permute-start(bf16[128,2048]{0,1:T(8,128)(2,1)S(1)} %get-tuple-element.1388), channel_id=1, source_target_pairs={{0,32},{32,64},{64,96},{96,128},{128,160},{160,192},{192,224},{1,3... | collective-permute-start | bytes 1572872 | tf_op jit(solution)/shard_map/while/body/eval_jaxpr/ppermute | solution.py:16
  136.7 10.2 %collective-permute-start = (bf16[128,2048]{0,1:T(8,128)(2,1)S(1)}, bf16[128,2048]{0,1:T(8,128)(2,1)S(1)}, u32[]{:S(2)}, u32[]{:S(2)}) collective-permute-start(bf16[128,2048]{0,1:T(8,128)(2,1)S(1)} %get-tuple-element.1388), channel_id=1, source_target_pairs={{0,32},{32,64},{64,96},{96,128},{128,160},{160,192},{192,224},{1,3... | collective-permute-start | bytes 1572872 | tf_op jit(solution)/shard_map/while/body/eval_jaxpr/ppermute | solution.py:16
  147.0 21.7 %collective-permute-start = (bf16[128,2048]{0,1:T(8,128)(2,1)S(1)}, bf16[128,2048]{0,1:T(8,128)(2,1)S(1)}, u32[]{:S(2)}, u32[]{:S(2)}) collective-permute-start(bf16[128,2048]{0,1:T(8,128)(2,1)S(1)} %get-tuple-element.1388), channel_id=1, source_target_pairs={{0,32},{32,64},{64,96},{96,128},{128,160},{160,192},{192,224},{1,3... | collective-permute-start | bytes 1572872 | tf_op jit(solution)/shard_map/while/body/eval_jaxpr/ppermute | solution.py:16
  168.7 13.6 %collective-permute-start = (bf16[128,2048]{0,1:T(8,128)(2,1)S(1)}, bf16[128,2048]{0,1:T(8,128)(2,1)S(1)}, u32[]{:S(2)}, u32[]{:S(2)}) collective-permute-start(bf16[128,2048]{0,1:T(8,128)(2,1)S(1)} %get-tuple-element.1388), channel_id=1, source_target_pairs={{0,32},{32,64},{64,96},{96,128},{128,160},{160,192},{192,224},{1,3... | collective-permute-start | bytes 1572872 | tf_op jit(solution)/shard_map/while/body/eval_jaxpr/ppermute | solution.py:16
  182.5 28.2 %collective-permute-start = (bf16[128,2048]{0,1:T(8,128)(2,1)S(1)}, bf16[128,2048]{0,1:T(8,128)(2,1)S(1)}, u32[]{:S(2)}, u32[]{:S(2)}) collective-permute-start(bf16[128,2048]{0,1:T(8,128)(2,1)S(1)} %get-tuple-element.1388), channel_id=1, source_target_pairs={{0,32},{32,64},{64,96},{96,128},{128,160},{160,192},{192,224},{1,3... | collective-permute-start | bytes 1572872 | tf_op jit(solution)/shard_map/while/body/eval_jaxpr/ppermute | solution.py:16
  210.8 16.1 %collective-permute-start = (bf16[128,2048]{0,1:T(8,128)(2,1)S(1)}, bf16[128,2048]{0,1:T(8,128)(2,1)S(1)}, u32[]{:S(2)}, u32[]{:S(2)}) collective-permute-start(bf16[128,2048]{0,1:T(8,128)(2,1)S(1)} %get-tuple-element.1388), channel_id=1, source_target_pairs={{0,32},{32,64},{64,96},{96,128},{128,160},{160,192},{192,224},{1,3... | collective-permute-start | bytes 1572872 | tf_op jit(solution)/shard_map/while/body/eval_jaxpr/ppermute | solution.py:16
  227.0 27.9 %collective-permute-start = (bf16[128,2048]{0,1:T(8,128)(2,1)S(1)}, bf16[128,2048]{0,1:T(8,128)(2,1)S(1)}, u32[]{:S(2)}, u32[]{:S(2)}) collective-permute-start(bf16[128,2048]{0,1:T(8,128)(2,1)S(1)} %get-tuple-element.1388), channel_id=1, source_target_pairs={{0,32},{32,64},{64,96},{96,128},{128,160},{160,192},{192,224},{1,3... | collective-permute-start | bytes 1572872 | tf_op jit(solution)/shard_map/while/body/eval_jaxpr/ppermute | solution.py:16
  264.1 5.6 copy-start.2
  279.9 16.6 %collective-permute-start.1 = (bf16[128,2048]{1,0:T(8,128)(2,1)}, bf16[128,2048]{1,0:T(8,128)(2,1)S(1)}, u32[]{:S(2)}, u32[]{:S(2)}) collective-permute-start(bf16[128,2048]{1,0:T(8,128)(2,1)} %get-tuple-element.1410), channel_id=1, source_target_pairs={{32,0},{64,32},{96,64},{128,96},{160,128},{192,160},{224,192},{33,... | collective-permute-start | bytes 1572872 | tf_op jit(solution)/shard_map/while/body/eval_jaxpr/ppermute | solution.py:16
  297.4 16.7 %collective-permute-start.1 = (bf16[128,2048]{1,0:T(8,128)(2,1)}, bf16[128,2048]{1,0:T(8,128)(2,1)S(1)}, u32[]{:S(2)}, u32[]{:S(2)}) collective-permute-start(bf16[128,2048]{1,0:T(8,128)(2,1)} %get-tuple-element.1410), channel_id=1, source_target_pairs={{32,0},{64,32},{96,64},{128,96},{160,128},{192,160},{224,192},{33,... | collective-permute-start | bytes 1572872 | tf_op jit(solution)/shard_map/while/body/eval_jaxpr/ppermute | solution.py:16
  314.9 16.8 %collective-permute-start.1 = (bf16[128,2048]{1,0:T(8,128)(2,1)}, bf16[128,2048]{1,0:T(8,128)(2,1)S(1)}, u32[]{:S(2)}, u32[]{:S(2)}) collective-permute-start(bf16[128,2048]{1,0:T(8,128)(2,1)} %get-tuple-element.1410), channel_id=1, source_target_pairs={{32,0},{64,32},{96,64},{128,96},{160,128},{192,160},{224,192},{33,... | collective-permute-start | bytes 1572872 | tf_op jit(solution)/shard_map/while/body/eval_jaxpr/ppermute | solution.py:16
  332.6 18.2 %collective-permute-start.1 = (bf16[128,2048]{1,0:T(8,128)(2,1)}, bf16[128,2048]{1,0:T(8,128)(2,1)S(1)}, u32[]{:S(2)}, u32[]{:S(2)}) collective-permute-start(bf16[128,2048]{1,0:T(8,128)(2,1)} %get-tuple-element.1410), channel_id=1, source_target_pairs={{32,0},{64,32},{96,64},{128,96},{160,128},{192,160},{224,192},{33,... | collective-permute-start | bytes 1572872 | tf_op jit(solution)/shard_map/while/body/eval_jaxpr/ppermute | solution.py:16
  351.7 20.6 %collective-permute-start.1 = (bf16[128,2048]{1,0:T(8,128)(2,1)}, bf16[128,2048]{1,0:T(8,128)(2,1)S(1)}, u32[]{:S(2)}, u32[]{:S(2)}) collective-permute-start(bf16[128,2048]{1,0:T(8,128)(2,1)} %get-tuple-element.1410), channel_id=1, source_target_pairs={{32,0},{64,32},{96,64},{128,96},{160,128},{192,160},{224,192},{33,... | collective-permute-start | bytes 1572872 | tf_op jit(solution)/shard_map/while/body/eval_jaxpr/ppermute | solution.py:16
  373.1 20.8 %collective-permute-start.1 = (bf16[128,2048]{1,0:T(8,128)(2,1)}, bf16[128,2048]{1,0:T(8,128)(2,1)S(1)}, u32[]{:S(2)}, u32[]{:S(2)}) collective-permute-start(bf16[128,2048]{1,0:T(8,128)(2,1)} %get-tuple-element.1410), channel_id=1, source_target_pairs={{32,0},{64,32},{96,64},{128,96},{160,128},{192,160},{224,192},{33,... | collective-permute-start | bytes 1572872 | tf_op jit(solution)/shard_map/while/body/eval_jaxpr/ppermute | solution.py:16
  394.7 104.8 %collective-permute-start.1 = (bf16[128,2048]{1,0:T(8,128)(2,1)}, bf16[128,2048]{1,0:T(8,128)(2,1)S(1)}, u32[]{:S(2)}, u32[]{:S(2)}) collective-permute-start(bf16[128,2048]{1,0:T(8,128)(2,1)} %get-tuple-element.1410), channel_id=1, source_target_pairs={{32,0},{64,32},{96,64},{128,96},{160,128},{192,160},{224,192},{33,... | collective-permute-start | bytes 1572872 | tf_op jit(solution)/shard_map/while/body/eval_jaxpr/ppermute | solution.py:16
  504.6 4.8 slice-start
  505.3 4.1 slice-start.1
  516.2 16.3 %collective-permute-start.1 = (bf16[128,2048]{1,0:T(8,128)(2,1)}, bf16[128,2048]{1,0:T(8,128)(2,1)S(1)}, u32[]{:S(2)}, u32[]{:S(2)}) collective-permute-start(bf16[128,2048]{1,0:T(8,128)(2,1)} %get-tuple-element.1410), channel_id=1, source_target_pairs={{32,0},{64,32},{96,64},{128,96},{160,128},{192,160},{224,192},{33,... | collective-permute-start | bytes 1572872 | tf_op jit(solution)/shard_map/while/body/eval_jaxpr/ppermute | solution.py:16
  537.6 4.8 slice-start
  538.3 4.1 slice-start.1
  549.2 16.0 %collective-permute-start.1 = (bf16[128,2048]{1,0:T(8,128)(2,1)}, bf16[128,2048]{1,0:T(8,128)(2,1)S(1)}, u32[]{:S(2)}, u32[]{:S(2)}) collective-permute-start(bf16[128,2048]{1,0:T(8,128)(2,1)} %get-tuple-element.1410), channel_id=1, source_target_pairs={{32,0},{64,32},{96,64},{128,96},{160,128},{192,160},{224,192},{33,... | collective-permute-start | bytes 1572872 | tf_op jit(solution)/shard_map/while/body/eval_jaxpr/ppermute | solution.py:16
  570.3 4.8 slice-start
  581.9 16.3 %collective-permute-start.1 = (bf16[128,2048]{1,0:T(8,128)(2,1)}, bf16[128,2048]{1,0:T(8,128)(2,1)S(1)}, u32[]{:S(2)}, u32[]{:S(2)}) collective-permute-start(bf16[128,2048]{1,0:T(8,128)(2,1)} %get-tuple-element.1410), channel_id=1, source_target_pairs={{32,0},{64,32},{96,64},{128,96},{160,128},{192,160},{224,192},{33,... | collective-permute-start | bytes 1572872 | tf_op jit(solution)/shard_map/while/body/eval_jaxpr/ppermute | solution.py:16
  603.2 4.8 slice-start
  603.9 4.1 slice-start.1
  614.8 10.1 %collective-permute-start.1 = (bf16[128,2048]{1,0:T(8,128)(2,1)}, bf16[128,2048]{1,0:T(8,128)(2,1)S(1)}, u32[]{:S(2)}, u32[]{:S(2)}) collective-permute-start(bf16[128,2048]{1,0:T(8,128)(2,1)} %get-tuple-element.1410), channel_id=1, source_target_pairs={{32,0},{64,32},{96,64},{128,96},{160,128},{192,160},{224,192},{33,... | collective-permute-start | bytes 1572872 | tf_op jit(solution)/shard_map/while/body/eval_jaxpr/ppermute | solution.py:16
  625.0 4.2 copy-start.1
  644.3 26.7 %copy-start.4 = (bf16[4,128,2048]{2,1,0:T(8,128)(2,1)S(1)}, bf16[4,128,2048]{2,1,0:T(8,128)(2,1)}, u32[]{:S(2)}) copy-start(bf16[4,128,2048]{2,1,0:T(8,128)(2,1)} %copy.62) | copy-start | bytes 6291460
  649.9 34.2 %collective-permute-start.2 = (f32[1024,2048]{1,0:T(8,128)}, f32[1024,2048]{1,0:T(8,128)}, u32[]{:S(2)}, u32[]{:S(2)}) collective-permute-start(f32[1024,2048]{1,0:T(8,128)} %fusion.109), channel_id=1, source_target_pairs={{0,1},{1,0},{2,3},{3,2},{4,5},{5,4},{6,7},{7,6},{8,9},{9,8},{10,11... | collective-permute-start | bytes 25165832 | tf_op jit(solution)/shard_map/ppermute | solution.py:220
  699.7 125.0 %collective-permute-start.10 = (bf16[64,2048]{1,0:T(8,128)(2,1)S(1)}, bf16[64,2048]{1,0:T(8,128)(2,1)S(1)}, u32[]{:S(2)}, u32[]{:S(2)}) collective-permute-start(bf16[64,2048]{1,0:T(8,128)(2,1)S(1)} %get-tuple-element.1187), channel_id=1, source_target_pairs={{0,16},{2,18},{4,20},{6,22},{8,24},{10,26},{12,28},{14,30},{16,0},... | collective-permute-start | bytes 786440 | tf_op jit(solution)/shard_map/ppermute | solution.py:27
  818.2 13.1 %collective-permute-start.11 = (bf16[64,2048]{1,0:T(8,128)(2,1)S(1)}, bf16[64,2048]{1,0:T(8,128)(2,1)S(1)}, u32[]{:S(2)}, u32[]{:S(2)}) collective-permute-start(bf16[64,2048]{1,0:T(8,128)(2,1)S(1)} %get-tuple-element.1186), channel_id=1, source_target_pairs={{0,18},{2,20},{4,22},{6,24},{8,26},{10,28},{12,30},{14,0},{16,2},{... | collective-permute-start | bytes 786440 | tf_op jit(solution)/shard_map/ppermute | solution.py:27
  819.0 19.6 %collective-permute-start.12 = (bf16[64,2048]{1,0:T(8,128)(2,1)S(1)}, bf16[64,2048]{1,0:T(8,128)(2,1)S(1)}, u32[]{:S(2)}, u32[]{:S(2)}) collective-permute-start(bf16[64,2048]{1,0:T(8,128)(2,1)S(1)} %get-tuple-element.1185), channel_id=1, source_target_pairs={{0,20},{2,22},{4,24},{6,26},{8,28},{10,30},{12,0},{14,2},{16,4},{1... | collective-permute-start | bytes 786440 | tf_op jit(solution)/shard_map/ppermute | solution.py:27
  819.0 23.8 %collective-permute-start.13 = (bf16[64,2048]{1,0:T(8,128)(2,1)S(1)}, bf16[64,2048]{1,0:T(8,128)(2,1)S(1)}, u32[]{:S(2)}, u32[]{:S(2)}) collective-permute-start(bf16[64,2048]{1,0:T(8,128)(2,1)S(1)} %get-tuple-element.1184), channel_id=1, source_target_pairs={{0,22},{2,24},{4,26},{6,28},{8,30},{10,0},{12,2},{14,4},{16,6},{18... | collective-permute-start | bytes 786440 | tf_op jit(solution)/shard_map/ppermute | solution.py:27
  819.1 32.4 %collective-permute-start.14 = (bf16[64,2048]{1,0:T(8,128)(2,1)S(1)}, bf16[64,2048]{1,0:T(8,128)(2,1)S(1)}, u32[]{:S(2)}, u32[]{:S(2)}) collective-permute-start(bf16[64,2048]{1,0:T(8,128)(2,1)S(1)} %get-tuple-element.1183), channel_id=1, source_target_pairs={{0,24},{2,26},{4,28},{6,30},{8,0},{10,2},{12,4},{14,6},{16,8},{18,... | collective-permute-start | bytes 786440 | tf_op jit(solution)/shard_map/ppermute | solution.py:27
  824.7 31.9 %collective-permute-start.15 = (bf16[64,2048]{1,0:T(8,128)(2,1)S(1)}, bf16[64,2048]{1,0:T(8,128)(2,1)S(1)}, u32[]{:S(2)}, u32[]{:S(2)}) collective-permute-start(bf16[64,2048]{1,0:T(8,128)(2,1)S(1)} %get-tuple-element.1182), channel_id=1, source_target_pairs={{0,26},{2,28},{4,30},{6,0},{8,2},{10,4},{12,6},{14,8},{16,10},{18,... | collective-permute-start | bytes 786440 | tf_op jit(solution)/shard_map/ppermute | solution.py:27
  831.3 25.7 %collective-permute-start.16 = (bf16[64,2048]{1,0:T(8,128)(2,1)S(1)}, bf16[64,2048]{1,0:T(8,128)(2,1)S(1)}, u32[]{:S(2)}, u32[]{:S(2)}) collective-permute-start(bf16[64,2048]{1,0:T(8,128)(2,1)S(1)} %get-tuple-element.1181), channel_id=1, source_target_pairs={{0,28},{2,30},{4,0},{6,2},{8,4},{10,6},{12,8},{14,10},{16,12},{18,... | collective-permute-start | bytes 786440 | tf_op jit(solution)/shard_map/ppermute | solution.py:27
  838.7 22.9 %collective-permute-start.17 = (bf16[64,2048]{1,0:T(8,128)(2,1)S(1)}, bf16[64,2048]{1,0:T(8,128)(2,1)S(1)}, u32[]{:S(2)}, u32[]{:S(2)}) collective-permute-start(bf16[64,2048]{1,0:T(8,128)(2,1)S(1)} %get-tuple-element.1180), channel_id=1, source_target_pairs={{0,30},{2,0},{4,2},{6,4},{8,6},{10,8},{12,10},{14,12},{16,14},{18,... | collective-permute-start | bytes 786440 | tf_op jit(solution)/shard_map/ppermute | solution.py:27
  842.9 28.2 %collective-permute-start.3 = (bf16[64,2048]{1,0:T(8,128)(2,1)S(1)}, bf16[64,2048]{1,0:T(8,128)(2,1)S(1)}, u32[]{:S(2)}, u32[]{:S(2)}) collective-permute-start(bf16[64,2048]{1,0:T(8,128)(2,1)S(1)} %get-tuple-element.1179), channel_id=1, source_target_pairs={{0,2},{2,4},{4,6},{6,8},{8,10},{10,12},{12,14},{14,16},{16,18},{18... | collective-permute-start | bytes 786440 | tf_op jit(solution)/shard_map/ppermute | solution.py:27
  851.4 19.6 %collective-permute-start.4 = (bf16[64,2048]{1,0:T(8,128)(2,1)S(1)}, bf16[64,2048]{1,0:T(8,128)(2,1)S(1)}, u32[]{:S(2)}, u32[]{:S(2)}) collective-permute-start(bf16[64,2048]{1,0:T(8,128)(2,1)S(1)} %get-tuple-element.1193), channel_id=1, source_target_pairs={{0,4},{2,6},{4,8},{6,10},{8,12},{10,14},{12,16},{14,18},{16,20},{1... | collective-permute-start | bytes 786440 | tf_op jit(solution)/shard_map/ppermute | solution.py:27
  856.5 20.8 %collective-permute-start.5 = (bf16[64,2048]{1,0:T(8,128)(2,1)S(1)}, bf16[64,2048]{1,0:T(8,128)(2,1)}, u32[]{:S(2)}, u32[]{:S(2)}) collective-permute-start(bf16[64,2048]{1,0:T(8,128)(2,1)S(1)} %get-tuple-element.1192), channel_id=1, source_target_pairs={{0,6},{2,8},{4,10},{6,12},{8,14},{10,16},{12,18},{14,20},{16,22},{... | collective-permute-start | bytes 786440 | tf_op jit(solution)/shard_map/ppermute | solution.py:27
  857.0 20.3 %collective-permute-start.6 = (bf16[64,2048]{1,0:T(8,128)(2,1)S(1)}, bf16[64,2048]{1,0:T(8,128)(2,1)}, u32[]{:S(2)}, u32[]{:S(2)}) collective-permute-start(bf16[64,2048]{1,0:T(8,128)(2,1)S(1)} %get-tuple-element.1191), channel_id=1, source_target_pairs={{0,8},{2,10},{4,12},{6,14},{8,16},{10,18},{12,20},{14,22},{16,24},... | collective-permute-start | bytes 786440 | tf_op jit(solution)/shard_map/ppermute | solution.py:27
  861.5 15.8 %collective-permute-start.7 = (bf16[64,2048]{1,0:T(8,128)(2,1)S(1)}, bf16[64,2048]{1,0:T(8,128)(2,1)}, u32[]{:S(2)}, u32[]{:S(2)}) collective-permute-start(bf16[64,2048]{1,0:T(8,128)(2,1)S(1)} %get-tuple-element.1190), channel_id=1, source_target_pairs={{0,10},{2,12},{4,14},{6,16},{8,18},{10,20},{12,22},{14,24},{16,26}... | collective-permute-start | bytes 786440 | tf_op jit(solution)/shard_map/ppermute | solution.py:27
  871.0 9.5 %collective-permute-start.8 = (bf16[64,2048]{1,0:T(8,128)(2,1)S(1)}, bf16[64,2048]{1,0:T(8,128)(2,1)}, u32[]{:S(2)}, u32[]{:S(2)}) collective-permute-start(bf16[64,2048]{1,0:T(8,128)(2,1)S(1)} %get-tuple-element.1189), channel_id=1, source_target_pairs={{0,12},{2,14},{4,16},{6,18},{8,20},{10,22},{12,24},{14,26},{16,28}... | collective-permute-start | bytes 786440 | tf_op jit(solution)/shard_map/ppermute | solution.py:27
  872.4 50.1 %collective-permute-start.9 = (bf16[64,2048]{1,0:T(8,128)(2,1)S(1)}, bf16[64,2048]{1,0:T(8,128)(2,1)}, u32[]{:S(2)}, u32[]{:S(2)}) collective-permute-start(bf16[64,2048]{1,0:T(8,128)(2,1)S(1)} %get-tuple-element.1188), channel_id=1, source_target_pairs={{0,14},{2,16},{4,18},{6,20},{8,22},{10,24},{12,26},{14,28},{16,30}... | collective-permute-start | bytes 786440 | tf_op jit(solution)/shard_map/ppermute | solution.py:27
  (9 other events, 18.0 us)

commit v7 on v5

--- a/solution.py
+++ b/solution.py
@@ -10,10 +10,10 @@
 epsilon = 1e-05
 
 
-def passed_along(block, axis, distance):
-    devices = range(lax.axis_size(axis))
-    route = [(i - distance, i) for i in devices if i - distance in devices]
-    return lax.ppermute(block, axis, route)
+def passed_along(block, axis, distance, senders):
+    if not senders:
+        return jnp.zeros_like(block)
+    return lax.ppermute(block, axis, [(i, i + distance) for i in senders])
 
 
 def allowed_pairs(pattern, outage):
@@ -152,12 +152,14 @@
         output, stashed, upstream_stash = lax.cond(
             active, forward_do_work, forward_no_work, stashed, upstream_stash
         )
-        passed = passed_along(output, "section", 1)
+        senders = [r for r in range(sections - 1) if 0 <= step - r < micro]
+        passed = passed_along(output, "section", 1, senders)
         return (passed, stashed, upstream_stash)
 
-    unused_rows, stashed, upstream_stash = lax.fori_loop(
-        0, steps_total, forward_step, (zero_rows, stash_init, upstream_init)
-    )
+    carry = (zero_rows, stash_init, upstream_init)
+    for step in range(steps_total):
+        carry = forward_step(step, carry)
+    unused_rows, stashed, upstream_stash = carry
     totals_init = jnp.zeros((micro, buses, width), jnp.bfloat16)
 
     def backward_step(step, carry):
@@ -184,10 +186,14 @@
             return (zero_rows, collected_in)
 
         lower, collected = lax.cond(active, backward_do_work, backward_no_work, collected)
-        passed = passed_along(lower, "section", -1)
+        senders = [r for r in range(1, sections) if 0 <= step - (sections - 1 - r) < micro]
+        passed = passed_along(lower, "section", -1, senders)
         return (passed, collected)
 
-    unused_rows, collected = lax.fori_loop(0, steps_total, backward_step, (zero_rows, totals_init))
+    carry = (zero_rows, totals_init)
+    for step in range(steps_total):
+        carry = backward_step(step, carry)
+    unused_rows, collected = carry
     cores = lax.axis_size("core")
     groups = lax.axis_size("dp_hi")
     core = lax.axis_index("core")

time: 908 us -> 1140 us (1.26)
  waiting for transfers between devices: 366 us -> 641 us
  blocking collectives: 214 us -> 122 us
  starting transfers between devices: 128 us -> 36 us
  local copies, waits for them, and re-layouts: 66.9 us -> 153 us
  loops' own time: 1.25 us -> 35.8 us
    ppermute x22 -> x20, waiting for transfers between devices: 358 us -> 633 us  [passed_along(): return lax.ppermute(block, axis, [(i, i + distance) for i in senders])]
    all_to_all x1, blocking collectives: 214 us -> 122 us  [per_device(): lax.all_to_all(half.astype(jnp.bfloat16), 'dp_hi', 0, 0, tiled=True)]
    ppermute x22 -> x20, starting transfers between devices: 128 us -> 35.9 us  [passed_along(): return lax.ppermute(block, axis, [(i, i + distance) for i in senders])]
    another operation x2 -> x23, local copies, waits for them, and re-layouts: 3.21 us -> 84.8 us
    another operation x11, loops' own time: 0.36 us -> 29.9 us  [backward_step(): lax.cond(active, backward_do_work, backward_no_work, collected)]
    unnamed x13 -> x2, local copies, waits for them, and re-layouts: 22.6 us -> 0.01 us
  transfers between devices with their start and end apart: 23 -> 21, of which waited for: 23 -> 9; matrix products, arithmetic and copies ran while one was open for 1% -> 1% of each run, Pallas kernels for 0% -> 0%
where the time goes in v7:
time: 1140 us; the launch traced here: 1130 us
  waiting for transfers between devices  641 us (56%)
  local copies, waits for them, and re-layouts  153 us (13%)
  blocking collectives  122 us (11%)
  matrix products  82 us (7%)
  other arithmetic  61.6 us (5%)
  starting transfers between devices  36 us (3%)
  loops' own time  35.8 us (3%)
    ppermute x20, waiting for transfers between devices, passed_along(): return lax.ppermute(block, axis, [(i, i + distance) for i in senders])  633 us
    all_to_all x1, blocking collectives, per_device(): lax.all_to_all(half.astype(jnp.bfloat16), 'dp_hi', 0, 0, tiled=True)  122 us
    another operation x23, local copies, waits for them, and re-layouts  84.8 us
    ppermute x20, starting transfers between devices, passed_along(): return lax.ppermute(block, axis, [(i, i + distance) for i in senders])  35.9 us
    another operation x11, loops' own time, backward_step(): lax.cond(active, backward_do_work, backward_no_work, collected)  29.9 us
  transfers between devices with their start and end apart: 21, of which 9 were waited for; matrix products, arithmetic and copies ran while one was open for 1% of the time, Pallas kernels for 0%

profile of v7, /device:TPU:96, one launch (start us, length us, event | category | flops | bytes accessed | tf_op | source)
XLA Modules:
  0.0 1131.9 jit_solution(17595025205379412273)
XLA Ops:
  2.3 25.7 %conditional.22 = (bf16[128,2048]{0,1:T(8,128)(2,1)}, f32[4,128,2048]{1,2,0:T(8,128)}, f32[4,128,1]{1,2,0:T(1,128)}, bf16[4,128,16,128]{3,2,1,0:T(8,128)(2,1)}, ...) conditional(s32[]{:T(128)} %convert_element_type.1177, () %tuple.279, ...), branch_computations={%region_1.2_spmd, %region_2.7_spmd} | conditional | flops 1216608640 | bytes 58789088 | solution.py:152
  8.3 4.7 convolution_convert_fusion
  30.1 10.9 collective-permute-done
  41.1 18.3 %conditional.23 = (bf16[128,2048]{0,1:T(8,128)(2,1)}, f32[4,128,2048]{1,2,0:T(8,128)}, f32[4,128,1]{1,2,0:T(1,128)}, bf16[4,128,16,128]{3,2,1,0:T(8,128)(2,1)}, ...) conditional(s32[]{:T(128)} %convert_element_type.1176, ...), branch_computations={%region_7.8_spmd, %region_8.13_spmd} | conditional | flops 1216608640 | bytes 28345488 | solution.py:152
  47.0 4.7 convolution_convert_fusion.1
  59.4 5.0 collective-permute-start.1
  64.4 10.1 collective-permute-done.1
  74.5 18.0 %conditional.24 = (bf16[128,2048]{0,1:T(8,128)(2,1)}, f32[4,128,2048]{1,2,0:T(8,128)}, f32[4,128,1]{1,2,0:T(1,128)}, bf16[4,128,16,128]{3,2,1,0:T(8,128)(2,1)}, ...) conditional(s32[]{:T(128)} %convert_element_type.1175, ...), branch_computations={%region_13.14_spmd, %region_14.19_spmd} | conditional | flops 1216608640 | bytes 28345488 | solution.py:152
  80.2 4.7 convolution_convert_fusion.2
  92.5 5.3 collective-permute-start.2
  97.8 9.2 collective-permute-done.2
  107.0 18.2 %conditional.25 = (bf16[128,2048]{0,1:T(8,128)(2,1)}, f32[4,128,2048]{1,2,0:T(8,128)}, f32[4,128,1]{1,2,0:T(1,128)}, bf16[4,128,16,128]{3,2,1,0:T(8,128)(2,1)}, ...) conditional(s32[]{:T(128)} %convert_element_type.1174, ...), branch_computations={%region_19.20_spmd, %region_20.25_spmd} | conditional | flops 1216608640 | bytes 28345488 | solution.py:152
  112.9 4.7 convolution_convert_fusion.3
  125.2 5.2 collective-permute-start.3
  130.4 8.2 collective-permute-done.3
  157.7 17.7 %conditional.32 = (f32[4,128,2048]{1,2,0:T(8,128)}, f32[4,128,1]{1,2,0:T(1,128)}, bf16[4,128,16,128]{3,2,1,0:T(8,128)(2,1)}, f32[4,16,128,128]{2,3,1,0:T(8,128)}...) conditional(s32[]{:T(128)} %convert_element_type.1167, ...), branch_computations={%region_61.62_spmd, %region_62.67_spmd} | conditional | flops 1217657216 | bytes 50889956 | solution.py:152
  160.2 10.7 copy.547
  175.5 5.7 conditional.33
  181.9 5.0 conditional.34
  187.7 5.1 conditional.35
  193.5 5.3 conditional.36
  199.5 5.0 conditional.37
  205.2 5.0 conditional.38
  210.9 5.1 conditional.39
  217.3 551.6 %collective-permute-done.16 = bf16[128,2048]{1,0:T(8,128)(2,1)S(1)} collective-permute-done((bf16[128,2048]{1,0:T(8,128)(2,1)}, bf16[128,2048]{1,0:T(8,128)(2,1)S(1)}, u32[]{:S(2)}, u32[]{:S(2)}) %collective-permute-start.16) | collective-permute-done | bytes 524320 | tf_op jit(solution)/shard_map/ppermute | solution.py:16
  768.9 46.0 %conditional.40 = (bf16[128,2048]{1,0:T(8,128)(2,1)}, bf16[4,128,2048]{1,2,0:T(8,128)(2,1)}) conditional(s32[]{:T(128)} %convert_element_type.1184, bf16[4,128,2048]{1,2,0:T(8,128)(2,1)} %get-tuple-element.2701, (s32[]{:T(128)}, bf16[4,128,2048]{1,2,0:T(8,128)(2,1)S(1)}, bf16[128,2048]{1,0:T(8,128)(2,1)S(1)}, ...), branch_computations={%region_102.103_spmd, %region_103.107_spmd} | conditional | flops 1353185280 | bytes 80018144 | solution.py:188
  773.3 4.5 copy.477
  782.9 5.4 copy.476
  797.0 5.5 copy.478
  802.5 7.5 fusion.572
  816.2 16.3 %collective-permute-done.17 = bf16[128,2048]{1,0:T(8,128)(2,1)S(1)} collective-permute-done((bf16[128,2048]{1,0:T(8,128)(2,1)}, bf16[128,2048]{1,0:T(8,128)(2,1)S(1)}, u32[]{:S(2)}, u32[]{:S(2)}) %collective-permute-start.17) | collective-permute-done | bytes 524320 | tf_op jit(solution)/shard_map/ppermute | solution.py:16
  832.6 45.8 %conditional.41 = (bf16[128,2048]{1,0:T(8,128)(2,1)}, bf16[4,128,2048]{1,2,0:T(8,128)(2,1)}) conditional(s32[]{:T(128)} %convert_element_type.1183, bf16[4,128,2048]{1,2,0:T(8,128)(2,1)} %get-tuple-element.2703, (s32[]{:T(128)}, bf16[4,128,2048]{1,2,0:T(8,128)(2,1)S(1)}, bf16[128,2048]{1,0:T(8,128)(2,1)S(1)}, ...), branch_computations={%region_107.108_spmd, %region_108.112_spmd} | conditional | flops 1353185280 | bytes 80018144 | solution.py:188
  846.3 5.4 copy.480
  860.4 5.5 copy.482
  865.9 7.5 fusion.610
  879.7 15.8 %collective-permute-done.18 = bf16[128,2048]{1,0:T(8,128)(2,1)S(1)} collective-permute-done((bf16[128,2048]{1,0:T(8,128)(2,1)}, bf16[128,2048]{1,0:T(8,128)(2,1)S(1)}, u32[]{:S(2)}, u32[]{:S(2)}) %collective-permute-start.18) | collective-permute-done | bytes 524320 | tf_op jit(solution)/shard_map/ppermute | solution.py:16
  895.5 45.8 %conditional.42 = (bf16[128,2048]{1,0:T(8,128)(2,1)}, bf16[4,128,2048]{1,2,0:T(8,128)(2,1)}) conditional(s32[]{:T(128)} %convert_element_type.1182, bf16[4,128,2048]{1,2,0:T(8,128)(2,1)} %get-tuple-element.2705, (s32[]{:T(128)}, bf16[4,128,2048]{1,2,0:T(8,128)(2,1)S(1)}, bf16[128,2048]{1,0:T(8,128)(2,1)S(1)}, ...), branch_computations={%region_112.113_spmd, %region_113.117_spmd} | conditional | flops 1353185280 | bytes 80018144 | solution.py:188
  909.2 5.4 copy.484
  923.3 5.5 copy.486
  928.8 7.5 fusion.648
  945.6 11.1 collective-permute-done.19
  956.8 26.7 %conditional.43 = (bf16[512,2048]{1,0:T(8,128)(2,1)S(1)}) conditional(s32[]{:T(128)} %convert_element_type.1181, (bf16[4,128,2048]{1,2,0:T(8,128)(2,1)}) %tuple.386, (s32[]{:T(128)}, bf16[4,128,2048]{1,2,0:T(8,128)(2,1)S(1)}, bf16[128,2048]{1,0:T(8,128)(2,1)S(1)}, pred[1,128,2048]{2,1,0:T(8,128)(4,1)S(1)}, f32[4,16,128,128]{2,3,1,0:T(8,128)}, ...), branch_computations={%region_117.118_spmd, %region_118.120_spmd} | conditional | flops 276559872 | bytes 49341532 | solution.py:188
  961.0 4.6 copy.490
  968.4 5.4 copy.489
  987.3 5.6 fusion.735
  992.8 7.7 collective-permute-done.20
  1000.6 7.2 add_convert_fusion
  1007.8 122.3 %all_to_all.9 = bf16[16,64,2048]{2,1,0:T(8,128)(2,1)S(1)} all-to-all(bf16[16,64,2048]{2,1,0:T(8,128)(2,1)S(1)} %bitcast.1242), channel_id=1, replica_groups=mesh['section'=8,'dp_hi'=16,'core'=2] {'dp_hi'}, dimensions={0} | all-to-all | bytes 8388608 | tf_op jit(solution)/shard_map/all_to_all | solution.py:215
  (247 shorter events, 215.1 us)
Async XLA Ops:
  14.4 2.2 copy-start.32
  19.5 2.7 copy-start
  23.2 4.8 copy-start.1
  28.0 13.0 %collective-permute-start = (bf16[128,2048]{0,1:T(8,128)(2,1)}, bf16[128,2048]{0,1:T(8,128)(2,1)}, u32[]{:S(2)}, u32[]{:S(2)}) collective-permute-start(bf16[128,2048]{0,1:T(8,128)(2,1)} %get-tuple-element.2618), channel_id=1, source_target_pairs={{0,32},{1,33},{2,34},{3,35},{4,36},{5,37},{6,38},{7,39},{8,40},{9,... | collective-permute-start | bytes 1572872 | tf_op jit(solution)/shard_map/ppermute | solution.py:16
  53.9 0.7 copy-start.33
  59.4 15.1 %collective-permute-start.1 = (bf16[128,2048]{0,1:T(8,128)(2,1)}, bf16[128,2048]{0,1:T(8,128)(2,1)}, u32[]{:S(2)}, u32[]{:S(2)}) collective-permute-start(bf16[128,2048]{0,1:T(8,128)(2,1)} %get-tuple-element.2625), channel_id=1, source_target_pairs={{0,32},{32,64},{1,33},{33,65},{2,34},{34,66},{3,35},{35,67},{4,36}... | collective-permute-start | bytes 1572872 | tf_op jit(solution)/shard_map/ppermute | solution.py:16
  87.1 0.7 copy-start.34
  92.5 14.5 %collective-permute-start.2 = (bf16[128,2048]{0,1:T(8,128)(2,1)}, bf16[128,2048]{0,1:T(8,128)(2,1)}, u32[]{:S(2)}, u32[]{:S(2)}) collective-permute-start(bf16[128,2048]{0,1:T(8,128)(2,1)} %get-tuple-element.2632), channel_id=1, source_target_pairs={{0,32},{32,64},{64,96},{1,33},{33,65},{65,97},{2,34},{34,66},{66,9... | collective-permute-start | bytes 1572872 | tf_op jit(solution)/shard_map/ppermute | solution.py:16
  119.8 0.7 copy-start.35
  125.2 13.5 %collective-permute-start.3 = (bf16[128,2048]{0,1:T(8,128)(2,1)}, bf16[128,2048]{0,1:T(8,128)(2,1)}, u32[]{:S(2)}, u32[]{:S(2)}) collective-permute-start(bf16[128,2048]{0,1:T(8,128)(2,1)} %get-tuple-element.2639), channel_id=1, source_target_pairs={{0,32},{32,64},{64,96},{96,128},{1,33},{33,65},{65,97},{97,129},{2... | collective-permute-start | bytes 1572872 | tf_op jit(solution)/shard_map/ppermute | solution.py:16
  139.5 1.5 collective-permute-start.4
  142.2 1.5 collective-permute-start.5
  144.6 1.5 collective-permute-start.6
  148.9 1.5 collective-permute-start.7
  151.2 1.5 collective-permute-start.8
  156.2 1.5 collective-permute-start.9
  181.2 0.7 collective-permute-start.10
  187.0 0.7 collective-permute-start.11
  192.8 0.7 collective-permute-start.12
  198.8 0.7 collective-permute-start.13
  204.5 0.7 collective-permute-start.14
  210.2 0.7 collective-permute-start.15
  216.0 552.9 %collective-permute-start.16 = (bf16[128,2048]{1,0:T(8,128)(2,1)}, bf16[128,2048]{1,0:T(8,128)(2,1)S(1)}, u32[]{:S(2)}, u32[]{:S(2)}) collective-permute-start(bf16[128,2048]{1,0:T(8,128)(2,1)} %get-tuple-element.2702), channel_id=1, source_target_pairs={{32,0},{64,32},{96,64},{128,96},{33,1},{65,33},{97,65},{129,97},{3... | collective-permute-start | bytes 1572872 | tf_op jit(solution)/shard_map/ppermute | solution.py:16
  769.4 2.7 copy-start.64
  788.3 2.7 copy-start.29
  791.0 1.9 copy-start.50
  795.4 0.8 copy-start.16
  797.0 5.5 copy-start.17
  814.9 17.6 %collective-permute-start.17 = (bf16[128,2048]{1,0:T(8,128)(2,1)}, bf16[128,2048]{1,0:T(8,128)(2,1)S(1)}, u32[]{:S(2)}, u32[]{:S(2)}) collective-permute-start(bf16[128,2048]{1,0:T(8,128)(2,1)} %get-tuple-element.2704), channel_id=1, source_target_pairs={{32,0},{64,32},{96,64},{33,1},{65,33},{97,65},{34,2},{66,34},{98,6... | collective-permute-start | bytes 1572872 | tf_op jit(solution)/shard_map/ppermute | solution.py:16
  832.7 2.7 copy-start.59
  851.7 2.7 copy-start.30
  854.4 1.9 copy-start.51
  858.8 0.8 copy-start.18
  860.4 5.5 copy-start.19
  878.4 17.0 %collective-permute-start.18 = (bf16[128,2048]{1,0:T(8,128)(2,1)}, bf16[128,2048]{1,0:T(8,128)(2,1)S(1)}, u32[]{:S(2)}, u32[]{:S(2)}) collective-permute-start(bf16[128,2048]{1,0:T(8,128)(2,1)} %get-tuple-element.2706), channel_id=1, source_target_pairs={{32,0},{64,32},{33,1},{65,33},{34,2},{66,34},{35,3},{67,35},{36,4}... | collective-permute-start | bytes 1572872 | tf_op jit(solution)/shard_map/ppermute | solution.py:16
  895.7 2.7 copy-start.56
  914.6 2.7 copy-start.31
  917.3 1.9 copy-start.52
  921.7 0.8 copy-start.20
  923.3 5.5 copy-start.21
  941.3 15.5 %collective-permute-start.19 = (bf16[128,2048]{1,0:T(8,128)(2,1)}, bf16[128,2048]{1,0:T(8,128)(2,1)S(1)}, u32[]{:S(2)}, u32[]{:S(2)}) collective-permute-start(bf16[128,2048]{1,0:T(8,128)(2,1)} %get-tuple-element.2708), channel_id=1, source_target_pairs={{32,0},{33,1},{34,2},{35,3},{36,4},{37,5},{38,6},{39,7},{40,8},{41... | collective-permute-start | bytes 1572872 | tf_op jit(solution)/shard_map/ppermute | solution.py:16
  973.8 2.8 copy-start.53
  983.5 3.8 copy-start.65
  987.2 13.4 %collective-permute-start.20 = (f32[1024,2048]{1,0:T(8,128)S(1)}, f32[1024,2048]{1,0:T(8,128)}, u32[]{:S(2)}, u32[]{:S(2)}) collective-permute-start(f32[1024,2048]{1,0:T(8,128)S(1)} %fusion.736), channel_id=1, source_target_pairs={{0,1},{1,0},{2,3},{3,2},{4,5},{5,4},{6,7},{7,6},{8,9},{9,8},{10,11... | collective-permute-start | bytes 25165832 | tf_op jit(solution)/shard_map/ppermute | solution.py:213

commit v8 on v5

--- a/solution.py
+++ b/solution.py
@@ -1,6 +1,8 @@
 import jax
 import jax.numpy as jnp
 from jax import lax
+from jax.experimental import pallas as pl
+from jax.experimental.pallas import tpu as pltpu
 from jax.sharding import Mesh, PartitionSpec as P
 
 HEADS = 16
@@ -35,6 +37,94 @@
     in_service = outage.astype(jnp.float32)
     self_mask = jnp.eye(buses, dtype=jnp.float32)
     return pair_mask[None] * jnp.maximum(in_service[:, None, :], self_mask[None])
+
+
+def feature_map(values):
+    return jnp.where(values > 0.0, values + 1.0, jnp.exp(jnp.minimum(values, 0.0)))
+
+
+def attention_forward_kernel(values_ref, hidden_ref, allowed_ref, out_ref, att_ref, tot_ref):
+    allowed = allowed_ref[...]
+    size = values_ref.shape[1] // HEADS
+
+    def head(h, carry):
+        cols = pl.ds(pl.multiple_of(h * size, size), size)
+        values = values_ref[:, cols]
+        features = feature_map(values.astype(jnp.float32)).astype(jnp.bfloat16)
+        kernel = (
+            lax.dot_general(
+                features, features, (((1,), (1,)), ((), ())), preferred_element_type=jnp.float32
+            )
+            * allowed
+        )
+        totals = jnp.sum(kernel, axis=-1, keepdims=True)
+        attention = kernel / totals
+        att_ref[h] = attention
+        tot_ref[h] = totals
+        gathered = jnp.dot(
+            attention.astype(jnp.bfloat16), values, preferred_element_type=jnp.float32
+        )
+        out_ref[:, cols] = (hidden_ref[:, cols].astype(jnp.float32) + gathered).astype(
+            jnp.bfloat16
+        )
+        return carry
+
+    lax.fori_loop(0, HEADS, head, 0)
+
+
+def attention_backward_kernel(up_ref, values_ref, att_ref, tot_ref, allowed_ref, out_ref):
+    allowed = allowed_ref[...]
+    size = values_ref.shape[1] // HEADS
+
+    def head(h, carry):
+        cols = pl.ds(pl.multiple_of(h * size, size), size)
+        grads = up_ref[:, cols]
+        values = values_ref[:, cols]
+        values_f = values.astype(jnp.float32)
+        features = feature_map(values_f).astype(jnp.bfloat16)
+        attention = att_ref[h]
+        value_grad = jnp.dot(
+            attention.T.astype(jnp.bfloat16), grads, preferred_element_type=jnp.float32
+        )
+        attention_grad = lax.dot_general(
+            grads, values, (((1,), (1,)), ((), ())), preferred_element_type=jnp.float32
+        )
+        row_terms = jnp.sum(attention_grad * attention, axis=-1, keepdims=True)
+        kernel_grad = (attention_grad - row_terms) / tot_ref[h] * allowed
+        feature_grad = jnp.dot(
+            kernel_grad.astype(jnp.bfloat16), features, preferred_element_type=jnp.float32
+        ) + jnp.dot(
+            kernel_grad.T.astype(jnp.bfloat16), features, preferred_element_type=jnp.float32
+        )
+        slope = jnp.where(values_f > 0.0, 1.0, jnp.exp(jnp.minimum(values_f, 0.0)))
+        out_ref[:, cols] = (value_grad + feature_grad * slope).astype(jnp.bfloat16)
+        return carry
+
+    lax.fori_loop(0, HEADS, head, 0)
+
+
+def attention_forward(values, hidden, allowed):
+    buses, width = values.shape
+    return pl.pallas_call(
+        attention_forward_kernel,
+        out_shape=(
+            jax.ShapeDtypeStruct((buses, width), jnp.bfloat16),
+            jax.ShapeDtypeStruct((HEADS, buses, buses), jnp.float32),
+            jax.ShapeDtypeStruct((HEADS, buses, 1), jnp.float32),
+        ),
+        in_specs=[pl.BlockSpec(memory_space=pltpu.VMEM)] * 3,
+        out_specs=[pl.BlockSpec(memory_space=pltpu.VMEM)] * 3,
+    )(values, hidden, allowed)
+
+
+def attention_backward(upstream, values, attention, totals, allowed):
+    buses, width = values.shape
+    return pl.pallas_call(
+        attention_backward_kernel,
+        out_shape=jax.ShapeDtypeStruct((buses, width), jnp.bfloat16),
+        in_specs=[pl.BlockSpec(memory_space=pltpu.VMEM)] * 5,
+        out_specs=pl.BlockSpec(memory_space=pltpu.VMEM),
+    )(upstream, values, attention, totals, allowed)
 
 
 def layer_forward(hidden, weight, allowed):
@@ -45,52 +135,23 @@
     inverse_std = lax.rsqrt(jnp.mean(centred * centred, axis=-1, keepdims=True) + epsilon)
     scaled = centred * inverse_std
     normed = scaled.astype(jnp.bfloat16)
-    values_b = (
-        jnp.dot(normed.reshape(-1, width), weight, preferred_element_type=jnp.float32)
-        .astype(jnp.bfloat16)
-        .reshape(split_shape)
-    )
-    features = (jax.nn.elu(values_b.astype(jnp.float32)) + 1.0).astype(jnp.bfloat16)
-    kernel = (
-        jnp.einsum("nihc,njhc->nhij", features, features, preferred_element_type=jnp.float32)
-        * allowed[:, None]
-    )
-    totals = jnp.sum(kernel, axis=-1, keepdims=True)
-    attention = kernel / totals
-    attention_b = attention.astype(jnp.bfloat16)
-    gathered = jnp.einsum(
-        "nhij,njhc->nihc", attention_b, values_b, preferred_element_type=jnp.float32
-    )
-    output = (hidden_f + gathered.reshape(num_states, buses, width)).astype(jnp.bfloat16)
-    return (output, (scaled, inverse_std, values_b, attention, totals))
+    values_b = jnp.dot(
+        normed.reshape(-1, width), weight, preferred_element_type=jnp.float32
+    ).astype(jnp.bfloat16)
+    output, attention, totals = attention_forward(values_b, hidden[0], allowed[0])
+    return (
+        output[None],
+        (scaled, inverse_std, values_b.reshape(split_shape), attention[None], totals[None]),
+    )
 
 
 def layer_backward(upstream, weight, allowed, kept_parts):
     scaled, inverse_std, values_b, attention, totals = kept_parts
     num_states, buses, width = upstream.shape
     grad_f = upstream.astype(jnp.float32)
-    grad_heads = upstream.reshape(values_b.shape)
-    values_f = values_b.astype(jnp.float32)
-    features = (jax.nn.elu(values_f) + 1.0).astype(jnp.bfloat16)
-    attention_b = attention.astype(jnp.bfloat16)
-    value_grad = jnp.einsum(
-        "nhij,nihc->njhc", attention_b, grad_heads, preferred_element_type=jnp.float32
-    )
-    attention_grad = jnp.einsum(
-        "nihc,njhc->nhij", grad_heads, values_b, preferred_element_type=jnp.float32
-    )
-    row_terms = jnp.sum(attention_grad * attention, axis=-1, keepdims=True)
-    kernel_grad = ((attention_grad - row_terms) / totals * allowed[:, None]).astype(jnp.bfloat16)
-    feature_grad = jnp.einsum(
-        "nhij,njhc->nihc", kernel_grad, features, preferred_element_type=jnp.float32
-    )
-    feature_grad = feature_grad + jnp.einsum(
-        "nhji,njhc->nihc", kernel_grad, features, preferred_element_type=jnp.float32
-    )
-    slope = jnp.where(values_f > 0.0, 1.0, jnp.exp(jnp.minimum(values_f, 0.0)))
-    value_total = (
-        (value_grad + feature_grad * slope).astype(jnp.bfloat16).reshape(num_states, buses, width)
-    )
+    value_total = attention_backward(
+        upstream[0], values_b.reshape(buses, width), attention[0], totals[0], allowed[0]
+    )[None]
     normed_grad = lax.dot_general(
         value_total.reshape(-1, width),
         weight,

time: 908 us -> 1060 us (1.17)
  waiting for transfers between devices: 366 us -> 493 us
  blocking collectives: 214 us -> 132 us
  Pallas kernels: 0 us -> 75.5 us
  starting transfers between devices: 128 us -> 173 us
  matrix products: 71.5 us -> 59.5 us
    ppermute x22, waiting for transfers between devices: 358 us -> 485 us  [passed_along(): return lax.ppermute(block, axis, route)]
    all_to_all x1, blocking collectives: 214 us -> 132 us  [per_device(): lax.all_to_all(half.astype(jnp.bfloat16), 'dp_hi', 0, 0, tiled=True)]
    pallas_call x0 -> x8, Pallas kernels: none -> 75.5 us  [the longest x4 41.1 us: attention_backward(): pl.pallas_call(attention_backward_kernel, out_shape=jax.ShapeDtypeStruct(...]
    ppermute x22, starting transfers between devices: 128 us -> 173 us  [passed_along(): return lax.ppermute(block, axis, route)]
    dot_general x24 -> x0, matrix products: 27.6 us -> none  [the longest x4 9.26 us: layer_backward(): jnp.einsum('nhij,nihc->njhc', attention_b, grad_heads, preferred_element_...]
    unnamed x13 -> x4, local copies, waits for them, and re-layouts: 22.6 us -> 0.01 us
    squeeze x0 -> x12, local copies, waits for them, and re-layouts: none -> 14.8 us  [the longest x4 9.29 us: layer_backward(): attention[0]]
    squeeze x0 -> x12, other arithmetic: none -> 12.6 us  [the longest x4 7.56 us: layer_backward(): upstream[0]]
where the time goes in v8:
time: 1060 us
  waiting for transfers between devices  493 us (47%)
  starting transfers between devices  173 us (16%)
  blocking collectives  132 us (12%)
  Pallas kernels  75.5 us (7%)
  local copies, waits for them, and re-layouts  67.6 us (6%)
  matrix products  59.5 us (6%)
  other arithmetic  56.5 us (5%)
    ppermute x22, waiting for transfers between devices, passed_along(): return lax.ppermute(block, axis, route)  485 us
    ppermute x22, starting transfers between devices, passed_along(): return lax.ppermute(block, axis, route)  173 us
    all_to_all x1, blocking collectives, per_device(): lax.all_to_all(half.astype(jnp.bfloat16), 'dp_hi', 0, 0, tiled=True)  132 us
    pallas_call x4, Pallas kernels, attention_backward(): pl.pallas_call(attention_backward_kernel, out_shape=jax.ShapeDtypeStruct(...  41.1 us
    pallas_call x4, Pallas kernels, attention_forward(): pl.pallas_call(attention_forward_kernel, out_shape=(jax.ShapeDtypeStruct(...  34.3 us
    dot_general x4, matrix products, layer_backward(): lax.dot_general(value_total.reshape(-1, width), weight, (((1,), (1,)), ((...  26.9 us
    dot_general x4, matrix products, layer_forward(): jnp.dot(normed.reshape(-1, width), weight, preferred_element_type=jnp.flo...  22.1 us
  transfers between devices with their start and end apart: 23, of which 23 were waited for; matrix products, arithmetic and copies ran while one was open for 1% of the time, Pallas kernels for 0%

profile of v8, /device:TPU:96, one launch (start us, length us, event | category | flops | bytes accessed | tf_op | source)
XLA Modules:
  0.0 1058.0 jit_solution(15835041922413398074)
XLA Ops:
  10.3 353.4 %while.48 = (s32[]{:T(128)}, bf16[128,2048]{1,0:T(8,128)(2,1)S(1)}, f32[4,128,2048]{2,1,0:T(8,128)}, f32[4,128,1]{1,2,0:T(1,128)S(1)}, bf16[4,128,16,128]{3,2,1,...) while((s32[]{:T(128)}, bf16[128,2048]{1,0:T(8,128)(2,1)S(1)}, ...), condition=%wide.region_7.8_spmd.clone, body=%wide.region_1.7_spmd.clone.sunk | while | flops 1079017856 | bytes 27028636 | solution.py:219
  10.4 24.3 %conditional.6 = (bf16[128,2048]{1,0:T(8,128)(2,1)}, f32[4,128,2048]{2,1,0:T(8,128)}, f32[4,128,1]{1,2,0:T(1,128)S(1)}, bf16[4,128,16,128]{3,2,1,0:T(8,128)(2,1)...) conditional(s32[]{:T(128)} %convert_element_type.132, ...), branch_computations={%region_2.2_spmd, %region_3.6_spmd} | conditional | flops 1079017856 | bytes 24931048 | solution.py:213
  18.2 8.6 branch_1_fun.8
  36.0 11.7 %collective-permute-done = bf16[128,2048]{1,0:T(8,128)(2,1)S(1)} collective-permute-done((bf16[128,2048]{1,0:T(8,128)(2,1)}, bf16[128,2048]{1,0:T(8,128)(2,1)S(1)}, u32[]{:S(2)}, u32[]{:S(2)}) %collective-permute-start) | collective-permute-done | bytes 524320 | tf_op jit(solution)/shard_map/while/body/eval_jaxpr/ppermute | solution.py:18
  47.8 24.4 %conditional.6 = (bf16[128,2048]{1,0:T(8,128)(2,1)}, f32[4,128,2048]{2,1,0:T(8,128)}, f32[4,128,1]{1,2,0:T(1,128)S(1)}, bf16[4,128,16,128]{3,2,1,0:T(8,128)(2,1)...) conditional(s32[]{:T(128)} %convert_element_type.132, ...), branch_computations={%region_2.2_spmd, %region_3.6_spmd} | conditional | flops 1079017856 | bytes 24931048 | solution.py:213
  55.5 8.6 branch_1_fun.8
  76.4 10.9 %collective-permute-done = bf16[128,2048]{1,0:T(8,128)(2,1)S(1)} collective-permute-done((bf16[128,2048]{1,0:T(8,128)(2,1)}, bf16[128,2048]{1,0:T(8,128)(2,1)S(1)}, u32[]{:S(2)}, u32[]{:S(2)}) %collective-permute-start) | collective-permute-done | bytes 524320 | tf_op jit(solution)/shard_map/while/body/eval_jaxpr/ppermute | solution.py:18
  87.3 24.2 %conditional.6 = (bf16[128,2048]{1,0:T(8,128)(2,1)}, f32[4,128,2048]{2,1,0:T(8,128)}, f32[4,128,1]{1,2,0:T(1,128)S(1)}, bf16[4,128,16,128]{3,2,1,0:T(8,128)(2,1)...) conditional(s32[]{:T(128)} %convert_element_type.132, ...), branch_computations={%region_2.2_spmd, %region_3.6_spmd} | conditional | flops 1079017856 | bytes 24931048 | solution.py:213
  95.0 8.6 branch_1_fun.8
  116.0 10.0 collective-permute-done
  125.9 24.2 %conditional.6 = (bf16[128,2048]{1,0:T(8,128)(2,1)}, f32[4,128,2048]{2,1,0:T(8,128)}, f32[4,128,1]{1,2,0:T(1,128)S(1)}, bf16[4,128,16,128]{3,2,1,0:T(8,128)(2,1)...) conditional(s32[]{:T(128)} %convert_element_type.132, ...), branch_computations={%region_2.2_spmd, %region_3.6_spmd} | conditional | flops 1079017856 | bytes 24931048 | solution.py:213
  133.7 8.6 branch_1_fun.8
  154.5 9.0 collective-permute-done
  164.4 27.7 %collective-permute-start = (bf16[128,2048]{1,0:T(8,128)(2,1)}, bf16[128,2048]{1,0:T(8,128)(2,1)S(1)}, u32[]{:S(2)}, u32[]{:S(2)}) collective-permute-start(bf16[128,2048]{1,0:T(8,128)(2,1)} %get-tuple-element.1275), channel_id=1, source_target_pairs={{0,32},{32,64},{64,96},{96,128},{128,160},{160,192},{192,224},{1,3... | collective-permute-start | bytes 1572872 | tf_op jit(solution)/shard_map/while/body/eval_jaxpr/ppermute | solution.py:18
  192.0 8.1 collective-permute-done
  205.3 7.2 collective-permute-done
  213.3 26.8 %collective-permute-start = (bf16[128,2048]{1,0:T(8,128)(2,1)}, bf16[128,2048]{1,0:T(8,128)(2,1)S(1)}, u32[]{:S(2)}, u32[]{:S(2)}) collective-permute-start(bf16[128,2048]{1,0:T(8,128)(2,1)} %get-tuple-element.1275), channel_id=1, source_target_pairs={{0,32},{32,64},{64,96},{96,128},{128,160},{160,192},{192,224},{1,3... | collective-permute-start | bytes 1572872 | tf_op jit(solution)/shard_map/while/body/eval_jaxpr/ppermute | solution.py:18
  240.2 7.0 collective-permute-done
  248.0 7.5 collective-permute-start
  255.5 7.0 collective-permute-done
  263.3 33.8 %collective-permute-start = (bf16[128,2048]{1,0:T(8,128)(2,1)}, bf16[128,2048]{1,0:T(8,128)(2,1)S(1)}, u32[]{:S(2)}, u32[]{:S(2)}) collective-permute-start(bf16[128,2048]{1,0:T(8,128)(2,1)} %get-tuple-element.1275), channel_id=1, source_target_pairs={{0,32},{32,64},{64,96},{96,128},{128,160},{160,192},{192,224},{1,3... | collective-permute-start | bytes 1572872 | tf_op jit(solution)/shard_map/while/body/eval_jaxpr/ppermute | solution.py:18
  304.9 10.3 collective-permute-start
  315.3 7.0 collective-permute-done
  323.1 33.7 %collective-permute-start = (bf16[128,2048]{1,0:T(8,128)(2,1)}, bf16[128,2048]{1,0:T(8,128)(2,1)S(1)}, u32[]{:S(2)}, u32[]{:S(2)}) collective-permute-start(bf16[128,2048]{1,0:T(8,128)(2,1)} %get-tuple-element.1275), channel_id=1, source_target_pairs={{0,32},{32,64},{64,96},{96,128},{128,160},{160,192},{192,224},{1,3... | collective-permute-start | bytes 1572872 | tf_op jit(solution)/shard_map/while/body/eval_jaxpr/ppermute | solution.py:18
  356.8 7.0 collective-permute-done
  374.4 524.8 %while.49 = (s32[]{:T(128)}, bf16[128,2048]{1,0:T(8,128)(2,1)S(1)}, bf16[4,128,2048]{2,1,0:T(8,128)(2,1)}, s32[]{:T(128)}, pred[]{:T(512)}, /*index=5*/bf16[4,12...) while((s32[]{:T(128)}, bf16[128,2048]{1,0:T(8,128)(2,1)S(1)}, ...), condition=%wide.region_13.14_spmd.clone, body=%wide.region_8.13_spmd.clone.sunk | while | flops 1076920320 | bytes 24878516 | solution.py:251
  375.8 16.2 %collective-permute-done.1 = bf16[128,2048]{1,0:T(8,128)(2,1)S(1)} collective-permute-done((bf16[128,2048]{1,0:T(8,128)(2,1)S(1)}, bf16[128,2048]{1,0:T(8,128)(2,1)S(1)}, u32[]{:S(2)}, u32[]{:S(2)}) %collective-permute-start.1) | collective-permute-done | bytes 524320 | tf_op jit(solution)/shard_map/while/body/eval_jaxpr/ppermute | solution.py:18
  393.4 31.1 %collective-permute-done.1 = bf16[128,2048]{1,0:T(8,128)(2,1)S(1)} collective-permute-done((bf16[128,2048]{1,0:T(8,128)(2,1)S(1)}, bf16[128,2048]{1,0:T(8,128)(2,1)S(1)}, u32[]{:S(2)}, u32[]{:S(2)}) %collective-permute-start.1) | collective-permute-done | bytes 524320 | tf_op jit(solution)/shard_map/while/body/eval_jaxpr/ppermute | solution.py:18
  425.9 12.5 %collective-permute-done.1 = bf16[128,2048]{1,0:T(8,128)(2,1)S(1)} collective-permute-done((bf16[128,2048]{1,0:T(8,128)(2,1)S(1)}, bf16[128,2048]{1,0:T(8,128)(2,1)S(1)}, u32[]{:S(2)}, u32[]{:S(2)}) %collective-permute-start.1) | collective-permute-done | bytes 524320 | tf_op jit(solution)/shard_map/while/body/eval_jaxpr/ppermute | solution.py:18
  439.8 41.5 %collective-permute-done.1 = bf16[128,2048]{1,0:T(8,128)(2,1)S(1)} collective-permute-done((bf16[128,2048]{1,0:T(8,128)(2,1)S(1)}, bf16[128,2048]{1,0:T(8,128)(2,1)S(1)}, u32[]{:S(2)}, u32[]{:S(2)}) %collective-permute-start.1) | collective-permute-done | bytes 524320 | tf_op jit(solution)/shard_map/while/body/eval_jaxpr/ppermute | solution.py:18
  482.7 15.2 %collective-permute-done.1 = bf16[128,2048]{1,0:T(8,128)(2,1)S(1)} collective-permute-done((bf16[128,2048]{1,0:T(8,128)(2,1)S(1)}, bf16[128,2048]{1,0:T(8,128)(2,1)S(1)}, u32[]{:S(2)}, u32[]{:S(2)}) %collective-permute-start.1) | collective-permute-done | bytes 524320 | tf_op jit(solution)/shard_map/while/body/eval_jaxpr/ppermute | solution.py:18
  499.3 9.8 collective-permute-done.1
  510.4 210.2 %collective-permute-done.1 = bf16[128,2048]{1,0:T(8,128)(2,1)S(1)} collective-permute-done((bf16[128,2048]{1,0:T(8,128)(2,1)S(1)}, bf16[128,2048]{1,0:T(8,128)(2,1)S(1)}, u32[]{:S(2)}, u32[]{:S(2)}) %collective-permute-start.1) | collective-permute-done | bytes 524320 | tf_op jit(solution)/shard_map/while/body/eval_jaxpr/ppermute | solution.py:18
  720.6 29.1 %conditional.7 = (bf16[128,2048]{1,0:T(8,128)(2,1)S(1)}, bf16[4,128,2048]{2,1,0:T(8,128)(2,1)}) conditional(s32[]{:T(128)} %convert_element_type.133, bf16[4,128,2048]{2,1,0:T(8,128)(2,1)} %get-tuple-element.1397, (pred[]{:T(512)}, s32[]{:T(128)}, bf16[4,128,2048]{2,1,0:T(8,128)(2,1)}, bf16[128,2048]{1,0:T(8,128)(2,1)S(1)}, ...), branch_computations={%region_9.9_spmd, %region_10.12_spmd} | conditional | flops 1076920320 | bytes 22781008 | solution.py:247
  728.9 10.3 branch_1_fun.9
  751.0 15.8 %collective-permute-done.1 = bf16[128,2048]{1,0:T(8,128)(2,1)S(1)} collective-permute-done((bf16[128,2048]{1,0:T(8,128)(2,1)S(1)}, bf16[128,2048]{1,0:T(8,128)(2,1)S(1)}, u32[]{:S(2)}, u32[]{:S(2)}) %collective-permute-start.1) | collective-permute-done | bytes 524320 | tf_op jit(solution)/shard_map/while/body/eval_jaxpr/ppermute | solution.py:18
  766.9 29.1 %conditional.7 = (bf16[128,2048]{1,0:T(8,128)(2,1)S(1)}, bf16[4,128,2048]{2,1,0:T(8,128)(2,1)}) conditional(s32[]{:T(128)} %convert_element_type.133, bf16[4,128,2048]{2,1,0:T(8,128)(2,1)} %get-tuple-element.1397, (pred[]{:T(512)}, s32[]{:T(128)}, bf16[4,128,2048]{2,1,0:T(8,128)(2,1)}, bf16[128,2048]{1,0:T(8,128)(2,1)S(1)}, ...), branch_computations={%region_9.9_spmd, %region_10.12_spmd} | conditional | flops 1076920320 | bytes 22781008 | solution.py:247
  775.1 10.3 branch_1_fun.9
  797.3 15.6 %collective-permute-done.1 = bf16[128,2048]{1,0:T(8,128)(2,1)S(1)} collective-permute-done((bf16[128,2048]{1,0:T(8,128)(2,1)S(1)}, bf16[128,2048]{1,0:T(8,128)(2,1)S(1)}, u32[]{:S(2)}, u32[]{:S(2)}) %collective-permute-start.1) | collective-permute-done | bytes 524320 | tf_op jit(solution)/shard_map/while/body/eval_jaxpr/ppermute | solution.py:18
  812.9 29.0 %conditional.7 = (bf16[128,2048]{1,0:T(8,128)(2,1)S(1)}, bf16[4,128,2048]{2,1,0:T(8,128)(2,1)}) conditional(s32[]{:T(128)} %convert_element_type.133, bf16[4,128,2048]{2,1,0:T(8,128)(2,1)} %get-tuple-element.1397, (pred[]{:T(512)}, s32[]{:T(128)}, bf16[4,128,2048]{2,1,0:T(8,128)(2,1)}, bf16[128,2048]{1,0:T(8,128)(2,1)S(1)}, ...), branch_computations={%region_9.9_spmd, %region_10.12_spmd} | conditional | flops 1076920320 | bytes 22781008 | solution.py:247
  821.1 10.3 branch_1_fun.9
  843.2 15.8 %collective-permute-done.1 = bf16[128,2048]{1,0:T(8,128)(2,1)S(1)} collective-permute-done((bf16[128,2048]{1,0:T(8,128)(2,1)S(1)}, bf16[128,2048]{1,0:T(8,128)(2,1)S(1)}, u32[]{:S(2)}, u32[]{:S(2)}) %collective-permute-start.1) | collective-permute-done | bytes 524320 | tf_op jit(solution)/shard_map/while/body/eval_jaxpr/ppermute | solution.py:18
  859.1 29.1 %conditional.7 = (bf16[128,2048]{1,0:T(8,128)(2,1)S(1)}, bf16[4,128,2048]{2,1,0:T(8,128)(2,1)}) conditional(s32[]{:T(128)} %convert_element_type.133, bf16[4,128,2048]{2,1,0:T(8,128)(2,1)} %get-tuple-element.1397, (pred[]{:T(512)}, s32[]{:T(128)}, bf16[4,128,2048]{2,1,0:T(8,128)(2,1)}, bf16[128,2048]{1,0:T(8,128)(2,1)S(1)}, ...), branch_computations={%region_9.9_spmd, %region_10.12_spmd} | conditional | flops 1076920320 | bytes 22781008 | solution.py:247
  867.3 10.3 branch_1_fun.9
  889.4 9.8 collective-permute-done.1
  909.4 7.7 collective-permute-done.2
  917.1 7.2 add_convert_fusion
  924.4 132.1 %all_to_all.9 = bf16[16,64,2048]{2,1,0:T(8,128)(2,1)S(1)} all-to-all(bf16[16,64,2048]{2,1,0:T(8,128)(2,1)S(1)} %bitcast.90), channel_id=1, replica_groups=mesh['section'=8,'dp_hi'=16,'core'=2] {'dp_hi'}, dimensions={0} | all-to-all | bytes 8388608 | tf_op jit(solution)/shard_map/all_to_all | solution.py:270
  (230 shorter events, 222.8 us)
Async XLA Ops:
  4.6 5.8 copy-start.5
  11.7 5.8 copy-start
  17.5 16.2 %copy-start.2 = (bf16[128,2048]{1,0:T(8,128)(2,1)S(1)}, bf16[128,2048]{1,0:T(8,128)(2,1)}, u32[]{:S(2)}) copy-start(bf16[128,2048]{1,0:T(8,128)(2,1)} %convolution_convert_fusion.values_ref) | copy-start | bytes 1572868 | tf_op jit(solution)/shard_map/while/body/eval_jaxpr/cond
  17.5 14.5 %copy-start.1 = (bf16[1,128,2048]{2,1,0:T(8,128)(2,1)S(1)}, bf16[1,128,2048]{2,1,0:T(8,128)(2,1)}, u32[]{:S(2)}) copy-start(bf16[1,128,2048]{2,1,0:T(8,128)(2,1)} %copy-done) | copy-start | bytes 1572868 | tf_op jit(solution)/shard_map/while/body/eval_jaxpr/cond
  26.8 6.6 copy-start.3
  34.7 13.0 %collective-permute-start = (bf16[128,2048]{1,0:T(8,128)(2,1)}, bf16[128,2048]{1,0:T(8,128)(2,1)S(1)}, u32[]{:S(2)}, u32[]{:S(2)}) collective-permute-start(bf16[128,2048]{1,0:T(8,128)(2,1)} %get-tuple-element.1275), channel_id=1, source_target_pairs={{0,32},{32,64},{64,96},{96,128},{128,160},{160,192},{192,224},{1,3... | collective-permute-start | bytes 1572872 | tf_op jit(solution)/shard_map/while/body/eval_jaxpr/ppermute | solution.py:18
  49.0 5.8 copy-start
  54.9 16.2 %copy-start.2 = (bf16[128,2048]{1,0:T(8,128)(2,1)S(1)}, bf16[128,2048]{1,0:T(8,128)(2,1)}, u32[]{:S(2)}) copy-start(bf16[128,2048]{1,0:T(8,128)(2,1)} %convolution_convert_fusion.values_ref) | copy-start | bytes 1572868 | tf_op jit(solution)/shard_map/while/body/eval_jaxpr/cond
  54.9 14.5 %copy-start.1 = (bf16[1,128,2048]{2,1,0:T(8,128)(2,1)S(1)}, bf16[1,128,2048]{2,1,0:T(8,128)(2,1)}, u32[]{:S(2)}) copy-start(bf16[1,128,2048]{2,1,0:T(8,128)(2,1)} %copy-done) | copy-start | bytes 1572868 | tf_op jit(solution)/shard_map/while/body/eval_jaxpr/cond
  64.1 6.6 copy-start.3
  72.1 15.1 %collective-permute-start = (bf16[128,2048]{1,0:T(8,128)(2,1)}, bf16[128,2048]{1,0:T(8,128)(2,1)S(1)}, u32[]{:S(2)}, u32[]{:S(2)}) collective-permute-start(bf16[128,2048]{1,0:T(8,128)(2,1)} %get-tuple-element.1275), channel_id=1, source_target_pairs={{0,32},{32,64},{64,96},{96,128},{128,160},{160,192},{192,224},{1,3... | collective-permute-start | bytes 1572872 | tf_op jit(solution)/shard_map/while/body/eval_jaxpr/ppermute | solution.py:18
  88.5 5.8 copy-start
  94.4 16.1 %copy-start.2 = (bf16[128,2048]{1,0:T(8,128)(2,1)S(1)}, bf16[128,2048]{1,0:T(8,128)(2,1)}, u32[]{:S(2)}) copy-start(bf16[128,2048]{1,0:T(8,128)(2,1)} %convolution_convert_fusion.values_ref) | copy-start | bytes 1572868 | tf_op jit(solution)/shard_map/while/body/eval_jaxpr/cond
  94.4 14.5 %copy-start.1 = (bf16[1,128,2048]{2,1,0:T(8,128)(2,1)S(1)}, bf16[1,128,2048]{2,1,0:T(8,128)(2,1)}, u32[]{:S(2)}) copy-start(bf16[1,128,2048]{2,1,0:T(8,128)(2,1)} %copy-done) | copy-start | bytes 1572868 | tf_op jit(solution)/shard_map/while/body/eval_jaxpr/cond
  103.6 6.6 copy-start.3
  111.5 14.4 %collective-permute-start = (bf16[128,2048]{1,0:T(8,128)(2,1)}, bf16[128,2048]{1,0:T(8,128)(2,1)S(1)}, u32[]{:S(2)}, u32[]{:S(2)}) collective-permute-start(bf16[128,2048]{1,0:T(8,128)(2,1)} %get-tuple-element.1275), channel_id=1, source_target_pairs={{0,32},{32,64},{64,96},{96,128},{128,160},{160,192},{192,224},{1,3... | collective-permute-start | bytes 1572872 | tf_op jit(solution)/shard_map/while/body/eval_jaxpr/ppermute | solution.py:18
  127.2 5.8 copy-start
  133.0 16.1 %copy-start.2 = (bf16[128,2048]{1,0:T(8,128)(2,1)S(1)}, bf16[128,2048]{1,0:T(8,128)(2,1)}, u32[]{:S(2)}) copy-start(bf16[128,2048]{1,0:T(8,128)(2,1)} %convolution_convert_fusion.values_ref) | copy-start | bytes 1572868 | tf_op jit(solution)/shard_map/while/body/eval_jaxpr/cond
  133.0 14.5 %copy-start.1 = (bf16[1,128,2048]{2,1,0:T(8,128)(2,1)S(1)}, bf16[1,128,2048]{2,1,0:T(8,128)(2,1)}, u32[]{:S(2)}) copy-start(bf16[1,128,2048]{2,1,0:T(8,128)(2,1)} %copy-done) | copy-start | bytes 1572868 | tf_op jit(solution)/shard_map/while/body/eval_jaxpr/cond
  142.3 6.5 copy-start.3
  150.1 13.4 %collective-permute-start = (bf16[128,2048]{1,0:T(8,128)(2,1)}, bf16[128,2048]{1,0:T(8,128)(2,1)S(1)}, u32[]{:S(2)}, u32[]{:S(2)}) collective-permute-start(bf16[128,2048]{1,0:T(8,128)(2,1)} %get-tuple-element.1275), channel_id=1, source_target_pairs={{0,32},{32,64},{64,96},{96,128},{128,160},{160,192},{192,224},{1,3... | collective-permute-start | bytes 1572872 | tf_op jit(solution)/shard_map/while/body/eval_jaxpr/ppermute | solution.py:18
  164.4 35.8 %collective-permute-start = (bf16[128,2048]{1,0:T(8,128)(2,1)}, bf16[128,2048]{1,0:T(8,128)(2,1)S(1)}, u32[]{:S(2)}, u32[]{:S(2)}) collective-permute-start(bf16[128,2048]{1,0:T(8,128)(2,1)} %get-tuple-element.1275), channel_id=1, source_target_pairs={{0,32},{32,64},{64,96},{96,128},{128,160},{160,192},{192,224},{1,3... | collective-permute-start | bytes 1572872 | tf_op jit(solution)/shard_map/while/body/eval_jaxpr/ppermute | solution.py:18
  201.0 11.5 %collective-permute-start = (bf16[128,2048]{1,0:T(8,128)(2,1)}, bf16[128,2048]{1,0:T(8,128)(2,1)S(1)}, u32[]{:S(2)}, u32[]{:S(2)}) collective-permute-start(bf16[128,2048]{1,0:T(8,128)(2,1)} %get-tuple-element.1275), channel_id=1, source_target_pairs={{0,32},{32,64},{64,96},{96,128},{128,160},{160,192},{192,224},{1,3... | collective-permute-start | bytes 1572872 | tf_op jit(solution)/shard_map/while/body/eval_jaxpr/ppermute | solution.py:18
  213.3 33.8 %collective-permute-start = (bf16[128,2048]{1,0:T(8,128)(2,1)}, bf16[128,2048]{1,0:T(8,128)(2,1)S(1)}, u32[]{:S(2)}, u32[]{:S(2)}) collective-permute-start(bf16[128,2048]{1,0:T(8,128)(2,1)} %get-tuple-element.1275), channel_id=1, source_target_pairs={{0,32},{32,64},{64,96},{96,128},{128,160},{160,192},{192,224},{1,3... | collective-permute-start | bytes 1572872 | tf_op jit(solution)/shard_map/while/body/eval_jaxpr/ppermute | solution.py:18
  248.0 14.5 %collective-permute-start = (bf16[128,2048]{1,0:T(8,128)(2,1)}, bf16[128,2048]{1,0:T(8,128)(2,1)S(1)}, u32[]{:S(2)}, u32[]{:S(2)}) collective-permute-start(bf16[128,2048]{1,0:T(8,128)(2,1)} %get-tuple-element.1275), channel_id=1, source_target_pairs={{0,32},{32,64},{64,96},{96,128},{128,160},{160,192},{192,224},{1,3... | collective-permute-start | bytes 1572872 | tf_op jit(solution)/shard_map/while/body/eval_jaxpr/ppermute | solution.py:18
  263.3 40.8 %collective-permute-start = (bf16[128,2048]{1,0:T(8,128)(2,1)}, bf16[128,2048]{1,0:T(8,128)(2,1)S(1)}, u32[]{:S(2)}, u32[]{:S(2)}) collective-permute-start(bf16[128,2048]{1,0:T(8,128)(2,1)} %get-tuple-element.1275), channel_id=1, source_target_pairs={{0,32},{32,64},{64,96},{96,128},{128,160},{160,192},{192,224},{1,3... | collective-permute-start | bytes 1572872 | tf_op jit(solution)/shard_map/while/body/eval_jaxpr/ppermute | solution.py:18
  304.9 17.3 %collective-permute-start = (bf16[128,2048]{1,0:T(8,128)(2,1)}, bf16[128,2048]{1,0:T(8,128)(2,1)S(1)}, u32[]{:S(2)}, u32[]{:S(2)}) collective-permute-start(bf16[128,2048]{1,0:T(8,128)(2,1)} %get-tuple-element.1275), channel_id=1, source_target_pairs={{0,32},{32,64},{64,96},{96,128},{128,160},{160,192},{192,224},{1,3... | collective-permute-start | bytes 1572872 | tf_op jit(solution)/shard_map/while/body/eval_jaxpr/ppermute | solution.py:18
  323.1 40.7 %collective-permute-start = (bf16[128,2048]{1,0:T(8,128)(2,1)}, bf16[128,2048]{1,0:T(8,128)(2,1)S(1)}, u32[]{:S(2)}, u32[]{:S(2)}) collective-permute-start(bf16[128,2048]{1,0:T(8,128)(2,1)} %get-tuple-element.1275), channel_id=1, source_target_pairs={{0,32},{32,64},{64,96},{96,128},{128,160},{160,192},{192,224},{1,3... | collective-permute-start | bytes 1572872 | tf_op jit(solution)/shard_map/while/body/eval_jaxpr/ppermute | solution.py:18
  374.5 17.5 %collective-permute-start.1 = (bf16[128,2048]{1,0:T(8,128)(2,1)S(1)}, bf16[128,2048]{1,0:T(8,128)(2,1)S(1)}, u32[]{:S(2)}, u32[]{:S(2)}) collective-permute-start(bf16[128,2048]{1,0:T(8,128)(2,1)S(1)} %get-tuple-element.1297), channel_id=1, source_target_pairs={{32,0},{64,32},{96,64},{128,96},{160,128},{192,160},{224,192},{33,... | collective-permute-start | bytes 1572872 | tf_op jit(solution)/shard_map/while/body/eval_jaxpr/ppermute | solution.py:18
  392.1 32.4 %collective-permute-start.1 = (bf16[128,2048]{1,0:T(8,128)(2,1)S(1)}, bf16[128,2048]{1,0:T(8,128)(2,1)S(1)}, u32[]{:S(2)}, u32[]{:S(2)}) collective-permute-start(bf16[128,2048]{1,0:T(8,128)(2,1)S(1)} %get-tuple-element.1297), channel_id=1, source_target_pairs={{32,0},{64,32},{96,64},{128,96},{160,128},{192,160},{224,192},{33,... | collective-permute-start | bytes 1572872 | tf_op jit(solution)/shard_map/while/body/eval_jaxpr/ppermute | solution.py:18
  424.6 13.8 %collective-permute-start.1 = (bf16[128,2048]{1,0:T(8,128)(2,1)S(1)}, bf16[128,2048]{1,0:T(8,128)(2,1)S(1)}, u32[]{:S(2)}, u32[]{:S(2)}) collective-permute-start(bf16[128,2048]{1,0:T(8,128)(2,1)S(1)} %get-tuple-element.1297), channel_id=1, source_target_pairs={{32,0},{64,32},{96,64},{128,96},{160,128},{192,160},{224,192},{33,... | collective-permute-start | bytes 1572872 | tf_op jit(solution)/shard_map/while/body/eval_jaxpr/ppermute | solution.py:18
  438.5 42.8 %collective-permute-start.1 = (bf16[128,2048]{1,0:T(8,128)(2,1)S(1)}, bf16[128,2048]{1,0:T(8,128)(2,1)S(1)}, u32[]{:S(2)}, u32[]{:S(2)}) collective-permute-start(bf16[128,2048]{1,0:T(8,128)(2,1)S(1)} %get-tuple-element.1297), channel_id=1, source_target_pairs={{32,0},{64,32},{96,64},{128,96},{160,128},{192,160},{224,192},{33,... | collective-permute-start | bytes 1572872 | tf_op jit(solution)/shard_map/while/body/eval_jaxpr/ppermute | solution.py:18
  481.4 16.5 %collective-permute-start.1 = (bf16[128,2048]{1,0:T(8,128)(2,1)S(1)}, bf16[128,2048]{1,0:T(8,128)(2,1)S(1)}, u32[]{:S(2)}, u32[]{:S(2)}) collective-permute-start(bf16[128,2048]{1,0:T(8,128)(2,1)S(1)} %get-tuple-element.1297), channel_id=1, source_target_pairs={{32,0},{64,32},{96,64},{128,96},{160,128},{192,160},{224,192},{33,... | collective-permute-start | bytes 1572872 | tf_op jit(solution)/shard_map/while/body/eval_jaxpr/ppermute | solution.py:18
  497.9 11.1 %collective-permute-start.1 = (bf16[128,2048]{1,0:T(8,128)(2,1)S(1)}, bf16[128,2048]{1,0:T(8,128)(2,1)S(1)}, u32[]{:S(2)}, u32[]{:S(2)}) collective-permute-start(bf16[128,2048]{1,0:T(8,128)(2,1)S(1)} %get-tuple-element.1297), channel_id=1, source_target_pairs={{32,0},{64,32},{96,64},{128,96},{160,128},{192,160},{224,192},{33,... | collective-permute-start | bytes 1572872 | tf_op jit(solution)/shard_map/while/body/eval_jaxpr/ppermute | solution.py:18
  509.1 211.5 %collective-permute-start.1 = (bf16[128,2048]{1,0:T(8,128)(2,1)S(1)}, bf16[128,2048]{1,0:T(8,128)(2,1)S(1)}, u32[]{:S(2)}, u32[]{:S(2)}) collective-permute-start(bf16[128,2048]{1,0:T(8,128)(2,1)S(1)} %get-tuple-element.1297), channel_id=1, source_target_pairs={{32,0},{64,32},{96,64},{128,96},{160,128},{192,160},{224,192},{33,... | collective-permute-start | bytes 1572872 | tf_op jit(solution)/shard_map/while/body/eval_jaxpr/ppermute | solution.py:18
  749.7 17.1 %collective-permute-start.1 = (bf16[128,2048]{1,0:T(8,128)(2,1)S(1)}, bf16[128,2048]{1,0:T(8,128)(2,1)S(1)}, u32[]{:S(2)}, u32[]{:S(2)}) collective-permute-start(bf16[128,2048]{1,0:T(8,128)(2,1)S(1)} %get-tuple-element.1297), channel_id=1, source_target_pairs={{32,0},{64,32},{96,64},{128,96},{160,128},{192,160},{224,192},{33,... | collective-permute-start | bytes 1572872 | tf_op jit(solution)/shard_map/while/body/eval_jaxpr/ppermute | solution.py:18
  796.0 16.9 %collective-permute-start.1 = (bf16[128,2048]{1,0:T(8,128)(2,1)S(1)}, bf16[128,2048]{1,0:T(8,128)(2,1)S(1)}, u32[]{:S(2)}, u32[]{:S(2)}) collective-permute-start(bf16[128,2048]{1,0:T(8,128)(2,1)S(1)} %get-tuple-element.1297), channel_id=1, source_target_pairs={{32,0},{64,32},{96,64},{128,96},{160,128},{192,160},{224,192},{33,... | collective-permute-start | bytes 1572872 | tf_op jit(solution)/shard_map/while/body/eval_jaxpr/ppermute | solution.py:18
  841.9 17.1 %collective-permute-start.1 = (bf16[128,2048]{1,0:T(8,128)(2,1)S(1)}, bf16[128,2048]{1,0:T(8,128)(2,1)S(1)}, u32[]{:S(2)}, u32[]{:S(2)}) collective-permute-start(bf16[128,2048]{1,0:T(8,128)(2,1)S(1)} %get-tuple-element.1297), channel_id=1, source_target_pairs={{32,0},{64,32},{96,64},{128,96},{160,128},{192,160},{224,192},{33,... | collective-permute-start | bytes 1572872 | tf_op jit(solution)/shard_map/while/body/eval_jaxpr/ppermute | solution.py:18
  888.1 11.1 %collective-permute-start.1 = (bf16[128,2048]{1,0:T(8,128)(2,1)S(1)}, bf16[128,2048]{1,0:T(8,128)(2,1)S(1)}, u32[]{:S(2)}, u32[]{:S(2)}) collective-permute-start(bf16[128,2048]{1,0:T(8,128)(2,1)S(1)} %get-tuple-element.1297), channel_id=1, source_target_pairs={{32,0},{64,32},{96,64},{128,96},{160,128},{192,160},{224,192},{33,... | collective-permute-start | bytes 1572872 | tf_op jit(solution)/shard_map/while/body/eval_jaxpr/ppermute | solution.py:18
  899.2 4.7 copy-start.4
  903.6 13.6 %collective-permute-start.2 = (f32[1024,2048]{1,0:T(8,128)S(1)}, f32[1024,2048]{1,0:T(8,128)}, u32[]{:S(2)}, u32[]{:S(2)}) collective-permute-start(f32[1024,2048]{1,0:T(8,128)S(1)} %fusion.31), channel_id=1, source_target_pairs={{0,1},{1,0},{2,3},{3,2},{4,5},{5,4},{6,7},{7,6},{8,9},{9,8},{10,11... | collective-permute-start | bytes 25165832 | tf_op jit(solution)/shard_map/ppermute | solution.py:268

commit v9 on v7

--- a/solution.py
+++ b/solution.py
@@ -1,3 +1,5 @@
+import functools
+
 import jax
 import jax.numpy as jnp
 from jax import lax
@@ -11,9 +13,13 @@
 
 
 def passed_along(block, axis, distance, senders):
-    if not senders:
-        return jnp.zeros_like(block)
     return lax.ppermute(block, axis, [(i, i + distance) for i in senders])
+
+
+def phases(sections, micro):
+    middle = sections // 2
+    bounds = [0, middle - 1, middle - 1 + micro, sections + micro - 1]
+    return [(lo, hi) for lo, hi in zip(bounds[:-1], bounds[1:]) if hi > lo]
 
 
 def allowed_pairs(pattern, outage):
@@ -123,7 +129,7 @@
     )
     upstream_init = jnp.zeros((micro, buses, width), jnp.bfloat16)
 
-    def forward_step(step, carry):
+    def forward_step(senders, step, carry):
         incoming, stashed, upstream_stash = carry
         slot_raw = step - rank
         active = (slot_raw >= 0) & (slot_raw < micro)
@@ -152,17 +158,17 @@
         output, stashed, upstream_stash = lax.cond(
             active, forward_do_work, forward_no_work, stashed, upstream_stash
         )
-        senders = [r for r in range(sections - 1) if 0 <= step - r < micro]
         passed = passed_along(output, "section", 1, senders)
         return (passed, stashed, upstream_stash)
 
     carry = (zero_rows, stash_init, upstream_init)
-    for step in range(steps_total):
-        carry = forward_step(step, carry)
+    for lo, hi in phases(sections, micro):
+        senders = [r for r in range(sections - 1) if any(0 <= t - r < micro for t in range(lo, hi))]
+        carry = lax.fori_loop(lo, hi, functools.partial(forward_step, senders), carry)
     unused_rows, stashed, upstream_stash = carry
     totals_init = jnp.zeros((micro, buses, width), jnp.bfloat16)
 
-    def backward_step(step, carry):
+    def backward_step(senders, step, carry):
         incoming, collected = carry
         slot_raw = step - (sections - 1 - rank)
         active = (slot_raw >= 0) & (slot_raw < micro)
@@ -186,13 +192,17 @@
             return (zero_rows, collected_in)
 
         lower, collected = lax.cond(active, backward_do_work, backward_no_work, collected)
-        senders = [r for r in range(1, sections) if 0 <= step - (sections - 1 - r) < micro]
         passed = passed_along(lower, "section", -1, senders)
         return (passed, collected)
 
     carry = (zero_rows, totals_init)
-    for step in range(steps_total):
-        carry = backward_step(step, carry)
+    for lo, hi in phases(sections, micro):
+        senders = [
+            r
+            for r in range(1, sections)
+            if any(0 <= t - (sections - 1 - r) < micro for t in range(lo, hi))
+        ]
+        carry = lax.fori_loop(lo, hi, functools.partial(backward_step, senders), carry)
     unused_rows, collected = carry
     cores = lax.axis_size("core")
     groups = lax.axis_size("dp_hi")

time: 1140 us -> 846 us (0.74)
  waiting for transfers between devices: 641 us -> 422 us
  local copies, waits for them, and re-layouts: 153 us -> 66.8 us
  loops' own time: 35.8 us -> 2.29 us
  blocking collectives: 122 us -> 154 us
  starting transfers between devices: 36 us -> 64.6 us
    ppermute x20 -> x22, waiting for transfers between devices: 633 us -> 415 us  [passed_along(): return lax.ppermute(block, axis, [(i, i + distance) for i in senders])]
    another operation x23 -> x2, local copies, waits for them, and re-layouts: 84.8 us -> 3.22 us
    all_to_all x1, blocking collectives: 122 us -> 154 us  [per_device(): lax.all_to_all(half.astype(jnp.bfloat16), 'dp_hi', 0, 0, tiled=True)]
    another operation x11, loops' own time: 29.9 us -> 0.41 us  [backward_step(): lax.cond(active, backward_do_work, backward_no_work, collected)]
    ppermute x20 -> x22, starting transfers between devices: 35.9 us -> 64.5 us  [passed_along(): return lax.ppermute(block, axis, [(i, i + distance) for i in senders])]
    unnamed x2 -> x15, local copies, waits for them, and re-layouts: 0.01 us -> 22.5 us
  transfers between devices with their start and end apart: 21 -> 23, of which waited for: 9 -> 16; matrix products, arithmetic and copies ran while one was open for 1% -> 1% of each run, Pallas kernels for 0% -> 0%
where the time goes in v9:
time: 846 us; the launch traced here: 834 us
  waiting for transfers between devices  422 us (50%)
  blocking collectives  154 us (18%)
  matrix products  71.4 us (8%)
  local copies, waits for them, and re-layouts  66.8 us (8%)
  starting transfers between devices  64.6 us (8%)
  other arithmetic  52.7 us (6%)
    ppermute x22, waiting for transfers between devices, passed_along(): return lax.ppermute(block, axis, [(i, i + distance) for i in senders])  415 us
    all_to_all x1, blocking collectives, per_device(): lax.all_to_all(half.astype(jnp.bfloat16), 'dp_hi', 0, 0, tiled=True)  154 us
    ppermute x22, starting transfers between devices, passed_along(): return lax.ppermute(block, axis, [(i, i + distance) for i in senders])  64.5 us
    unnamed x15, local copies, waits for them, and re-layouts  22.5 us
    dot_general x4, matrix products, layer_forward(): jnp.dot(normed.reshape(-1, width), weight, preferred_element_type=jnp.flo...  18.8 us
  transfers between devices with their start and end apart: 23, of which 16 were waited for; matrix products, arithmetic and copies ran while one was open for 1% of the time, Pallas kernels for 0%

profile of v9, /device:TPU:96, one launch (start us, length us, event | category | flops | bytes accessed | tf_op | source)
XLA Modules:
  0.0 834.4 jit_solution(3683525756873182334)
XLA Ops:
  13.2 76.1 %while.144 = (s32[]{:T(128)}, bf16[128,2048]{0,1:T(8,128)(2,1)S(1)}, f32[4,128,2048]{1,2,0:T(8,128)}, f32[4,128,1]{1,2,0:T(1,128)S(1)}, bf16[4,128,16,128]{3,2,1...) while((s32[]{:T(128)}, bf16[128,2048]{0,1:T(8,128)(2,1)S(1)}, ...), condition=%wide.region_8.9_spmd.clone, body=%wide.region_1.8_spmd.clone.sunk | while | flops 1216641408 | bytes 26020904 | solution.py:167
  13.2 11.5 %conditional.18 = (bf16[128,2048]{0,1:T(8,128)(2,1)S(1)}, f32[4,128,2048]{1,2,0:T(8,128)}, f32[4,128,1]{1,2,0:T(1,128)S(1)}, bf16[4,128,16,128]{3,2,1,0:T(8,128)...) conditional(s32[]{:T(128)} %convert_element_type.710, ...), branch_computations={%region_2.2_spmd, %region_3.7_spmd} | conditional | flops 1216641408 | bytes 23923316 | solution.py:158
  13.9 4.7 convolution_convert_fusion
  26.0 11.4 %collective-permute-done = bf16[128,2048]{0,1:T(8,128)(2,1)S(1)} collective-permute-done((bf16[128,2048]{0,1:T(8,128)(2,1)S(1)}, bf16[128,2048]{0,1:T(8,128)(2,1)S(1)}, u32[]{:S(2)}, u32[]{:S(2)}) %collective-permute-start) | collective-permute-done | bytes 524320 | tf_op jit(solution)/shard_map/while/body/eval_jaxpr/ppermute | solution.py:16
  37.4 11.4 %conditional.18 = (bf16[128,2048]{0,1:T(8,128)(2,1)S(1)}, f32[4,128,2048]{1,2,0:T(8,128)}, f32[4,128,1]{1,2,0:T(1,128)S(1)}, bf16[4,128,16,128]{3,2,1,0:T(8,128)...) conditional(s32[]{:T(128)} %convert_element_type.710, ...), branch_computations={%region_2.2_spmd, %region_3.7_spmd} | conditional | flops 1216641408 | bytes 23923316 | solution.py:158
  38.0 4.7 convolution_convert_fusion
  48.8 4.5 collective-permute-start
  53.3 10.6 %collective-permute-done = bf16[128,2048]{0,1:T(8,128)(2,1)S(1)} collective-permute-done((bf16[128,2048]{0,1:T(8,128)(2,1)S(1)}, bf16[128,2048]{0,1:T(8,128)(2,1)S(1)}, u32[]{:S(2)}, u32[]{:S(2)}) %collective-permute-start) | collective-permute-done | bytes 524320 | tf_op jit(solution)/shard_map/while/body/eval_jaxpr/ppermute | solution.py:16
  63.8 11.4 %conditional.18 = (bf16[128,2048]{0,1:T(8,128)(2,1)S(1)}, f32[4,128,2048]{1,2,0:T(8,128)}, f32[4,128,1]{1,2,0:T(1,128)S(1)}, bf16[4,128,16,128]{3,2,1,0:T(8,128)...) conditional(s32[]{:T(128)} %convert_element_type.710, ...), branch_computations={%region_2.2_spmd, %region_3.7_spmd} | conditional | flops 1216641408 | bytes 23923316 | solution.py:158
  64.4 4.7 convolution_convert_fusion
  75.2 4.4 collective-permute-start
  79.6 9.6 %collective-permute-done = bf16[128,2048]{0,1:T(8,128)(2,1)S(1)} collective-permute-done((bf16[128,2048]{0,1:T(8,128)(2,1)S(1)}, bf16[128,2048]{0,1:T(8,128)(2,1)S(1)}, u32[]{:S(2)}, u32[]{:S(2)}) %collective-permute-start) | collective-permute-done | bytes 524320 | tf_op jit(solution)/shard_map/while/body/eval_jaxpr/ppermute | solution.py:16
  89.3 81.0 %while.145 = (s32[]{:T(128)}, bf16[128,2048]{0,1:T(8,128)(2,1)S(1)}, f32[4,128,2048]{1,2,0:T(8,128)}, f32[4,128,1]{1,2,0:T(1,128)S(1)}, bf16[4,128,16,128]{3,2,1...) while((s32[]{:T(128)}, bf16[128,2048]{0,1:T(8,128)(2,1)S(1)}, ...), condition=%wide.region_16.17_spmd.clone, body=%wide.region_9.16_spmd.clone.sunk | while | flops 1216641408 | bytes 26020924 | solution.py:167
  89.3 11.3 %conditional.19 = (bf16[128,2048]{0,1:T(8,128)(2,1)S(1)}, f32[4,128,2048]{1,2,0:T(8,128)}, f32[4,128,1]{1,2,0:T(1,128)S(1)}, bf16[4,128,16,128]{3,2,1,0:T(8,128)...) conditional(s32[]{:T(128)} %convert_element_type.711, ...), branch_computations={%region_10.10_spmd, %region_11.15_spmd} | conditional | flops 1216641408 | bytes 23923316 | solution.py:158
  89.9 4.7 convolution_convert_fusion.1
  100.6 4.4 collective-permute-start.1
  105.1 8.7 %collective-permute-done.1 = bf16[128,2048]{0,1:T(8,128)(2,1)S(1)} collective-permute-done((bf16[128,2048]{0,1:T(8,128)(2,1)S(1)}, bf16[128,2048]{0,1:T(8,128)(2,1)S(1)}, u32[]{:S(2)}, u32[]{:S(2)}) %collective-permute-start.1) | collective-permute-done | bytes 524320 | tf_op jit(solution)/shard_map/while/body/eval_jaxpr/ppermute | solution.py:16
  113.9 15.7 %collective-permute-start.1 = (bf16[128,2048]{0,1:T(8,128)(2,1)S(1)}, bf16[128,2048]{0,1:T(8,128)(2,1)S(1)}, u32[]{:S(2)}, u32[]{:S(2)}) collective-permute-start(bf16[128,2048]{0,1:T(8,128)(2,1)S(1)} %get-tuple-element.4039), channel_id=1, source_target_pairs={{0,32},{32,64},{64,96},{96,128},{128,160},{160,192},{192,224},{1,3... | collective-permute-start | bytes 1572872 | tf_op jit(solution)/shard_map/while/body/eval_jaxpr/ppermute | solution.py:16
  129.6 7.8 collective-permute-done.1
  137.5 4.4 collective-permute-start.1
  141.9 6.9 collective-permute-done.1
  148.9 14.7 %collective-permute-start.1 = (bf16[128,2048]{0,1:T(8,128)(2,1)S(1)}, bf16[128,2048]{0,1:T(8,128)(2,1)S(1)}, u32[]{:S(2)}, u32[]{:S(2)}) collective-permute-start(bf16[128,2048]{0,1:T(8,128)(2,1)S(1)} %get-tuple-element.4039), channel_id=1, source_target_pairs={{0,32},{32,64},{64,96},{96,128},{128,160},{160,192},{192,224},{1,3... | collective-permute-start | bytes 1572872 | tf_op jit(solution)/shard_map/while/body/eval_jaxpr/ppermute | solution.py:16
  163.6 6.6 collective-permute-done.1
  174.2 5.4 copy.148
  183.4 5.5 copy.146
  191.6 4.5 copy.147
  197.8 4.9 while.147
  202.7 304.2 %while.148 = (s32[]{:T(128)}, bf16[128,2048]{1,0:T(8,128)(2,1)S(1)}, bf16[4,128,2048]{1,2,0:T(8,128)(2,1)}, s32[]{:T(128)}, pred[]{:T(512)}, /*index=5*/bf16[4,1...) while((s32[]{:T(128)}, bf16[128,2048]{1,0:T(8,128)(2,1)S(1)}, ...), condition=%wide.region_38.39_spmd.clone, body=%wide.region_32.38_spmd.clone.sunk | while | flops 1353218048 | bytes 71172632 | solution.py:205
  204.9 13.6 %collective-permute-done.4 = bf16[128,2048]{1,0:T(8,128)(2,1)S(1)} collective-permute-done((bf16[128,2048]{1,0:T(8,128)(2,1)}, bf16[128,2048]{1,0:T(8,128)(2,1)S(1)}, u32[]{:S(2)}, u32[]{:S(2)}) %collective-permute-start.4) | collective-permute-done | bytes 524320 | tf_op jit(solution)/shard_map/while/body/eval_jaxpr/ppermute | solution.py:16
  220.6 27.7 %collective-permute-done.4 = bf16[128,2048]{1,0:T(8,128)(2,1)S(1)} collective-permute-done((bf16[128,2048]{1,0:T(8,128)(2,1)}, bf16[128,2048]{1,0:T(8,128)(2,1)S(1)}, u32[]{:S(2)}, u32[]{:S(2)}) %collective-permute-start.4) | collective-permute-done | bytes 524320 | tf_op jit(solution)/shard_map/while/body/eval_jaxpr/ppermute | solution.py:16
  250.4 16.5 %collective-permute-done.4 = bf16[128,2048]{1,0:T(8,128)(2,1)S(1)} collective-permute-done((bf16[128,2048]{1,0:T(8,128)(2,1)}, bf16[128,2048]{1,0:T(8,128)(2,1)S(1)}, u32[]{:S(2)}, u32[]{:S(2)}) %collective-permute-start.4) | collective-permute-done | bytes 524320 | tf_op jit(solution)/shard_map/while/body/eval_jaxpr/ppermute | solution.py:16
  269.1 237.9 %collective-permute-done.4 = bf16[128,2048]{1,0:T(8,128)(2,1)S(1)} collective-permute-done((bf16[128,2048]{1,0:T(8,128)(2,1)}, bf16[128,2048]{1,0:T(8,128)(2,1)S(1)}, u32[]{:S(2)}, u32[]{:S(2)}) %collective-permute-start.4) | collective-permute-done | bytes 524320 | tf_op jit(solution)/shard_map/while/body/eval_jaxpr/ppermute | solution.py:16
  507.0 129.4 %while.149 = (s32[]{:T(128)}, bf16[128,2048]{1,0:T(8,128)(2,1)S(1)}, bf16[4,128,2048]{1,2,0:T(8,128)(2,1)}, s32[]{:T(128)}, pred[]{:T(512)}, /*index=5*/bf16[4,1...) while((s32[]{:T(128)}, bf16[128,2048]{1,0:T(8,128)(2,1)S(1)}, ...), condition=%wide.region_45.46_spmd.clone, body=%wide.region_39.45_spmd.clone.sunk | while | flops 1353218048 | bytes 71172632 | solution.py:205
  507.2 16.7 %conditional.23 = (bf16[128,2048]{1,0:T(8,128)(2,1)}, bf16[4,128,2048]{1,2,0:T(8,128)(2,1)}) conditional(s32[]{:T(128)} %convert_element_type.715, bf16[4,128,2048]{1,2,0:T(8,128)(2,1)} %get-tuple-element.4493, (pred[]{:T(512)}, s32[]{:T(128)}, bf16[4,128,2048]{2,1,0:T(8,128)(2,1)}, bf16[128,2048]{1,0:T(8,128)(2,1)S(1)}, ...), branch_computations={%region_40.40_spmd, %region_41.44_spmd} | conditional | flops 1353218048 | bytes 69075104 | solution.py:194
  525.2 16.0 %collective-permute-done.5 = bf16[128,2048]{1,0:T(8,128)(2,1)S(1)} collective-permute-done((bf16[128,2048]{1,0:T(8,128)(2,1)}, bf16[128,2048]{1,0:T(8,128)(2,1)S(1)}, u32[]{:S(2)}, u32[]{:S(2)}) %collective-permute-start.5) | collective-permute-done | bytes 524320 | tf_op jit(solution)/shard_map/while/body/eval_jaxpr/ppermute | solution.py:16
  541.2 16.7 %conditional.23 = (bf16[128,2048]{1,0:T(8,128)(2,1)}, bf16[4,128,2048]{1,2,0:T(8,128)(2,1)}) conditional(s32[]{:T(128)} %convert_element_type.715, bf16[4,128,2048]{1,2,0:T(8,128)(2,1)} %get-tuple-element.4493, (pred[]{:T(512)}, s32[]{:T(128)}, bf16[4,128,2048]{2,1,0:T(8,128)(2,1)}, bf16[128,2048]{1,0:T(8,128)(2,1)S(1)}, ...), branch_computations={%region_40.40_spmd, %region_41.44_spmd} | conditional | flops 1353218048 | bytes 69075104 | solution.py:194
  559.1 15.9 %collective-permute-done.5 = bf16[128,2048]{1,0:T(8,128)(2,1)S(1)} collective-permute-done((bf16[128,2048]{1,0:T(8,128)(2,1)}, bf16[128,2048]{1,0:T(8,128)(2,1)S(1)}, u32[]{:S(2)}, u32[]{:S(2)}) %collective-permute-start.5) | collective-permute-done | bytes 524320 | tf_op jit(solution)/shard_map/while/body/eval_jaxpr/ppermute | solution.py:16
  575.1 16.7 %conditional.23 = (bf16[128,2048]{1,0:T(8,128)(2,1)}, bf16[4,128,2048]{1,2,0:T(8,128)(2,1)}) conditional(s32[]{:T(128)} %convert_element_type.715, bf16[4,128,2048]{1,2,0:T(8,128)(2,1)} %get-tuple-element.4493, (pred[]{:T(512)}, s32[]{:T(128)}, bf16[4,128,2048]{2,1,0:T(8,128)(2,1)}, bf16[128,2048]{1,0:T(8,128)(2,1)S(1)}, ...), branch_computations={%region_40.40_spmd, %region_41.44_spmd} | conditional | flops 1353218048 | bytes 69075104 | solution.py:194
  584.9 4.2 fusion.183
  593.0 15.4 %collective-permute-done.5 = bf16[128,2048]{1,0:T(8,128)(2,1)S(1)} collective-permute-done((bf16[128,2048]{1,0:T(8,128)(2,1)}, bf16[128,2048]{1,0:T(8,128)(2,1)S(1)}, u32[]{:S(2)}, u32[]{:S(2)}) %collective-permute-start.5) | collective-permute-done | bytes 524320 | tf_op jit(solution)/shard_map/while/body/eval_jaxpr/ppermute | solution.py:16
  608.4 16.7 %conditional.23 = (bf16[128,2048]{1,0:T(8,128)(2,1)}, bf16[4,128,2048]{1,2,0:T(8,128)(2,1)}) conditional(s32[]{:T(128)} %convert_element_type.715, bf16[4,128,2048]{1,2,0:T(8,128)(2,1)} %get-tuple-element.4493, (pred[]{:T(512)}, s32[]{:T(128)}, bf16[4,128,2048]{2,1,0:T(8,128)(2,1)}, bf16[128,2048]{1,0:T(8,128)(2,1)S(1)}, ...), branch_computations={%region_40.40_spmd, %region_41.44_spmd} | conditional | flops 1353218048 | bytes 69075104 | solution.py:194
  618.2 4.2 fusion.183
  626.4 10.0 %collective-permute-done.5 = bf16[128,2048]{1,0:T(8,128)(2,1)S(1)} collective-permute-done((bf16[128,2048]{1,0:T(8,128)(2,1)}, bf16[128,2048]{1,0:T(8,128)(2,1)S(1)}, u32[]{:S(2)}, u32[]{:S(2)}) %collective-permute-start.5) | collective-permute-done | bytes 524320 | tf_op jit(solution)/shard_map/while/body/eval_jaxpr/ppermute | solution.py:16
  640.5 10.7 %copy.144 = bf16[4,128,2048]{1,0,2:T(4,128)(2,1)} copy(bf16[4,128,2048]{1,2,0:T(8,128)(2,1)S(1)} %copy-done.3) | data formatting | bytes 4194304 | tf_op jit(solution)/shard_map/convert_element_type | solution.py:211
  658.2 5.6 fusion.224
  663.8 7.7 collective-permute-done.6
  671.5 7.2 add_convert_fusion
  678.7 153.7 %all_to_all.9 = bf16[16,64,2048]{2,1,0:T(8,128)(2,1)S(1)} all-to-all(bf16[16,64,2048]{2,1,0:T(8,128)(2,1)S(1)} %bitcast.379), channel_id=1, replica_groups=mesh['section'=8,'dp_hi'=16,'core'=2] {'dp_hi'}, dimensions={0} | all-to-all | bytes 8388608 | tf_op jit(solution)/shard_map/all_to_all | solution.py:225
  (246 shorter events, 152.0 us)
Async XLA Ops:
  9.8 3.3 copy-start.5
  9.8 3.3 copy-start.7
  24.7 12.7 %collective-permute-start = (bf16[128,2048]{0,1:T(8,128)(2,1)S(1)}, bf16[128,2048]{0,1:T(8,128)(2,1)S(1)}, u32[]{:S(2)}, u32[]{:S(2)}) collective-permute-start(bf16[128,2048]{0,1:T(8,128)(2,1)S(1)} %get-tuple-element.4015), channel_id=1, source_target_pairs={{0,32},{32,64},{64,96},{1,33},{33,65},{65,97},{2,34},{34,66},{66,9... | collective-permute-start | bytes 1572872 | tf_op jit(solution)/shard_map/while/body/eval_jaxpr/ppermute | solution.py:16
  48.8 15.0 %collective-permute-start = (bf16[128,2048]{0,1:T(8,128)(2,1)S(1)}, bf16[128,2048]{0,1:T(8,128)(2,1)S(1)}, u32[]{:S(2)}, u32[]{:S(2)}) collective-permute-start(bf16[128,2048]{0,1:T(8,128)(2,1)S(1)} %get-tuple-element.4015), channel_id=1, source_target_pairs={{0,32},{32,64},{64,96},{1,33},{33,65},{65,97},{2,34},{34,66},{66,9... | collective-permute-start | bytes 1572872 | tf_op jit(solution)/shard_map/while/body/eval_jaxpr/ppermute | solution.py:16
  75.2 14.1 %collective-permute-start = (bf16[128,2048]{0,1:T(8,128)(2,1)S(1)}, bf16[128,2048]{0,1:T(8,128)(2,1)S(1)}, u32[]{:S(2)}, u32[]{:S(2)}) collective-permute-start(bf16[128,2048]{0,1:T(8,128)(2,1)S(1)} %get-tuple-element.4015), channel_id=1, source_target_pairs={{0,32},{32,64},{64,96},{1,33},{33,65},{65,97},{2,34},{34,66},{66,9... | collective-permute-start | bytes 1572872 | tf_op jit(solution)/shard_map/while/body/eval_jaxpr/ppermute | solution.py:16
  100.6 13.2 %collective-permute-start.1 = (bf16[128,2048]{0,1:T(8,128)(2,1)S(1)}, bf16[128,2048]{0,1:T(8,128)(2,1)S(1)}, u32[]{:S(2)}, u32[]{:S(2)}) collective-permute-start(bf16[128,2048]{0,1:T(8,128)(2,1)S(1)} %get-tuple-element.4039), channel_id=1, source_target_pairs={{0,32},{32,64},{64,96},{96,128},{128,160},{160,192},{192,224},{1,3... | collective-permute-start | bytes 1572872 | tf_op jit(solution)/shard_map/while/body/eval_jaxpr/ppermute | solution.py:16
  113.9 23.5 %collective-permute-start.1 = (bf16[128,2048]{0,1:T(8,128)(2,1)S(1)}, bf16[128,2048]{0,1:T(8,128)(2,1)S(1)}, u32[]{:S(2)}, u32[]{:S(2)}) collective-permute-start(bf16[128,2048]{0,1:T(8,128)(2,1)S(1)} %get-tuple-element.4039), channel_id=1, source_target_pairs={{0,32},{32,64},{64,96},{96,128},{128,160},{160,192},{192,224},{1,3... | collective-permute-start | bytes 1572872 | tf_op jit(solution)/shard_map/while/body/eval_jaxpr/ppermute | solution.py:16
  137.5 11.3 %collective-permute-start.1 = (bf16[128,2048]{0,1:T(8,128)(2,1)S(1)}, bf16[128,2048]{0,1:T(8,128)(2,1)S(1)}, u32[]{:S(2)}, u32[]{:S(2)}) collective-permute-start(bf16[128,2048]{0,1:T(8,128)(2,1)S(1)} %get-tuple-element.4039), channel_id=1, source_target_pairs={{0,32},{32,64},{64,96},{96,128},{128,160},{160,192},{192,224},{1,3... | collective-permute-start | bytes 1572872 | tf_op jit(solution)/shard_map/while/body/eval_jaxpr/ppermute | solution.py:16
  148.9 21.4 %collective-permute-start.1 = (bf16[128,2048]{0,1:T(8,128)(2,1)S(1)}, bf16[128,2048]{0,1:T(8,128)(2,1)S(1)}, u32[]{:S(2)}, u32[]{:S(2)}) collective-permute-start(bf16[128,2048]{0,1:T(8,128)(2,1)S(1)} %get-tuple-element.4039), channel_id=1, source_target_pairs={{0,32},{32,64},{64,96},{96,128},{128,160},{160,192},{192,224},{1,3... | collective-permute-start | bytes 1572872 | tf_op jit(solution)/shard_map/while/body/eval_jaxpr/ppermute | solution.py:16
  170.9 0.7 collective-permute-start.2
  171.7 0.7 collective-permute-start.2
  172.6 0.7 collective-permute-start.2
  173.5 0.7 collective-permute-start.2
  183.4 5.5 copy-start.4
  198.9 0.7 collective-permute-start.3
  200.5 0.7 collective-permute-start.3
  202.0 0.7 collective-permute-start.3
  203.6 14.9 %collective-permute-start.4 = (bf16[128,2048]{1,0:T(8,128)(2,1)}, bf16[128,2048]{1,0:T(8,128)(2,1)S(1)}, u32[]{:S(2)}, u32[]{:S(2)}) collective-permute-start(bf16[128,2048]{1,0:T(8,128)(2,1)} %get-tuple-element.4102), channel_id=1, source_target_pairs={{32,0},{64,32},{96,64},{128,96},{160,128},{192,160},{224,192},{33,... | collective-permute-start | bytes 1572872 | tf_op jit(solution)/shard_map/while/body/eval_jaxpr/ppermute | solution.py:16
  219.3 29.0 %collective-permute-start.4 = (bf16[128,2048]{1,0:T(8,128)(2,1)}, bf16[128,2048]{1,0:T(8,128)(2,1)S(1)}, u32[]{:S(2)}, u32[]{:S(2)}) collective-permute-start(bf16[128,2048]{1,0:T(8,128)(2,1)} %get-tuple-element.4102), channel_id=1, source_target_pairs={{32,0},{64,32},{96,64},{128,96},{160,128},{192,160},{224,192},{33,... | collective-permute-start | bytes 1572872 | tf_op jit(solution)/shard_map/while/body/eval_jaxpr/ppermute | solution.py:16
  249.2 17.8 %collective-permute-start.4 = (bf16[128,2048]{1,0:T(8,128)(2,1)}, bf16[128,2048]{1,0:T(8,128)(2,1)S(1)}, u32[]{:S(2)}, u32[]{:S(2)}) collective-permute-start(bf16[128,2048]{1,0:T(8,128)(2,1)} %get-tuple-element.4102), channel_id=1, source_target_pairs={{32,0},{64,32},{96,64},{128,96},{160,128},{192,160},{224,192},{33,... | collective-permute-start | bytes 1572872 | tf_op jit(solution)/shard_map/while/body/eval_jaxpr/ppermute | solution.py:16
  267.8 239.2 %collective-permute-start.4 = (bf16[128,2048]{1,0:T(8,128)(2,1)}, bf16[128,2048]{1,0:T(8,128)(2,1)S(1)}, u32[]{:S(2)}, u32[]{:S(2)}) collective-permute-start(bf16[128,2048]{1,0:T(8,128)(2,1)} %get-tuple-element.4102), channel_id=1, source_target_pairs={{32,0},{64,32},{96,64},{128,96},{160,128},{192,160},{224,192},{33,... | collective-permute-start | bytes 1572872 | tf_op jit(solution)/shard_map/while/body/eval_jaxpr/ppermute | solution.py:16
  510.4 1.9 copy-start.2
  512.3 4.8 slice-start.4
  513.0 4.1 slice-start.5
  523.9 17.3 %collective-permute-start.5 = (bf16[128,2048]{1,0:T(8,128)(2,1)}, bf16[128,2048]{1,0:T(8,128)(2,1)S(1)}, u32[]{:S(2)}, u32[]{:S(2)}) collective-permute-start(bf16[128,2048]{1,0:T(8,128)(2,1)} %get-tuple-element.4119), channel_id=1, source_target_pairs={{32,0},{64,32},{96,64},{33,1},{65,33},{97,65},{34,2},{66,34},{98,6... | collective-permute-start | bytes 1572872 | tf_op jit(solution)/shard_map/while/body/eval_jaxpr/ppermute | solution.py:16
  544.3 1.9 copy-start.2
  546.2 4.8 slice-start.4
  546.9 4.1 slice-start.5
  557.8 17.2 %collective-permute-start.5 = (bf16[128,2048]{1,0:T(8,128)(2,1)}, bf16[128,2048]{1,0:T(8,128)(2,1)S(1)}, u32[]{:S(2)}, u32[]{:S(2)}) collective-permute-start(bf16[128,2048]{1,0:T(8,128)(2,1)} %get-tuple-element.4119), channel_id=1, source_target_pairs={{32,0},{64,32},{96,64},{33,1},{65,33},{97,65},{34,2},{66,34},{98,6... | collective-permute-start | bytes 1572872 | tf_op jit(solution)/shard_map/while/body/eval_jaxpr/ppermute | solution.py:16
  578.2 1.9 copy-start.2
  580.1 4.8 slice-start.4
  580.8 4.0 slice-start.5
  591.7 16.7 %collective-permute-start.5 = (bf16[128,2048]{1,0:T(8,128)(2,1)}, bf16[128,2048]{1,0:T(8,128)(2,1)S(1)}, u32[]{:S(2)}, u32[]{:S(2)}) collective-permute-start(bf16[128,2048]{1,0:T(8,128)(2,1)} %get-tuple-element.4119), channel_id=1, source_target_pairs={{32,0},{64,32},{96,64},{33,1},{65,33},{97,65},{34,2},{66,34},{98,6... | collective-permute-start | bytes 1572872 | tf_op jit(solution)/shard_map/while/body/eval_jaxpr/ppermute | solution.py:16
  611.5 1.9 copy-start.2
  613.4 4.8 slice-start.4
  614.2 4.0 slice-start.5
  625.1 11.3 %collective-permute-start.5 = (bf16[128,2048]{1,0:T(8,128)(2,1)}, bf16[128,2048]{1,0:T(8,128)(2,1)S(1)}, u32[]{:S(2)}, u32[]{:S(2)}) collective-permute-start(bf16[128,2048]{1,0:T(8,128)(2,1)} %get-tuple-element.4119), channel_id=1, source_target_pairs={{32,0},{64,32},{96,64},{33,1},{65,33},{97,65},{34,2},{66,34},{98,6... | collective-permute-start | bytes 1572872 | tf_op jit(solution)/shard_map/while/body/eval_jaxpr/ppermute | solution.py:16
  636.3 4.2 copy-start.3
  654.2 1.6 copy-start.6
  658.1 13.4 %collective-permute-start.6 = (f32[1024,2048]{1,0:T(8,128)S(1)}, f32[1024,2048]{1,0:T(8,128)}, u32[]{:S(2)}, u32[]{:S(2)}) collective-permute-start(f32[1024,2048]{1,0:T(8,128)S(1)} %fusion.225), channel_id=1, source_target_pairs={{0,1},{1,0},{2,3},{3,2},{4,5},{5,4},{6,7},{7,6},{8,9},{9,8},{10,11... | collective-permute-start | bytes 25165832 | tf_op jit(solution)/shard_map/ppermute | solution.py:223

commit v10 on v9

--- a/solution.py
+++ b/solution.py
@@ -20,6 +20,19 @@
     middle = sections // 2
     bounds = [0, middle - 1, middle - 1 + micro, sections + micro - 1]
     return [(lo, hi) for lo, hi in zip(bounds[:-1], bounds[1:]) if hi > lo]
+
+
+def scatter_sum(block, axis):
+    count = lax.axis_size(axis)
+    me = lax.axis_index(axis)
+    pieces = block.reshape(count, block.shape[0] // count, block.shape[1])
+    total = lax.dynamic_index_in_dim(pieces, me, 0, keepdims=False)
+    for shift in range(1, count):
+        sent = lax.dynamic_index_in_dim(pieces, (me + shift) % count, 0, keepdims=False)
+        route = [(i, (i + shift) % count) for i in range(count)]
+        received = lax.ppermute(sent.astype(jnp.bfloat16), axis, route)
+        total = total + received.astype(jnp.float32)
+    return total
 
 
 def allowed_pairs(pattern, outage):
@@ -205,16 +218,18 @@
         carry = lax.fori_loop(lo, hi, functools.partial(backward_step, senders), carry)
     unused_rows, collected = carry
     cores = lax.axis_size("core")
-    groups = lax.axis_size("dp_hi")
+    ys = lax.axis_size("y")
+    zs = lax.axis_size("z")
     core = lax.axis_index("core")
-    rows_each = width // (groups * cores)
-    normed_all = stashed[0].astype(jnp.bfloat16).reshape(micro * buses, groups, cores, rows_each)
+    rows_each = width // (zs * ys * cores)
+    normed_all = stashed[0].astype(jnp.bfloat16).reshape(micro * buses, zs, ys, cores, rows_each)
+    normed_all = jnp.transpose(normed_all, (0, 3, 2, 1, 4))
     totals_all = collected.reshape(micro * buses, width)
 
     def partial_grad(which):
-        chosen = lax.dynamic_index_in_dim(normed_all, which, 2, keepdims=False)
+        chosen = lax.dynamic_index_in_dim(normed_all, which, 1, keepdims=False)
         return lax.dot_general(
-            chosen.reshape(micro * buses, groups * rows_each),
+            chosen.reshape(micro * buses, width // cores),
             totals_all,
             (((0,), (0,)), ((), ())),
             preferred_element_type=jnp.float32,
@@ -222,15 +237,14 @@
 
     received = lax.ppermute(partial_grad(1 - core), "core", [(0, 1), (1, 0)])
     half = lax.optimization_barrier(partial_grad(core)) + received
-    swapped = lax.all_to_all(half.astype(jnp.bfloat16), "dp_hi", 0, 0, tiled=True)
-    summed = jnp.sum(swapped.reshape(groups, rows_each, width).astype(jnp.float32), axis=0)
+    summed = scatter_sum(scatter_sum(half, "y"), "z")
     return summed[None]
 
 
 def solution(mesh):
     sections, dp = mesh.devices.shape
-    split = Mesh(mesh.devices.reshape(sections, dp // 2, 2), ("section", "dp_hi", "core"))
-    rows = ("dp_hi", "core")
+    split = Mesh(mesh.devices.reshape(sections, 4, dp // 8, 2), ("section", "z", "y", "core"))
+    rows = ("z", "y", "core")
     in_specs = (
         P(rows, None, None),
         P(rows, None),

time: 846 us -> 817 us (0.966)
  blocking collectives: 154 us -> 0 us
  waiting for transfers between devices: 422 us -> 489 us
  starting transfers between devices: 64.6 us -> 111 us
    all_to_all x1 -> x0, blocking collectives: 154 us -> none  [per_device(): lax.all_to_all(half.astype(jnp.bfloat16), 'dp_hi', 0, 0, tiled=True)]
    ppermute x0 -> x6, waiting for transfers between devices: none -> 66.7 us  [scatter_sum(): received = lax.ppermute(sent.astype(jnp.bfloat16), axis, route)]
    ppermute x0 -> x6, starting transfers between devices: none -> 46.3 us  [scatter_sum(): received = lax.ppermute(sent.astype(jnp.bfloat16), axis, route)]
    add x0 -> x2, other arithmetic: none -> 14.8 us  [the longest x1 11.7 us: per_device(): half = lax.optimization_barrier(partial_grad(core)) + received]
  transfers between devices with their start and end apart: 23 -> 29, of which waited for: 16 -> 20; matrix products, arithmetic and copies ran while one was open for 1% -> 1% of each run, Pallas kernels for 0% -> 0%
where the time goes in v10:
time: 817 us; the launch traced here: 808 us
  waiting for transfers between devices  489 us (60%)
  starting transfers between devices  111 us (14%)
  matrix products  74.7 us (9%)
  local copies, waits for them, and re-layouts  70.5 us (9%)
  other arithmetic  60.5 us (7%)
    ppermute x22, waiting for transfers between devices, passed_along(): return lax.ppermute(block, axis, [(i, i + distance) for i in senders])  415 us
    ppermute x6, waiting for transfers between devices, scatter_sum(): received = lax.ppermute(sent.astype(jnp.bfloat16), axis, route)  66.7 us
    ppermute x22, starting transfers between devices, passed_along(): return lax.ppermute(block, axis, [(i, i + distance) for i in senders])  64.5 us
    ppermute x6, starting transfers between devices, scatter_sum(): received = lax.ppermute(sent.astype(jnp.bfloat16), axis, route)  46.3 us
    unnamed x15, local copies, waits for them, and re-layouts  22.7 us
    dot_general x4, matrix products, layer_forward(): jnp.dot(normed.reshape(-1, width), weight, preferred_element_type=jnp.flo...  18.8 us
    dot_general x4, matrix products, layer_backward(): lax.dot_general(value_total.reshape(-1, width), weight, (((1,), (1,)), ((...  16.7 us
  transfers between devices with their start and end apart: 29, of which 20 were waited for; matrix products, arithmetic and copies ran while one was open for 1% of the time, Pallas kernels for 0%

profile of v10, /device:TPU:96, one launch (start us, length us, event | category | flops | bytes accessed | tf_op | source)
XLA Modules:
  0.0 808.3 jit_solution(237225903830235084)
XLA Ops:
  13.2 76.1 %while.144 = (s32[]{:T(128)}, bf16[128,2048]{0,1:T(8,128)(2,1)S(1)}, f32[4,128,2048]{1,2,0:T(8,128)}, f32[4,128,1]{1,2,0:T(1,128)S(1)}, bf16[4,128,16,128]{3,2,1...) while((s32[]{:T(128)}, bf16[128,2048]{0,1:T(8,128)(2,1)S(1)}, ...), condition=%wide.region_8.9_spmd.clone, body=%wide.region_1.8_spmd.clone.sunk | while | flops 1216641408 | bytes 26020904 | solution.py:180
  13.2 11.5 %conditional.18 = (bf16[128,2048]{0,1:T(8,128)(2,1)S(1)}, f32[4,128,2048]{1,2,0:T(8,128)}, f32[4,128,1]{1,2,0:T(1,128)S(1)}, bf16[4,128,16,128]{3,2,1,0:T(8,128)...) conditional(s32[]{:T(128)} %convert_element_type.796, ...), branch_computations={%region_2.2_spmd, %region_3.7_spmd} | conditional | flops 1216641408 | bytes 23923316 | solution.py:171
  13.8 4.7 convolution_convert_fusion
  26.0 11.4 %collective-permute-done = bf16[128,2048]{0,1:T(8,128)(2,1)S(1)} collective-permute-done((bf16[128,2048]{0,1:T(8,128)(2,1)S(1)}, bf16[128,2048]{0,1:T(8,128)(2,1)S(1)}, u32[]{:S(2)}, u32[]{:S(2)}) %collective-permute-start) | collective-permute-done | bytes 524320 | tf_op jit(solution)/shard_map/while/body/eval_jaxpr/ppermute | solution.py:16
  37.4 11.3 %conditional.18 = (bf16[128,2048]{0,1:T(8,128)(2,1)S(1)}, f32[4,128,2048]{1,2,0:T(8,128)}, f32[4,128,1]{1,2,0:T(1,128)S(1)}, bf16[4,128,16,128]{3,2,1,0:T(8,128)...) conditional(s32[]{:T(128)} %convert_element_type.796, ...), branch_computations={%region_2.2_spmd, %region_3.7_spmd} | conditional | flops 1216641408 | bytes 23923316 | solution.py:171
  38.0 4.7 convolution_convert_fusion
  48.7 4.5 collective-permute-start
  53.2 10.6 %collective-permute-done = bf16[128,2048]{0,1:T(8,128)(2,1)S(1)} collective-permute-done((bf16[128,2048]{0,1:T(8,128)(2,1)S(1)}, bf16[128,2048]{0,1:T(8,128)(2,1)S(1)}, u32[]{:S(2)}, u32[]{:S(2)}) %collective-permute-start) | collective-permute-done | bytes 524320 | tf_op jit(solution)/shard_map/while/body/eval_jaxpr/ppermute | solution.py:16
  63.8 11.3 %conditional.18 = (bf16[128,2048]{0,1:T(8,128)(2,1)S(1)}, f32[4,128,2048]{1,2,0:T(8,128)}, f32[4,128,1]{1,2,0:T(1,128)S(1)}, bf16[4,128,16,128]{3,2,1,0:T(8,128)...) conditional(s32[]{:T(128)} %convert_element_type.796, ...), branch_computations={%region_2.2_spmd, %region_3.7_spmd} | conditional | flops 1216641408 | bytes 23923316 | solution.py:171
  64.4 4.7 convolution_convert_fusion
  79.6 9.7 %collective-permute-done = bf16[128,2048]{0,1:T(8,128)(2,1)S(1)} collective-permute-done((bf16[128,2048]{0,1:T(8,128)(2,1)S(1)}, bf16[128,2048]{0,1:T(8,128)(2,1)S(1)}, u32[]{:S(2)}, u32[]{:S(2)}) %collective-permute-start) | collective-permute-done | bytes 524320 | tf_op jit(solution)/shard_map/while/body/eval_jaxpr/ppermute | solution.py:16
  89.2 81.0 %while.145 = (s32[]{:T(128)}, bf16[128,2048]{0,1:T(8,128)(2,1)S(1)}, f32[4,128,2048]{1,2,0:T(8,128)}, f32[4,128,1]{1,2,0:T(1,128)S(1)}, bf16[4,128,16,128]{3,2,1...) while((s32[]{:T(128)}, bf16[128,2048]{0,1:T(8,128)(2,1)S(1)}, ...), condition=%wide.region_16.17_spmd.clone, body=%wide.region_9.16_spmd.clone.sunk | while | flops 1216641408 | bytes 26020924 | solution.py:180
  89.2 11.4 %conditional.19 = (bf16[128,2048]{0,1:T(8,128)(2,1)S(1)}, f32[4,128,2048]{1,2,0:T(8,128)}, f32[4,128,1]{1,2,0:T(1,128)S(1)}, bf16[4,128,16,128]{3,2,1,0:T(8,128)...) conditional(s32[]{:T(128)} %convert_element_type.797, ...), branch_computations={%region_10.10_spmd, %region_11.15_spmd} | conditional | flops 1216641408 | bytes 23923316 | solution.py:171
  89.8 4.7 convolution_convert_fusion.1
  105.0 8.7 %collective-permute-done.1 = bf16[128,2048]{0,1:T(8,128)(2,1)S(1)} collective-permute-done((bf16[128,2048]{0,1:T(8,128)(2,1)S(1)}, bf16[128,2048]{0,1:T(8,128)(2,1)S(1)}, u32[]{:S(2)}, u32[]{:S(2)}) %collective-permute-start.1) | collective-permute-done | bytes 524320 | tf_op jit(solution)/shard_map/while/body/eval_jaxpr/ppermute | solution.py:16
  113.8 15.7 %collective-permute-start.1 = (bf16[128,2048]{0,1:T(8,128)(2,1)S(1)}, bf16[128,2048]{0,1:T(8,128)(2,1)S(1)}, u32[]{:S(2)}, u32[]{:S(2)}) collective-permute-start(bf16[128,2048]{0,1:T(8,128)(2,1)S(1)} %get-tuple-element.4045), channel_id=1, source_target_pairs={{0,32},{32,64},{64,96},{96,128},{128,160},{160,192},{192,224},{1,3... | collective-permute-start | bytes 1572872 | tf_op jit(solution)/shard_map/while/body/eval_jaxpr/ppermute | solution.py:16
  129.5 7.8 collective-permute-done.1
  137.4 4.4 collective-permute-start.1
  141.9 6.9 collective-permute-done.1
  148.8 14.7 %collective-permute-start.1 = (bf16[128,2048]{0,1:T(8,128)(2,1)S(1)}, bf16[128,2048]{0,1:T(8,128)(2,1)S(1)}, u32[]{:S(2)}, u32[]{:S(2)}) collective-permute-start(bf16[128,2048]{0,1:T(8,128)(2,1)S(1)} %get-tuple-element.4045), channel_id=1, source_target_pairs={{0,32},{32,64},{64,96},{96,128},{128,160},{160,192},{192,224},{1,3... | collective-permute-start | bytes 1572872 | tf_op jit(solution)/shard_map/while/body/eval_jaxpr/ppermute | solution.py:16
  163.5 6.6 collective-permute-done.1
  173.8 5.4 copy.151
  183.0 5.5 copy.149
  191.2 4.5 copy.150
  197.4 5.0 while.147
  202.4 304.3 %while.148 = (s32[]{:T(128)}, bf16[128,2048]{1,0:T(8,128)(2,1)S(1)}, bf16[4,128,2048]{1,2,0:T(8,128)(2,1)}, s32[]{:T(128)}, pred[]{:T(512)}, /*index=5*/bf16[4,1...) while((s32[]{:T(128)}, bf16[128,2048]{1,0:T(8,128)(2,1)S(1)}, ...), condition=%wide.region_38.39_spmd.clone, body=%wide.region_32.38_spmd.clone.sunk | while | flops 1353218048 | bytes 71172632 | solution.py:218
  204.5 13.6 %collective-permute-done.4 = bf16[128,2048]{1,0:T(8,128)(2,1)S(1)} collective-permute-done((bf16[128,2048]{1,0:T(8,128)(2,1)}, bf16[128,2048]{1,0:T(8,128)(2,1)S(1)}, u32[]{:S(2)}, u32[]{:S(2)}) %collective-permute-start.4) | collective-permute-done | bytes 524320 | tf_op jit(solution)/shard_map/while/body/eval_jaxpr/ppermute | solution.py:16
  220.3 27.7 %collective-permute-done.4 = bf16[128,2048]{1,0:T(8,128)(2,1)S(1)} collective-permute-done((bf16[128,2048]{1,0:T(8,128)(2,1)}, bf16[128,2048]{1,0:T(8,128)(2,1)S(1)}, u32[]{:S(2)}, u32[]{:S(2)}) %collective-permute-start.4) | collective-permute-done | bytes 524320 | tf_op jit(solution)/shard_map/while/body/eval_jaxpr/ppermute | solution.py:16
  250.1 16.4 %collective-permute-done.4 = bf16[128,2048]{1,0:T(8,128)(2,1)S(1)} collective-permute-done((bf16[128,2048]{1,0:T(8,128)(2,1)}, bf16[128,2048]{1,0:T(8,128)(2,1)S(1)}, u32[]{:S(2)}, u32[]{:S(2)}) %collective-permute-start.4) | collective-permute-done | bytes 524320 | tf_op jit(solution)/shard_map/while/body/eval_jaxpr/ppermute | solution.py:16
  268.6 238.0 %collective-permute-done.4 = bf16[128,2048]{1,0:T(8,128)(2,1)S(1)} collective-permute-done((bf16[128,2048]{1,0:T(8,128)(2,1)}, bf16[128,2048]{1,0:T(8,128)(2,1)S(1)}, u32[]{:S(2)}, u32[]{:S(2)}) %collective-permute-start.4) | collective-permute-done | bytes 524320 | tf_op jit(solution)/shard_map/while/body/eval_jaxpr/ppermute | solution.py:16
  506.6 129.6 %while.149 = (s32[]{:T(128)}, bf16[128,2048]{1,0:T(8,128)(2,1)S(1)}, bf16[4,128,2048]{1,2,0:T(8,128)(2,1)}, s32[]{:T(128)}, pred[]{:T(512)}, /*index=5*/bf16[4,1...) while((s32[]{:T(128)}, bf16[128,2048]{1,0:T(8,128)(2,1)S(1)}, ...), condition=%wide.region_45.46_spmd.clone, body=%wide.region_39.45_spmd.clone.sunk | while | flops 1353218048 | bytes 71172632 | solution.py:218
  507.0 16.7 %conditional.23 = (bf16[128,2048]{1,0:T(8,128)(2,1)}, bf16[4,128,2048]{1,2,0:T(8,128)(2,1)}) conditional(s32[]{:T(128)} %convert_element_type.801, bf16[4,128,2048]{1,2,0:T(8,128)(2,1)} %get-tuple-element.4499, (pred[]{:T(512)}, s32[]{:T(128)}, bf16[4,128,2048]{2,1,0:T(8,128)(2,1)}, bf16[128,2048]{1,0:T(8,128)(2,1)S(1)}, ...), branch_computations={%region_40.40_spmd, %region_41.44_spmd} | conditional | flops 1353218048 | bytes 69075104 | solution.py:207
  525.0 16.0 %collective-permute-done.5 = bf16[128,2048]{1,0:T(8,128)(2,1)S(1)} collective-permute-done((bf16[128,2048]{1,0:T(8,128)(2,1)}, bf16[128,2048]{1,0:T(8,128)(2,1)S(1)}, u32[]{:S(2)}, u32[]{:S(2)}) %collective-permute-start.5) | collective-permute-done | bytes 524320 | tf_op jit(solution)/shard_map/while/body/eval_jaxpr/ppermute | solution.py:16
  541.0 16.7 %conditional.23 = (bf16[128,2048]{1,0:T(8,128)(2,1)}, bf16[4,128,2048]{1,2,0:T(8,128)(2,1)}) conditional(s32[]{:T(128)} %convert_element_type.801, bf16[4,128,2048]{1,2,0:T(8,128)(2,1)} %get-tuple-element.4499, (pred[]{:T(512)}, s32[]{:T(128)}, bf16[4,128,2048]{2,1,0:T(8,128)(2,1)}, bf16[128,2048]{1,0:T(8,128)(2,1)S(1)}, ...), branch_computations={%region_40.40_spmd, %region_41.44_spmd} | conditional | flops 1353218048 | bytes 69075104 | solution.py:207
  558.9 16.0 %collective-permute-done.5 = bf16[128,2048]{1,0:T(8,128)(2,1)S(1)} collective-permute-done((bf16[128,2048]{1,0:T(8,128)(2,1)}, bf16[128,2048]{1,0:T(8,128)(2,1)S(1)}, u32[]{:S(2)}, u32[]{:S(2)}) %collective-permute-start.5) | collective-permute-done | bytes 524320 | tf_op jit(solution)/shard_map/while/body/eval_jaxpr/ppermute | solution.py:16
  574.9 16.7 %conditional.23 = (bf16[128,2048]{1,0:T(8,128)(2,1)}, bf16[4,128,2048]{1,2,0:T(8,128)(2,1)}) conditional(s32[]{:T(128)} %convert_element_type.801, bf16[4,128,2048]{1,2,0:T(8,128)(2,1)} %get-tuple-element.4499, (pred[]{:T(512)}, s32[]{:T(128)}, bf16[4,128,2048]{2,1,0:T(8,128)(2,1)}, bf16[128,2048]{1,0:T(8,128)(2,1)S(1)}, ...), branch_computations={%region_40.40_spmd, %region_41.44_spmd} | conditional | flops 1353218048 | bytes 69075104 | solution.py:207
  592.9 15.4 %collective-permute-done.5 = bf16[128,2048]{1,0:T(8,128)(2,1)S(1)} collective-permute-done((bf16[128,2048]{1,0:T(8,128)(2,1)}, bf16[128,2048]{1,0:T(8,128)(2,1)S(1)}, u32[]{:S(2)}, u32[]{:S(2)}) %collective-permute-start.5) | collective-permute-done | bytes 524320 | tf_op jit(solution)/shard_map/while/body/eval_jaxpr/ppermute | solution.py:16
  608.3 16.7 %conditional.23 = (bf16[128,2048]{1,0:T(8,128)(2,1)}, bf16[4,128,2048]{1,2,0:T(8,128)(2,1)}) conditional(s32[]{:T(128)} %convert_element_type.801, bf16[4,128,2048]{1,2,0:T(8,128)(2,1)} %get-tuple-element.4499, (pred[]{:T(512)}, s32[]{:T(128)}, bf16[4,128,2048]{2,1,0:T(8,128)(2,1)}, bf16[128,2048]{1,0:T(8,128)(2,1)S(1)}, ...), branch_computations={%region_40.40_spmd, %region_41.44_spmd} | conditional | flops 1353218048 | bytes 69075104 | solution.py:207
  626.2 10.0 %collective-permute-done.5 = bf16[128,2048]{1,0:T(8,128)(2,1)S(1)} collective-permute-done((bf16[128,2048]{1,0:T(8,128)(2,1)}, bf16[128,2048]{1,0:T(8,128)(2,1)S(1)}, u32[]{:S(2)}, u32[]{:S(2)}) %collective-permute-start.5) | collective-permute-done | bytes 524320 | tf_op jit(solution)/shard_map/while/body/eval_jaxpr/ppermute | solution.py:16
  640.3 10.7 %copy.146 = bf16[4,128,2048]{1,0,2:T(4,128)(2,1)} copy(bf16[4,128,2048]{1,2,0:T(8,128)(2,1)S(1)} %copy-done.3) | data formatting | bytes 4194304 | tf_op jit(solution)/shard_map/convert_element_type | solution.py:225
  655.8 5.6 fusion.236
  661.5 5.6 fusion.235
  667.0 7.8 collective-permute-done.6
  674.9 11.7 %add.513 = f32[1024,2048]{1,0:T(8,128)} add(f32[1024,2048]{1,0:T(8,128)} %fusion.235, f32[1024,2048]{1,0:T(8,128)} %collective-permute-done.6) | non-fusion elementwise | flops 2097152 | bytes 25165824 | tf_op jit(solution)/shard_map/add | solution.py:239
  695.8 20.8 %collective-permute-done.7 = bf16[256,2048]{1,0:T(8,128)(2,1)} collective-permute-done((bf16[256,2048]{1,0:T(8,128)(2,1)S(1)}, bf16[256,2048]{1,0:T(8,128)(2,1)}, u32[]{:S(2)}, u32[]{:S(2)}) %collective-permute-start.7) | collective-permute-done | bytes 1048608 | tf_op jit(solution)/shard_map/ppermute | solution.py:33
  716.5 23.6 %collective-permute-done.8 = bf16[256,2048]{1,0:T(8,128)(2,1)} collective-permute-done((bf16[256,2048]{1,0:T(8,128)(2,1)S(1)}, bf16[256,2048]{1,0:T(8,128)(2,1)}, u32[]{:S(2)}, u32[]{:S(2)}) %collective-permute-start.8) | collective-permute-done | bytes 1048608 | tf_op jit(solution)/shard_map/ppermute | solution.py:33
  743.5 40.4 %collective-permute-start.11 = (bf16[64,2048]{1,0:T(8,128)(2,1)S(1)}, bf16[64,2048]{1,0:T(8,128)(2,1)S(1)}, u32[]{:S(2)}, u32[]{:S(2)}) collective-permute-start(bf16[64,2048]{1,0:T(8,128)(2,1)S(1)} %get-tuple-element.3484), channel_id=1, source_target_pairs={{0,16},{8,24},{16,0},{24,8},{1,17},{9,25},{17,1},{25,9},{2,18},{10... | collective-permute-start | bytes 786440 | tf_op jit(solution)/shard_map/ppermute | solution.py:33
  788.2 18.0 %collective-permute-done.11 = bf16[64,2048]{1,0:T(8,128)(2,1)S(1)} collective-permute-done((bf16[64,2048]{1,0:T(8,128)(2,1)S(1)}, bf16[64,2048]{1,0:T(8,128)(2,1)S(1)}, u32[]{:S(2)}, u32[]{:S(2)}) %collective-permute-start.11) | collective-permute-done | bytes 262176 | tf_op jit(solution)/shard_map/ppermute | solution.py:33
  (262 shorter events, 183.6 us)
Async XLA Ops:
  9.8 3.3 copy-start.5
  9.8 3.3 copy-start.7
  24.6 12.7 %collective-permute-start = (bf16[128,2048]{0,1:T(8,128)(2,1)S(1)}, bf16[128,2048]{0,1:T(8,128)(2,1)S(1)}, u32[]{:S(2)}, u32[]{:S(2)}) collective-permute-start(bf16[128,2048]{0,1:T(8,128)(2,1)S(1)} %get-tuple-element.4021), channel_id=1, source_target_pairs={{0,32},{32,64},{64,96},{1,33},{33,65},{65,97},{2,34},{34,66},{66,9... | collective-permute-start | bytes 1572872 | tf_op jit(solution)/shard_map/while/body/eval_jaxpr/ppermute | solution.py:16
  48.7 15.1 %collective-permute-start = (bf16[128,2048]{0,1:T(8,128)(2,1)S(1)}, bf16[128,2048]{0,1:T(8,128)(2,1)S(1)}, u32[]{:S(2)}, u32[]{:S(2)}) collective-permute-start(bf16[128,2048]{0,1:T(8,128)(2,1)S(1)} %get-tuple-element.4021), channel_id=1, source_target_pairs={{0,32},{32,64},{64,96},{1,33},{33,65},{65,97},{2,34},{34,66},{66,9... | collective-permute-start | bytes 1572872 | tf_op jit(solution)/shard_map/while/body/eval_jaxpr/ppermute | solution.py:16
  75.2 14.1 %collective-permute-start = (bf16[128,2048]{0,1:T(8,128)(2,1)S(1)}, bf16[128,2048]{0,1:T(8,128)(2,1)S(1)}, u32[]{:S(2)}, u32[]{:S(2)}) collective-permute-start(bf16[128,2048]{0,1:T(8,128)(2,1)S(1)} %get-tuple-element.4021), channel_id=1, source_target_pairs={{0,32},{32,64},{64,96},{1,33},{33,65},{65,97},{2,34},{34,66},{66,9... | collective-permute-start | bytes 1572872 | tf_op jit(solution)/shard_map/while/body/eval_jaxpr/ppermute | solution.py:16
  100.6 13.1 %collective-permute-start.1 = (bf16[128,2048]{0,1:T(8,128)(2,1)S(1)}, bf16[128,2048]{0,1:T(8,128)(2,1)S(1)}, u32[]{:S(2)}, u32[]{:S(2)}) collective-permute-start(bf16[128,2048]{0,1:T(8,128)(2,1)S(1)} %get-tuple-element.4045), channel_id=1, source_target_pairs={{0,32},{32,64},{64,96},{96,128},{128,160},{160,192},{192,224},{1,3... | collective-permute-start | bytes 1572872 | tf_op jit(solution)/shard_map/while/body/eval_jaxpr/ppermute | solution.py:16
  113.8 23.5 %collective-permute-start.1 = (bf16[128,2048]{0,1:T(8,128)(2,1)S(1)}, bf16[128,2048]{0,1:T(8,128)(2,1)S(1)}, u32[]{:S(2)}, u32[]{:S(2)}) collective-permute-start(bf16[128,2048]{0,1:T(8,128)(2,1)S(1)} %get-tuple-element.4045), channel_id=1, source_target_pairs={{0,32},{32,64},{64,96},{96,128},{128,160},{160,192},{192,224},{1,3... | collective-permute-start | bytes 1572872 | tf_op jit(solution)/shard_map/while/body/eval_jaxpr/ppermute | solution.py:16
  137.4 11.3 %collective-permute-start.1 = (bf16[128,2048]{0,1:T(8,128)(2,1)S(1)}, bf16[128,2048]{0,1:T(8,128)(2,1)S(1)}, u32[]{:S(2)}, u32[]{:S(2)}) collective-permute-start(bf16[128,2048]{0,1:T(8,128)(2,1)S(1)} %get-tuple-element.4045), channel_id=1, source_target_pairs={{0,32},{32,64},{64,96},{96,128},{128,160},{160,192},{192,224},{1,3... | collective-permute-start | bytes 1572872 | tf_op jit(solution)/shard_map/while/body/eval_jaxpr/ppermute | solution.py:16
  148.8 21.4 %collective-permute-start.1 = (bf16[128,2048]{0,1:T(8,128)(2,1)S(1)}, bf16[128,2048]{0,1:T(8,128)(2,1)S(1)}, u32[]{:S(2)}, u32[]{:S(2)}) collective-permute-start(bf16[128,2048]{0,1:T(8,128)(2,1)S(1)} %get-tuple-element.4045), channel_id=1, source_target_pairs={{0,32},{32,64},{64,96},{96,128},{128,160},{160,192},{192,224},{1,3... | collective-permute-start | bytes 1572872 | tf_op jit(solution)/shard_map/while/body/eval_jaxpr/ppermute | solution.py:16
  170.5 0.7 collective-permute-start.2
  171.3 0.7 collective-permute-start.2
  172.2 0.7 collective-permute-start.2
  173.0 0.7 collective-permute-start.2
  183.0 5.5 copy-start.4
  198.5 0.7 collective-permute-start.3
  200.1 0.7 collective-permute-start.3
  201.7 0.7 collective-permute-start.3
  203.2 14.9 %collective-permute-start.4 = (bf16[128,2048]{1,0:T(8,128)(2,1)}, bf16[128,2048]{1,0:T(8,128)(2,1)S(1)}, u32[]{:S(2)}, u32[]{:S(2)}) collective-permute-start(bf16[128,2048]{1,0:T(8,128)(2,1)} %get-tuple-element.4108), channel_id=1, source_target_pairs={{32,0},{64,32},{96,64},{128,96},{160,128},{192,160},{224,192},{33,... | collective-permute-start | bytes 1572872 | tf_op jit(solution)/shard_map/while/body/eval_jaxpr/ppermute | solution.py:16
  219.0 29.0 %collective-permute-start.4 = (bf16[128,2048]{1,0:T(8,128)(2,1)}, bf16[128,2048]{1,0:T(8,128)(2,1)S(1)}, u32[]{:S(2)}, u32[]{:S(2)}) collective-permute-start(bf16[128,2048]{1,0:T(8,128)(2,1)} %get-tuple-element.4108), channel_id=1, source_target_pairs={{32,0},{64,32},{96,64},{128,96},{160,128},{192,160},{224,192},{33,... | collective-permute-start | bytes 1572872 | tf_op jit(solution)/shard_map/while/body/eval_jaxpr/ppermute | solution.py:16
  248.8 17.7 %collective-permute-start.4 = (bf16[128,2048]{1,0:T(8,128)(2,1)}, bf16[128,2048]{1,0:T(8,128)(2,1)S(1)}, u32[]{:S(2)}, u32[]{:S(2)}) collective-permute-start(bf16[128,2048]{1,0:T(8,128)(2,1)} %get-tuple-element.4108), channel_id=1, source_target_pairs={{32,0},{64,32},{96,64},{128,96},{160,128},{192,160},{224,192},{33,... | collective-permute-start | bytes 1572872 | tf_op jit(solution)/shard_map/while/body/eval_jaxpr/ppermute | solution.py:16
  267.4 239.3 %collective-permute-start.4 = (bf16[128,2048]{1,0:T(8,128)(2,1)}, bf16[128,2048]{1,0:T(8,128)(2,1)S(1)}, u32[]{:S(2)}, u32[]{:S(2)}) collective-permute-start(bf16[128,2048]{1,0:T(8,128)(2,1)} %get-tuple-element.4108), channel_id=1, source_target_pairs={{32,0},{64,32},{96,64},{128,96},{160,128},{192,160},{224,192},{33,... | collective-permute-start | bytes 1572872 | tf_op jit(solution)/shard_map/while/body/eval_jaxpr/ppermute | solution.py:16
  510.2 1.9 copy-start.2
  512.1 4.8 slice-start.4
  512.8 4.1 slice-start.5
  523.7 17.3 %collective-permute-start.5 = (bf16[128,2048]{1,0:T(8,128)(2,1)}, bf16[128,2048]{1,0:T(8,128)(2,1)S(1)}, u32[]{:S(2)}, u32[]{:S(2)}) collective-permute-start(bf16[128,2048]{1,0:T(8,128)(2,1)} %get-tuple-element.4125), channel_id=1, source_target_pairs={{32,0},{64,32},{96,64},{33,1},{65,33},{97,65},{34,2},{66,34},{98,6... | collective-permute-start | bytes 1572872 | tf_op jit(solution)/shard_map/while/body/eval_jaxpr/ppermute | solution.py:16
  544.1 1.9 copy-start.2
  546.0 4.8 slice-start.4
  546.7 4.1 slice-start.5
  557.6 17.3 %collective-permute-start.5 = (bf16[128,2048]{1,0:T(8,128)(2,1)}, bf16[128,2048]{1,0:T(8,128)(2,1)S(1)}, u32[]{:S(2)}, u32[]{:S(2)}) collective-permute-start(bf16[128,2048]{1,0:T(8,128)(2,1)} %get-tuple-element.4125), channel_id=1, source_target_pairs={{32,0},{64,32},{96,64},{33,1},{65,33},{97,65},{34,2},{66,34},{98,6... | collective-permute-start | bytes 1572872 | tf_op jit(solution)/shard_map/while/body/eval_jaxpr/ppermute | solution.py:16
  578.0 1.9 copy-start.2
  579.9 4.8 slice-start.4
  580.7 4.0 slice-start.5
  591.6 16.7 %collective-permute-start.5 = (bf16[128,2048]{1,0:T(8,128)(2,1)}, bf16[128,2048]{1,0:T(8,128)(2,1)S(1)}, u32[]{:S(2)}, u32[]{:S(2)}) collective-permute-start(bf16[128,2048]{1,0:T(8,128)(2,1)} %get-tuple-element.4125), channel_id=1, source_target_pairs={{32,0},{64,32},{96,64},{33,1},{65,33},{97,65},{34,2},{66,34},{98,6... | collective-permute-start | bytes 1572872 | tf_op jit(solution)/shard_map/while/body/eval_jaxpr/ppermute | solution.py:16
  611.4 1.9 copy-start.2
  613.3 4.8 slice-start.4
  614.0 4.1 slice-start.5
  624.9 11.3 %collective-permute-start.5 = (bf16[128,2048]{1,0:T(8,128)(2,1)}, bf16[128,2048]{1,0:T(8,128)(2,1)S(1)}, u32[]{:S(2)}, u32[]{:S(2)}) collective-permute-start(bf16[128,2048]{1,0:T(8,128)(2,1)} %get-tuple-element.4125), channel_id=1, source_target_pairs={{32,0},{64,32},{96,64},{33,1},{65,33},{97,65},{34,2},{66,34},{98,6... | collective-permute-start | bytes 1572872 | tf_op jit(solution)/shard_map/while/body/eval_jaxpr/ppermute | solution.py:16
  636.2 4.1 copy-start.3
  654.2 1.6 copy-start.6
  661.4 13.5 %collective-permute-start.6 = (f32[1024,2048]{1,0:T(8,128)}, f32[1024,2048]{1,0:T(8,128)}, u32[]{:S(2)}, u32[]{:S(2)}) collective-permute-start(f32[1024,2048]{1,0:T(8,128)} %fusion.236), channel_id=1, source_target_pairs={{0,1},{1,0},{2,3},{3,2},{4,5},{5,4},{6,7},{7,6},{8,9},{9,8},{10,11... | collective-permute-start | bytes 25165832 | tf_op jit(solution)/shard_map/ppermute | solution.py:238
  689.9 26.7 %collective-permute-start.7 = (bf16[256,2048]{1,0:T(8,128)(2,1)S(1)}, bf16[256,2048]{1,0:T(8,128)(2,1)}, u32[]{:S(2)}, u32[]{:S(2)}) collective-permute-start(bf16[256,2048]{1,0:T(8,128)(2,1)S(1)} %get-tuple-element.3479), channel_id=1, source_target_pairs={{0,2},{2,4},{4,6},{6,0},{1,3},{3,5},{5,7},{7,1},{8,10},{10,12},{12... | collective-permute-start | bytes 3145736 | tf_op jit(solution)/shard_map/ppermute | solution.py:33
  691.6 48.6 %collective-permute-start.8 = (bf16[256,2048]{1,0:T(8,128)(2,1)S(1)}, bf16[256,2048]{1,0:T(8,128)(2,1)}, u32[]{:S(2)}, u32[]{:S(2)}) collective-permute-start(bf16[256,2048]{1,0:T(8,128)(2,1)S(1)} %get-tuple-element.3481), channel_id=1, source_target_pairs={{0,4},{2,6},{4,0},{6,2},{1,5},{3,7},{5,1},{7,3},{8,12},{10,14},{12... | collective-permute-start | bytes 3145736 | tf_op jit(solution)/shard_map/ppermute | solution.py:33
  694.4 45.8 %collective-permute-start.9 = (bf16[256,2048]{1,0:T(8,128)(2,1)S(1)}, bf16[256,2048]{1,0:T(8,128)(2,1)}, u32[]{:S(2)}, u32[]{:S(2)}) collective-permute-start(bf16[256,2048]{1,0:T(8,128)(2,1)S(1)} %get-tuple-element.3480), channel_id=1, source_target_pairs={{0,6},{2,0},{4,2},{6,4},{1,7},{3,1},{5,3},{7,5},{8,14},{10,8},{12,... | collective-permute-start | bytes 3145736 | tf_op jit(solution)/shard_map/ppermute | solution.py:33
  743.5 44.8 %collective-permute-start.10 = (bf16[64,2048]{1,0:T(8,128)(2,1)S(1)}, bf16[64,2048]{1,0:T(8,128)(2,1)S(1)}, u32[]{:S(2)}, u32[]{:S(2)}) collective-permute-start(bf16[64,2048]{1,0:T(8,128)(2,1)S(1)} %get-tuple-element.3482), channel_id=1, source_target_pairs={{0,8},{8,16},{16,24},{24,0},{1,9},{9,17},{17,25},{25,1},{2,10},{10... | collective-permute-start | bytes 786440 | tf_op jit(solution)/shard_map/ppermute | solution.py:33
  743.5 62.7 %collective-permute-start.11 = (bf16[64,2048]{1,0:T(8,128)(2,1)S(1)}, bf16[64,2048]{1,0:T(8,128)(2,1)S(1)}, u32[]{:S(2)}, u32[]{:S(2)}) collective-permute-start(bf16[64,2048]{1,0:T(8,128)(2,1)S(1)} %get-tuple-element.3484), channel_id=1, source_target_pairs={{0,16},{8,24},{16,0},{24,8},{1,17},{9,25},{17,1},{25,9},{2,18},{10... | collective-permute-start | bytes 786440 | tf_op jit(solution)/shard_map/ppermute | solution.py:33
  783.9 22.3 %collective-permute-start.12 = (bf16[64,2048]{1,0:T(8,128)(2,1)S(1)}, bf16[64,2048]{1,0:T(8,128)(2,1)}, u32[]{:S(2)}, u32[]{:S(2)}) collective-permute-start(bf16[64,2048]{1,0:T(8,128)(2,1)S(1)} %get-tuple-element.3483), channel_id=1, source_target_pairs={{0,24},{8,0},{16,8},{24,16},{1,25},{9,1},{17,9},{25,17},{2,26},{10... | collective-permute-start | bytes 786440 | tf_op jit(solution)/shard_map/ppermute | solution.py:33

commit v11 on v10

--- a/solution.py
+++ b/solution.py
@@ -208,7 +208,23 @@
         passed = passed_along(lower, "section", -1, senders)
         return (passed, collected)
 
-    carry = (zero_rows, totals_init)
+    cores = lax.axis_size("core")
+    ys = lax.axis_size("y")
+    zs = lax.axis_size("z")
+    core = lax.axis_index("core")
+    swap = [(0, 1), (1, 0)]
+    rows_each = width // (zs * ys * cores)
+    normed_all = stashed[0].astype(jnp.bfloat16).reshape(micro * buses, zs, ys, cores, rows_each)
+    normed_all = jnp.transpose(normed_all, (3, 2, 1, 4, 0)).reshape(
+        cores, width // cores, micro * buses
+    )
+    mine = lax.dynamic_index_in_dim(normed_all, core, 0, keepdims=False)
+    theirs = lax.ppermute(
+        lax.dynamic_index_in_dim(normed_all, 1 - core, 0, keepdims=False), "core", swap
+    )
+    left, carry = lax.optimization_barrier(
+        (jnp.concatenate([mine, theirs], axis=1), (zero_rows, totals_init))
+    )
     for lo, hi in phases(sections, micro):
         senders = [
             r
@@ -217,26 +233,9 @@
         ]
         carry = lax.fori_loop(lo, hi, functools.partial(backward_step, senders), carry)
     unused_rows, collected = carry
-    cores = lax.axis_size("core")
-    ys = lax.axis_size("y")
-    zs = lax.axis_size("z")
-    core = lax.axis_index("core")
-    rows_each = width // (zs * ys * cores)
-    normed_all = stashed[0].astype(jnp.bfloat16).reshape(micro * buses, zs, ys, cores, rows_each)
-    normed_all = jnp.transpose(normed_all, (0, 3, 2, 1, 4))
-    totals_all = collected.reshape(micro * buses, width)
-
-    def partial_grad(which):
-        chosen = lax.dynamic_index_in_dim(normed_all, which, 1, keepdims=False)
-        return lax.dot_general(
-            chosen.reshape(micro * buses, width // cores),
-            totals_all,
-            (((0,), (0,)), ((), ())),
-            preferred_element_type=jnp.float32,
-        )
-
-    received = lax.ppermute(partial_grad(1 - core), "core", [(0, 1), (1, 0)])
-    half = lax.optimization_barrier(partial_grad(core)) + received
+    own = collected.reshape(micro * buses, width)
+    right = jnp.concatenate([own, lax.ppermute(own, "core", swap)], axis=0)
+    half = jnp.dot(left, right, preferred_element_type=jnp.float32)
     summed = scatter_sum(scatter_sum(half, "y"), "z")
     return summed[None]
 

time: 817 us -> 818 us (level)
  waiting for transfers between devices: 489 us -> 511 us
  other arithmetic: 60.5 us -> 50.3 us
    ppermute x22, waiting for transfers between devices: 415 us -> 439 us  [passed_along(): return lax.ppermute(block, axis, [(i, i + distance) for i in senders])]
    add x1 -> x0, other arithmetic: 11.7 us -> none  [per_device(): half = lax.optimization_barrier(partial_grad(core)) + received]
  transfers between devices with their start and end apart: 29 -> 30, of which waited for: 20 -> 20; matrix products, arithmetic and copies ran while one was open for 1% -> 2% of each run, Pallas kernels for 0% -> 0%
where the time goes in v11:
time: 818 us; the launch traced here: 809 us
  waiting for transfers between devices  511 us (62%)
  starting transfers between devices  105 us (13%)
  local copies, waits for them, and re-layouts  70.5 us (9%)
  matrix products  69.7 us (9%)
  other arithmetic  50.3 us (6%)
    ppermute x22, waiting for transfers between devices, passed_along(): return lax.ppermute(block, axis, [(i, i + distance) for i in senders])  439 us
    ppermute x6, waiting for transfers between devices, scatter_sum(): received = lax.ppermute(sent.astype(jnp.bfloat16), axis, route)  67.5 us
    ppermute x22, starting transfers between devices, passed_along(): return lax.ppermute(block, axis, [(i, i + distance) for i in senders])  64.5 us
    ppermute x6, starting transfers between devices, scatter_sum(): received = lax.ppermute(sent.astype(jnp.bfloat16), axis, route)  40.6 us
    unnamed x15, local copies, waits for them, and re-layouts  24.6 us
    dot_general x4, matrix products, layer_forward(): jnp.dot(normed.reshape(-1, width), weight, preferred_element_type=jnp.flo...  18.8 us
    dot_general x4, matrix products, layer_backward(): lax.dot_general(value_total.reshape(-1, width), weight, (((1,), (1,)), ((...  16.7 us
  transfers between devices with their start and end apart: 30, of which 20 were waited for; matrix products, arithmetic and copies ran while one was open for 2% of the time, Pallas kernels for 0%

profile of v11, /device:TPU:96, one launch (start us, length us, event | category | flops | bytes accessed | tf_op | source)
XLA Modules:
  0.0 809.0 jit_solution(5769686347360126263)
XLA Ops:
  13.1 76.0 %while.144 = (s32[]{:T(128)}, bf16[128,2048]{0,1:T(8,128)(2,1)S(1)}, f32[4,128,2048]{1,2,0:T(8,128)}, f32[4,128,1]{1,2,0:T(1,128)S(1)}, bf16[4,128,16,128]{3,2,1...) while((s32[]{:T(128)}, bf16[128,2048]{0,1:T(8,128)(2,1)S(1)}, ...), condition=%wide.region_8.9_spmd.clone, body=%wide.region_1.8_spmd.clone.sunk | while | flops 1216641408 | bytes 26020904 | solution.py:180
  13.2 11.4 %conditional.18 = (bf16[128,2048]{0,1:T(8,128)(2,1)S(1)}, f32[4,128,2048]{1,2,0:T(8,128)}, f32[4,128,1]{1,2,0:T(1,128)S(1)}, bf16[4,128,16,128]{3,2,1,0:T(8,128)...) conditional(s32[]{:T(128)} %convert_element_type.796, ...), branch_computations={%region_2.2_spmd, %region_3.7_spmd} | conditional | flops 1216641408 | bytes 23923316 | solution.py:171
  13.8 4.7 convolution_convert_fusion
  25.9 11.4 %collective-permute-done = bf16[128,2048]{0,1:T(8,128)(2,1)S(1)} collective-permute-done((bf16[128,2048]{0,1:T(8,128)(2,1)S(1)}, bf16[128,2048]{0,1:T(8,128)(2,1)S(1)}, u32[]{:S(2)}, u32[]{:S(2)}) %collective-permute-start) | collective-permute-done | bytes 524320 | tf_op jit(solution)/shard_map/while/body/eval_jaxpr/ppermute | solution.py:16
  37.4 11.4 %conditional.18 = (bf16[128,2048]{0,1:T(8,128)(2,1)S(1)}, f32[4,128,2048]{1,2,0:T(8,128)}, f32[4,128,1]{1,2,0:T(1,128)S(1)}, bf16[4,128,16,128]{3,2,1,0:T(8,128)...) conditional(s32[]{:T(128)} %convert_element_type.796, ...), branch_computations={%region_2.2_spmd, %region_3.7_spmd} | conditional | flops 1216641408 | bytes 23923316 | solution.py:171
  38.0 4.7 convolution_convert_fusion
  48.7 4.5 collective-permute-start
  53.2 10.6 %collective-permute-done = bf16[128,2048]{0,1:T(8,128)(2,1)S(1)} collective-permute-done((bf16[128,2048]{0,1:T(8,128)(2,1)S(1)}, bf16[128,2048]{0,1:T(8,128)(2,1)S(1)}, u32[]{:S(2)}, u32[]{:S(2)}) %collective-permute-start) | collective-permute-done | bytes 524320 | tf_op jit(solution)/shard_map/while/body/eval_jaxpr/ppermute | solution.py:16
  63.8 11.3 %conditional.18 = (bf16[128,2048]{0,1:T(8,128)(2,1)S(1)}, f32[4,128,2048]{1,2,0:T(8,128)}, f32[4,128,1]{1,2,0:T(1,128)S(1)}, bf16[4,128,16,128]{3,2,1,0:T(8,128)...) conditional(s32[]{:T(128)} %convert_element_type.796, ...), branch_computations={%region_2.2_spmd, %region_3.7_spmd} | conditional | flops 1216641408 | bytes 23923316 | solution.py:171
  64.4 4.7 convolution_convert_fusion
  75.1 4.4 collective-permute-start
  79.5 9.6 %collective-permute-done = bf16[128,2048]{0,1:T(8,128)(2,1)S(1)} collective-permute-done((bf16[128,2048]{0,1:T(8,128)(2,1)S(1)}, bf16[128,2048]{0,1:T(8,128)(2,1)S(1)}, u32[]{:S(2)}, u32[]{:S(2)}) %collective-permute-start) | collective-permute-done | bytes 524320 | tf_op jit(solution)/shard_map/while/body/eval_jaxpr/ppermute | solution.py:16
  89.2 81.0 %while.145 = (s32[]{:T(128)}, bf16[128,2048]{0,1:T(8,128)(2,1)S(1)}, f32[4,128,2048]{1,2,0:T(8,128)}, f32[4,128,1]{1,2,0:T(1,128)S(1)}, bf16[4,128,16,128]{3,2,1...) while((s32[]{:T(128)}, bf16[128,2048]{0,1:T(8,128)(2,1)S(1)}, ...), condition=%wide.region_16.17_spmd.clone, body=%wide.region_9.16_spmd.clone.sunk | while | flops 1216641408 | bytes 26020924 | solution.py:180
  89.2 11.4 %conditional.19 = (bf16[128,2048]{0,1:T(8,128)(2,1)S(1)}, f32[4,128,2048]{1,2,0:T(8,128)}, f32[4,128,1]{1,2,0:T(1,128)S(1)}, bf16[4,128,16,128]{3,2,1,0:T(8,128)...) conditional(s32[]{:T(128)} %convert_element_type.797, ...), branch_computations={%region_10.10_spmd, %region_11.15_spmd} | conditional | flops 1216641408 | bytes 23923316 | solution.py:171
  89.8 4.7 convolution_convert_fusion.1
  100.6 4.4 collective-permute-start.1
  105.0 8.7 %collective-permute-done.1 = bf16[128,2048]{0,1:T(8,128)(2,1)S(1)} collective-permute-done((bf16[128,2048]{0,1:T(8,128)(2,1)S(1)}, bf16[128,2048]{0,1:T(8,128)(2,1)S(1)}, u32[]{:S(2)}, u32[]{:S(2)}) %collective-permute-start.1) | collective-permute-done | bytes 524320 | tf_op jit(solution)/shard_map/while/body/eval_jaxpr/ppermute | solution.py:16
  113.8 15.7 %collective-permute-start.1 = (bf16[128,2048]{0,1:T(8,128)(2,1)S(1)}, bf16[128,2048]{0,1:T(8,128)(2,1)S(1)}, u32[]{:S(2)}, u32[]{:S(2)}) collective-permute-start(bf16[128,2048]{0,1:T(8,128)(2,1)S(1)} %get-tuple-element.4051), channel_id=1, source_target_pairs={{0,32},{32,64},{64,96},{96,128},{128,160},{160,192},{192,224},{1,3... | collective-permute-start | bytes 1572872 | tf_op jit(solution)/shard_map/while/body/eval_jaxpr/ppermute | solution.py:16
  129.5 7.8 collective-permute-done.1
  137.4 4.4 collective-permute-start.1
  141.8 6.9 collective-permute-done.1
  148.8 14.7 %collective-permute-start.1 = (bf16[128,2048]{0,1:T(8,128)(2,1)S(1)}, bf16[128,2048]{0,1:T(8,128)(2,1)S(1)}, u32[]{:S(2)}, u32[]{:S(2)}) collective-permute-start(bf16[128,2048]{0,1:T(8,128)(2,1)S(1)} %get-tuple-element.4051), channel_id=1, source_target_pairs={{0,32},{32,64},{64,96},{96,128},{128,160},{160,192},{192,224},{1,3... | collective-permute-start | bytes 1572872 | tf_op jit(solution)/shard_map/while/body/eval_jaxpr/ppermute | solution.py:16
  163.5 6.6 collective-permute-done.1
  176.2 9.8 %copy.145 = bf16[4,128,2048]{1,0,2:T(4,128)(2,1)S(1)} copy(bf16[4,128,2048]{1,2,0:T(8,128)(2,1)S(1)} %convert_element_type.451) | data formatting | bytes 4194304 | tf_op jit(solution)/shard_map/convert_element_type | solution.py:217
  191.2 5.7 copy.150
  196.8 5.5 copy.148
  205.0 4.5 copy.149
  214.0 4.8 while.147
  218.8 330.3 %while.148 = (s32[]{:T(128)}, bf16[128,2048]{1,0:T(8,128)(2,1)S(1)}, bf16[4,128,2048]{1,2,0:T(8,128)(2,1)}, s32[]{:T(128)}, pred[]{:T(512)}, /*index=5*/bf16[4,1...) while((s32[]{:T(128)}, bf16[128,2048]{1,0:T(8,128)(2,1)S(1)}, ...), condition=%wide.region_38.39_spmd.clone, body=%wide.region_32.38_spmd.clone.sunk | while | flops 1353218048 | bytes 71172632 | solution.py:234
  221.3 19.0 %collective-permute-done.4 = bf16[128,2048]{1,0:T(8,128)(2,1)S(1)} collective-permute-done((bf16[128,2048]{1,0:T(8,128)(2,1)}, bf16[128,2048]{1,0:T(8,128)(2,1)S(1)}, u32[]{:S(2)}, u32[]{:S(2)}) %collective-permute-start.4) | collective-permute-done | bytes 524320 | tf_op jit(solution)/shard_map/while/body/eval_jaxpr/ppermute | solution.py:16
  242.4 32.6 %collective-permute-done.4 = bf16[128,2048]{1,0:T(8,128)(2,1)S(1)} collective-permute-done((bf16[128,2048]{1,0:T(8,128)(2,1)}, bf16[128,2048]{1,0:T(8,128)(2,1)S(1)}, u32[]{:S(2)}, u32[]{:S(2)}) %collective-permute-start.4) | collective-permute-done | bytes 524320 | tf_op jit(solution)/shard_map/while/body/eval_jaxpr/ppermute | solution.py:16
  277.1 20.7 %collective-permute-done.4 = bf16[128,2048]{1,0:T(8,128)(2,1)S(1)} collective-permute-done((bf16[128,2048]{1,0:T(8,128)(2,1)}, bf16[128,2048]{1,0:T(8,128)(2,1)S(1)}, u32[]{:S(2)}, u32[]{:S(2)}) %collective-permute-start.4) | collective-permute-done | bytes 524320 | tf_op jit(solution)/shard_map/while/body/eval_jaxpr/ppermute | solution.py:16
  300.0 249.0 %collective-permute-done.4 = bf16[128,2048]{1,0:T(8,128)(2,1)S(1)} collective-permute-done((bf16[128,2048]{1,0:T(8,128)(2,1)}, bf16[128,2048]{1,0:T(8,128)(2,1)S(1)}, u32[]{:S(2)}, u32[]{:S(2)}) %collective-permute-start.4) | collective-permute-done | bytes 524320 | tf_op jit(solution)/shard_map/while/body/eval_jaxpr/ppermute | solution.py:16
  549.0 127.8 %while.149 = (s32[]{:T(128)}, bf16[128,2048]{1,0:T(8,128)(2,1)S(1)}, bf16[4,128,2048]{1,2,0:T(8,128)(2,1)}, s32[]{:T(128)}, pred[]{:T(512)}, /*index=5*/bf16[4,1...) while((s32[]{:T(128)}, bf16[128,2048]{1,0:T(8,128)(2,1)S(1)}, ...), condition=%wide.region_45.46_spmd.clone, body=%wide.region_39.45_spmd.clone.sunk | while | flops 1353218048 | bytes 71172632 | solution.py:234
  549.0 16.7 %conditional.23 = (bf16[128,2048]{1,0:T(8,128)(2,1)}, bf16[4,128,2048]{1,2,0:T(8,128)(2,1)}) conditional(s32[]{:T(128)} %convert_element_type.801, bf16[4,128,2048]{1,2,0:T(8,128)(2,1)} %get-tuple-element.4505, (pred[]{:T(512)}, s32[]{:T(128)}, bf16[4,128,2048]{2,1,0:T(8,128)(2,1)}, bf16[128,2048]{1,0:T(8,128)(2,1)S(1)}, ...), branch_computations={%region_40.40_spmd, %region_41.44_spmd} | conditional | flops 1353218048 | bytes 69075104 | solution.py:207
  567.0 16.0 %collective-permute-done.5 = bf16[128,2048]{1,0:T(8,128)(2,1)S(1)} collective-permute-done((bf16[128,2048]{1,0:T(8,128)(2,1)}, bf16[128,2048]{1,0:T(8,128)(2,1)S(1)}, u32[]{:S(2)}, u32[]{:S(2)}) %collective-permute-start.5) | collective-permute-done | bytes 524320 | tf_op jit(solution)/shard_map/while/body/eval_jaxpr/ppermute | solution.py:16
  583.0 16.7 %conditional.23 = (bf16[128,2048]{1,0:T(8,128)(2,1)}, bf16[4,128,2048]{1,2,0:T(8,128)(2,1)}) conditional(s32[]{:T(128)} %convert_element_type.801, bf16[4,128,2048]{1,2,0:T(8,128)(2,1)} %get-tuple-element.4505, (pred[]{:T(512)}, s32[]{:T(128)}, bf16[4,128,2048]{2,1,0:T(8,128)(2,1)}, bf16[128,2048]{1,0:T(8,128)(2,1)S(1)}, ...), branch_computations={%region_40.40_spmd, %region_41.44_spmd} | conditional | flops 1353218048 | bytes 69075104 | solution.py:207
  600.9 15.2 %collective-permute-done.5 = bf16[128,2048]{1,0:T(8,128)(2,1)S(1)} collective-permute-done((bf16[128,2048]{1,0:T(8,128)(2,1)}, bf16[128,2048]{1,0:T(8,128)(2,1)S(1)}, u32[]{:S(2)}, u32[]{:S(2)}) %collective-permute-start.5) | collective-permute-done | bytes 524320 | tf_op jit(solution)/shard_map/while/body/eval_jaxpr/ppermute | solution.py:16
  616.1 16.7 %conditional.23 = (bf16[128,2048]{1,0:T(8,128)(2,1)}, bf16[4,128,2048]{1,2,0:T(8,128)(2,1)}) conditional(s32[]{:T(128)} %convert_element_type.801, bf16[4,128,2048]{1,2,0:T(8,128)(2,1)} %get-tuple-element.4505, (pred[]{:T(512)}, s32[]{:T(128)}, bf16[4,128,2048]{2,1,0:T(8,128)(2,1)}, bf16[128,2048]{1,0:T(8,128)(2,1)S(1)}, ...), branch_computations={%region_40.40_spmd, %region_41.44_spmd} | conditional | flops 1353218048 | bytes 69075104 | solution.py:207
  634.1 14.8 %collective-permute-done.5 = bf16[128,2048]{1,0:T(8,128)(2,1)S(1)} collective-permute-done((bf16[128,2048]{1,0:T(8,128)(2,1)}, bf16[128,2048]{1,0:T(8,128)(2,1)S(1)}, u32[]{:S(2)}, u32[]{:S(2)}) %collective-permute-start.5) | collective-permute-done | bytes 524320 | tf_op jit(solution)/shard_map/while/body/eval_jaxpr/ppermute | solution.py:16
  648.9 16.7 %conditional.23 = (bf16[128,2048]{1,0:T(8,128)(2,1)}, bf16[4,128,2048]{1,2,0:T(8,128)(2,1)}) conditional(s32[]{:T(128)} %convert_element_type.801, bf16[4,128,2048]{1,2,0:T(8,128)(2,1)} %get-tuple-element.4505, (pred[]{:T(512)}, s32[]{:T(128)}, bf16[4,128,2048]{2,1,0:T(8,128)(2,1)}, bf16[128,2048]{1,0:T(8,128)(2,1)S(1)}, ...), branch_computations={%region_40.40_spmd, %region_41.44_spmd} | conditional | flops 1353218048 | bytes 69075104 | solution.py:207
  666.8 10.0 %collective-permute-done.5 = bf16[128,2048]{1,0:T(8,128)(2,1)S(1)} collective-permute-done((bf16[128,2048]{1,0:T(8,128)(2,1)}, bf16[128,2048]{1,0:T(8,128)(2,1)S(1)}, u32[]{:S(2)}, u32[]{:S(2)}) %collective-permute-start.5) | collective-permute-done | bytes 524320 | tf_op jit(solution)/shard_map/while/body/eval_jaxpr/ppermute | solution.py:16
  676.8 4.3 copy.162
  681.1 4.5 collective-permute-done.7
  685.6 6.2 fusion.213
  700.8 43.0 %collective-permute-done.10 = bf16[256,2048]{1,0:T(8,128)(2,1)} collective-permute-done((bf16[256,2048]{1,0:T(8,128)(2,1)S(1)}, bf16[256,2048]{1,0:T(8,128)(2,1)}, u32[]{:S(2)}, u32[]{:S(2)}) %collective-permute-start.10) | collective-permute-done | bytes 1048608 | tf_op jit(solution)/shard_map/ppermute | solution.py:33
  750.6 35.2 %collective-permute-start.12 = (bf16[64,2048]{1,0:T(8,128)(2,1)S(1)}, bf16[64,2048]{1,0:T(8,128)(2,1)S(1)}, u32[]{:S(2)}, u32[]{:S(2)}) collective-permute-start(bf16[64,2048]{1,0:T(8,128)(2,1)S(1)} %get-tuple-element.3490), channel_id=1, source_target_pairs={{0,16},{8,24},{16,0},{24,8},{1,17},{9,25},{17,1},{25,9},{2,18},{10... | collective-permute-start | bytes 786440 | tf_op jit(solution)/shard_map/ppermute | solution.py:33
  789.6 17.3 %collective-permute-done.12 = bf16[64,2048]{1,0:T(8,128)(2,1)S(1)} collective-permute-done((bf16[64,2048]{1,0:T(8,128)(2,1)S(1)}, bf16[64,2048]{1,0:T(8,128)(2,1)S(1)}, u32[]{:S(2)}, u32[]{:S(2)}) %collective-permute-start.12) | collective-permute-done | bytes 262176 | tf_op jit(solution)/shard_map/ppermute | solution.py:33
  (262 shorter events, 175.1 us)
Async XLA Ops:
  9.8 3.3 copy-start.4
  9.9 3.3 copy-start.7
  24.6 12.7 %collective-permute-start = (bf16[128,2048]{0,1:T(8,128)(2,1)S(1)}, bf16[128,2048]{0,1:T(8,128)(2,1)S(1)}, u32[]{:S(2)}, u32[]{:S(2)}) collective-permute-start(bf16[128,2048]{0,1:T(8,128)(2,1)S(1)} %get-tuple-element.4027), channel_id=1, source_target_pairs={{0,32},{32,64},{64,96},{1,33},{33,65},{65,97},{2,34},{34,66},{66,9... | collective-permute-start | bytes 1572872 | tf_op jit(solution)/shard_map/while/body/eval_jaxpr/ppermute | solution.py:16
  48.7 15.1 %collective-permute-start = (bf16[128,2048]{0,1:T(8,128)(2,1)S(1)}, bf16[128,2048]{0,1:T(8,128)(2,1)S(1)}, u32[]{:S(2)}, u32[]{:S(2)}) collective-permute-start(bf16[128,2048]{0,1:T(8,128)(2,1)S(1)} %get-tuple-element.4027), channel_id=1, source_target_pairs={{0,32},{32,64},{64,96},{1,33},{33,65},{65,97},{2,34},{34,66},{66,9... | collective-permute-start | bytes 1572872 | tf_op jit(solution)/shard_map/while/body/eval_jaxpr/ppermute | solution.py:16
  75.1 14.1 %collective-permute-start = (bf16[128,2048]{0,1:T(8,128)(2,1)S(1)}, bf16[128,2048]{0,1:T(8,128)(2,1)S(1)}, u32[]{:S(2)}, u32[]{:S(2)}) collective-permute-start(bf16[128,2048]{0,1:T(8,128)(2,1)S(1)} %get-tuple-element.4027), channel_id=1, source_target_pairs={{0,32},{32,64},{64,96},{1,33},{33,65},{65,97},{2,34},{34,66},{66,9... | collective-permute-start | bytes 1572872 | tf_op jit(solution)/shard_map/while/body/eval_jaxpr/ppermute | solution.py:16
  100.6 13.1 %collective-permute-start.1 = (bf16[128,2048]{0,1:T(8,128)(2,1)S(1)}, bf16[128,2048]{0,1:T(8,128)(2,1)S(1)}, u32[]{:S(2)}, u32[]{:S(2)}) collective-permute-start(bf16[128,2048]{0,1:T(8,128)(2,1)S(1)} %get-tuple-element.4051), channel_id=1, source_target_pairs={{0,32},{32,64},{64,96},{96,128},{128,160},{160,192},{192,224},{1,3... | collective-permute-start | bytes 1572872 | tf_op jit(solution)/shard_map/while/body/eval_jaxpr/ppermute | solution.py:16
  113.8 23.5 %collective-permute-start.1 = (bf16[128,2048]{0,1:T(8,128)(2,1)S(1)}, bf16[128,2048]{0,1:T(8,128)(2,1)S(1)}, u32[]{:S(2)}, u32[]{:S(2)}) collective-permute-start(bf16[128,2048]{0,1:T(8,128)(2,1)S(1)} %get-tuple-element.4051), channel_id=1, source_target_pairs={{0,32},{32,64},{64,96},{96,128},{128,160},{160,192},{192,224},{1,3... | collective-permute-start | bytes 1572872 | tf_op jit(solution)/shard_map/while/body/eval_jaxpr/ppermute | solution.py:16
  137.4 11.3 %collective-permute-start.1 = (bf16[128,2048]{0,1:T(8,128)(2,1)S(1)}, bf16[128,2048]{0,1:T(8,128)(2,1)S(1)}, u32[]{:S(2)}, u32[]{:S(2)}) collective-permute-start(bf16[128,2048]{0,1:T(8,128)(2,1)S(1)} %get-tuple-element.4051), channel_id=1, source_target_pairs={{0,32},{32,64},{64,96},{96,128},{128,160},{160,192},{192,224},{1,3... | collective-permute-start | bytes 1572872 | tf_op jit(solution)/shard_map/while/body/eval_jaxpr/ppermute | solution.py:16
  148.8 21.4 %collective-permute-start.1 = (bf16[128,2048]{0,1:T(8,128)(2,1)S(1)}, bf16[128,2048]{0,1:T(8,128)(2,1)S(1)}, u32[]{:S(2)}, u32[]{:S(2)}) collective-permute-start(bf16[128,2048]{0,1:T(8,128)(2,1)S(1)} %get-tuple-element.4051), channel_id=1, source_target_pairs={{0,32},{32,64},{64,96},{96,128},{128,160},{160,192},{192,224},{1,3... | collective-permute-start | bytes 1572872 | tf_op jit(solution)/shard_map/while/body/eval_jaxpr/ppermute | solution.py:16
  170.5 0.7 collective-permute-start.2
  171.3 0.7 collective-permute-start.2
  172.2 0.7 collective-permute-start.2
  173.0 0.7 collective-permute-start.2
  191.1 18.4 %collective-permute-start.6 = (bf16[1024,512]{1,0:T(8,128)(2,1)}, bf16[1024,512]{1,0:T(8,128)(2,1)}, u32[]{:S(2)}, u32[]{:S(2)}) collective-permute-start(bf16[1024,512]{1,0:T(8,128)(2,1)} %get-tuple-element.3492), channel_id=1, source_target_pairs={{0,1},{1,0},{2,3},{3,2},{4,5},{5,4},{6,7},{7,6},{8,9},{9,8},{10,11... | collective-permute-start | bytes 3145736 | tf_op jit(solution)/shard_map/ppermute | solution.py:222
  196.8 5.5 copy-start.3
  214.9 0.7 collective-permute-start.3
  216.5 0.7 collective-permute-start.3
  218.0 0.7 collective-permute-start.3
  220.0 20.3 %collective-permute-start.4 = (bf16[128,2048]{1,0:T(8,128)(2,1)}, bf16[128,2048]{1,0:T(8,128)(2,1)S(1)}, u32[]{:S(2)}, u32[]{:S(2)}) collective-permute-start(bf16[128,2048]{1,0:T(8,128)(2,1)} %get-tuple-element.4114), channel_id=1, source_target_pairs={{32,0},{64,32},{96,64},{128,96},{160,128},{192,160},{224,192},{33,... | collective-permute-start | bytes 1572872 | tf_op jit(solution)/shard_map/while/body/eval_jaxpr/ppermute | solution.py:16
  241.2 33.8 %collective-permute-start.4 = (bf16[128,2048]{1,0:T(8,128)(2,1)}, bf16[128,2048]{1,0:T(8,128)(2,1)S(1)}, u32[]{:S(2)}, u32[]{:S(2)}) collective-permute-start(bf16[128,2048]{1,0:T(8,128)(2,1)} %get-tuple-element.4114), channel_id=1, source_target_pairs={{32,0},{64,32},{96,64},{128,96},{160,128},{192,160},{224,192},{33,... | collective-permute-start | bytes 1572872 | tf_op jit(solution)/shard_map/while/body/eval_jaxpr/ppermute | solution.py:16
  275.8 22.0 %collective-permute-start.4 = (bf16[128,2048]{1,0:T(8,128)(2,1)}, bf16[128,2048]{1,0:T(8,128)(2,1)S(1)}, u32[]{:S(2)}, u32[]{:S(2)}) collective-permute-start(bf16[128,2048]{1,0:T(8,128)(2,1)} %get-tuple-element.4114), channel_id=1, source_target_pairs={{32,0},{64,32},{96,64},{128,96},{160,128},{192,160},{224,192},{33,... | collective-permute-start | bytes 1572872 | tf_op jit(solution)/shard_map/while/body/eval_jaxpr/ppermute | solution.py:16
  298.7 250.3 %collective-permute-start.4 = (bf16[128,2048]{1,0:T(8,128)(2,1)}, bf16[128,2048]{1,0:T(8,128)(2,1)S(1)}, u32[]{:S(2)}, u32[]{:S(2)}) collective-permute-start(bf16[128,2048]{1,0:T(8,128)(2,1)} %get-tuple-element.4114), channel_id=1, source_target_pairs={{32,0},{64,32},{96,64},{128,96},{160,128},{192,160},{224,192},{33,... | collective-permute-start | bytes 1572872 | tf_op jit(solution)/shard_map/while/body/eval_jaxpr/ppermute | solution.py:16
  552.1 1.9 copy-start.2
  554.1 4.8 slice-start.4
  554.8 4.1 slice-start.5
  565.7 17.3 %collective-permute-start.5 = (bf16[128,2048]{1,0:T(8,128)(2,1)}, bf16[128,2048]{1,0:T(8,128)(2,1)S(1)}, u32[]{:S(2)}, u32[]{:S(2)}) collective-permute-start(bf16[128,2048]{1,0:T(8,128)(2,1)} %get-tuple-element.4131), channel_id=1, source_target_pairs={{32,0},{64,32},{96,64},{33,1},{65,33},{97,65},{34,2},{66,34},{98,6... | collective-permute-start | bytes 1572872 | tf_op jit(solution)/shard_map/while/body/eval_jaxpr/ppermute | solution.py:16
  586.1 1.9 copy-start.2
  588.0 4.8 slice-start.4
  588.7 4.0 slice-start.5
  599.6 16.5 %collective-permute-start.5 = (bf16[128,2048]{1,0:T(8,128)(2,1)}, bf16[128,2048]{1,0:T(8,128)(2,1)S(1)}, u32[]{:S(2)}, u32[]{:S(2)}) collective-permute-start(bf16[128,2048]{1,0:T(8,128)(2,1)} %get-tuple-element.4131), channel_id=1, source_target_pairs={{32,0},{64,32},{96,64},{33,1},{65,33},{97,65},{34,2},{66,34},{98,6... | collective-permute-start | bytes 1572872 | tf_op jit(solution)/shard_map/while/body/eval_jaxpr/ppermute | solution.py:16
  619.2 1.9 copy-start.2
  621.1 4.8 slice-start.4
  621.9 4.1 slice-start.5
  632.8 16.1 %collective-permute-start.5 = (bf16[128,2048]{1,0:T(8,128)(2,1)}, bf16[128,2048]{1,0:T(8,128)(2,1)S(1)}, u32[]{:S(2)}, u32[]{:S(2)}) collective-permute-start(bf16[128,2048]{1,0:T(8,128)(2,1)} %get-tuple-element.4131), channel_id=1, source_target_pairs={{32,0},{64,32},{96,64},{33,1},{65,33},{97,65},{34,2},{66,34},{98,6... | collective-permute-start | bytes 1572872 | tf_op jit(solution)/shard_map/while/body/eval_jaxpr/ppermute | solution.py:16
  652.0 1.9 copy-start.2
  653.9 4.8 slice-start.4
  654.6 4.1 slice-start.5
  665.6 11.3 %collective-permute-start.5 = (bf16[128,2048]{1,0:T(8,128)(2,1)}, bf16[128,2048]{1,0:T(8,128)(2,1)S(1)}, u32[]{:S(2)}, u32[]{:S(2)}) collective-permute-start(bf16[128,2048]{1,0:T(8,128)(2,1)} %get-tuple-element.4131), channel_id=1, source_target_pairs={{32,0},{64,32},{96,64},{33,1},{65,33},{97,65},{34,2},{66,34},{98,6... | collective-permute-start | bytes 1572872 | tf_op jit(solution)/shard_map/while/body/eval_jaxpr/ppermute | solution.py:16
  676.8 8.8 %copy-start.6 = (bf16[1024,1024]{1,0:T(8,128)(2,1)S(1)}, bf16[1024,1024]{1,0:T(8,128)(2,1)}, u32[]{:S(2)}) copy-start(bf16[1024,1024]{1,0:T(8,128)(2,1)} %pad_maximum_fusion) | copy-start | bytes 6291460
  681.1 4.5 collective-permute-start.7
  691.8 3.2 copy-start.5
  695.5 48.2 %collective-permute-start.10 = (bf16[256,2048]{1,0:T(8,128)(2,1)S(1)}, bf16[256,2048]{1,0:T(8,128)(2,1)}, u32[]{:S(2)}, u32[]{:S(2)}) collective-permute-start(bf16[256,2048]{1,0:T(8,128)(2,1)S(1)} %get-tuple-element.3486), channel_id=1, source_target_pairs={{0,6},{2,0},{4,2},{6,4},{1,7},{3,1},{5,3},{7,5},{8,14},{10,8},{12,... | collective-permute-start | bytes 3145736 | tf_op jit(solution)/shard_map/ppermute | solution.py:33
  698.6 48.7 %collective-permute-start.8 = (bf16[256,2048]{1,0:T(8,128)(2,1)S(1)}, bf16[256,2048]{1,0:T(8,128)(2,1)}, u32[]{:S(2)}, u32[]{:S(2)}) collective-permute-start(bf16[256,2048]{1,0:T(8,128)(2,1)S(1)} %get-tuple-element.3485), channel_id=1, source_target_pairs={{0,2},{2,4},{4,6},{6,0},{1,3},{3,5},{5,7},{7,1},{8,10},{10,12},{12... | collective-permute-start | bytes 3145736 | tf_op jit(solution)/shard_map/ppermute | solution.py:33
  698.6 48.7 %collective-permute-start.9 = (bf16[256,2048]{1,0:T(8,128)(2,1)S(1)}, bf16[256,2048]{1,0:T(8,128)(2,1)}, u32[]{:S(2)}, u32[]{:S(2)}) collective-permute-start(bf16[256,2048]{1,0:T(8,128)(2,1)S(1)} %get-tuple-element.3487), channel_id=1, source_target_pairs={{0,4},{2,6},{4,0},{6,2},{1,5},{3,7},{5,1},{7,3},{8,12},{10,14},{12... | collective-permute-start | bytes 3145736 | tf_op jit(solution)/shard_map/ppermute | solution.py:33
  750.6 39.0 %collective-permute-start.11 = (bf16[64,2048]{1,0:T(8,128)(2,1)S(1)}, bf16[64,2048]{1,0:T(8,128)(2,1)S(1)}, u32[]{:S(2)}, u32[]{:S(2)}) collective-permute-start(bf16[64,2048]{1,0:T(8,128)(2,1)S(1)} %get-tuple-element.3488), channel_id=1, source_target_pairs={{0,8},{8,16},{16,24},{24,0},{1,9},{9,17},{17,25},{25,1},{2,10},{10... | collective-permute-start | bytes 786440 | tf_op jit(solution)/shard_map/ppermute | solution.py:33
  750.6 56.3 %collective-permute-start.12 = (bf16[64,2048]{1,0:T(8,128)(2,1)S(1)}, bf16[64,2048]{1,0:T(8,128)(2,1)S(1)}, u32[]{:S(2)}, u32[]{:S(2)}) collective-permute-start(bf16[64,2048]{1,0:T(8,128)(2,1)S(1)} %get-tuple-element.3490), channel_id=1, source_target_pairs={{0,16},{8,24},{16,0},{24,8},{1,17},{9,25},{17,1},{25,9},{2,18},{10... | collective-permute-start | bytes 786440 | tf_op jit(solution)/shard_map/ppermute | solution.py:33
  785.9 21.0 %collective-permute-start.13 = (bf16[64,2048]{1,0:T(8,128)(2,1)S(1)}, bf16[64,2048]{1,0:T(8,128)(2,1)}, u32[]{:S(2)}, u32[]{:S(2)}) collective-permute-start(bf16[64,2048]{1,0:T(8,128)(2,1)S(1)} %get-tuple-element.3489), channel_id=1, source_target_pairs={{0,24},{8,0},{16,8},{24,16},{1,25},{9,1},{17,9},{25,17},{2,26},{10... | collective-permute-start | bytes 786440 | tf_op jit(solution)/shard_map/ppermute | solution.py:33

commit v12 on v11

--- a/solution.py
+++ b/solution.py
@@ -222,9 +222,8 @@
     theirs = lax.ppermute(
         lax.dynamic_index_in_dim(normed_all, 1 - core, 0, keepdims=False), "core", swap
     )
-    left, carry = lax.optimization_barrier(
-        (jnp.concatenate([mine, theirs], axis=1), (zero_rows, totals_init))
-    )
+    left = jnp.concatenate([mine, theirs], axis=1)
+    carry = (zero_rows, totals_init)
     for lo, hi in phases(sections, micro):
         senders = [
             r

time: 818 us -> 799 us (0.977)
  waiting for transfers between devices: 511 us -> 486 us
    ppermute x22, waiting for transfers between devices: 439 us -> 415 us  [passed_along(): return lax.ppermute(block, axis, [(i, i + distance) for i in senders])]
    unnamed x15 -> x13, local copies, waits for them, and re-layouts: 24.6 us -> 24.4 us
  transfers between devices with their start and end apart: 30 -> 30, of which waited for: 20 -> 20; matrix products, arithmetic and copies ran while one was open for 2% -> 3% of each run, Pallas kernels for 0% -> 0%
where the time goes in v12:
time: 799 us; the launch traced here: 790 us
  waiting for transfers between devices  486 us (61%)
  starting transfers between devices  111 us (14%)
  local copies, waits for them, and re-layouts  73.4 us (9%)
  matrix products  69.8 us (9%)
  other arithmetic  47.5 us (6%)
    ppermute x22, waiting for transfers between devices, passed_along(): return lax.ppermute(block, axis, [(i, i + distance) for i in senders])  415 us
    ppermute x6, waiting for transfers between devices, scatter_sum(): received = lax.ppermute(sent.astype(jnp.bfloat16), axis, route)  68.8 us
    ppermute x22, starting transfers between devices, passed_along(): return lax.ppermute(block, axis, [(i, i + distance) for i in senders])  64.5 us
    ppermute x6, starting transfers between devices, scatter_sum(): received = lax.ppermute(sent.astype(jnp.bfloat16), axis, route)  46 us
    unnamed x13, local copies, waits for them, and re-layouts  24.4 us
    dot_general x4, matrix products, layer_forward(): jnp.dot(normed.reshape(-1, width), weight, preferred_element_type=jnp.flo...  18.8 us
    dot_general x4, matrix products, layer_backward(): lax.dot_general(value_total.reshape(-1, width), weight, (((1,), (1,)), ((...  16.7 us
  transfers between devices with their start and end apart: 30, of which 20 were waited for; matrix products, arithmetic and copies ran while one was open for 3% of the time, Pallas kernels for 0%

profile of v12, /device:TPU:96, one launch (start us, length us, event | category | flops | bytes accessed | tf_op | source)
XLA Modules:
  0.0 789.6 jit_solution(4767475039734974512)
XLA Ops:
  13.2 76.1 %while.144 = (s32[]{:T(128)}, bf16[128,2048]{0,1:T(8,128)(2,1)S(1)}, f32[4,128,2048]{1,2,0:T(8,128)}, f32[4,128,1]{1,2,0:T(1,128)S(1)}, bf16[4,128,16,128]{3,2,1...) while((s32[]{:T(128)}, bf16[128,2048]{0,1:T(8,128)(2,1)S(1)}, ...), condition=%wide.region_8.9_spmd.clone, body=%wide.region_1.8_spmd.clone.sunk | while | flops 1216641408 | bytes 26020904 | solution.py:180
  13.2 11.5 %conditional.18 = (bf16[128,2048]{0,1:T(8,128)(2,1)S(1)}, f32[4,128,2048]{1,2,0:T(8,128)}, f32[4,128,1]{1,2,0:T(1,128)S(1)}, bf16[4,128,16,128]{3,2,1,0:T(8,128)...) conditional(s32[]{:T(128)} %convert_element_type.796, ...), branch_computations={%region_2.2_spmd, %region_3.7_spmd} | conditional | flops 1216641408 | bytes 23923316 | solution.py:171
  13.8 4.7 convolution_convert_fusion
  26.0 11.4 %collective-permute-done = bf16[128,2048]{0,1:T(8,128)(2,1)S(1)} collective-permute-done((bf16[128,2048]{0,1:T(8,128)(2,1)S(1)}, bf16[128,2048]{0,1:T(8,128)(2,1)S(1)}, u32[]{:S(2)}, u32[]{:S(2)}) %collective-permute-start) | collective-permute-done | bytes 524320 | tf_op jit(solution)/shard_map/while/body/eval_jaxpr/ppermute | solution.py:16
  37.4 11.4 %conditional.18 = (bf16[128,2048]{0,1:T(8,128)(2,1)S(1)}, f32[4,128,2048]{1,2,0:T(8,128)}, f32[4,128,1]{1,2,0:T(1,128)S(1)}, bf16[4,128,16,128]{3,2,1,0:T(8,128)...) conditional(s32[]{:T(128)} %convert_element_type.796, ...), branch_computations={%region_2.2_spmd, %region_3.7_spmd} | conditional | flops 1216641408 | bytes 23923316 | solution.py:171
  38.0 4.7 convolution_convert_fusion
  48.7 4.5 collective-permute-start
  53.3 10.6 %collective-permute-done = bf16[128,2048]{0,1:T(8,128)(2,1)S(1)} collective-permute-done((bf16[128,2048]{0,1:T(8,128)(2,1)S(1)}, bf16[128,2048]{0,1:T(8,128)(2,1)S(1)}, u32[]{:S(2)}, u32[]{:S(2)}) %collective-permute-start) | collective-permute-done | bytes 524320 | tf_op jit(solution)/shard_map/while/body/eval_jaxpr/ppermute | solution.py:16
  63.8 11.4 %conditional.18 = (bf16[128,2048]{0,1:T(8,128)(2,1)S(1)}, f32[4,128,2048]{1,2,0:T(8,128)}, f32[4,128,1]{1,2,0:T(1,128)S(1)}, bf16[4,128,16,128]{3,2,1,0:T(8,128)...) conditional(s32[]{:T(128)} %convert_element_type.796, ...), branch_computations={%region_2.2_spmd, %region_3.7_spmd} | conditional | flops 1216641408 | bytes 23923316 | solution.py:171
  64.4 4.7 convolution_convert_fusion
  75.2 4.4 collective-permute-start
  79.6 9.6 %collective-permute-done = bf16[128,2048]{0,1:T(8,128)(2,1)S(1)} collective-permute-done((bf16[128,2048]{0,1:T(8,128)(2,1)S(1)}, bf16[128,2048]{0,1:T(8,128)(2,1)S(1)}, u32[]{:S(2)}, u32[]{:S(2)}) %collective-permute-start) | collective-permute-done | bytes 524320 | tf_op jit(solution)/shard_map/while/body/eval_jaxpr/ppermute | solution.py:16
  89.2 81.0 %while.145 = (s32[]{:T(128)}, bf16[128,2048]{0,1:T(8,128)(2,1)S(1)}, f32[4,128,2048]{1,2,0:T(8,128)}, f32[4,128,1]{1,2,0:T(1,128)S(1)}, bf16[4,128,16,128]{3,2,1...) while((s32[]{:T(128)}, bf16[128,2048]{0,1:T(8,128)(2,1)S(1)}, ...), condition=%wide.region_16.17_spmd.clone, body=%wide.region_9.16_spmd.clone.sunk | while | flops 1216641408 | bytes 26020924 | solution.py:180
  89.2 11.3 %conditional.19 = (bf16[128,2048]{0,1:T(8,128)(2,1)S(1)}, f32[4,128,2048]{1,2,0:T(8,128)}, f32[4,128,1]{1,2,0:T(1,128)S(1)}, bf16[4,128,16,128]{3,2,1,0:T(8,128)...) conditional(s32[]{:T(128)} %convert_element_type.797, ...), branch_computations={%region_10.10_spmd, %region_11.15_spmd} | conditional | flops 1216641408 | bytes 23923316 | solution.py:171
  89.8 4.7 convolution_convert_fusion.1
  100.6 4.4 collective-permute-start.1
  105.0 8.7 %collective-permute-done.1 = bf16[128,2048]{0,1:T(8,128)(2,1)S(1)} collective-permute-done((bf16[128,2048]{0,1:T(8,128)(2,1)S(1)}, bf16[128,2048]{0,1:T(8,128)(2,1)S(1)}, u32[]{:S(2)}, u32[]{:S(2)}) %collective-permute-start.1) | collective-permute-done | bytes 524320 | tf_op jit(solution)/shard_map/while/body/eval_jaxpr/ppermute | solution.py:16
  113.8 15.7 %collective-permute-start.1 = (bf16[128,2048]{0,1:T(8,128)(2,1)S(1)}, bf16[128,2048]{0,1:T(8,128)(2,1)S(1)}, u32[]{:S(2)}, u32[]{:S(2)}) collective-permute-start(bf16[128,2048]{0,1:T(8,128)(2,1)S(1)} %get-tuple-element.4045), channel_id=1, source_target_pairs={{0,32},{32,64},{64,96},{96,128},{128,160},{160,192},{192,224},{1,3... | collective-permute-start | bytes 1572872 | tf_op jit(solution)/shard_map/while/body/eval_jaxpr/ppermute | solution.py:16
  129.5 7.8 collective-permute-done.1
  137.4 4.4 collective-permute-start.1
  141.8 6.9 collective-permute-done.1
  148.8 14.8 %collective-permute-start.1 = (bf16[128,2048]{0,1:T(8,128)(2,1)S(1)}, bf16[128,2048]{0,1:T(8,128)(2,1)S(1)}, u32[]{:S(2)}, u32[]{:S(2)}) collective-permute-start(bf16[128,2048]{0,1:T(8,128)(2,1)S(1)} %get-tuple-element.4045), channel_id=1, source_target_pairs={{0,32},{32,64},{64,96},{96,128},{128,160},{160,192},{192,224},{1,3... | collective-permute-start | bytes 1572872 | tf_op jit(solution)/shard_map/while/body/eval_jaxpr/ppermute | solution.py:16
  163.6 6.6 collective-permute-done.1
  173.8 5.4 copy.148
  179.1 5.6 copy.150
  187.4 4.5 copy.149
  193.6 4.8 while.147
  198.4 304.4 %while.148 = (s32[]{:T(128)}, bf16[128,2048]{1,0:T(8,128)(2,1)S(1)}, bf16[4,128,2048]{1,2,0:T(8,128)(2,1)}, s32[]{:T(128)}, pred[]{:T(512)}, /*index=5*/bf16[4,1...) while((s32[]{:T(128)}, bf16[128,2048]{1,0:T(8,128)(2,1)S(1)}, ...), condition=%wide.region_38.39_spmd.clone, body=%wide.region_32.38_spmd.clone.sunk | while | flops 1353218048 | bytes 71172632 | solution.py:233
  200.8 13.6 %collective-permute-done.4 = bf16[128,2048]{1,0:T(8,128)(2,1)S(1)} collective-permute-done((bf16[128,2048]{1,0:T(8,128)(2,1)}, bf16[128,2048]{1,0:T(8,128)(2,1)S(1)}, u32[]{:S(2)}, u32[]{:S(2)}) %collective-permute-start.4) | collective-permute-done | bytes 524320 | tf_op jit(solution)/shard_map/while/body/eval_jaxpr/ppermute | solution.py:16
  216.5 27.6 %collective-permute-done.4 = bf16[128,2048]{1,0:T(8,128)(2,1)S(1)} collective-permute-done((bf16[128,2048]{1,0:T(8,128)(2,1)}, bf16[128,2048]{1,0:T(8,128)(2,1)S(1)}, u32[]{:S(2)}, u32[]{:S(2)}) %collective-permute-start.4) | collective-permute-done | bytes 524320 | tf_op jit(solution)/shard_map/while/body/eval_jaxpr/ppermute | solution.py:16
  246.3 16.5 %collective-permute-done.4 = bf16[128,2048]{1,0:T(8,128)(2,1)S(1)} collective-permute-done((bf16[128,2048]{1,0:T(8,128)(2,1)}, bf16[128,2048]{1,0:T(8,128)(2,1)S(1)}, u32[]{:S(2)}, u32[]{:S(2)}) %collective-permute-start.4) | collective-permute-done | bytes 524320 | tf_op jit(solution)/shard_map/while/body/eval_jaxpr/ppermute | solution.py:16
  264.9 237.9 %collective-permute-done.4 = bf16[128,2048]{1,0:T(8,128)(2,1)S(1)} collective-permute-done((bf16[128,2048]{1,0:T(8,128)(2,1)}, bf16[128,2048]{1,0:T(8,128)(2,1)S(1)}, u32[]{:S(2)}, u32[]{:S(2)}) %collective-permute-start.4) | collective-permute-done | bytes 524320 | tf_op jit(solution)/shard_map/while/body/eval_jaxpr/ppermute | solution.py:16
  502.8 129.1 %while.149 = (s32[]{:T(128)}, bf16[128,2048]{1,0:T(8,128)(2,1)S(1)}, bf16[4,128,2048]{1,2,0:T(8,128)(2,1)}, s32[]{:T(128)}, pred[]{:T(512)}, /*index=5*/bf16[4,1...) while((s32[]{:T(128)}, bf16[128,2048]{1,0:T(8,128)(2,1)S(1)}, ...), condition=%wide.region_45.46_spmd.clone, body=%wide.region_39.45_spmd.clone.sunk | while | flops 1353218048 | bytes 71172632 | solution.py:233
  502.8 16.7 %conditional.23 = (bf16[128,2048]{1,0:T(8,128)(2,1)}, bf16[4,128,2048]{1,2,0:T(8,128)(2,1)}) conditional(s32[]{:T(128)} %convert_element_type.801, bf16[4,128,2048]{1,2,0:T(8,128)(2,1)} %get-tuple-element.4499, (pred[]{:T(512)}, s32[]{:T(128)}, bf16[4,128,2048]{2,1,0:T(8,128)(2,1)}, bf16[128,2048]{1,0:T(8,128)(2,1)S(1)}, ...), branch_computations={%region_40.40_spmd, %region_41.44_spmd} | conditional | flops 1353218048 | bytes 69075104 | solution.py:207
  520.8 15.9 %collective-permute-done.5 = bf16[128,2048]{1,0:T(8,128)(2,1)S(1)} collective-permute-done((bf16[128,2048]{1,0:T(8,128)(2,1)}, bf16[128,2048]{1,0:T(8,128)(2,1)S(1)}, u32[]{:S(2)}, u32[]{:S(2)}) %collective-permute-start.5) | collective-permute-done | bytes 524320 | tf_op jit(solution)/shard_map/while/body/eval_jaxpr/ppermute | solution.py:16
  536.7 16.7 %conditional.23 = (bf16[128,2048]{1,0:T(8,128)(2,1)}, bf16[4,128,2048]{1,2,0:T(8,128)(2,1)}) conditional(s32[]{:T(128)} %convert_element_type.801, bf16[4,128,2048]{1,2,0:T(8,128)(2,1)} %get-tuple-element.4499, (pred[]{:T(512)}, s32[]{:T(128)}, bf16[4,128,2048]{2,1,0:T(8,128)(2,1)}, bf16[128,2048]{1,0:T(8,128)(2,1)S(1)}, ...), branch_computations={%region_40.40_spmd, %region_41.44_spmd} | conditional | flops 1353218048 | bytes 69075104 | solution.py:207
  554.7 16.0 %collective-permute-done.5 = bf16[128,2048]{1,0:T(8,128)(2,1)S(1)} collective-permute-done((bf16[128,2048]{1,0:T(8,128)(2,1)}, bf16[128,2048]{1,0:T(8,128)(2,1)S(1)}, u32[]{:S(2)}, u32[]{:S(2)}) %collective-permute-start.5) | collective-permute-done | bytes 524320 | tf_op jit(solution)/shard_map/while/body/eval_jaxpr/ppermute | solution.py:16
  570.7 16.7 %conditional.23 = (bf16[128,2048]{1,0:T(8,128)(2,1)}, bf16[4,128,2048]{1,2,0:T(8,128)(2,1)}) conditional(s32[]{:T(128)} %convert_element_type.801, bf16[4,128,2048]{1,2,0:T(8,128)(2,1)} %get-tuple-element.4499, (pred[]{:T(512)}, s32[]{:T(128)}, bf16[4,128,2048]{2,1,0:T(8,128)(2,1)}, bf16[128,2048]{1,0:T(8,128)(2,1)S(1)}, ...), branch_computations={%region_40.40_spmd, %region_41.44_spmd} | conditional | flops 1353218048 | bytes 69075104 | solution.py:207
  588.7 15.3 %collective-permute-done.5 = bf16[128,2048]{1,0:T(8,128)(2,1)S(1)} collective-permute-done((bf16[128,2048]{1,0:T(8,128)(2,1)}, bf16[128,2048]{1,0:T(8,128)(2,1)S(1)}, u32[]{:S(2)}, u32[]{:S(2)}) %collective-permute-start.5) | collective-permute-done | bytes 524320 | tf_op jit(solution)/shard_map/while/body/eval_jaxpr/ppermute | solution.py:16
  604.0 16.7 %conditional.23 = (bf16[128,2048]{1,0:T(8,128)(2,1)}, bf16[4,128,2048]{1,2,0:T(8,128)(2,1)}) conditional(s32[]{:T(128)} %convert_element_type.801, bf16[4,128,2048]{1,2,0:T(8,128)(2,1)} %get-tuple-element.4499, (pred[]{:T(512)}, s32[]{:T(128)}, bf16[4,128,2048]{2,1,0:T(8,128)(2,1)}, bf16[128,2048]{1,0:T(8,128)(2,1)S(1)}, ...), branch_computations={%region_40.40_spmd, %region_41.44_spmd} | conditional | flops 1353218048 | bytes 69075104 | solution.py:207
  621.9 10.0 %collective-permute-done.5 = bf16[128,2048]{1,0:T(8,128)(2,1)S(1)} collective-permute-done((bf16[128,2048]{1,0:T(8,128)(2,1)}, bf16[128,2048]{1,0:T(8,128)(2,1)S(1)}, u32[]{:S(2)}, u32[]{:S(2)}) %collective-permute-start.5) | collective-permute-done | bytes 524320 | tf_op jit(solution)/shard_map/while/body/eval_jaxpr/ppermute | solution.py:16
  631.9 4.4 copy.162
  638.8 10.8 %copy.145 = bf16[4,128,2048]{1,0,2:T(4,128)(2,1)} copy(bf16[4,128,2048]{1,2,0:T(8,128)(2,1)S(1)} %convert_element_type.451) | data formatting | bytes 4194304 | tf_op jit(solution)/shard_map/convert_element_type | solution.py:217
  659.6 6.2 fusion.213
  675.1 43.1 %collective-permute-done.10 = bf16[256,2048]{1,0:T(8,128)(2,1)} collective-permute-done((bf16[256,2048]{1,0:T(8,128)(2,1)S(1)}, bf16[256,2048]{1,0:T(8,128)(2,1)}, u32[]{:S(2)}, u32[]{:S(2)}) %collective-permute-start.10) | collective-permute-done | bytes 1048608 | tf_op jit(solution)/shard_map/ppermute | solution.py:33
  725.0 40.3 %collective-permute-start.12 = (bf16[64,2048]{1,0:T(8,128)(2,1)S(1)}, bf16[64,2048]{1,0:T(8,128)(2,1)S(1)}, u32[]{:S(2)}, u32[]{:S(2)}) collective-permute-start(bf16[64,2048]{1,0:T(8,128)(2,1)S(1)} %get-tuple-element.3484), channel_id=1, source_target_pairs={{0,16},{8,24},{16,0},{24,8},{1,17},{9,25},{17,1},{25,9},{2,18},{10... | collective-permute-start | bytes 786440 | tf_op jit(solution)/shard_map/ppermute | solution.py:33
  765.3 4.2 collective-permute-done.11
  769.6 18.0 %collective-permute-done.12 = bf16[64,2048]{1,0:T(8,128)(2,1)S(1)} collective-permute-done((bf16[64,2048]{1,0:T(8,128)(2,1)S(1)}, bf16[64,2048]{1,0:T(8,128)(2,1)S(1)}, u32[]{:S(2)}, u32[]{:S(2)}) %collective-permute-start.12) | collective-permute-done | bytes 262176 | tf_op jit(solution)/shard_map/ppermute | solution.py:33
  (259 shorter events, 173.7 us)
Async XLA Ops:
  9.8 3.3 copy-start.4
  9.8 3.3 copy-start.6
  24.7 12.7 %collective-permute-start = (bf16[128,2048]{0,1:T(8,128)(2,1)S(1)}, bf16[128,2048]{0,1:T(8,128)(2,1)S(1)}, u32[]{:S(2)}, u32[]{:S(2)}) collective-permute-start(bf16[128,2048]{0,1:T(8,128)(2,1)S(1)} %get-tuple-element.4021), channel_id=1, source_target_pairs={{0,32},{32,64},{64,96},{1,33},{33,65},{65,97},{2,34},{34,66},{66,9... | collective-permute-start | bytes 1572872 | tf_op jit(solution)/shard_map/while/body/eval_jaxpr/ppermute | solution.py:16
  48.7 15.1 %collective-permute-start = (bf16[128,2048]{0,1:T(8,128)(2,1)S(1)}, bf16[128,2048]{0,1:T(8,128)(2,1)S(1)}, u32[]{:S(2)}, u32[]{:S(2)}) collective-permute-start(bf16[128,2048]{0,1:T(8,128)(2,1)S(1)} %get-tuple-element.4021), channel_id=1, source_target_pairs={{0,32},{32,64},{64,96},{1,33},{33,65},{65,97},{2,34},{34,66},{66,9... | collective-permute-start | bytes 1572872 | tf_op jit(solution)/shard_map/while/body/eval_jaxpr/ppermute | solution.py:16
  75.2 14.1 %collective-permute-start = (bf16[128,2048]{0,1:T(8,128)(2,1)S(1)}, bf16[128,2048]{0,1:T(8,128)(2,1)S(1)}, u32[]{:S(2)}, u32[]{:S(2)}) collective-permute-start(bf16[128,2048]{0,1:T(8,128)(2,1)S(1)} %get-tuple-element.4021), channel_id=1, source_target_pairs={{0,32},{32,64},{64,96},{1,33},{33,65},{65,97},{2,34},{34,66},{66,9... | collective-permute-start | bytes 1572872 | tf_op jit(solution)/shard_map/while/body/eval_jaxpr/ppermute | solution.py:16
  100.6 13.1 %collective-permute-start.1 = (bf16[128,2048]{0,1:T(8,128)(2,1)S(1)}, bf16[128,2048]{0,1:T(8,128)(2,1)S(1)}, u32[]{:S(2)}, u32[]{:S(2)}) collective-permute-start(bf16[128,2048]{0,1:T(8,128)(2,1)S(1)} %get-tuple-element.4045), channel_id=1, source_target_pairs={{0,32},{32,64},{64,96},{96,128},{128,160},{160,192},{192,224},{1,3... | collective-permute-start | bytes 1572872 | tf_op jit(solution)/shard_map/while/body/eval_jaxpr/ppermute | solution.py:16
  113.8 23.5 %collective-permute-start.1 = (bf16[128,2048]{0,1:T(8,128)(2,1)S(1)}, bf16[128,2048]{0,1:T(8,128)(2,1)S(1)}, u32[]{:S(2)}, u32[]{:S(2)}) collective-permute-start(bf16[128,2048]{0,1:T(8,128)(2,1)S(1)} %get-tuple-element.4045), channel_id=1, source_target_pairs={{0,32},{32,64},{64,96},{96,128},{128,160},{160,192},{192,224},{1,3... | collective-permute-start | bytes 1572872 | tf_op jit(solution)/shard_map/while/body/eval_jaxpr/ppermute | solution.py:16
  137.4 11.3 %collective-permute-start.1 = (bf16[128,2048]{0,1:T(8,128)(2,1)S(1)}, bf16[128,2048]{0,1:T(8,128)(2,1)S(1)}, u32[]{:S(2)}, u32[]{:S(2)}) collective-permute-start(bf16[128,2048]{0,1:T(8,128)(2,1)S(1)} %get-tuple-element.4045), channel_id=1, source_target_pairs={{0,32},{32,64},{64,96},{96,128},{128,160},{160,192},{192,224},{1,3... | collective-permute-start | bytes 1572872 | tf_op jit(solution)/shard_map/while/body/eval_jaxpr/ppermute | solution.py:16
  148.8 21.4 %collective-permute-start.1 = (bf16[128,2048]{0,1:T(8,128)(2,1)S(1)}, bf16[128,2048]{0,1:T(8,128)(2,1)S(1)}, u32[]{:S(2)}, u32[]{:S(2)}) collective-permute-start(bf16[128,2048]{0,1:T(8,128)(2,1)S(1)} %get-tuple-element.4045), channel_id=1, source_target_pairs={{0,32},{32,64},{64,96},{96,128},{128,160},{160,192},{192,224},{1,3... | collective-permute-start | bytes 1572872 | tf_op jit(solution)/shard_map/while/body/eval_jaxpr/ppermute | solution.py:16
  170.5 0.7 collective-permute-start.2
  171.3 0.7 collective-permute-start.2
  172.2 0.7 collective-permute-start.2
  173.1 0.7 collective-permute-start.2
  179.1 5.6 copy-start.3
  194.5 0.7 collective-permute-start.3
  196.1 0.7 collective-permute-start.3
  197.7 0.7 collective-permute-start.3
  199.5 14.9 %collective-permute-start.4 = (bf16[128,2048]{1,0:T(8,128)(2,1)}, bf16[128,2048]{1,0:T(8,128)(2,1)S(1)}, u32[]{:S(2)}, u32[]{:S(2)}) collective-permute-start(bf16[128,2048]{1,0:T(8,128)(2,1)} %get-tuple-element.4108), channel_id=1, source_target_pairs={{32,0},{64,32},{96,64},{128,96},{160,128},{192,160},{224,192},{33,... | collective-permute-start | bytes 1572872 | tf_op jit(solution)/shard_map/while/body/eval_jaxpr/ppermute | solution.py:16
  215.2 28.9 %collective-permute-start.4 = (bf16[128,2048]{1,0:T(8,128)(2,1)}, bf16[128,2048]{1,0:T(8,128)(2,1)S(1)}, u32[]{:S(2)}, u32[]{:S(2)}) collective-permute-start(bf16[128,2048]{1,0:T(8,128)(2,1)} %get-tuple-element.4108), channel_id=1, source_target_pairs={{32,0},{64,32},{96,64},{128,96},{160,128},{192,160},{224,192},{33,... | collective-permute-start | bytes 1572872 | tf_op jit(solution)/shard_map/while/body/eval_jaxpr/ppermute | solution.py:16
  245.0 17.8 %collective-permute-start.4 = (bf16[128,2048]{1,0:T(8,128)(2,1)}, bf16[128,2048]{1,0:T(8,128)(2,1)S(1)}, u32[]{:S(2)}, u32[]{:S(2)}) collective-permute-start(bf16[128,2048]{1,0:T(8,128)(2,1)} %get-tuple-element.4108), channel_id=1, source_target_pairs={{32,0},{64,32},{96,64},{128,96},{160,128},{192,160},{224,192},{33,... | collective-permute-start | bytes 1572872 | tf_op jit(solution)/shard_map/while/body/eval_jaxpr/ppermute | solution.py:16
  263.6 239.2 %collective-permute-start.4 = (bf16[128,2048]{1,0:T(8,128)(2,1)}, bf16[128,2048]{1,0:T(8,128)(2,1)S(1)}, u32[]{:S(2)}, u32[]{:S(2)}) collective-permute-start(bf16[128,2048]{1,0:T(8,128)(2,1)} %get-tuple-element.4108), channel_id=1, source_target_pairs={{32,0},{64,32},{96,64},{128,96},{160,128},{192,160},{224,192},{33,... | collective-permute-start | bytes 1572872 | tf_op jit(solution)/shard_map/while/body/eval_jaxpr/ppermute | solution.py:16
  505.9 1.9 copy-start.2
  507.9 4.8 slice-start.4
  508.6 4.1 slice-start.5
  519.5 17.2 %collective-permute-start.5 = (bf16[128,2048]{1,0:T(8,128)(2,1)}, bf16[128,2048]{1,0:T(8,128)(2,1)S(1)}, u32[]{:S(2)}, u32[]{:S(2)}) collective-permute-start(bf16[128,2048]{1,0:T(8,128)(2,1)} %get-tuple-element.4125), channel_id=1, source_target_pairs={{32,0},{64,32},{96,64},{33,1},{65,33},{97,65},{34,2},{66,34},{98,6... | collective-permute-start | bytes 1572872 | tf_op jit(solution)/shard_map/while/body/eval_jaxpr/ppermute | solution.py:16
  539.9 1.9 copy-start.2
  541.8 4.8 slice-start.4
  542.5 4.0 slice-start.5
  553.4 17.3 %collective-permute-start.5 = (bf16[128,2048]{1,0:T(8,128)(2,1)}, bf16[128,2048]{1,0:T(8,128)(2,1)S(1)}, u32[]{:S(2)}, u32[]{:S(2)}) collective-permute-start(bf16[128,2048]{1,0:T(8,128)(2,1)} %get-tuple-element.4125), channel_id=1, source_target_pairs={{32,0},{64,32},{96,64},{33,1},{65,33},{97,65},{34,2},{66,34},{98,6... | collective-permute-start | bytes 1572872 | tf_op jit(solution)/shard_map/while/body/eval_jaxpr/ppermute | solution.py:16
  573.8 1.9 copy-start.2
  575.8 4.8 slice-start.4
  576.5 4.1 slice-start.5
  587.4 16.6 %collective-permute-start.5 = (bf16[128,2048]{1,0:T(8,128)(2,1)}, bf16[128,2048]{1,0:T(8,128)(2,1)S(1)}, u32[]{:S(2)}, u32[]{:S(2)}) collective-permute-start(bf16[128,2048]{1,0:T(8,128)(2,1)} %get-tuple-element.4125), channel_id=1, source_target_pairs={{32,0},{64,32},{96,64},{33,1},{65,33},{97,65},{34,2},{66,34},{98,6... | collective-permute-start | bytes 1572872 | tf_op jit(solution)/shard_map/while/body/eval_jaxpr/ppermute | solution.py:16
  607.1 1.9 copy-start.2
  609.0 4.8 slice-start.4
  609.8 4.0 slice-start.5
  620.7 11.3 %collective-permute-start.5 = (bf16[128,2048]{1,0:T(8,128)(2,1)}, bf16[128,2048]{1,0:T(8,128)(2,1)S(1)}, u32[]{:S(2)}, u32[]{:S(2)}) collective-permute-start(bf16[128,2048]{1,0:T(8,128)(2,1)} %get-tuple-element.4125), channel_id=1, source_target_pairs={{32,0},{64,32},{96,64},{33,1},{65,33},{97,65},{34,2},{66,34},{98,6... | collective-permute-start | bytes 1572872 | tf_op jit(solution)/shard_map/while/body/eval_jaxpr/ppermute | solution.py:16
  636.3 23.3 %collective-permute-start.7 = (bf16[512,2048]{1,0:T(8,128)(2,1)}, bf16[512,2048]{1,0:T(8,128)(2,1)}, u32[]{:S(2)}, u32[]{:S(2)}) collective-permute-start(bf16[512,2048]{1,0:T(8,128)(2,1)} %bitcast.94), channel_id=1, source_target_pairs={{0,1},{1,0},{2,3},{3,2},{4,5},{5,4},{6,7},{7,6},{8,9},{9,8},{10,11... | collective-permute-start | bytes 6291464 | tf_op jit(solution)/shard_map/ppermute | solution.py:236
  656.6 3.0 collective-permute-start.6
  665.8 3.2 copy-start.5
  669.5 48.6 %collective-permute-start.10 = (bf16[256,2048]{1,0:T(8,128)(2,1)S(1)}, bf16[256,2048]{1,0:T(8,128)(2,1)}, u32[]{:S(2)}, u32[]{:S(2)}) collective-permute-start(bf16[256,2048]{1,0:T(8,128)(2,1)S(1)} %get-tuple-element.3480), channel_id=1, source_target_pairs={{0,6},{2,0},{4,2},{6,4},{1,7},{3,1},{5,3},{7,5},{8,14},{10,8},{12,... | collective-permute-start | bytes 3145736 | tf_op jit(solution)/shard_map/ppermute | solution.py:33
  672.7 48.9 %collective-permute-start.8 = (bf16[256,2048]{1,0:T(8,128)(2,1)S(1)}, bf16[256,2048]{1,0:T(8,128)(2,1)}, u32[]{:S(2)}, u32[]{:S(2)}) collective-permute-start(bf16[256,2048]{1,0:T(8,128)(2,1)S(1)} %get-tuple-element.3479), channel_id=1, source_target_pairs={{0,2},{2,4},{4,6},{6,0},{1,3},{3,5},{5,7},{7,1},{8,10},{10,12},{12... | collective-permute-start | bytes 3145736 | tf_op jit(solution)/shard_map/ppermute | solution.py:33
  672.7 48.9 %collective-permute-start.9 = (bf16[256,2048]{1,0:T(8,128)(2,1)S(1)}, bf16[256,2048]{1,0:T(8,128)(2,1)}, u32[]{:S(2)}, u32[]{:S(2)}) collective-permute-start(bf16[256,2048]{1,0:T(8,128)(2,1)S(1)} %get-tuple-element.3481), channel_id=1, source_target_pairs={{0,4},{2,6},{4,0},{6,2},{1,5},{3,7},{5,1},{7,3},{8,12},{10,14},{12... | collective-permute-start | bytes 3145736 | tf_op jit(solution)/shard_map/ppermute | solution.py:33
  724.9 44.7 %collective-permute-start.11 = (bf16[64,2048]{1,0:T(8,128)(2,1)S(1)}, bf16[64,2048]{1,0:T(8,128)(2,1)S(1)}, u32[]{:S(2)}, u32[]{:S(2)}) collective-permute-start(bf16[64,2048]{1,0:T(8,128)(2,1)S(1)} %get-tuple-element.3482), channel_id=1, source_target_pairs={{0,8},{8,16},{16,24},{24,0},{1,9},{9,17},{17,25},{25,1},{2,10},{10... | collective-permute-start | bytes 786440 | tf_op jit(solution)/shard_map/ppermute | solution.py:33
  725.0 62.6 %collective-permute-start.12 = (bf16[64,2048]{1,0:T(8,128)(2,1)S(1)}, bf16[64,2048]{1,0:T(8,128)(2,1)S(1)}, u32[]{:S(2)}, u32[]{:S(2)}) collective-permute-start(bf16[64,2048]{1,0:T(8,128)(2,1)S(1)} %get-tuple-element.3484), channel_id=1, source_target_pairs={{0,16},{8,24},{16,0},{24,8},{1,17},{9,25},{17,1},{25,9},{2,18},{10... | collective-permute-start | bytes 786440 | tf_op jit(solution)/shard_map/ppermute | solution.py:33
  765.3 22.3 %collective-permute-start.13 = (bf16[64,2048]{1,0:T(8,128)(2,1)S(1)}, bf16[64,2048]{1,0:T(8,128)(2,1)}, u32[]{:S(2)}, u32[]{:S(2)}) collective-permute-start(bf16[64,2048]{1,0:T(8,128)(2,1)S(1)} %get-tuple-element.3483), channel_id=1, source_target_pairs={{0,24},{8,0},{16,8},{24,16},{1,25},{9,1},{17,9},{25,17},{2,26},{10... | collective-permute-start | bytes 786440 | tf_op jit(solution)/shard_map/ppermute | solution.py:33

commit v13 on v12

--- a/solution.py
+++ b/solution.py
@@ -214,16 +214,24 @@
     core = lax.axis_index("core")
     swap = [(0, 1), (1, 0)]
     rows_each = width // (zs * ys * cores)
-    normed_all = stashed[0].astype(jnp.bfloat16).reshape(micro * buses, zs, ys, cores, rows_each)
-    normed_all = jnp.transpose(normed_all, (3, 2, 1, 4, 0)).reshape(
-        cores, width // cores, micro * buses
-    )
-    mine = lax.dynamic_index_in_dim(normed_all, core, 0, keepdims=False)
-    theirs = lax.ppermute(
-        lax.dynamic_index_in_dim(normed_all, 1 - core, 0, keepdims=False), "core", swap
-    )
-    left = jnp.concatenate([mine, theirs], axis=1)
-    carry = (zero_rows, totals_init)
+
+    def prepare(scaled):
+        normed_all = scaled.astype(jnp.bfloat16).reshape(micro * buses, zs, ys, cores, rows_each)
+        normed_all = jnp.transpose(normed_all, (3, 2, 1, 4, 0)).reshape(
+            cores, width // cores, micro * buses
+        )
+        return (
+            lax.dynamic_index_in_dim(normed_all, core, 0, keepdims=False),
+            lax.dynamic_index_in_dim(normed_all, 1 - core, 0, keepdims=False),
+        )
+
+    def skip(scaled):
+        empty = jnp.zeros((width // cores, micro * buses), jnp.bfloat16)
+        return (empty, empty)
+
+    early = rank < sections // 2
+    prepared = lax.cond(early, prepare, skip, stashed[0])
+    prepared, carry = lax.optimization_barrier((prepared, (zero_rows, totals_init)))
     for lo, hi in phases(sections, micro):
         senders = [
             r
@@ -232,6 +240,8 @@
         ]
         carry = lax.fori_loop(lo, hi, functools.partial(backward_step, senders), carry)
     unused_rows, collected = carry
+    mine, sent = lax.cond(early, lambda p, s: p, lambda p, s: prepare(s), prepared, stashed[0])
+    left = jnp.concatenate([mine, lax.ppermute(sent, "core", swap)], axis=1)
     own = collected.reshape(micro * buses, width)
     right = jnp.concatenate([own, lax.ppermute(own, "core", swap)], axis=0)
     half = jnp.dot(left, right, preferred_element_type=jnp.float32)

time: 799 us -> 801 us (level)
  starting transfers between devices: 111 us -> 127 us
  waiting for transfers between devices: 486 us -> 472 us
    ppermute x22, waiting for transfers between devices: 415 us -> 399 us  [passed_along(): return lax.ppermute(block, axis, [(i, i + distance) for i in senders])]
    ppermute x6, starting transfers between devices: 46 us -> 61.3 us  [scatter_sum(): received = lax.ppermute(sent.astype(jnp.bfloat16), axis, route)]
    cond x32 -> x34, local copies, waits for them, and re-layouts: 1.13 us -> 12.1 us
    convert_element_type x1 -> x0, local copies, waits for them, and re-layouts: 10.8 us -> none  [per_device(): stashed[0].astype(jnp.bfloat16)]
  transfers between devices with their start and end apart: 30 -> 30, of which waited for: 20 -> 20; matrix products, arithmetic and copies ran while one was open for 3% -> 0% of each run, Pallas kernels for 0% -> 0%
where the time goes in v13:
time: 801 us; the launch traced here: 791 us
  waiting for transfers between devices  472 us (59%)
  starting transfers between devices  127 us (16%)
  local copies, waits for them, and re-layouts  73.1 us (9%)
  matrix products  70.1 us (9%)
  other arithmetic  47.5 us (6%)
    ppermute x22, waiting for transfers between devices, passed_along(): return lax.ppermute(block, axis, [(i, i + distance) for i in senders])  399 us
    ppermute x6, waiting for transfers between devices, scatter_sum(): received = lax.ppermute(sent.astype(jnp.bfloat16), axis, route)  68.6 us
    ppermute x22, starting transfers between devices, passed_along(): return lax.ppermute(block, axis, [(i, i + distance) for i in senders])  64.7 us
    ppermute x6, starting transfers between devices, scatter_sum(): received = lax.ppermute(sent.astype(jnp.bfloat16), axis, route)  61.3 us
    unnamed x13, local copies, waits for them, and re-layouts  24.8 us
    dot_general x4, matrix products, layer_forward(): jnp.dot(normed.reshape(-1, width), weight, preferred_element_type=jnp.flo...  18.8 us
    dot_general x4, matrix products, layer_backward(): lax.dot_general(value_total.reshape(-1, width), weight, (((1,), (1,)), ((...  16.7 us
  transfers between devices with their start and end apart: 30, of which 20 were waited for; matrix products, arithmetic and copies ran while one was open for 0% of the time, Pallas kernels for 0%

profile of v13, /device:TPU:96, one launch (start us, length us, event | category | flops | bytes accessed | tf_op | source)
XLA Modules:
  0.0 791.4 jit_solution(4854175749713856765)
XLA Ops:
  13.1 76.2 %while.144 = (s32[]{:T(128)}, bf16[128,2048]{0,1:T(8,128)(2,1)S(1)}, f32[4,128,2048]{1,2,0:T(8,128)}, f32[4,128,1]{1,2,0:T(1,128)S(1)}, bf16[4,128,16,128]{3,2,1...) while((s32[]{:T(128)}, bf16[128,2048]{0,1:T(8,128)(2,1)S(1)}, ...), condition=%wide.region_8.9_spmd.clone, body=%wide.region_1.8_spmd.clone.sunk | while | flops 1216641408 | bytes 26020904 | solution.py:180
  13.1 11.5 %conditional.22 = (bf16[128,2048]{0,1:T(8,128)(2,1)S(1)}, f32[4,128,2048]{1,2,0:T(8,128)}, f32[4,128,1]{1,2,0:T(1,128)S(1)}, bf16[4,128,16,128]{3,2,1,0:T(8,128)...) conditional(s32[]{:T(128)} %convert_element_type.805, ...), branch_computations={%region_2.2_spmd, %region_3.7_spmd} | conditional | flops 1216641408 | bytes 23923316 | solution.py:171
  13.8 4.7 convolution_convert_fusion
  26.0 11.4 %collective-permute-done = bf16[128,2048]{0,1:T(8,128)(2,1)S(1)} collective-permute-done((bf16[128,2048]{0,1:T(8,128)(2,1)S(1)}, bf16[128,2048]{0,1:T(8,128)(2,1)S(1)}, u32[]{:S(2)}, u32[]{:S(2)}) %collective-permute-start) | collective-permute-done | bytes 524320 | tf_op jit(solution)/shard_map/while/body/eval_jaxpr/ppermute | solution.py:16
  37.4 11.3 %conditional.22 = (bf16[128,2048]{0,1:T(8,128)(2,1)S(1)}, f32[4,128,2048]{1,2,0:T(8,128)}, f32[4,128,1]{1,2,0:T(1,128)S(1)}, bf16[4,128,16,128]{3,2,1,0:T(8,128)...) conditional(s32[]{:T(128)} %convert_element_type.805, ...), branch_computations={%region_2.2_spmd, %region_3.7_spmd} | conditional | flops 1216641408 | bytes 23923316 | solution.py:171
  38.0 4.7 convolution_convert_fusion
  48.7 4.6 collective-permute-start
  53.3 10.6 %collective-permute-done = bf16[128,2048]{0,1:T(8,128)(2,1)S(1)} collective-permute-done((bf16[128,2048]{0,1:T(8,128)(2,1)S(1)}, bf16[128,2048]{0,1:T(8,128)(2,1)S(1)}, u32[]{:S(2)}, u32[]{:S(2)}) %collective-permute-start) | collective-permute-done | bytes 524320 | tf_op jit(solution)/shard_map/while/body/eval_jaxpr/ppermute | solution.py:16
  63.9 11.4 %conditional.22 = (bf16[128,2048]{0,1:T(8,128)(2,1)S(1)}, f32[4,128,2048]{1,2,0:T(8,128)}, f32[4,128,1]{1,2,0:T(1,128)S(1)}, bf16[4,128,16,128]{3,2,1,0:T(8,128)...) conditional(s32[]{:T(128)} %convert_element_type.805, ...), branch_computations={%region_2.2_spmd, %region_3.7_spmd} | conditional | flops 1216641408 | bytes 23923316 | solution.py:171
  64.5 4.7 convolution_convert_fusion
  75.3 4.3 collective-permute-start
  79.7 9.7 %collective-permute-done = bf16[128,2048]{0,1:T(8,128)(2,1)S(1)} collective-permute-done((bf16[128,2048]{0,1:T(8,128)(2,1)S(1)}, bf16[128,2048]{0,1:T(8,128)(2,1)S(1)}, u32[]{:S(2)}, u32[]{:S(2)}) %collective-permute-start) | collective-permute-done | bytes 524320 | tf_op jit(solution)/shard_map/while/body/eval_jaxpr/ppermute | solution.py:16
  89.3 81.1 %while.145 = (s32[]{:T(128)}, bf16[128,2048]{0,1:T(8,128)(2,1)S(1)}, f32[4,128,2048]{1,2,0:T(8,128)}, f32[4,128,1]{1,2,0:T(1,128)S(1)}, bf16[4,128,16,128]{3,2,1...) while((s32[]{:T(128)}, bf16[128,2048]{0,1:T(8,128)(2,1)S(1)}, ...), condition=%wide.region_16.17_spmd.clone, body=%wide.region_9.16_spmd.clone.sunk | while | flops 1216641408 | bytes 26020924 | solution.py:180
  89.3 11.3 %conditional.23 = (bf16[128,2048]{0,1:T(8,128)(2,1)S(1)}, f32[4,128,2048]{1,2,0:T(8,128)}, f32[4,128,1]{1,2,0:T(1,128)S(1)}, bf16[4,128,16,128]{3,2,1,0:T(8,128)...) conditional(s32[]{:T(128)} %convert_element_type.806, ...), branch_computations={%region_10.10_spmd, %region_11.15_spmd} | conditional | flops 1216641408 | bytes 23923316 | solution.py:171
  89.9 4.7 convolution_convert_fusion.1
  100.7 4.5 collective-permute-start.1
  105.1 8.7 %collective-permute-done.1 = bf16[128,2048]{0,1:T(8,128)(2,1)S(1)} collective-permute-done((bf16[128,2048]{0,1:T(8,128)(2,1)S(1)}, bf16[128,2048]{0,1:T(8,128)(2,1)S(1)}, u32[]{:S(2)}, u32[]{:S(2)}) %collective-permute-start.1) | collective-permute-done | bytes 524320 | tf_op jit(solution)/shard_map/while/body/eval_jaxpr/ppermute | solution.py:16
  114.0 15.7 %collective-permute-start.1 = (bf16[128,2048]{0,1:T(8,128)(2,1)S(1)}, bf16[128,2048]{0,1:T(8,128)(2,1)S(1)}, u32[]{:S(2)}, u32[]{:S(2)}) collective-permute-start(bf16[128,2048]{0,1:T(8,128)(2,1)S(1)} %get-tuple-element.4191), channel_id=1, source_target_pairs={{0,32},{32,64},{64,96},{96,128},{128,160},{160,192},{192,224},{1,3... | collective-permute-start | bytes 1572872 | tf_op jit(solution)/shard_map/while/body/eval_jaxpr/ppermute | solution.py:16
  129.6 7.8 collective-permute-done.1
  137.5 4.4 collective-permute-start.1
  141.9 6.9 collective-permute-done.1
  148.9 14.8 %collective-permute-start.1 = (bf16[128,2048]{0,1:T(8,128)(2,1)S(1)}, bf16[128,2048]{0,1:T(8,128)(2,1)S(1)}, u32[]{:S(2)}, u32[]{:S(2)}) collective-permute-start(bf16[128,2048]{0,1:T(8,128)(2,1)S(1)} %get-tuple-element.4191), channel_id=1, source_target_pairs={{0,32},{32,64},{64,96},{96,128},{128,160},{160,192},{192,224},{1,3... | collective-permute-start | bytes 1572872 | tf_op jit(solution)/shard_map/while/body/eval_jaxpr/ppermute | solution.py:16
  163.8 6.6 collective-permute-done.1
  174.0 5.4 copy.213
  179.5 17.7 %conditional.8 = (bf16[1024,512]{1,0:T(8,128)(2,1)}, bf16[1024,512]{1,0:T(8,128)(2,1)}) conditional(s32[]{:T(128)} %convert_element_type.455, () %tuple.251, (f32[4,128,2048]{1,2,0:T(8,128)}, s32[]{:T(128)}) %tuple.288), branch_computations={%region_25.26_spmd, %region_26.27_spmd} | conditional | flops 1048583 | bytes 23068772 | solution.py:233
  181.9 9.8 %copy.251 = bf16[4,128,2048]{1,0,2:T(4,128)(2,1)S(1)} copy(bf16[4,128,2048]{1,2,0:T(8,128)(2,1)S(1)} %convert_element_type.483) | data formatting | bytes 4194304 | tf_op jit(solution)/shard_map/cond
  197.2 6.0 copy.211
  205.8 4.5 copy.212
  212.0 4.8 while.147
  216.7 289.0 %while.148 = (s32[]{:T(128)}, bf16[128,2048]{1,0:T(8,128)(2,1)S(1)}, bf16[4,128,2048]{1,2,0:T(8,128)(2,1)}, s32[]{:T(128)}, pred[]{:T(512)}, /*index=5*/bf16[4,1...) while((s32[]{:T(128)}, bf16[128,2048]{1,0:T(8,128)(2,1)S(1)}, ...), condition=%wide.region_42.43_spmd.clone, body=%wide.region_36.42_spmd.clone.sunk | while | flops 1353218048 | bytes 71172632 | solution.py:241
  219.1 13.8 %collective-permute-done.4 = bf16[128,2048]{1,0:T(8,128)(2,1)S(1)} collective-permute-done((bf16[128,2048]{1,0:T(8,128)(2,1)}, bf16[128,2048]{1,0:T(8,128)(2,1)S(1)}, u32[]{:S(2)}, u32[]{:S(2)}) %collective-permute-start.4) | collective-permute-done | bytes 524320 | tf_op jit(solution)/shard_map/while/body/eval_jaxpr/ppermute | solution.py:16
  235.0 27.6 %collective-permute-done.4 = bf16[128,2048]{1,0:T(8,128)(2,1)S(1)} collective-permute-done((bf16[128,2048]{1,0:T(8,128)(2,1)}, bf16[128,2048]{1,0:T(8,128)(2,1)S(1)}, u32[]{:S(2)}, u32[]{:S(2)}) %collective-permute-start.4) | collective-permute-done | bytes 524320 | tf_op jit(solution)/shard_map/while/body/eval_jaxpr/ppermute | solution.py:16
  264.7 16.5 %collective-permute-done.4 = bf16[128,2048]{1,0:T(8,128)(2,1)S(1)} collective-permute-done((bf16[128,2048]{1,0:T(8,128)(2,1)}, bf16[128,2048]{1,0:T(8,128)(2,1)S(1)}, u32[]{:S(2)}, u32[]{:S(2)}) %collective-permute-start.4) | collective-permute-done | bytes 524320 | tf_op jit(solution)/shard_map/while/body/eval_jaxpr/ppermute | solution.py:16
  283.4 222.3 %collective-permute-done.4 = bf16[128,2048]{1,0:T(8,128)(2,1)S(1)} collective-permute-done((bf16[128,2048]{1,0:T(8,128)(2,1)}, bf16[128,2048]{1,0:T(8,128)(2,1)S(1)}, u32[]{:S(2)}, u32[]{:S(2)}) %collective-permute-start.4) | collective-permute-done | bytes 524320 | tf_op jit(solution)/shard_map/while/body/eval_jaxpr/ppermute | solution.py:16
  505.7 129.2 %while.149 = (s32[]{:T(128)}, bf16[128,2048]{1,0:T(8,128)(2,1)S(1)}, bf16[4,128,2048]{1,2,0:T(8,128)(2,1)}, s32[]{:T(128)}, pred[]{:T(512)}, /*index=5*/bf16[4,1...) while((s32[]{:T(128)}, bf16[128,2048]{1,0:T(8,128)(2,1)S(1)}, ...), condition=%wide.region_49.50_spmd.clone, body=%wide.region_43.49_spmd.clone.sunk | while | flops 1353218048 | bytes 71172632 | solution.py:241
  505.7 16.7 %conditional.27 = (bf16[128,2048]{1,0:T(8,128)(2,1)}, bf16[4,128,2048]{1,2,0:T(8,128)(2,1)}) conditional(s32[]{:T(128)} %convert_element_type.810, bf16[4,128,2048]{1,2,0:T(8,128)(2,1)} %get-tuple-element.4649, (pred[]{:T(512)}, s32[]{:T(128)}, bf16[4,128,2048]{2,1,0:T(8,128)(2,1)}, bf16[128,2048]{1,0:T(8,128)(2,1)S(1)}, ...), branch_computations={%region_44.44_spmd, %region_45.48_spmd} | conditional | flops 1353218048 | bytes 69075104 | solution.py:207
  523.6 15.9 %collective-permute-done.5 = bf16[128,2048]{1,0:T(8,128)(2,1)S(1)} collective-permute-done((bf16[128,2048]{1,0:T(8,128)(2,1)}, bf16[128,2048]{1,0:T(8,128)(2,1)S(1)}, u32[]{:S(2)}, u32[]{:S(2)}) %collective-permute-start.5) | collective-permute-done | bytes 524320 | tf_op jit(solution)/shard_map/while/body/eval_jaxpr/ppermute | solution.py:16
  539.6 16.7 %conditional.27 = (bf16[128,2048]{1,0:T(8,128)(2,1)}, bf16[4,128,2048]{1,2,0:T(8,128)(2,1)}) conditional(s32[]{:T(128)} %convert_element_type.810, bf16[4,128,2048]{1,2,0:T(8,128)(2,1)} %get-tuple-element.4649, (pred[]{:T(512)}, s32[]{:T(128)}, bf16[4,128,2048]{2,1,0:T(8,128)(2,1)}, bf16[128,2048]{1,0:T(8,128)(2,1)S(1)}, ...), branch_computations={%region_44.44_spmd, %region_45.48_spmd} | conditional | flops 1353218048 | bytes 69075104 | solution.py:207
  557.5 16.1 %collective-permute-done.5 = bf16[128,2048]{1,0:T(8,128)(2,1)S(1)} collective-permute-done((bf16[128,2048]{1,0:T(8,128)(2,1)}, bf16[128,2048]{1,0:T(8,128)(2,1)S(1)}, u32[]{:S(2)}, u32[]{:S(2)}) %collective-permute-start.5) | collective-permute-done | bytes 524320 | tf_op jit(solution)/shard_map/while/body/eval_jaxpr/ppermute | solution.py:16
  573.6 16.7 %conditional.27 = (bf16[128,2048]{1,0:T(8,128)(2,1)}, bf16[4,128,2048]{1,2,0:T(8,128)(2,1)}) conditional(s32[]{:T(128)} %convert_element_type.810, bf16[4,128,2048]{1,2,0:T(8,128)(2,1)} %get-tuple-element.4649, (pred[]{:T(512)}, s32[]{:T(128)}, bf16[4,128,2048]{2,1,0:T(8,128)(2,1)}, bf16[128,2048]{1,0:T(8,128)(2,1)S(1)}, ...), branch_computations={%region_44.44_spmd, %region_45.48_spmd} | conditional | flops 1353218048 | bytes 69075104 | solution.py:207
  591.6 15.3 %collective-permute-done.5 = bf16[128,2048]{1,0:T(8,128)(2,1)S(1)} collective-permute-done((bf16[128,2048]{1,0:T(8,128)(2,1)}, bf16[128,2048]{1,0:T(8,128)(2,1)S(1)}, u32[]{:S(2)}, u32[]{:S(2)}) %collective-permute-start.5) | collective-permute-done | bytes 524320 | tf_op jit(solution)/shard_map/while/body/eval_jaxpr/ppermute | solution.py:16
  606.9 16.7 %conditional.27 = (bf16[128,2048]{1,0:T(8,128)(2,1)}, bf16[4,128,2048]{1,2,0:T(8,128)(2,1)}) conditional(s32[]{:T(128)} %convert_element_type.810, bf16[4,128,2048]{1,2,0:T(8,128)(2,1)} %get-tuple-element.4649, (pred[]{:T(512)}, s32[]{:T(128)}, bf16[4,128,2048]{2,1,0:T(8,128)(2,1)}, bf16[128,2048]{1,0:T(8,128)(2,1)S(1)}, ...), branch_computations={%region_44.44_spmd, %region_45.48_spmd} | conditional | flops 1353218048 | bytes 69075104 | solution.py:207
  624.8 10.0 %collective-permute-done.5 = bf16[128,2048]{1,0:T(8,128)(2,1)S(1)} collective-permute-done((bf16[128,2048]{1,0:T(8,128)(2,1)}, bf16[128,2048]{1,0:T(8,128)(2,1)S(1)}, u32[]{:S(2)}, u32[]{:S(2)}) %collective-permute-start.5) | collective-permute-done | bytes 524320 | tf_op jit(solution)/shard_map/while/body/eval_jaxpr/ppermute | solution.py:16
  644.7 6.6 fusion.213
  661.4 43.1 %collective-permute-done.10 = bf16[256,2048]{1,0:T(8,128)(2,1)} collective-permute-done((bf16[256,2048]{1,0:T(8,128)(2,1)}, bf16[256,2048]{1,0:T(8,128)(2,1)}, u32[]{:S(2)}, u32[]{:S(2)}) %collective-permute-start.10) | collective-permute-done | bytes 1048608 | tf_op jit(solution)/shard_map/ppermute | solution.py:33
  711.0 55.7 %collective-permute-start.12 = (bf16[64,2048]{1,0:T(8,128)(2,1)S(1)}, bf16[64,2048]{1,0:T(8,128)(2,1)S(1)}, u32[]{:S(2)}, u32[]{:S(2)}) collective-permute-start(bf16[64,2048]{1,0:T(8,128)(2,1)S(1)} %get-tuple-element.3632), channel_id=1, source_target_pairs={{0,16},{8,24},{16,0},{24,8},{1,17},{9,25},{17,1},{25,9},{2,18},{10... | collective-permute-start | bytes 786440 | tf_op jit(solution)/shard_map/ppermute | solution.py:33
  766.7 4.3 collective-permute-done.11
  771.1 18.0 %collective-permute-done.12 = bf16[64,2048]{1,0:T(8,128)(2,1)S(1)} collective-permute-done((bf16[64,2048]{1,0:T(8,128)(2,1)S(1)}, bf16[64,2048]{1,0:T(8,128)(2,1)S(1)}, u32[]{:S(2)}, u32[]{:S(2)}) %collective-permute-start.12) | collective-permute-done | bytes 262176 | tf_op jit(solution)/shard_map/ppermute | solution.py:33
  (262 shorter events, 180.9 us)
Async XLA Ops:
  9.8 3.3 copy-start.4
  9.8 3.3 copy-start.6
  24.7 12.7 %collective-permute-start = (bf16[128,2048]{0,1:T(8,128)(2,1)S(1)}, bf16[128,2048]{0,1:T(8,128)(2,1)S(1)}, u32[]{:S(2)}, u32[]{:S(2)}) collective-permute-start(bf16[128,2048]{0,1:T(8,128)(2,1)S(1)} %get-tuple-element.4167), channel_id=1, source_target_pairs={{0,32},{32,64},{64,96},{1,33},{33,65},{65,97},{2,34},{34,66},{66,9... | collective-permute-start | bytes 1572872 | tf_op jit(solution)/shard_map/while/body/eval_jaxpr/ppermute | solution.py:16
  48.7 15.2 %collective-permute-start = (bf16[128,2048]{0,1:T(8,128)(2,1)S(1)}, bf16[128,2048]{0,1:T(8,128)(2,1)S(1)}, u32[]{:S(2)}, u32[]{:S(2)}) collective-permute-start(bf16[128,2048]{0,1:T(8,128)(2,1)S(1)} %get-tuple-element.4167), channel_id=1, source_target_pairs={{0,32},{32,64},{64,96},{1,33},{33,65},{65,97},{2,34},{34,66},{66,9... | collective-permute-start | bytes 1572872 | tf_op jit(solution)/shard_map/while/body/eval_jaxpr/ppermute | solution.py:16
  75.3 14.0 %collective-permute-start = (bf16[128,2048]{0,1:T(8,128)(2,1)S(1)}, bf16[128,2048]{0,1:T(8,128)(2,1)S(1)}, u32[]{:S(2)}, u32[]{:S(2)}) collective-permute-start(bf16[128,2048]{0,1:T(8,128)(2,1)S(1)} %get-tuple-element.4167), channel_id=1, source_target_pairs={{0,32},{32,64},{64,96},{1,33},{33,65},{65,97},{2,34},{34,66},{66,9... | collective-permute-start | bytes 1572872 | tf_op jit(solution)/shard_map/while/body/eval_jaxpr/ppermute | solution.py:16
  100.7 13.2 %collective-permute-start.1 = (bf16[128,2048]{0,1:T(8,128)(2,1)S(1)}, bf16[128,2048]{0,1:T(8,128)(2,1)S(1)}, u32[]{:S(2)}, u32[]{:S(2)}) collective-permute-start(bf16[128,2048]{0,1:T(8,128)(2,1)S(1)} %get-tuple-element.4191), channel_id=1, source_target_pairs={{0,32},{32,64},{64,96},{96,128},{128,160},{160,192},{192,224},{1,3... | collective-permute-start | bytes 1572872 | tf_op jit(solution)/shard_map/while/body/eval_jaxpr/ppermute | solution.py:16
  114.0 23.5 %collective-permute-start.1 = (bf16[128,2048]{0,1:T(8,128)(2,1)S(1)}, bf16[128,2048]{0,1:T(8,128)(2,1)S(1)}, u32[]{:S(2)}, u32[]{:S(2)}) collective-permute-start(bf16[128,2048]{0,1:T(8,128)(2,1)S(1)} %get-tuple-element.4191), channel_id=1, source_target_pairs={{0,32},{32,64},{64,96},{96,128},{128,160},{160,192},{192,224},{1,3... | collective-permute-start | bytes 1572872 | tf_op jit(solution)/shard_map/while/body/eval_jaxpr/ppermute | solution.py:16
  137.5 11.3 %collective-permute-start.1 = (bf16[128,2048]{0,1:T(8,128)(2,1)S(1)}, bf16[128,2048]{0,1:T(8,128)(2,1)S(1)}, u32[]{:S(2)}, u32[]{:S(2)}) collective-permute-start(bf16[128,2048]{0,1:T(8,128)(2,1)S(1)} %get-tuple-element.4191), channel_id=1, source_target_pairs={{0,32},{32,64},{64,96},{96,128},{128,160},{160,192},{192,224},{1,3... | collective-permute-start | bytes 1572872 | tf_op jit(solution)/shard_map/while/body/eval_jaxpr/ppermute | solution.py:16
  148.9 21.5 %collective-permute-start.1 = (bf16[128,2048]{0,1:T(8,128)(2,1)S(1)}, bf16[128,2048]{0,1:T(8,128)(2,1)S(1)}, u32[]{:S(2)}, u32[]{:S(2)}) collective-permute-start(bf16[128,2048]{0,1:T(8,128)(2,1)S(1)} %get-tuple-element.4191), channel_id=1, source_target_pairs={{0,32},{32,64},{64,96},{96,128},{128,160},{160,192},{192,224},{1,3... | collective-permute-start | bytes 1572872 | tf_op jit(solution)/shard_map/while/body/eval_jaxpr/ppermute | solution.py:16
  170.7 0.7 collective-permute-start.2
  171.6 0.7 collective-permute-start.2
  172.4 0.7 collective-permute-start.2
  173.3 0.7 collective-permute-start.2
  197.2 6.0 copy-start.3
  212.8 0.7 collective-permute-start.3
  214.4 0.7 collective-permute-start.3
  216.0 0.7 collective-permute-start.3
  217.8 15.1 %collective-permute-start.4 = (bf16[128,2048]{1,0:T(8,128)(2,1)}, bf16[128,2048]{1,0:T(8,128)(2,1)S(1)}, u32[]{:S(2)}, u32[]{:S(2)}) collective-permute-start(bf16[128,2048]{1,0:T(8,128)(2,1)} %get-tuple-element.4254), channel_id=1, source_target_pairs={{32,0},{64,32},{96,64},{128,96},{160,128},{192,160},{224,192},{33,... | collective-permute-start | bytes 1572872 | tf_op jit(solution)/shard_map/while/body/eval_jaxpr/ppermute | solution.py:16
  233.7 28.8 %collective-permute-start.4 = (bf16[128,2048]{1,0:T(8,128)(2,1)}, bf16[128,2048]{1,0:T(8,128)(2,1)S(1)}, u32[]{:S(2)}, u32[]{:S(2)}) collective-permute-start(bf16[128,2048]{1,0:T(8,128)(2,1)} %get-tuple-element.4254), channel_id=1, source_target_pairs={{32,0},{64,32},{96,64},{128,96},{160,128},{192,160},{224,192},{33,... | collective-permute-start | bytes 1572872 | tf_op jit(solution)/shard_map/while/body/eval_jaxpr/ppermute | solution.py:16
  263.4 17.8 %collective-permute-start.4 = (bf16[128,2048]{1,0:T(8,128)(2,1)}, bf16[128,2048]{1,0:T(8,128)(2,1)S(1)}, u32[]{:S(2)}, u32[]{:S(2)}) collective-permute-start(bf16[128,2048]{1,0:T(8,128)(2,1)} %get-tuple-element.4254), channel_id=1, source_target_pairs={{32,0},{64,32},{96,64},{128,96},{160,128},{192,160},{224,192},{33,... | collective-permute-start | bytes 1572872 | tf_op jit(solution)/shard_map/while/body/eval_jaxpr/ppermute | solution.py:16
  282.1 223.6 %collective-permute-start.4 = (bf16[128,2048]{1,0:T(8,128)(2,1)}, bf16[128,2048]{1,0:T(8,128)(2,1)S(1)}, u32[]{:S(2)}, u32[]{:S(2)}) collective-permute-start(bf16[128,2048]{1,0:T(8,128)(2,1)} %get-tuple-element.4254), channel_id=1, source_target_pairs={{32,0},{64,32},{96,64},{128,96},{160,128},{192,160},{224,192},{33,... | collective-permute-start | bytes 1572872 | tf_op jit(solution)/shard_map/while/body/eval_jaxpr/ppermute | solution.py:16
  508.8 1.9 copy-start.2
  510.7 4.8 slice-start.4
  511.4 4.1 slice-start.5
  522.4 17.2 %collective-permute-start.5 = (bf16[128,2048]{1,0:T(8,128)(2,1)}, bf16[128,2048]{1,0:T(8,128)(2,1)S(1)}, u32[]{:S(2)}, u32[]{:S(2)}) collective-permute-start(bf16[128,2048]{1,0:T(8,128)(2,1)} %get-tuple-element.4271), channel_id=1, source_target_pairs={{32,0},{64,32},{96,64},{33,1},{65,33},{97,65},{34,2},{66,34},{98,6... | collective-permute-start | bytes 1572872 | tf_op jit(solution)/shard_map/while/body/eval_jaxpr/ppermute | solution.py:16
  542.7 1.9 copy-start.2
  544.6 4.8 slice-start.4
  545.3 4.1 slice-start.5
  556.3 17.3 %collective-permute-start.5 = (bf16[128,2048]{1,0:T(8,128)(2,1)}, bf16[128,2048]{1,0:T(8,128)(2,1)S(1)}, u32[]{:S(2)}, u32[]{:S(2)}) collective-permute-start(bf16[128,2048]{1,0:T(8,128)(2,1)} %get-tuple-element.4271), channel_id=1, source_target_pairs={{32,0},{64,32},{96,64},{33,1},{65,33},{97,65},{34,2},{66,34},{98,6... | collective-permute-start | bytes 1572872 | tf_op jit(solution)/shard_map/while/body/eval_jaxpr/ppermute | solution.py:16
  576.7 1.9 copy-start.2
  578.6 4.8 slice-start.4
  579.3 4.1 slice-start.5
  590.3 16.6 %collective-permute-start.5 = (bf16[128,2048]{1,0:T(8,128)(2,1)}, bf16[128,2048]{1,0:T(8,128)(2,1)S(1)}, u32[]{:S(2)}, u32[]{:S(2)}) collective-permute-start(bf16[128,2048]{1,0:T(8,128)(2,1)} %get-tuple-element.4271), channel_id=1, source_target_pairs={{32,0},{64,32},{96,64},{33,1},{65,33},{97,65},{34,2},{66,34},{98,6... | collective-permute-start | bytes 1572872 | tf_op jit(solution)/shard_map/while/body/eval_jaxpr/ppermute | solution.py:16
  610.0 1.9 copy-start.2
  611.9 4.8 slice-start.4
  612.6 4.1 slice-start.5
  623.6 11.3 %collective-permute-start.5 = (bf16[128,2048]{1,0:T(8,128)(2,1)}, bf16[128,2048]{1,0:T(8,128)(2,1)S(1)}, u32[]{:S(2)}, u32[]{:S(2)}) collective-permute-start(bf16[128,2048]{1,0:T(8,128)(2,1)} %get-tuple-element.4271), channel_id=1, source_target_pairs={{32,0},{64,32},{96,64},{33,1},{65,33},{97,65},{34,2},{66,34},{98,6... | collective-permute-start | bytes 1572872 | tf_op jit(solution)/shard_map/while/body/eval_jaxpr/ppermute | solution.py:16
  639.0 5.7 collective-permute-start.7
  640.2 4.4 collective-permute-start.6
  651.2 3.2 copy-start.5
  655.9 48.5 %collective-permute-start.10 = (bf16[256,2048]{1,0:T(8,128)(2,1)}, bf16[256,2048]{1,0:T(8,128)(2,1)}, u32[]{:S(2)}, u32[]{:S(2)}) collective-permute-start(bf16[256,2048]{1,0:T(8,128)(2,1)} %get-tuple-element.3628), channel_id=1, source_target_pairs={{0,6},{2,0},{4,2},{6,4},{1,7},{3,1},{5,3},{7,5},{8,14},{10,8},{12,... | collective-permute-start | bytes 3145736 | tf_op jit(solution)/shard_map/ppermute | solution.py:33
  659.0 48.7 %collective-permute-start.8 = (bf16[256,2048]{1,0:T(8,128)(2,1)S(1)}, bf16[256,2048]{1,0:T(8,128)(2,1)}, u32[]{:S(2)}, u32[]{:S(2)}) collective-permute-start(bf16[256,2048]{1,0:T(8,128)(2,1)S(1)} %get-tuple-element.3627), channel_id=1, source_target_pairs={{0,2},{2,4},{4,6},{6,0},{1,3},{3,5},{5,7},{7,1},{8,10},{10,12},{12... | collective-permute-start | bytes 3145736 | tf_op jit(solution)/shard_map/ppermute | solution.py:33
  659.0 48.7 %collective-permute-start.9 = (bf16[256,2048]{1,0:T(8,128)(2,1)S(1)}, bf16[256,2048]{1,0:T(8,128)(2,1)}, u32[]{:S(2)}, u32[]{:S(2)}) collective-permute-start(bf16[256,2048]{1,0:T(8,128)(2,1)S(1)} %get-tuple-element.3629), channel_id=1, source_target_pairs={{0,4},{2,6},{4,0},{6,2},{1,5},{3,7},{5,1},{7,3},{8,12},{10,14},{12... | collective-permute-start | bytes 3145736 | tf_op jit(solution)/shard_map/ppermute | solution.py:33
  710.9 60.1 %collective-permute-start.11 = (bf16[64,2048]{1,0:T(8,128)(2,1)S(1)}, bf16[64,2048]{1,0:T(8,128)(2,1)S(1)}, u32[]{:S(2)}, u32[]{:S(2)}) collective-permute-start(bf16[64,2048]{1,0:T(8,128)(2,1)S(1)} %get-tuple-element.3630), channel_id=1, source_target_pairs={{0,8},{8,16},{16,24},{24,0},{1,9},{9,17},{17,25},{25,1},{2,10},{10... | collective-permute-start | bytes 786440 | tf_op jit(solution)/shard_map/ppermute | solution.py:33
  711.0 78.1 %collective-permute-start.12 = (bf16[64,2048]{1,0:T(8,128)(2,1)S(1)}, bf16[64,2048]{1,0:T(8,128)(2,1)S(1)}, u32[]{:S(2)}, u32[]{:S(2)}) collective-permute-start(bf16[64,2048]{1,0:T(8,128)(2,1)S(1)} %get-tuple-element.3632), channel_id=1, source_target_pairs={{0,16},{8,24},{16,0},{24,8},{1,17},{9,25},{17,1},{25,9},{2,18},{10... | collective-permute-start | bytes 786440 | tf_op jit(solution)/shard_map/ppermute | solution.py:33
  766.7 22.3 %collective-permute-start.13 = (bf16[64,2048]{1,0:T(8,128)(2,1)S(1)}, bf16[64,2048]{1,0:T(8,128)(2,1)}, u32[]{:S(2)}, u32[]{:S(2)}) collective-permute-start(bf16[64,2048]{1,0:T(8,128)(2,1)S(1)} %get-tuple-element.3631), channel_id=1, source_target_pairs={{0,24},{8,0},{16,8},{24,16},{1,25},{9,1},{17,9},{25,17},{2,26},{10... | collective-permute-start | bytes 786440 | tf_op jit(solution)/shard_map/ppermute | solution.py:33

commit v14 on v12

--- a/solution.py
+++ b/solution.py
@@ -159,10 +159,16 @@
                     for whole_array, new_piece in zip(stash_in, kept_parts)
                 )
             )
-            predicted = jnp.sum(output.astype(jnp.float32) * readout, axis=-1)
-            misfit = predicted - lax.dynamic_index_in_dim(targets, slot, 0, keepdims=True)
-            cotangent = (misfit[..., None] * readout).astype(jnp.bfloat16)
-            upstream_out = lax.dynamic_update_index_in_dim(upstream_in, cotangent, slot, 0)
+
+            def loss_grad(upstream_kept):
+                predicted = jnp.sum(output.astype(jnp.float32) * readout, axis=-1)
+                misfit = predicted - lax.dynamic_index_in_dim(targets, slot, 0, keepdims=True)
+                cotangent = (misfit[..., None] * readout).astype(jnp.bfloat16)
+                return lax.dynamic_update_index_in_dim(upstream_kept, cotangent, slot, 0)
+
+            upstream_out = lax.cond(
+                rank == sections - 1, loss_grad, lambda upstream_kept: upstream_kept, upstream_in
+            )
             return (output[0], stash_out, upstream_out)
 
         def forward_no_work(stash_in, upstream_in):

time: 799 us -> 829 us (1.038)
  starting transfers between devices: 111 us -> 130 us
  waiting for transfers between devices: 486 us -> 501 us
    ppermute x6, starting transfers between devices: 46 us -> 62 us  [scatter_sum(): received = lax.ppermute(sent.astype(jnp.bfloat16), axis, route)]
    ppermute x22, waiting for transfers between devices: 415 us -> 429 us  [passed_along(): return lax.ppermute(block, axis, [(i, i + distance) for i in senders])]
    unnamed x13 -> x8, local copies, waits for them, and re-layouts: 24.4 us -> 13.1 us
  transfers between devices with their start and end apart: 30 -> 30, of which waited for: 20 -> 20; matrix products, arithmetic and copies ran while one was open for 3% -> 1% of each run, Pallas kernels for 0% -> 0%
where the time goes in v14:
time: 829 us; the launch traced here: 820 us
  waiting for transfers between devices  501 us (60%)
  starting transfers between devices  130 us (16%)
  matrix products  73.7 us (9%)
  local copies, waits for them, and re-layouts  65.5 us (8%)
  other arithmetic  47.7 us (6%)
    ppermute x22, waiting for transfers between devices, passed_along(): return lax.ppermute(block, axis, [(i, i + distance) for i in senders])  429 us
    ppermute x6, waiting for transfers between devices, scatter_sum(): received = lax.ppermute(sent.astype(jnp.bfloat16), axis, route)  69.3 us
    ppermute x22, starting transfers between devices, passed_along(): return lax.ppermute(block, axis, [(i, i + distance) for i in senders])  67.6 us
    ppermute x6, starting transfers between devices, scatter_sum(): received = lax.ppermute(sent.astype(jnp.bfloat16), axis, route)  62 us
    dot_general x4, matrix products, layer_forward(): jnp.dot(normed.reshape(-1, width), weight, preferred_element_type=jnp.flo...  18.8 us
    dot_general x4, matrix products, layer_backward(): lax.dot_general(value_total.reshape(-1, width), weight, (((1,), (1,)), ((...  16.7 us
  transfers between devices with their start and end apart: 30, of which 20 were waited for; matrix products, arithmetic and copies ran while one was open for 1% of the time, Pallas kernels for 0%

profile of v14, /device:TPU:96, one launch (start us, length us, event | category | flops | bytes accessed | tf_op | source)
XLA Modules:
  0.0 820.1 jit_solution(12778842790649225856)
XLA Ops:
  10.3 84.5 %while.153 = (s32[]{:T(128)}, bf16[128,2048]{1,0:T(8,128)(2,1)S(1)}, f32[4,128,2048]{2,1,0:T(8,128)}, f32[4,128,1]{1,2,0:T(1,128)S(1)}, bf16[4,128,16,128]{3,2,1...) while((s32[]{:T(128)}, bf16[128,2048]{1,0:T(8,128)(2,1)S(1)}, ...), condition=%wide.region_10.11_spmd.clone, body=%wide.region_1.10_spmd.clone.sunk | while | flops 1216641408 | bytes 28643968 | solution.py:186
  10.3 14.0 %conditional.21 = (bf16[128,2048]{1,0:T(8,128)(2,1)}, f32[4,128,2048]{2,1,0:T(8,128)}, f32[4,128,1]{1,2,0:T(1,128)S(1)}, bf16[4,128,16,128]{3,2,1,0:T(8,128)(2,1...) conditional(s32[]{:T(128)} %convert_element_type.791, ...), branch_computations={%region_2.2_spmd, %region_3.9_spmd} | conditional | flops 1216641408 | bytes 26546374 | solution.py:177
  12.0 4.7 convolution_convert_fusion
  25.7 11.7 %collective-permute-done = bf16[128,2048]{1,0:T(8,128)(2,1)S(1)} collective-permute-done((bf16[128,2048]{1,0:T(8,128)(2,1)}, bf16[128,2048]{1,0:T(8,128)(2,1)S(1)}, u32[]{:S(2)}, u32[]{:S(2)}) %collective-permute-start) | collective-permute-done | bytes 524320 | tf_op jit(solution)/shard_map/while/body/eval_jaxpr/ppermute | solution.py:16
  37.4 13.9 %conditional.21 = (bf16[128,2048]{1,0:T(8,128)(2,1)}, f32[4,128,2048]{2,1,0:T(8,128)}, f32[4,128,1]{1,2,0:T(1,128)S(1)}, bf16[4,128,16,128]{3,2,1,0:T(8,128)(2,1...) conditional(s32[]{:T(128)} %convert_element_type.791, ...), branch_computations={%region_2.2_spmd, %region_3.9_spmd} | conditional | flops 1216641408 | bytes 26546374 | solution.py:177
  39.0 4.7 convolution_convert_fusion
  51.3 4.4 collective-permute-start
  55.7 10.9 %collective-permute-done = bf16[128,2048]{1,0:T(8,128)(2,1)S(1)} collective-permute-done((bf16[128,2048]{1,0:T(8,128)(2,1)}, bf16[128,2048]{1,0:T(8,128)(2,1)S(1)}, u32[]{:S(2)}, u32[]{:S(2)}) %collective-permute-start) | collective-permute-done | bytes 524320 | tf_op jit(solution)/shard_map/while/body/eval_jaxpr/ppermute | solution.py:16
  66.6 13.9 %conditional.21 = (bf16[128,2048]{1,0:T(8,128)(2,1)}, f32[4,128,2048]{2,1,0:T(8,128)}, f32[4,128,1]{1,2,0:T(1,128)S(1)}, bf16[4,128,16,128]{3,2,1,0:T(8,128)(2,1...) conditional(s32[]{:T(128)} %convert_element_type.791, ...), branch_computations={%region_2.2_spmd, %region_3.9_spmd} | conditional | flops 1216641408 | bytes 26546374 | solution.py:177
  68.2 4.7 convolution_convert_fusion
  80.6 4.3 collective-permute-start
  84.9 10.0 %collective-permute-done = bf16[128,2048]{1,0:T(8,128)(2,1)S(1)} collective-permute-done((bf16[128,2048]{1,0:T(8,128)(2,1)}, bf16[128,2048]{1,0:T(8,128)(2,1)S(1)}, u32[]{:S(2)}, u32[]{:S(2)}) %collective-permute-start) | collective-permute-done | bytes 524320 | tf_op jit(solution)/shard_map/while/body/eval_jaxpr/ppermute | solution.py:16
  94.8 90.4 %while.154 = (s32[]{:T(128)}, bf16[128,2048]{1,0:T(8,128)(2,1)S(1)}, f32[4,128,2048]{2,1,0:T(8,128)}, f32[4,128,1]{1,2,0:T(1,128)S(1)}, bf16[4,128,16,128]{3,2,1...) while((s32[]{:T(128)}, bf16[128,2048]{1,0:T(8,128)(2,1)S(1)}, ...), condition=%wide.region_20.21_spmd.clone, body=%wide.region_11.20_spmd.clone.sunk | while | flops 1216641408 | bytes 28643988 | solution.py:186
  94.8 13.9 %conditional.22 = (bf16[128,2048]{1,0:T(8,128)(2,1)}, f32[4,128,2048]{2,1,0:T(8,128)}, f32[4,128,1]{1,2,0:T(1,128)S(1)}, bf16[4,128,16,128]{3,2,1,0:T(8,128)(2,1...) conditional(s32[]{:T(128)} %convert_element_type.792, ...), branch_computations={%region_12.12_spmd, %region_13.19_spmd} | conditional | flops 1216641408 | bytes 26546374 | solution.py:177
  96.4 4.7 convolution_convert_fusion.1
  108.8 4.3 collective-permute-start.1
  113.1 9.0 %collective-permute-done.1 = bf16[128,2048]{1,0:T(8,128)(2,1)S(1)} collective-permute-done((bf16[128,2048]{1,0:T(8,128)(2,1)}, bf16[128,2048]{1,0:T(8,128)(2,1)S(1)}, u32[]{:S(2)}, u32[]{:S(2)}) %collective-permute-start.1) | collective-permute-done | bytes 524320 | tf_op jit(solution)/shard_map/while/body/eval_jaxpr/ppermute | solution.py:16
  123.0 17.4 %collective-permute-start.1 = (bf16[128,2048]{1,0:T(8,128)(2,1)}, bf16[128,2048]{1,0:T(8,128)(2,1)S(1)}, u32[]{:S(2)}, u32[]{:S(2)}) collective-permute-start(bf16[128,2048]{1,0:T(8,128)(2,1)} %get-tuple-element.4132), channel_id=1, source_target_pairs={{0,32},{32,64},{64,96},{96,128},{128,160},{160,192},{192,224},{1,3... | collective-permute-start | bytes 1572872 | tf_op jit(solution)/shard_map/while/body/eval_jaxpr/ppermute | solution.py:16
  140.4 8.1 collective-permute-done.1
  149.4 4.3 collective-permute-start.1
  153.7 7.2 collective-permute-done.1
  161.7 16.5 %collective-permute-start.1 = (bf16[128,2048]{1,0:T(8,128)(2,1)}, bf16[128,2048]{1,0:T(8,128)(2,1)S(1)}, u32[]{:S(2)}, u32[]{:S(2)}) collective-permute-start(bf16[128,2048]{1,0:T(8,128)(2,1)} %get-tuple-element.4132), channel_id=1, source_target_pairs={{0,32},{32,64},{64,96},{96,128},{128,160},{160,192},{192,224},{1,3... | collective-permute-start | bytes 1572872 | tf_op jit(solution)/shard_map/while/body/eval_jaxpr/ppermute | solution.py:16
  178.3 7.0 collective-permute-done.1
  185.2 6.8 while.155
  192.1 5.4 copy.135
  197.4 4.5 copy.136
  203.6 4.8 while.156
  208.4 316.6 %while.157 = (s32[]{:T(128)}, bf16[128,2048]{1,0:T(8,128)(2,1)S(1)}, bf16[4,128,2048]{1,2,0:T(8,128)(2,1)}, s32[]{:T(128)}, pred[]{:T(512)}, /*index=5*/bf16[4,1...) while((s32[]{:T(128)}, bf16[128,2048]{1,0:T(8,128)(2,1)S(1)}, ...), condition=%wide.region_44.45_spmd.clone, body=%wide.region_38.44_spmd.clone.sunk | while | flops 1353218048 | bytes 71172632 | solution.py:239
  210.7 13.7 %collective-permute-done.4 = bf16[128,2048]{1,0:T(8,128)(2,1)S(1)} collective-permute-done((bf16[128,2048]{1,0:T(8,128)(2,1)}, bf16[128,2048]{1,0:T(8,128)(2,1)S(1)}, u32[]{:S(2)}, u32[]{:S(2)}) %collective-permute-start.4) | collective-permute-done | bytes 524320 | tf_op jit(solution)/shard_map/while/body/eval_jaxpr/ppermute | solution.py:16
  226.6 29.4 %collective-permute-done.4 = bf16[128,2048]{1,0:T(8,128)(2,1)S(1)} collective-permute-done((bf16[128,2048]{1,0:T(8,128)(2,1)}, bf16[128,2048]{1,0:T(8,128)(2,1)S(1)}, u32[]{:S(2)}, u32[]{:S(2)}) %collective-permute-start.4) | collective-permute-done | bytes 524320 | tf_op jit(solution)/shard_map/while/body/eval_jaxpr/ppermute | solution.py:16
  258.1 16.4 %collective-permute-done.4 = bf16[128,2048]{1,0:T(8,128)(2,1)S(1)} collective-permute-done((bf16[128,2048]{1,0:T(8,128)(2,1)}, bf16[128,2048]{1,0:T(8,128)(2,1)S(1)}, u32[]{:S(2)}, u32[]{:S(2)}) %collective-permute-start.4) | collective-permute-done | bytes 524320 | tf_op jit(solution)/shard_map/while/body/eval_jaxpr/ppermute | solution.py:16
  276.6 248.4 %collective-permute-done.4 = bf16[128,2048]{1,0:T(8,128)(2,1)S(1)} collective-permute-done((bf16[128,2048]{1,0:T(8,128)(2,1)}, bf16[128,2048]{1,0:T(8,128)(2,1)S(1)}, u32[]{:S(2)}, u32[]{:S(2)}) %collective-permute-start.4) | collective-permute-done | bytes 524320 | tf_op jit(solution)/shard_map/while/body/eval_jaxpr/ppermute | solution.py:16
  525.0 129.2 %while.158 = (s32[]{:T(128)}, bf16[128,2048]{1,0:T(8,128)(2,1)S(1)}, bf16[4,128,2048]{1,2,0:T(8,128)(2,1)}, s32[]{:T(128)}, pred[]{:T(512)}, /*index=5*/bf16[4,1...) while((s32[]{:T(128)}, bf16[128,2048]{1,0:T(8,128)(2,1)S(1)}, ...), condition=%wide.region_51.52_spmd.clone, body=%wide.region_45.51_spmd.clone.sunk | while | flops 1353218048 | bytes 71172632 | solution.py:239
  525.0 16.7 %conditional.26 = (bf16[128,2048]{1,0:T(8,128)(2,1)}, bf16[4,128,2048]{1,2,0:T(8,128)(2,1)}) conditional(s32[]{:T(128)} %convert_element_type.796, bf16[4,128,2048]{1,2,0:T(8,128)(2,1)} %get-tuple-element.4586, (pred[]{:T(512)}, s32[]{:T(128)}, bf16[4,128,2048]{2,1,0:T(8,128)(2,1)}, bf16[128,2048]{1,0:T(8,128)(2,1)S(1)}, ...), branch_computations={%region_46.46_spmd, %region_47.50_spmd} | conditional | flops 1353218048 | bytes 69075104 | solution.py:213
  542.9 15.9 %collective-permute-done.5 = bf16[128,2048]{1,0:T(8,128)(2,1)S(1)} collective-permute-done((bf16[128,2048]{1,0:T(8,128)(2,1)}, bf16[128,2048]{1,0:T(8,128)(2,1)S(1)}, u32[]{:S(2)}, u32[]{:S(2)}) %collective-permute-start.5) | collective-permute-done | bytes 524320 | tf_op jit(solution)/shard_map/while/body/eval_jaxpr/ppermute | solution.py:16
  558.9 16.7 %conditional.26 = (bf16[128,2048]{1,0:T(8,128)(2,1)}, bf16[4,128,2048]{1,2,0:T(8,128)(2,1)}) conditional(s32[]{:T(128)} %convert_element_type.796, bf16[4,128,2048]{1,2,0:T(8,128)(2,1)} %get-tuple-element.4586, (pred[]{:T(512)}, s32[]{:T(128)}, bf16[4,128,2048]{2,1,0:T(8,128)(2,1)}, bf16[128,2048]{1,0:T(8,128)(2,1)S(1)}, ...), branch_computations={%region_46.46_spmd, %region_47.50_spmd} | conditional | flops 1353218048 | bytes 69075104 | solution.py:213
  576.8 16.1 %collective-permute-done.5 = bf16[128,2048]{1,0:T(8,128)(2,1)S(1)} collective-permute-done((bf16[128,2048]{1,0:T(8,128)(2,1)}, bf16[128,2048]{1,0:T(8,128)(2,1)S(1)}, u32[]{:S(2)}, u32[]{:S(2)}) %collective-permute-start.5) | collective-permute-done | bytes 524320 | tf_op jit(solution)/shard_map/while/body/eval_jaxpr/ppermute | solution.py:16
  592.9 16.7 %conditional.26 = (bf16[128,2048]{1,0:T(8,128)(2,1)}, bf16[4,128,2048]{1,2,0:T(8,128)(2,1)}) conditional(s32[]{:T(128)} %convert_element_type.796, bf16[4,128,2048]{1,2,0:T(8,128)(2,1)} %get-tuple-element.4586, (pred[]{:T(512)}, s32[]{:T(128)}, bf16[4,128,2048]{2,1,0:T(8,128)(2,1)}, bf16[128,2048]{1,0:T(8,128)(2,1)S(1)}, ...), branch_computations={%region_46.46_spmd, %region_47.50_spmd} | conditional | flops 1353218048 | bytes 69075104 | solution.py:213
  610.9 15.3 %collective-permute-done.5 = bf16[128,2048]{1,0:T(8,128)(2,1)S(1)} collective-permute-done((bf16[128,2048]{1,0:T(8,128)(2,1)}, bf16[128,2048]{1,0:T(8,128)(2,1)S(1)}, u32[]{:S(2)}, u32[]{:S(2)}) %collective-permute-start.5) | collective-permute-done | bytes 524320 | tf_op jit(solution)/shard_map/while/body/eval_jaxpr/ppermute | solution.py:16
  626.2 16.7 %conditional.26 = (bf16[128,2048]{1,0:T(8,128)(2,1)}, bf16[4,128,2048]{1,2,0:T(8,128)(2,1)}) conditional(s32[]{:T(128)} %convert_element_type.796, bf16[4,128,2048]{1,2,0:T(8,128)(2,1)} %get-tuple-element.4586, (pred[]{:T(512)}, s32[]{:T(128)}, bf16[4,128,2048]{2,1,0:T(8,128)(2,1)}, bf16[128,2048]{1,0:T(8,128)(2,1)S(1)}, ...), branch_computations={%region_46.46_spmd, %region_47.50_spmd} | conditional | flops 1353218048 | bytes 69075104 | solution.py:213
  636.0 4.2 fusion.180
  644.2 10.0 %collective-permute-done.5 = bf16[128,2048]{1,0:T(8,128)(2,1)S(1)} collective-permute-done((bf16[128,2048]{1,0:T(8,128)(2,1)}, bf16[128,2048]{1,0:T(8,128)(2,1)S(1)}, u32[]{:S(2)}, u32[]{:S(2)}) %collective-permute-start.5) | collective-permute-done | bytes 524320 | tf_op jit(solution)/shard_map/while/body/eval_jaxpr/ppermute | solution.py:16
  654.2 4.2 copy.144
  673.4 6.2 fusion.210
  688.7 43.2 %collective-permute-done.10 = bf16[256,2048]{1,0:T(8,128)(2,1)} collective-permute-done((bf16[256,2048]{1,0:T(8,128)(2,1)S(1)}, bf16[256,2048]{1,0:T(8,128)(2,1)}, u32[]{:S(2)}, u32[]{:S(2)}) %collective-permute-start.10) | collective-permute-done | bytes 1048608 | tf_op jit(solution)/shard_map/ppermute | solution.py:33
  738.8 56.6 %collective-permute-start.12 = (bf16[64,2048]{1,0:T(8,128)(2,1)S(1)}, bf16[64,2048]{1,0:T(8,128)(2,1)S(1)}, u32[]{:S(2)}, u32[]{:S(2)}) collective-permute-start(bf16[64,2048]{1,0:T(8,128)(2,1)S(1)} %get-tuple-element.3571), channel_id=1, source_target_pairs={{0,16},{8,24},{16,0},{24,8},{1,17},{9,25},{17,1},{25,9},{2,18},{10... | collective-permute-start | bytes 786440 | tf_op jit(solution)/shard_map/ppermute | solution.py:33
  795.4 4.6 collective-permute-done.11
  800.0 18.0 %collective-permute-done.12 = bf16[64,2048]{1,0:T(8,128)(2,1)S(1)} collective-permute-done((bf16[64,2048]{1,0:T(8,128)(2,1)S(1)}, bf16[64,2048]{1,0:T(8,128)(2,1)S(1)}, u32[]{:S(2)}, u32[]{:S(2)}) %collective-permute-start.12) | collective-permute-done | bytes 262176 | tf_op jit(solution)/shard_map/ppermute | solution.py:33
  (254 shorter events, 183.9 us)
Async XLA Ops:
  7.0 3.2 copy-start.3
  7.1 3.2 copy-start.5
  24.4 13.1 %collective-permute-start = (bf16[128,2048]{1,0:T(8,128)(2,1)}, bf16[128,2048]{1,0:T(8,128)(2,1)S(1)}, u32[]{:S(2)}, u32[]{:S(2)}) collective-permute-start(bf16[128,2048]{1,0:T(8,128)(2,1)} %get-tuple-element.4108), channel_id=1, source_target_pairs={{0,32},{32,64},{64,96},{1,33},{33,65},{65,97},{2,34},{34,66},{66,9... | collective-permute-start | bytes 1572872 | tf_op jit(solution)/shard_map/while/body/eval_jaxpr/ppermute | solution.py:16
  51.3 15.3 %collective-permute-start = (bf16[128,2048]{1,0:T(8,128)(2,1)}, bf16[128,2048]{1,0:T(8,128)(2,1)S(1)}, u32[]{:S(2)}, u32[]{:S(2)}) collective-permute-start(bf16[128,2048]{1,0:T(8,128)(2,1)} %get-tuple-element.4108), channel_id=1, source_target_pairs={{0,32},{32,64},{64,96},{1,33},{33,65},{65,97},{2,34},{34,66},{66,9... | collective-permute-start | bytes 1572872 | tf_op jit(solution)/shard_map/while/body/eval_jaxpr/ppermute | solution.py:16
  80.6 14.3 %collective-permute-start = (bf16[128,2048]{1,0:T(8,128)(2,1)}, bf16[128,2048]{1,0:T(8,128)(2,1)S(1)}, u32[]{:S(2)}, u32[]{:S(2)}) collective-permute-start(bf16[128,2048]{1,0:T(8,128)(2,1)} %get-tuple-element.4108), channel_id=1, source_target_pairs={{0,32},{32,64},{64,96},{1,33},{33,65},{65,97},{2,34},{34,66},{66,9... | collective-permute-start | bytes 1572872 | tf_op jit(solution)/shard_map/while/body/eval_jaxpr/ppermute | solution.py:16
  108.8 13.4 %collective-permute-start.1 = (bf16[128,2048]{1,0:T(8,128)(2,1)}, bf16[128,2048]{1,0:T(8,128)(2,1)S(1)}, u32[]{:S(2)}, u32[]{:S(2)}) collective-permute-start(bf16[128,2048]{1,0:T(8,128)(2,1)} %get-tuple-element.4132), channel_id=1, source_target_pairs={{0,32},{32,64},{64,96},{96,128},{128,160},{160,192},{192,224},{1,3... | collective-permute-start | bytes 1572872 | tf_op jit(solution)/shard_map/while/body/eval_jaxpr/ppermute | solution.py:16
  123.0 25.5 %collective-permute-start.1 = (bf16[128,2048]{1,0:T(8,128)(2,1)}, bf16[128,2048]{1,0:T(8,128)(2,1)S(1)}, u32[]{:S(2)}, u32[]{:S(2)}) collective-permute-start(bf16[128,2048]{1,0:T(8,128)(2,1)} %get-tuple-element.4132), channel_id=1, source_target_pairs={{0,32},{32,64},{64,96},{96,128},{128,160},{160,192},{192,224},{1,3... | collective-permute-start | bytes 1572872 | tf_op jit(solution)/shard_map/while/body/eval_jaxpr/ppermute | solution.py:16
  149.4 11.5 %collective-permute-start.1 = (bf16[128,2048]{1,0:T(8,128)(2,1)}, bf16[128,2048]{1,0:T(8,128)(2,1)S(1)}, u32[]{:S(2)}, u32[]{:S(2)}) collective-permute-start(bf16[128,2048]{1,0:T(8,128)(2,1)} %get-tuple-element.4132), channel_id=1, source_target_pairs={{0,32},{32,64},{64,96},{96,128},{128,160},{160,192},{192,224},{1,3... | collective-permute-start | bytes 1572872 | tf_op jit(solution)/shard_map/while/body/eval_jaxpr/ppermute | solution.py:16
  161.7 23.5 %collective-permute-start.1 = (bf16[128,2048]{1,0:T(8,128)(2,1)}, bf16[128,2048]{1,0:T(8,128)(2,1)S(1)}, u32[]{:S(2)}, u32[]{:S(2)}) collective-permute-start(bf16[128,2048]{1,0:T(8,128)(2,1)} %get-tuple-element.4132), channel_id=1, source_target_pairs={{0,32},{32,64},{64,96},{96,128},{128,160},{160,192},{192,224},{1,3... | collective-permute-start | bytes 1572872 | tf_op jit(solution)/shard_map/while/body/eval_jaxpr/ppermute | solution.py:16
  186.6 0.7 collective-permute-start.2
  188.2 0.7 collective-permute-start.2
  189.8 0.7 collective-permute-start.2
  191.3 0.7 collective-permute-start.2
  204.5 0.7 collective-permute-start.3
  206.1 0.7 collective-permute-start.3
  207.7 0.7 collective-permute-start.3
  209.4 15.0 %collective-permute-start.4 = (bf16[128,2048]{1,0:T(8,128)(2,1)}, bf16[128,2048]{1,0:T(8,128)(2,1)S(1)}, u32[]{:S(2)}, u32[]{:S(2)}) collective-permute-start(bf16[128,2048]{1,0:T(8,128)(2,1)} %get-tuple-element.4195), channel_id=1, source_target_pairs={{32,0},{64,32},{96,64},{128,96},{160,128},{192,160},{224,192},{33,... | collective-permute-start | bytes 1572872 | tf_op jit(solution)/shard_map/while/body/eval_jaxpr/ppermute | solution.py:16
  225.3 30.7 %collective-permute-start.4 = (bf16[128,2048]{1,0:T(8,128)(2,1)}, bf16[128,2048]{1,0:T(8,128)(2,1)S(1)}, u32[]{:S(2)}, u32[]{:S(2)}) collective-permute-start(bf16[128,2048]{1,0:T(8,128)(2,1)} %get-tuple-element.4195), channel_id=1, source_target_pairs={{32,0},{64,32},{96,64},{128,96},{160,128},{192,160},{224,192},{33,... | collective-permute-start | bytes 1572872 | tf_op jit(solution)/shard_map/while/body/eval_jaxpr/ppermute | solution.py:16
  256.8 17.7 %collective-permute-start.4 = (bf16[128,2048]{1,0:T(8,128)(2,1)}, bf16[128,2048]{1,0:T(8,128)(2,1)S(1)}, u32[]{:S(2)}, u32[]{:S(2)}) collective-permute-start(bf16[128,2048]{1,0:T(8,128)(2,1)} %get-tuple-element.4195), channel_id=1, source_target_pairs={{32,0},{64,32},{96,64},{128,96},{160,128},{192,160},{224,192},{33,... | collective-permute-start | bytes 1572872 | tf_op jit(solution)/shard_map/while/body/eval_jaxpr/ppermute | solution.py:16
  275.3 249.7 %collective-permute-start.4 = (bf16[128,2048]{1,0:T(8,128)(2,1)}, bf16[128,2048]{1,0:T(8,128)(2,1)S(1)}, u32[]{:S(2)}, u32[]{:S(2)}) collective-permute-start(bf16[128,2048]{1,0:T(8,128)(2,1)} %get-tuple-element.4195), channel_id=1, source_target_pairs={{32,0},{64,32},{96,64},{128,96},{160,128},{192,160},{224,192},{33,... | collective-permute-start | bytes 1572872 | tf_op jit(solution)/shard_map/while/body/eval_jaxpr/ppermute | solution.py:16
  528.1 1.9 copy-start.2
  530.0 4.8 slice-start.4
  530.7 4.1 slice-start.5
  541.6 17.2 %collective-permute-start.5 = (bf16[128,2048]{1,0:T(8,128)(2,1)}, bf16[128,2048]{1,0:T(8,128)(2,1)S(1)}, u32[]{:S(2)}, u32[]{:S(2)}) collective-permute-start(bf16[128,2048]{1,0:T(8,128)(2,1)} %get-tuple-element.4212), channel_id=1, source_target_pairs={{32,0},{64,32},{96,64},{33,1},{65,33},{97,65},{34,2},{66,34},{98,6... | collective-permute-start | bytes 1572872 | tf_op jit(solution)/shard_map/while/body/eval_jaxpr/ppermute | solution.py:16
  562.0 1.9 copy-start.2
  563.9 4.8 slice-start.4
  564.6 4.1 slice-start.5
  575.5 17.3 %collective-permute-start.5 = (bf16[128,2048]{1,0:T(8,128)(2,1)}, bf16[128,2048]{1,0:T(8,128)(2,1)S(1)}, u32[]{:S(2)}, u32[]{:S(2)}) collective-permute-start(bf16[128,2048]{1,0:T(8,128)(2,1)} %get-tuple-element.4212), channel_id=1, source_target_pairs={{32,0},{64,32},{96,64},{33,1},{65,33},{97,65},{34,2},{66,34},{98,6... | collective-permute-start | bytes 1572872 | tf_op jit(solution)/shard_map/while/body/eval_jaxpr/ppermute | solution.py:16
  596.0 1.9 copy-start.2
  597.9 4.8 slice-start.4
  598.6 4.1 slice-start.5
  609.6 16.6 %collective-permute-start.5 = (bf16[128,2048]{1,0:T(8,128)(2,1)}, bf16[128,2048]{1,0:T(8,128)(2,1)S(1)}, u32[]{:S(2)}, u32[]{:S(2)}) collective-permute-start(bf16[128,2048]{1,0:T(8,128)(2,1)} %get-tuple-element.4212), channel_id=1, source_target_pairs={{32,0},{64,32},{96,64},{33,1},{65,33},{97,65},{34,2},{66,34},{98,6... | collective-permute-start | bytes 1572872 | tf_op jit(solution)/shard_map/while/body/eval_jaxpr/ppermute | solution.py:16
  629.3 1.9 copy-start.2
  631.2 4.8 slice-start.4
  632.0 4.1 slice-start.5
  642.9 11.3 %collective-permute-start.5 = (bf16[128,2048]{1,0:T(8,128)(2,1)}, bf16[128,2048]{1,0:T(8,128)(2,1)S(1)}, u32[]{:S(2)}, u32[]{:S(2)}) collective-permute-start(bf16[128,2048]{1,0:T(8,128)(2,1)} %get-tuple-element.4212), channel_id=1, source_target_pairs={{32,0},{64,32},{96,64},{33,1},{65,33},{97,65},{34,2},{66,34},{98,6... | collective-permute-start | bytes 1572872 | tf_op jit(solution)/shard_map/while/body/eval_jaxpr/ppermute | solution.py:16
  658.3 15.1 %collective-permute-start.7 = (bf16[512,2048]{1,0:T(8,128)(2,1)}, bf16[512,2048]{1,0:T(8,128)(2,1)}, u32[]{:S(2)}, u32[]{:S(2)}) collective-permute-start(bf16[512,2048]{1,0:T(8,128)(2,1)} %bitcast.94), channel_id=1, source_target_pairs={{0,1},{1,0},{2,3},{3,2},{4,5},{5,4},{6,7},{7,6},{8,9},{9,8},{10,11... | collective-permute-start | bytes 6291464 | tf_op jit(solution)/shard_map/ppermute | solution.py:242
  670.4 3.0 collective-permute-start.6
  679.7 3.2 copy-start.4
  683.4 48.5 %collective-permute-start.10 = (bf16[256,2048]{1,0:T(8,128)(2,1)S(1)}, bf16[256,2048]{1,0:T(8,128)(2,1)}, u32[]{:S(2)}, u32[]{:S(2)}) collective-permute-start(bf16[256,2048]{1,0:T(8,128)(2,1)S(1)} %get-tuple-element.3567), channel_id=1, source_target_pairs={{0,6},{2,0},{4,2},{6,4},{1,7},{3,1},{5,3},{7,5},{8,14},{10,8},{12,... | collective-permute-start | bytes 3145736 | tf_op jit(solution)/shard_map/ppermute | solution.py:33
  686.5 48.9 %collective-permute-start.8 = (bf16[256,2048]{1,0:T(8,128)(2,1)S(1)}, bf16[256,2048]{1,0:T(8,128)(2,1)}, u32[]{:S(2)}, u32[]{:S(2)}) collective-permute-start(bf16[256,2048]{1,0:T(8,128)(2,1)S(1)} %get-tuple-element.3566), channel_id=1, source_target_pairs={{0,2},{2,4},{4,6},{6,0},{1,3},{3,5},{5,7},{7,1},{8,10},{10,12},{12... | collective-permute-start | bytes 3145736 | tf_op jit(solution)/shard_map/ppermute | solution.py:33
  686.5 48.9 %collective-permute-start.9 = (bf16[256,2048]{1,0:T(8,128)(2,1)S(1)}, bf16[256,2048]{1,0:T(8,128)(2,1)}, u32[]{:S(2)}, u32[]{:S(2)}) collective-permute-start(bf16[256,2048]{1,0:T(8,128)(2,1)S(1)} %get-tuple-element.3568), channel_id=1, source_target_pairs={{0,4},{2,6},{4,0},{6,2},{1,5},{3,7},{5,1},{7,3},{8,12},{10,14},{12... | collective-permute-start | bytes 3145736 | tf_op jit(solution)/shard_map/ppermute | solution.py:33
  738.7 61.3 %collective-permute-start.11 = (bf16[64,2048]{1,0:T(8,128)(2,1)S(1)}, bf16[64,2048]{1,0:T(8,128)(2,1)S(1)}, u32[]{:S(2)}, u32[]{:S(2)}) collective-permute-start(bf16[64,2048]{1,0:T(8,128)(2,1)S(1)} %get-tuple-element.3569), channel_id=1, source_target_pairs={{0,8},{8,16},{16,24},{24,0},{1,9},{9,17},{17,25},{25,1},{2,10},{10... | collective-permute-start | bytes 786440 | tf_op jit(solution)/shard_map/ppermute | solution.py:33
  738.8 79.2 %collective-permute-start.12 = (bf16[64,2048]{1,0:T(8,128)(2,1)S(1)}, bf16[64,2048]{1,0:T(8,128)(2,1)S(1)}, u32[]{:S(2)}, u32[]{:S(2)}) collective-permute-start(bf16[64,2048]{1,0:T(8,128)(2,1)S(1)} %get-tuple-element.3571), channel_id=1, source_target_pairs={{0,16},{8,24},{16,0},{24,8},{1,17},{9,25},{17,1},{25,9},{2,18},{10... | collective-permute-start | bytes 786440 | tf_op jit(solution)/shard_map/ppermute | solution.py:33
  795.4 22.6 %collective-permute-start.13 = (bf16[64,2048]{1,0:T(8,128)(2,1)S(1)}, bf16[64,2048]{1,0:T(8,128)(2,1)}, u32[]{:S(2)}, u32[]{:S(2)}) collective-permute-start(bf16[64,2048]{1,0:T(8,128)(2,1)S(1)} %get-tuple-element.3570), channel_id=1, source_target_pairs={{0,24},{8,0},{16,8},{24,16},{1,25},{9,1},{17,9},{25,17},{2,26},{10... | collective-permute-start | bytes 786440 | tf_op jit(solution)/shard_map/ppermute | solution.py:33

commit v15 on v12

--- a/solution.py
+++ b/solution.py
@@ -235,7 +235,12 @@
     own = collected.reshape(micro * buses, width)
     right = jnp.concatenate([own, lax.ppermute(own, "core", swap)], axis=0)
     half = jnp.dot(left, right, preferred_element_type=jnp.float32)
-    summed = scatter_sum(scatter_sum(half, "y"), "z")
+    columns = width // 2
+    along_y = scatter_sum(scatter_sum(half[:, :columns], "y"), "z")
+    by_z = half[:, columns:].reshape(ys, zs, rows_each, columns)
+    by_z = jnp.swapaxes(by_z, 0, 1).reshape(ys * zs * rows_each, columns)
+    along_z = scatter_sum(scatter_sum(by_z, "z"), "y")
+    summed = jnp.concatenate([along_y, along_z], axis=1)
     return summed[None]
 
 

time: 799 us -> 795 us (level)
  waiting for transfers between devices: 486 us -> 432 us
  starting transfers between devices: 111 us -> 155 us
    ppermute x6 -> x12, waiting for transfers between devices: 68.8 us -> 14.4 us  [scatter_sum(): received = lax.ppermute(sent.astype(jnp.bfloat16), axis, route)]
    ppermute x6 -> x12, starting transfers between devices: 46 us -> 89.8 us  [scatter_sum(): received = lax.ppermute(sent.astype(jnp.bfloat16), axis, route)]
    unnamed x13 -> x15, local copies, waits for them, and re-layouts: 24.4 us -> 25.1 us
  transfers between devices with their start and end apart: 30 -> 36, of which waited for: 20 -> 20; matrix products, arithmetic and copies ran while one was open for 3% -> 3% of each run, Pallas kernels for 0% -> 0%
where the time goes in v15:
time: 795 us; the launch traced here: 786 us
  waiting for transfers between devices  432 us (54%)
  starting transfers between devices  155 us (19%)
  local copies, waits for them, and re-layouts  79.8 us (10%)
  matrix products  69.7 us (9%)
  other arithmetic  47.4 us (6%)
    ppermute x22, waiting for transfers between devices, passed_along(): return lax.ppermute(block, axis, [(i, i + distance) for i in senders])  415 us
    ppermute x12, starting transfers between devices, scatter_sum(): received = lax.ppermute(sent.astype(jnp.bfloat16), axis, route)  89.8 us
    ppermute x22, starting transfers between devices, passed_along(): return lax.ppermute(block, axis, [(i, i + distance) for i in senders])  64.5 us
    unnamed x15, local copies, waits for them, and re-layouts  25.1 us
    dot_general x4, matrix products, layer_forward(): jnp.dot(normed.reshape(-1, width), weight, preferred_element_type=jnp.flo...  18.8 us
    dot_general x4, matrix products, layer_backward(): lax.dot_general(value_total.reshape(-1, width), weight, (((1,), (1,)), ((...  16.7 us
  transfers between devices with their start and end apart: 36, of which 20 were waited for; matrix products, arithmetic and copies ran while one was open for 3% of the time, Pallas kernels for 0%

profile of v15, /device:TPU:96, one launch (start us, length us, event | category | flops | bytes accessed | tf_op | source)
XLA Modules:
  0.0 785.8 jit_solution(12649824672549303912)
XLA Ops:
  13.2 76.1 %while.144 = (s32[]{:T(128)}, bf16[128,2048]{0,1:T(8,128)(2,1)S(1)}, f32[4,128,2048]{1,2,0:T(8,128)}, f32[4,128,1]{1,2,0:T(1,128)S(1)}, bf16[4,128,16,128]{3,2,1...) while((s32[]{:T(128)}, bf16[128,2048]{0,1:T(8,128)(2,1)S(1)}, ...), condition=%wide.region_8.9_spmd.clone, body=%wide.region_1.8_spmd.clone.sunk | while | flops 1216641408 | bytes 26020904 | solution.py:180
  13.2 11.5 %conditional.18 = (bf16[128,2048]{0,1:T(8,128)(2,1)S(1)}, f32[4,128,2048]{1,2,0:T(8,128)}, f32[4,128,1]{1,2,0:T(1,128)S(1)}, bf16[4,128,16,128]{3,2,1,0:T(8,128)...) conditional(s32[]{:T(128)} %convert_element_type.892, ...), branch_computations={%region_2.2_spmd, %region_3.7_spmd} | conditional | flops 1216641408 | bytes 23923316 | solution.py:171
  13.8 4.7 convolution_convert_fusion
  26.0 11.4 %collective-permute-done = bf16[128,2048]{0,1:T(8,128)(2,1)S(1)} collective-permute-done((bf16[128,2048]{0,1:T(8,128)(2,1)S(1)}, bf16[128,2048]{0,1:T(8,128)(2,1)S(1)}, u32[]{:S(2)}, u32[]{:S(2)}) %collective-permute-start) | collective-permute-done | bytes 524320 | tf_op jit(solution)/shard_map/while/body/eval_jaxpr/ppermute | solution.py:16
  37.4 11.4 %conditional.18 = (bf16[128,2048]{0,1:T(8,128)(2,1)S(1)}, f32[4,128,2048]{1,2,0:T(8,128)}, f32[4,128,1]{1,2,0:T(1,128)S(1)}, bf16[4,128,16,128]{3,2,1,0:T(8,128)...) conditional(s32[]{:T(128)} %convert_element_type.892, ...), branch_computations={%region_2.2_spmd, %region_3.7_spmd} | conditional | flops 1216641408 | bytes 23923316 | solution.py:171
  38.0 4.7 convolution_convert_fusion
  48.8 4.5 collective-permute-start
  53.3 10.6 %collective-permute-done = bf16[128,2048]{0,1:T(8,128)(2,1)S(1)} collective-permute-done((bf16[128,2048]{0,1:T(8,128)(2,1)S(1)}, bf16[128,2048]{0,1:T(8,128)(2,1)S(1)}, u32[]{:S(2)}, u32[]{:S(2)}) %collective-permute-start) | collective-permute-done | bytes 524320 | tf_op jit(solution)/shard_map/while/body/eval_jaxpr/ppermute | solution.py:16
  63.9 11.4 %conditional.18 = (bf16[128,2048]{0,1:T(8,128)(2,1)S(1)}, f32[4,128,2048]{1,2,0:T(8,128)}, f32[4,128,1]{1,2,0:T(1,128)S(1)}, bf16[4,128,16,128]{3,2,1,0:T(8,128)...) conditional(s32[]{:T(128)} %convert_element_type.892, ...), branch_computations={%region_2.2_spmd, %region_3.7_spmd} | conditional | flops 1216641408 | bytes 23923316 | solution.py:171
  64.5 4.7 convolution_convert_fusion
  75.2 4.4 collective-permute-start
  79.7 9.7 %collective-permute-done = bf16[128,2048]{0,1:T(8,128)(2,1)S(1)} collective-permute-done((bf16[128,2048]{0,1:T(8,128)(2,1)S(1)}, bf16[128,2048]{0,1:T(8,128)(2,1)S(1)}, u32[]{:S(2)}, u32[]{:S(2)}) %collective-permute-start) | collective-permute-done | bytes 524320 | tf_op jit(solution)/shard_map/while/body/eval_jaxpr/ppermute | solution.py:16
  89.3 81.1 %while.145 = (s32[]{:T(128)}, bf16[128,2048]{0,1:T(8,128)(2,1)S(1)}, f32[4,128,2048]{1,2,0:T(8,128)}, f32[4,128,1]{1,2,0:T(1,128)S(1)}, bf16[4,128,16,128]{3,2,1...) while((s32[]{:T(128)}, bf16[128,2048]{0,1:T(8,128)(2,1)S(1)}, ...), condition=%wide.region_16.17_spmd.clone, body=%wide.region_9.16_spmd.clone.sunk | while | flops 1216641408 | bytes 26020924 | solution.py:180
  89.3 11.4 %conditional.19 = (bf16[128,2048]{0,1:T(8,128)(2,1)S(1)}, f32[4,128,2048]{1,2,0:T(8,128)}, f32[4,128,1]{1,2,0:T(1,128)S(1)}, bf16[4,128,16,128]{3,2,1,0:T(8,128)...) conditional(s32[]{:T(128)} %convert_element_type.893, ...), branch_computations={%region_10.10_spmd, %region_11.15_spmd} | conditional | flops 1216641408 | bytes 23923316 | solution.py:171
  89.9 4.7 convolution_convert_fusion.1
  100.8 4.4 collective-permute-start.1
  105.1 8.7 %collective-permute-done.1 = bf16[128,2048]{0,1:T(8,128)(2,1)S(1)} collective-permute-done((bf16[128,2048]{0,1:T(8,128)(2,1)S(1)}, bf16[128,2048]{0,1:T(8,128)(2,1)S(1)}, u32[]{:S(2)}, u32[]{:S(2)}) %collective-permute-start.1) | collective-permute-done | bytes 524320 | tf_op jit(solution)/shard_map/while/body/eval_jaxpr/ppermute | solution.py:16
  114.0 15.7 %collective-permute-start.1 = (bf16[128,2048]{0,1:T(8,128)(2,1)S(1)}, bf16[128,2048]{0,1:T(8,128)(2,1)S(1)}, u32[]{:S(2)}, u32[]{:S(2)}) collective-permute-start(bf16[128,2048]{0,1:T(8,128)(2,1)S(1)} %get-tuple-element.4053), channel_id=1, source_target_pairs={{0,32},{32,64},{64,96},{96,128},{128,160},{160,192},{192,224},{1,3... | collective-permute-start | bytes 1572872 | tf_op jit(solution)/shard_map/while/body/eval_jaxpr/ppermute | solution.py:16
  129.7 7.8 collective-permute-done.1
  137.6 4.4 collective-permute-start.1
  142.0 6.9 collective-permute-done.1
  149.0 14.7 %collective-permute-start.1 = (bf16[128,2048]{0,1:T(8,128)(2,1)S(1)}, bf16[128,2048]{0,1:T(8,128)(2,1)S(1)}, u32[]{:S(2)}, u32[]{:S(2)}) collective-permute-start(bf16[128,2048]{0,1:T(8,128)(2,1)S(1)} %get-tuple-element.4053), channel_id=1, source_target_pairs={{0,32},{32,64},{64,96},{96,128},{128,160},{160,192},{192,224},{1,3... | collective-permute-start | bytes 1572872 | tf_op jit(solution)/shard_map/while/body/eval_jaxpr/ppermute | solution.py:16
  163.8 6.6 collective-permute-done.1
  174.0 5.4 copy.149
  179.4 5.6 copy.151
  187.6 4.5 copy.150
  193.8 4.8 while.147
  198.5 304.7 %while.148 = (s32[]{:T(128)}, bf16[128,2048]{1,0:T(8,128)(2,1)S(1)}, bf16[4,128,2048]{1,2,0:T(8,128)(2,1)}, s32[]{:T(128)}, pred[]{:T(512)}, /*index=5*/bf16[4,1...) while((s32[]{:T(128)}, bf16[128,2048]{1,0:T(8,128)(2,1)S(1)}, ...), condition=%wide.region_38.39_spmd.clone, body=%wide.region_32.38_spmd.clone.sunk | while | flops 1353218048 | bytes 71172632 | solution.py:233
  200.9 13.6 %collective-permute-done.4 = bf16[128,2048]{1,0:T(8,128)(2,1)S(1)} collective-permute-done((bf16[128,2048]{1,0:T(8,128)(2,1)}, bf16[128,2048]{1,0:T(8,128)(2,1)S(1)}, u32[]{:S(2)}, u32[]{:S(2)}) %collective-permute-start.4) | collective-permute-done | bytes 524320 | tf_op jit(solution)/shard_map/while/body/eval_jaxpr/ppermute | solution.py:16
  216.6 27.7 %collective-permute-done.4 = bf16[128,2048]{1,0:T(8,128)(2,1)S(1)} collective-permute-done((bf16[128,2048]{1,0:T(8,128)(2,1)}, bf16[128,2048]{1,0:T(8,128)(2,1)S(1)}, u32[]{:S(2)}, u32[]{:S(2)}) %collective-permute-start.4) | collective-permute-done | bytes 524320 | tf_op jit(solution)/shard_map/while/body/eval_jaxpr/ppermute | solution.py:16
  246.5 16.4 %collective-permute-done.4 = bf16[128,2048]{1,0:T(8,128)(2,1)S(1)} collective-permute-done((bf16[128,2048]{1,0:T(8,128)(2,1)}, bf16[128,2048]{1,0:T(8,128)(2,1)S(1)}, u32[]{:S(2)}, u32[]{:S(2)}) %collective-permute-start.4) | collective-permute-done | bytes 524320 | tf_op jit(solution)/shard_map/while/body/eval_jaxpr/ppermute | solution.py:16
  265.1 238.2 %collective-permute-done.4 = bf16[128,2048]{1,0:T(8,128)(2,1)S(1)} collective-permute-done((bf16[128,2048]{1,0:T(8,128)(2,1)}, bf16[128,2048]{1,0:T(8,128)(2,1)S(1)}, u32[]{:S(2)}, u32[]{:S(2)}) %collective-permute-start.4) | collective-permute-done | bytes 524320 | tf_op jit(solution)/shard_map/while/body/eval_jaxpr/ppermute | solution.py:16
  503.2 129.2 %while.149 = (s32[]{:T(128)}, bf16[128,2048]{1,0:T(8,128)(2,1)S(1)}, bf16[4,128,2048]{1,2,0:T(8,128)(2,1)}, s32[]{:T(128)}, pred[]{:T(512)}, /*index=5*/bf16[4,1...) while((s32[]{:T(128)}, bf16[128,2048]{1,0:T(8,128)(2,1)S(1)}, ...), condition=%wide.region_45.46_spmd.clone, body=%wide.region_39.45_spmd.clone.sunk | while | flops 1353218048 | bytes 71172632 | solution.py:233
  503.3 16.7 %conditional.23 = (bf16[128,2048]{1,0:T(8,128)(2,1)}, bf16[4,128,2048]{1,2,0:T(8,128)(2,1)}) conditional(s32[]{:T(128)} %convert_element_type.897, bf16[4,128,2048]{1,2,0:T(8,128)(2,1)} %get-tuple-element.4507, (pred[]{:T(512)}, s32[]{:T(128)}, bf16[4,128,2048]{2,1,0:T(8,128)(2,1)}, bf16[128,2048]{1,0:T(8,128)(2,1)S(1)}, ...), branch_computations={%region_40.40_spmd, %region_41.44_spmd} | conditional | flops 1353218048 | bytes 69075104 | solution.py:207
  521.2 16.0 %collective-permute-done.5 = bf16[128,2048]{1,0:T(8,128)(2,1)S(1)} collective-permute-done((bf16[128,2048]{1,0:T(8,128)(2,1)}, bf16[128,2048]{1,0:T(8,128)(2,1)S(1)}, u32[]{:S(2)}, u32[]{:S(2)}) %collective-permute-start.5) | collective-permute-done | bytes 524320 | tf_op jit(solution)/shard_map/while/body/eval_jaxpr/ppermute | solution.py:16
  537.2 16.7 %conditional.23 = (bf16[128,2048]{1,0:T(8,128)(2,1)}, bf16[4,128,2048]{1,2,0:T(8,128)(2,1)}) conditional(s32[]{:T(128)} %convert_element_type.897, bf16[4,128,2048]{1,2,0:T(8,128)(2,1)} %get-tuple-element.4507, (pred[]{:T(512)}, s32[]{:T(128)}, bf16[4,128,2048]{2,1,0:T(8,128)(2,1)}, bf16[128,2048]{1,0:T(8,128)(2,1)S(1)}, ...), branch_computations={%region_40.40_spmd, %region_41.44_spmd} | conditional | flops 1353218048 | bytes 69075104 | solution.py:207
  555.1 16.1 %collective-permute-done.5 = bf16[128,2048]{1,0:T(8,128)(2,1)S(1)} collective-permute-done((bf16[128,2048]{1,0:T(8,128)(2,1)}, bf16[128,2048]{1,0:T(8,128)(2,1)S(1)}, u32[]{:S(2)}, u32[]{:S(2)}) %collective-permute-start.5) | collective-permute-done | bytes 524320 | tf_op jit(solution)/shard_map/while/body/eval_jaxpr/ppermute | solution.py:16
  571.2 16.7 %conditional.23 = (bf16[128,2048]{1,0:T(8,128)(2,1)}, bf16[4,128,2048]{1,2,0:T(8,128)(2,1)}) conditional(s32[]{:T(128)} %convert_element_type.897, bf16[4,128,2048]{1,2,0:T(8,128)(2,1)} %get-tuple-element.4507, (pred[]{:T(512)}, s32[]{:T(128)}, bf16[4,128,2048]{2,1,0:T(8,128)(2,1)}, bf16[128,2048]{1,0:T(8,128)(2,1)S(1)}, ...), branch_computations={%region_40.40_spmd, %region_41.44_spmd} | conditional | flops 1353218048 | bytes 69075104 | solution.py:207
  589.2 15.3 %collective-permute-done.5 = bf16[128,2048]{1,0:T(8,128)(2,1)S(1)} collective-permute-done((bf16[128,2048]{1,0:T(8,128)(2,1)}, bf16[128,2048]{1,0:T(8,128)(2,1)S(1)}, u32[]{:S(2)}, u32[]{:S(2)}) %collective-permute-start.5) | collective-permute-done | bytes 524320 | tf_op jit(solution)/shard_map/while/body/eval_jaxpr/ppermute | solution.py:16
  604.5 16.7 %conditional.23 = (bf16[128,2048]{1,0:T(8,128)(2,1)}, bf16[4,128,2048]{1,2,0:T(8,128)(2,1)}) conditional(s32[]{:T(128)} %convert_element_type.897, bf16[4,128,2048]{1,2,0:T(8,128)(2,1)} %get-tuple-element.4507, (pred[]{:T(512)}, s32[]{:T(128)}, bf16[4,128,2048]{2,1,0:T(8,128)(2,1)}, bf16[128,2048]{1,0:T(8,128)(2,1)S(1)}, ...), branch_computations={%region_40.40_spmd, %region_41.44_spmd} | conditional | flops 1353218048 | bytes 69075104 | solution.py:207
  622.4 10.0 %collective-permute-done.5 = bf16[128,2048]{1,0:T(8,128)(2,1)S(1)} collective-permute-done((bf16[128,2048]{1,0:T(8,128)(2,1)}, bf16[128,2048]{1,0:T(8,128)(2,1)S(1)}, u32[]{:S(2)}, u32[]{:S(2)}) %collective-permute-start.5) | collective-permute-done | bytes 524320 | tf_op jit(solution)/shard_map/while/body/eval_jaxpr/ppermute | solution.py:16
  639.3 10.8 %copy.146 = bf16[4,128,2048]{1,0,2:T(4,128)(2,1)} copy(bf16[4,128,2048]{1,2,0:T(8,128)(2,1)S(1)} %convert_element_type.505) | data formatting | bytes 4194304 | tf_op jit(solution)/shard_map/convert_element_type | solution.py:217
  660.1 6.2 fusion.213
  681.9 40.5 %collective-permute-start.15 = (bf16[256,1024]{1,0:T(8,128)(2,1)S(1)}, bf16[256,1024]{1,0:T(8,128)(2,1)}, u32[]{:S(2)}, u32[]{:S(2)}) collective-permute-start(bf16[256,1024]{1,0:T(8,128)(2,1)S(1)} %get-tuple-element.3486), channel_id=1, source_target_pairs={{0,16},{8,24},{16,0},{24,8},{1,17},{9,25},{17,1},{25,9},{2,18},{10... | collective-permute-start | bytes 1572872 | tf_op jit(solution)/shard_map/ppermute | solution.py:33
  722.4 14.3 %collective-permute-start.16 = (bf16[256,1024]{1,0:T(8,128)(2,1)S(1)}, bf16[256,1024]{1,0:T(8,128)(2,1)S(1)}, u32[]{:S(2)}, u32[]{:S(2)}) collective-permute-start(bf16[256,1024]{1,0:T(8,128)(2,1)S(1)} %get-tuple-element.3485), channel_id=1, source_target_pairs={{0,24},{8,0},{16,8},{24,16},{1,25},{9,1},{17,9},{25,17},{2,26},{10... | collective-permute-start | bytes 1572872 | tf_op jit(solution)/shard_map/ppermute | solution.py:33
  738.9 5.0 collective-permute-start.12
  743.8 19.8 %collective-permute-start.13 = (bf16[64,1024]{1,0:T(8,128)(2,1)S(1)}, bf16[64,1024]{1,0:T(8,128)(2,1)S(1)}, u32[]{:S(2)}, u32[]{:S(2)}) collective-permute-start(bf16[64,1024]{1,0:T(8,128)(2,1)S(1)} %get-tuple-element.3490), channel_id=1, source_target_pairs={{0,24},{8,0},{16,8},{24,16},{1,25},{9,1},{17,9},{25,17},{2,26},{10... | collective-permute-start | bytes 393224 | tf_op jit(solution)/shard_map/ppermute | solution.py:33
  763.6 10.7 %collective-permute-done.15 = bf16[256,1024]{1,0:T(8,128)(2,1)} collective-permute-done((bf16[256,1024]{1,0:T(8,128)(2,1)S(1)}, bf16[256,1024]{1,0:T(8,128)(2,1)}, u32[]{:S(2)}, u32[]{:S(2)}) %collective-permute-start.15) | collective-permute-done | bytes 524320 | tf_op jit(solution)/shard_map/ppermute | solution.py:33
  (280 shorter events, 189.4 us)
Async XLA Ops:
  9.8 3.3 copy-start.6
  9.9 3.3 copy-start.7
  24.7 12.7 %collective-permute-start = (bf16[128,2048]{0,1:T(8,128)(2,1)S(1)}, bf16[128,2048]{0,1:T(8,128)(2,1)S(1)}, u32[]{:S(2)}, u32[]{:S(2)}) collective-permute-start(bf16[128,2048]{0,1:T(8,128)(2,1)S(1)} %get-tuple-element.4029), channel_id=1, source_target_pairs={{0,32},{32,64},{64,96},{1,33},{33,65},{65,97},{2,34},{34,66},{66,9... | collective-permute-start | bytes 1572872 | tf_op jit(solution)/shard_map/while/body/eval_jaxpr/ppermute | solution.py:16
  48.8 15.0 %collective-permute-start = (bf16[128,2048]{0,1:T(8,128)(2,1)S(1)}, bf16[128,2048]{0,1:T(8,128)(2,1)S(1)}, u32[]{:S(2)}, u32[]{:S(2)}) collective-permute-start(bf16[128,2048]{0,1:T(8,128)(2,1)S(1)} %get-tuple-element.4029), channel_id=1, source_target_pairs={{0,32},{32,64},{64,96},{1,33},{33,65},{65,97},{2,34},{34,66},{66,9... | collective-permute-start | bytes 1572872 | tf_op jit(solution)/shard_map/while/body/eval_jaxpr/ppermute | solution.py:16
  75.2 14.1 %collective-permute-start = (bf16[128,2048]{0,1:T(8,128)(2,1)S(1)}, bf16[128,2048]{0,1:T(8,128)(2,1)S(1)}, u32[]{:S(2)}, u32[]{:S(2)}) collective-permute-start(bf16[128,2048]{0,1:T(8,128)(2,1)S(1)} %get-tuple-element.4029), channel_id=1, source_target_pairs={{0,32},{32,64},{64,96},{1,33},{33,65},{65,97},{2,34},{34,66},{66,9... | collective-permute-start | bytes 1572872 | tf_op jit(solution)/shard_map/while/body/eval_jaxpr/ppermute | solution.py:16
  100.8 13.1 %collective-permute-start.1 = (bf16[128,2048]{0,1:T(8,128)(2,1)S(1)}, bf16[128,2048]{0,1:T(8,128)(2,1)S(1)}, u32[]{:S(2)}, u32[]{:S(2)}) collective-permute-start(bf16[128,2048]{0,1:T(8,128)(2,1)S(1)} %get-tuple-element.4053), channel_id=1, source_target_pairs={{0,32},{32,64},{64,96},{96,128},{128,160},{160,192},{192,224},{1,3... | collective-permute-start | bytes 1572872 | tf_op jit(solution)/shard_map/while/body/eval_jaxpr/ppermute | solution.py:16
  114.0 23.6 %collective-permute-start.1 = (bf16[128,2048]{0,1:T(8,128)(2,1)S(1)}, bf16[128,2048]{0,1:T(8,128)(2,1)S(1)}, u32[]{:S(2)}, u32[]{:S(2)}) collective-permute-start(bf16[128,2048]{0,1:T(8,128)(2,1)S(1)} %get-tuple-element.4053), channel_id=1, source_target_pairs={{0,32},{32,64},{64,96},{96,128},{128,160},{160,192},{192,224},{1,3... | collective-permute-start | bytes 1572872 | tf_op jit(solution)/shard_map/while/body/eval_jaxpr/ppermute | solution.py:16
  137.6 11.3 %collective-permute-start.1 = (bf16[128,2048]{0,1:T(8,128)(2,1)S(1)}, bf16[128,2048]{0,1:T(8,128)(2,1)S(1)}, u32[]{:S(2)}, u32[]{:S(2)}) collective-permute-start(bf16[128,2048]{0,1:T(8,128)(2,1)S(1)} %get-tuple-element.4053), channel_id=1, source_target_pairs={{0,32},{32,64},{64,96},{96,128},{128,160},{160,192},{192,224},{1,3... | collective-permute-start | bytes 1572872 | tf_op jit(solution)/shard_map/while/body/eval_jaxpr/ppermute | solution.py:16
  149.0 21.4 %collective-permute-start.1 = (bf16[128,2048]{0,1:T(8,128)(2,1)S(1)}, bf16[128,2048]{0,1:T(8,128)(2,1)S(1)}, u32[]{:S(2)}, u32[]{:S(2)}) collective-permute-start(bf16[128,2048]{0,1:T(8,128)(2,1)S(1)} %get-tuple-element.4053), channel_id=1, source_target_pairs={{0,32},{32,64},{64,96},{96,128},{128,160},{160,192},{192,224},{1,3... | collective-permute-start | bytes 1572872 | tf_op jit(solution)/shard_map/while/body/eval_jaxpr/ppermute | solution.py:16
  170.7 0.7 collective-permute-start.2
  171.6 0.7 collective-permute-start.2
  172.4 0.7 collective-permute-start.2
  173.3 0.7 collective-permute-start.2
  179.4 5.6 copy-start.5
  194.7 0.7 collective-permute-start.3
  196.3 0.7 collective-permute-start.3
  197.8 0.7 collective-permute-start.3
  199.6 14.9 %collective-permute-start.4 = (bf16[128,2048]{1,0:T(8,128)(2,1)}, bf16[128,2048]{1,0:T(8,128)(2,1)S(1)}, u32[]{:S(2)}, u32[]{:S(2)}) collective-permute-start(bf16[128,2048]{1,0:T(8,128)(2,1)} %get-tuple-element.4116), channel_id=1, source_target_pairs={{32,0},{64,32},{96,64},{128,96},{160,128},{192,160},{224,192},{33,... | collective-permute-start | bytes 1572872 | tf_op jit(solution)/shard_map/while/body/eval_jaxpr/ppermute | solution.py:16
  215.3 29.0 %collective-permute-start.4 = (bf16[128,2048]{1,0:T(8,128)(2,1)}, bf16[128,2048]{1,0:T(8,128)(2,1)S(1)}, u32[]{:S(2)}, u32[]{:S(2)}) collective-permute-start(bf16[128,2048]{1,0:T(8,128)(2,1)} %get-tuple-element.4116), channel_id=1, source_target_pairs={{32,0},{64,32},{96,64},{128,96},{160,128},{192,160},{224,192},{33,... | collective-permute-start | bytes 1572872 | tf_op jit(solution)/shard_map/while/body/eval_jaxpr/ppermute | solution.py:16
  245.2 17.7 %collective-permute-start.4 = (bf16[128,2048]{1,0:T(8,128)(2,1)}, bf16[128,2048]{1,0:T(8,128)(2,1)S(1)}, u32[]{:S(2)}, u32[]{:S(2)}) collective-permute-start(bf16[128,2048]{1,0:T(8,128)(2,1)} %get-tuple-element.4116), channel_id=1, source_target_pairs={{32,0},{64,32},{96,64},{128,96},{160,128},{192,160},{224,192},{33,... | collective-permute-start | bytes 1572872 | tf_op jit(solution)/shard_map/while/body/eval_jaxpr/ppermute | solution.py:16
  263.8 239.5 %collective-permute-start.4 = (bf16[128,2048]{1,0:T(8,128)(2,1)}, bf16[128,2048]{1,0:T(8,128)(2,1)S(1)}, u32[]{:S(2)}, u32[]{:S(2)}) collective-permute-start(bf16[128,2048]{1,0:T(8,128)(2,1)} %get-tuple-element.4116), channel_id=1, source_target_pairs={{32,0},{64,32},{96,64},{128,96},{160,128},{192,160},{224,192},{33,... | collective-permute-start | bytes 1572872 | tf_op jit(solution)/shard_map/while/body/eval_jaxpr/ppermute | solution.py:16
  508.3 4.8 slice-start.4
  509.0 4.1 slice-start.5
  519.9 17.3 %collective-permute-start.5 = (bf16[128,2048]{1,0:T(8,128)(2,1)}, bf16[128,2048]{1,0:T(8,128)(2,1)S(1)}, u32[]{:S(2)}, u32[]{:S(2)}) collective-permute-start(bf16[128,2048]{1,0:T(8,128)(2,1)} %get-tuple-element.4133), channel_id=1, source_target_pairs={{32,0},{64,32},{96,64},{33,1},{65,33},{97,65},{34,2},{66,34},{98,6... | collective-permute-start | bytes 1572872 | tf_op jit(solution)/shard_map/while/body/eval_jaxpr/ppermute | solution.py:16
  542.2 4.8 slice-start.4
  542.9 4.1 slice-start.5
  553.8 17.3 %collective-permute-start.5 = (bf16[128,2048]{1,0:T(8,128)(2,1)}, bf16[128,2048]{1,0:T(8,128)(2,1)S(1)}, u32[]{:S(2)}, u32[]{:S(2)}) collective-permute-start(bf16[128,2048]{1,0:T(8,128)(2,1)} %get-tuple-element.4133), channel_id=1, source_target_pairs={{32,0},{64,32},{96,64},{33,1},{65,33},{97,65},{34,2},{66,34},{98,6... | collective-permute-start | bytes 1572872 | tf_op jit(solution)/shard_map/while/body/eval_jaxpr/ppermute | solution.py:16
  576.2 4.8 slice-start.4
  576.9 4.1 slice-start.5
  587.9 16.6 %collective-permute-start.5 = (bf16[128,2048]{1,0:T(8,128)(2,1)}, bf16[128,2048]{1,0:T(8,128)(2,1)S(1)}, u32[]{:S(2)}, u32[]{:S(2)}) collective-permute-start(bf16[128,2048]{1,0:T(8,128)(2,1)} %get-tuple-element.4133), channel_id=1, source_target_pairs={{32,0},{64,32},{96,64},{33,1},{65,33},{97,65},{34,2},{66,34},{98,6... | collective-permute-start | bytes 1572872 | tf_op jit(solution)/shard_map/while/body/eval_jaxpr/ppermute | solution.py:16
  609.5 4.8 slice-start.4
  610.2 4.1 slice-start.5
  621.1 11.3 %collective-permute-start.5 = (bf16[128,2048]{1,0:T(8,128)(2,1)}, bf16[128,2048]{1,0:T(8,128)(2,1)S(1)}, u32[]{:S(2)}, u32[]{:S(2)}) collective-permute-start(bf16[128,2048]{1,0:T(8,128)(2,1)} %get-tuple-element.4133), channel_id=1, source_target_pairs={{32,0},{64,32},{96,64},{33,1},{65,33},{97,65},{34,2},{66,34},{98,6... | collective-permute-start | bytes 1572872 | tf_op jit(solution)/shard_map/while/body/eval_jaxpr/ppermute | solution.py:16
  636.8 23.3 %collective-permute-start.7 = (bf16[512,2048]{1,0:T(8,128)(2,1)}, bf16[512,2048]{1,0:T(8,128)(2,1)}, u32[]{:S(2)}, u32[]{:S(2)}) collective-permute-start(bf16[512,2048]{1,0:T(8,128)(2,1)} %bitcast.94), channel_id=1, source_target_pairs={{0,1},{1,0},{2,3},{3,2},{4,5},{5,4},{6,7},{7,6},{8,9},{9,8},{10,11... | collective-permute-start | bytes 6291464 | tf_op jit(solution)/shard_map/ppermute | solution.py:236
  657.1 3.0 collective-permute-start.6
  671.7 50.6 %collective-permute-start.10 = (bf16[256,1024]{1,0:T(8,128)(2,1)S(1)}, bf16[256,1024]{1,0:T(8,128)(2,1)}, u32[]{:S(2)}, u32[]{:S(2)}) collective-permute-start(bf16[256,1024]{1,0:T(8,128)(2,1)S(1)} %get-tuple-element.3482), channel_id=1, source_target_pairs={{0,6},{2,0},{4,2},{6,4},{1,7},{3,1},{5,3},{7,5},{8,14},{10,8},{12,... | collective-permute-start | bytes 1572872 | tf_op jit(solution)/shard_map/ppermute | solution.py:33
  674.7 61.9 %collective-permute-start.8 = (bf16[256,1024]{1,0:T(8,128)(2,1)S(1)}, bf16[256,1024]{1,0:T(8,128)(2,1)}, u32[]{:S(2)}, u32[]{:S(2)}) collective-permute-start(bf16[256,1024]{1,0:T(8,128)(2,1)S(1)} %get-tuple-element.3481), channel_id=1, source_target_pairs={{0,2},{2,4},{4,6},{6,0},{1,3},{3,5},{5,7},{7,1},{8,10},{10,12},{12... | collective-permute-start | bytes 1572872 | tf_op jit(solution)/shard_map/ppermute | solution.py:33
  674.7 61.9 %collective-permute-start.9 = (bf16[256,1024]{1,0:T(8,128)(2,1)S(1)}, bf16[256,1024]{1,0:T(8,128)(2,1)}, u32[]{:S(2)}, u32[]{:S(2)}) collective-permute-start(bf16[256,1024]{1,0:T(8,128)(2,1)S(1)} %get-tuple-element.3483), channel_id=1, source_target_pairs={{0,4},{2,6},{4,0},{6,2},{1,5},{3,7},{5,1},{7,3},{8,12},{10,14},{12... | collective-permute-start | bytes 1572872 | tf_op jit(solution)/shard_map/ppermute | solution.py:33
  679.6 2.0 copy-start.3
  681.8 62.0 %collective-permute-start.14 = (bf16[256,1024]{1,0:T(8,128)(2,1)S(1)}, bf16[256,1024]{1,0:T(8,128)(2,1)}, u32[]{:S(2)}, u32[]{:S(2)}) collective-permute-start(bf16[256,1024]{1,0:T(8,128)(2,1)S(1)} %get-tuple-element.3484), channel_id=1, source_target_pairs={{0,8},{8,16},{16,24},{24,0},{1,9},{9,17},{17,25},{25,1},{2,10},{10... | collective-permute-start | bytes 1572872 | tf_op jit(solution)/shard_map/ppermute | solution.py:33
  681.9 92.4 %collective-permute-start.15 = (bf16[256,1024]{1,0:T(8,128)(2,1)S(1)}, bf16[256,1024]{1,0:T(8,128)(2,1)}, u32[]{:S(2)}, u32[]{:S(2)}) collective-permute-start(bf16[256,1024]{1,0:T(8,128)(2,1)S(1)} %get-tuple-element.3486), channel_id=1, source_target_pairs={{0,16},{8,24},{16,0},{24,8},{1,17},{9,25},{17,1},{25,9},{2,18},{10... | collective-permute-start | bytes 1572872 | tf_op jit(solution)/shard_map/ppermute | solution.py:33
  722.4 51.9 %collective-permute-start.16 = (bf16[256,1024]{1,0:T(8,128)(2,1)S(1)}, bf16[256,1024]{1,0:T(8,128)(2,1)S(1)}, u32[]{:S(2)}, u32[]{:S(2)}) collective-permute-start(bf16[256,1024]{1,0:T(8,128)(2,1)S(1)} %get-tuple-element.3485), channel_id=1, source_target_pairs={{0,24},{8,0},{16,8},{24,16},{1,25},{9,1},{17,9},{25,17},{2,26},{10... | collective-permute-start | bytes 1572872 | tf_op jit(solution)/shard_map/ppermute | solution.py:33
  738.8 40.3 %collective-permute-start.11 = (bf16[64,1024]{1,0:T(8,128)(2,1)S(1)}, bf16[64,1024]{1,0:T(8,128)(2,1)S(1)}, u32[]{:S(2)}, u32[]{:S(2)}) collective-permute-start(bf16[64,1024]{1,0:T(8,128)(2,1)S(1)} %get-tuple-element.3489), channel_id=1, source_target_pairs={{0,8},{8,16},{16,24},{24,0},{1,9},{9,17},{17,25},{25,1},{2,10},{10... | collective-permute-start | bytes 393224 | tf_op jit(solution)/shard_map/ppermute | solution.py:33
  738.9 42.1 %collective-permute-start.12 = (bf16[64,1024]{1,0:T(8,128)(2,1)S(1)}, bf16[64,1024]{1,0:T(8,128)(2,1)S(1)}, u32[]{:S(2)}, u32[]{:S(2)}) collective-permute-start(bf16[64,1024]{1,0:T(8,128)(2,1)S(1)} %get-tuple-element.3491), channel_id=1, source_target_pairs={{0,16},{8,24},{16,0},{24,8},{1,17},{9,25},{17,1},{25,9},{2,18},{10... | collective-permute-start | bytes 393224 | tf_op jit(solution)/shard_map/ppermute | solution.py:33
  743.8 37.1 %collective-permute-start.13 = (bf16[64,1024]{1,0:T(8,128)(2,1)S(1)}, bf16[64,1024]{1,0:T(8,128)(2,1)S(1)}, u32[]{:S(2)}, u32[]{:S(2)}) collective-permute-start(bf16[64,1024]{1,0:T(8,128)(2,1)S(1)} %get-tuple-element.3490), channel_id=1, source_target_pairs={{0,24},{8,0},{16,8},{24,16},{1,25},{9,1},{17,9},{25,17},{2,26},{10... | collective-permute-start | bytes 393224 | tf_op jit(solution)/shard_map/ppermute | solution.py:33
  776.2 6.6 collective-permute-start.17
  778.2 6.5 collective-permute-start.18
  779.1 5.6 collective-permute-start.19
  (5 other events, 9.6 us)

commit v16 on v15

--- a/solution.py
+++ b/solution.py
@@ -222,7 +222,6 @@
     theirs = lax.ppermute(
         lax.dynamic_index_in_dim(normed_all, 1 - core, 0, keepdims=False), "core", swap
     )
-    left = jnp.concatenate([mine, theirs], axis=1)
     carry = (zero_rows, totals_init)
     for lo, hi in phases(sections, micro):
         senders = [
@@ -233,8 +232,10 @@
         carry = lax.fori_loop(lo, hi, functools.partial(backward_step, senders), carry)
     unused_rows, collected = carry
     own = collected.reshape(micro * buses, width)
-    right = jnp.concatenate([own, lax.ppermute(own, "core", swap)], axis=0)
-    half = jnp.dot(left, right, preferred_element_type=jnp.float32)
+    received = lax.ppermute(own, "core", swap)
+    half = lax.optimization_barrier(
+        jnp.dot(mine, own, preferred_element_type=jnp.float32)
+    ) + jnp.dot(theirs, received, preferred_element_type=jnp.float32)
     columns = width // 2
     along_y = scatter_sum(scatter_sum(half[:, :columns], "y"), "z")
     by_z = half[:, columns:].reshape(ys, zs, rows_each, columns)

time: 795 us -> 799 us (level)
    unnamed x15 -> x17, local copies, waits for them, and re-layouts: 25.1 us -> 25.1 us
  transfers between devices with their start and end apart: 36 -> 36, of which waited for: 20 -> 19; matrix products, arithmetic and copies ran while one was open for 3% -> 4% of each run, Pallas kernels for 0% -> 0%
where the time goes in v16:
time: 799 us; the launch traced here: 790 us
  waiting for transfers between devices  429 us (54%)
  starting transfers between devices  154 us (19%)
  local copies, waits for them, and re-layouts  79.6 us (10%)
  matrix products  77 us (10%)
  other arithmetic  47.4 us (6%)
    ppermute x22, waiting for transfers between devices, passed_along(): return lax.ppermute(block, axis, [(i, i + distance) for i in senders])  415 us
    ppermute x12, starting transfers between devices, scatter_sum(): received = lax.ppermute(sent.astype(jnp.bfloat16), axis, route)  89.4 us
    ppermute x22, starting transfers between devices, passed_along(): return lax.ppermute(block, axis, [(i, i + distance) for i in senders])  64.5 us
    unnamed x17, local copies, waits for them, and re-layouts  25.1 us
    dot_general x4, matrix products, layer_forward(): jnp.dot(normed.reshape(-1, width), weight, preferred_element_type=jnp.flo...  18.8 us
    dot_general x4, matrix products, layer_backward(): lax.dot_general(value_total.reshape(-1, width), weight, (((1,), (1,)), ((...  16.7 us
  transfers between devices with their start and end apart: 36, of which 19 were waited for; matrix products, arithmetic and copies ran while one was open for 4% of the time, Pallas kernels for 0%

profile of v16, /device:TPU:96, one launch (start us, length us, event | category | flops | bytes accessed | tf_op | source)
XLA Modules:
  0.0 790.0 jit_solution(5874382573795358394)
XLA Ops:
  13.2 76.1 %while.144 = (s32[]{:T(128)}, bf16[128,2048]{0,1:T(8,128)(2,1)S(1)}, f32[4,128,2048]{1,2,0:T(8,128)}, f32[4,128,1]{1,2,0:T(1,128)S(1)}, bf16[4,128,16,128]{3,2,1...) while((s32[]{:T(128)}, bf16[128,2048]{0,1:T(8,128)(2,1)S(1)}, ...), condition=%wide.region_8.9_spmd.clone, body=%wide.region_1.8_spmd.clone.sunk | while | flops 1216641408 | bytes 26020904 | solution.py:180
  13.2 11.5 %conditional.18 = (bf16[128,2048]{0,1:T(8,128)(2,1)S(1)}, f32[4,128,2048]{1,2,0:T(8,128)}, f32[4,128,1]{1,2,0:T(1,128)S(1)}, bf16[4,128,16,128]{3,2,1,0:T(8,128)...) conditional(s32[]{:T(128)} %convert_element_type.892, ...), branch_computations={%region_2.2_spmd, %region_3.7_spmd} | conditional | flops 1216641408 | bytes 23923316 | solution.py:171
  13.8 4.7 convolution_convert_fusion
  26.0 11.4 %collective-permute-done = bf16[128,2048]{0,1:T(8,128)(2,1)S(1)} collective-permute-done((bf16[128,2048]{0,1:T(8,128)(2,1)S(1)}, bf16[128,2048]{0,1:T(8,128)(2,1)S(1)}, u32[]{:S(2)}, u32[]{:S(2)}) %collective-permute-start) | collective-permute-done | bytes 524320 | tf_op jit(solution)/shard_map/while/body/eval_jaxpr/ppermute | solution.py:16
  37.4 11.4 %conditional.18 = (bf16[128,2048]{0,1:T(8,128)(2,1)S(1)}, f32[4,128,2048]{1,2,0:T(8,128)}, f32[4,128,1]{1,2,0:T(1,128)S(1)}, bf16[4,128,16,128]{3,2,1,0:T(8,128)...) conditional(s32[]{:T(128)} %convert_element_type.892, ...), branch_computations={%region_2.2_spmd, %region_3.7_spmd} | conditional | flops 1216641408 | bytes 23923316 | solution.py:171
  38.0 4.7 convolution_convert_fusion
  48.8 4.5 collective-permute-start
  53.3 10.6 %collective-permute-done = bf16[128,2048]{0,1:T(8,128)(2,1)S(1)} collective-permute-done((bf16[128,2048]{0,1:T(8,128)(2,1)S(1)}, bf16[128,2048]{0,1:T(8,128)(2,1)S(1)}, u32[]{:S(2)}, u32[]{:S(2)}) %collective-permute-start) | collective-permute-done | bytes 524320 | tf_op jit(solution)/shard_map/while/body/eval_jaxpr/ppermute | solution.py:16
  63.9 11.4 %conditional.18 = (bf16[128,2048]{0,1:T(8,128)(2,1)S(1)}, f32[4,128,2048]{1,2,0:T(8,128)}, f32[4,128,1]{1,2,0:T(1,128)S(1)}, bf16[4,128,16,128]{3,2,1,0:T(8,128)...) conditional(s32[]{:T(128)} %convert_element_type.892, ...), branch_computations={%region_2.2_spmd, %region_3.7_spmd} | conditional | flops 1216641408 | bytes 23923316 | solution.py:171
  64.5 4.7 convolution_convert_fusion
  75.2 4.4 collective-permute-start
  79.7 9.7 %collective-permute-done = bf16[128,2048]{0,1:T(8,128)(2,1)S(1)} collective-permute-done((bf16[128,2048]{0,1:T(8,128)(2,1)S(1)}, bf16[128,2048]{0,1:T(8,128)(2,1)S(1)}, u32[]{:S(2)}, u32[]{:S(2)}) %collective-permute-start) | collective-permute-done | bytes 524320 | tf_op jit(solution)/shard_map/while/body/eval_jaxpr/ppermute | solution.py:16
  89.3 81.1 %while.145 = (s32[]{:T(128)}, bf16[128,2048]{0,1:T(8,128)(2,1)S(1)}, f32[4,128,2048]{1,2,0:T(8,128)}, f32[4,128,1]{1,2,0:T(1,128)S(1)}, bf16[4,128,16,128]{3,2,1...) while((s32[]{:T(128)}, bf16[128,2048]{0,1:T(8,128)(2,1)S(1)}, ...), condition=%wide.region_16.17_spmd.clone, body=%wide.region_9.16_spmd.clone.sunk | while | flops 1216641408 | bytes 26020924 | solution.py:180
  89.3 11.4 %conditional.19 = (bf16[128,2048]{0,1:T(8,128)(2,1)S(1)}, f32[4,128,2048]{1,2,0:T(8,128)}, f32[4,128,1]{1,2,0:T(1,128)S(1)}, bf16[4,128,16,128]{3,2,1,0:T(8,128)...) conditional(s32[]{:T(128)} %convert_element_type.893, ...), branch_computations={%region_10.10_spmd, %region_11.15_spmd} | conditional | flops 1216641408 | bytes 23923316 | solution.py:171
  89.9 4.7 convolution_convert_fusion.1
  105.1 8.7 %collective-permute-done.1 = bf16[128,2048]{0,1:T(8,128)(2,1)S(1)} collective-permute-done((bf16[128,2048]{0,1:T(8,128)(2,1)S(1)}, bf16[128,2048]{0,1:T(8,128)(2,1)S(1)}, u32[]{:S(2)}, u32[]{:S(2)}) %collective-permute-start.1) | collective-permute-done | bytes 524320 | tf_op jit(solution)/shard_map/while/body/eval_jaxpr/ppermute | solution.py:16
  114.0 15.7 %collective-permute-start.1 = (bf16[128,2048]{0,1:T(8,128)(2,1)S(1)}, bf16[128,2048]{0,1:T(8,128)(2,1)S(1)}, u32[]{:S(2)}, u32[]{:S(2)}) collective-permute-start(bf16[128,2048]{0,1:T(8,128)(2,1)S(1)} %get-tuple-element.4051), channel_id=1, source_target_pairs={{0,32},{32,64},{64,96},{96,128},{128,160},{160,192},{192,224},{1,3... | collective-permute-start | bytes 1572872 | tf_op jit(solution)/shard_map/while/body/eval_jaxpr/ppermute | solution.py:16
  129.7 7.8 collective-permute-done.1
  137.6 4.4 collective-permute-start.1
  142.0 6.9 collective-permute-done.1
  149.0 14.7 %collective-permute-start.1 = (bf16[128,2048]{0,1:T(8,128)(2,1)S(1)}, bf16[128,2048]{0,1:T(8,128)(2,1)S(1)}, u32[]{:S(2)}, u32[]{:S(2)}) collective-permute-start(bf16[128,2048]{0,1:T(8,128)(2,1)S(1)} %get-tuple-element.4051), channel_id=1, source_target_pairs={{0,32},{32,64},{64,96},{96,128},{128,160},{160,192},{192,224},{1,3... | collective-permute-start | bytes 1572872 | tf_op jit(solution)/shard_map/while/body/eval_jaxpr/ppermute | solution.py:16
  163.8 6.6 collective-permute-done.1
  174.0 5.4 copy.149
  179.4 5.6 copy.151
  187.6 4.5 copy.150
  193.8 4.8 while.147
  198.5 304.7 %while.148 = (s32[]{:T(128)}, bf16[128,2048]{1,0:T(8,128)(2,1)S(1)}, bf16[4,128,2048]{1,2,0:T(8,128)(2,1)}, s32[]{:T(128)}, pred[]{:T(512)}, /*index=5*/bf16[4,1...) while((s32[]{:T(128)}, bf16[128,2048]{1,0:T(8,128)(2,1)S(1)}, ...), condition=%wide.region_38.39_spmd.clone, body=%wide.region_32.38_spmd.clone.sunk | while | flops 1353218048 | bytes 71172632 | solution.py:232
  200.9 13.6 %collective-permute-done.4 = bf16[128,2048]{1,0:T(8,128)(2,1)S(1)} collective-permute-done((bf16[128,2048]{1,0:T(8,128)(2,1)}, bf16[128,2048]{1,0:T(8,128)(2,1)S(1)}, u32[]{:S(2)}, u32[]{:S(2)}) %collective-permute-start.4) | collective-permute-done | bytes 524320 | tf_op jit(solution)/shard_map/while/body/eval_jaxpr/ppermute | solution.py:16
  216.6 27.7 %collective-permute-done.4 = bf16[128,2048]{1,0:T(8,128)(2,1)S(1)} collective-permute-done((bf16[128,2048]{1,0:T(8,128)(2,1)}, bf16[128,2048]{1,0:T(8,128)(2,1)S(1)}, u32[]{:S(2)}, u32[]{:S(2)}) %collective-permute-start.4) | collective-permute-done | bytes 524320 | tf_op jit(solution)/shard_map/while/body/eval_jaxpr/ppermute | solution.py:16
  246.5 16.4 %collective-permute-done.4 = bf16[128,2048]{1,0:T(8,128)(2,1)S(1)} collective-permute-done((bf16[128,2048]{1,0:T(8,128)(2,1)}, bf16[128,2048]{1,0:T(8,128)(2,1)S(1)}, u32[]{:S(2)}, u32[]{:S(2)}) %collective-permute-start.4) | collective-permute-done | bytes 524320 | tf_op jit(solution)/shard_map/while/body/eval_jaxpr/ppermute | solution.py:16
  265.1 238.2 %collective-permute-done.4 = bf16[128,2048]{1,0:T(8,128)(2,1)S(1)} collective-permute-done((bf16[128,2048]{1,0:T(8,128)(2,1)}, bf16[128,2048]{1,0:T(8,128)(2,1)S(1)}, u32[]{:S(2)}, u32[]{:S(2)}) %collective-permute-start.4) | collective-permute-done | bytes 524320 | tf_op jit(solution)/shard_map/while/body/eval_jaxpr/ppermute | solution.py:16
  503.2 129.2 %while.149 = (s32[]{:T(128)}, bf16[128,2048]{1,0:T(8,128)(2,1)S(1)}, bf16[4,128,2048]{1,2,0:T(8,128)(2,1)}, s32[]{:T(128)}, pred[]{:T(512)}, /*index=5*/bf16[4,1...) while((s32[]{:T(128)}, bf16[128,2048]{1,0:T(8,128)(2,1)S(1)}, ...), condition=%wide.region_45.46_spmd.clone, body=%wide.region_39.45_spmd.clone.sunk | while | flops 1353218048 | bytes 71172632 | solution.py:232
  503.3 16.7 %conditional.23 = (bf16[128,2048]{1,0:T(8,128)(2,1)}, bf16[4,128,2048]{1,2,0:T(8,128)(2,1)}) conditional(s32[]{:T(128)} %convert_element_type.897, bf16[4,128,2048]{1,2,0:T(8,128)(2,1)} %get-tuple-element.4505, (pred[]{:T(512)}, s32[]{:T(128)}, bf16[4,128,2048]{2,1,0:T(8,128)(2,1)}, bf16[128,2048]{1,0:T(8,128)(2,1)S(1)}, ...), branch_computations={%region_40.40_spmd, %region_41.44_spmd} | conditional | flops 1353218048 | bytes 69075104 | solution.py:207
  521.2 16.0 %collective-permute-done.5 = bf16[128,2048]{1,0:T(8,128)(2,1)S(1)} collective-permute-done((bf16[128,2048]{1,0:T(8,128)(2,1)}, bf16[128,2048]{1,0:T(8,128)(2,1)S(1)}, u32[]{:S(2)}, u32[]{:S(2)}) %collective-permute-start.5) | collective-permute-done | bytes 524320 | tf_op jit(solution)/shard_map/while/body/eval_jaxpr/ppermute | solution.py:16
  537.2 16.7 %conditional.23 = (bf16[128,2048]{1,0:T(8,128)(2,1)}, bf16[4,128,2048]{1,2,0:T(8,128)(2,1)}) conditional(s32[]{:T(128)} %convert_element_type.897, bf16[4,128,2048]{1,2,0:T(8,128)(2,1)} %get-tuple-element.4505, (pred[]{:T(512)}, s32[]{:T(128)}, bf16[4,128,2048]{2,1,0:T(8,128)(2,1)}, bf16[128,2048]{1,0:T(8,128)(2,1)S(1)}, ...), branch_computations={%region_40.40_spmd, %region_41.44_spmd} | conditional | flops 1353218048 | bytes 69075104 | solution.py:207
  555.1 16.1 %collective-permute-done.5 = bf16[128,2048]{1,0:T(8,128)(2,1)S(1)} collective-permute-done((bf16[128,2048]{1,0:T(8,128)(2,1)}, bf16[128,2048]{1,0:T(8,128)(2,1)S(1)}, u32[]{:S(2)}, u32[]{:S(2)}) %collective-permute-start.5) | collective-permute-done | bytes 524320 | tf_op jit(solution)/shard_map/while/body/eval_jaxpr/ppermute | solution.py:16
  571.2 16.7 %conditional.23 = (bf16[128,2048]{1,0:T(8,128)(2,1)}, bf16[4,128,2048]{1,2,0:T(8,128)(2,1)}) conditional(s32[]{:T(128)} %convert_element_type.897, bf16[4,128,2048]{1,2,0:T(8,128)(2,1)} %get-tuple-element.4505, (pred[]{:T(512)}, s32[]{:T(128)}, bf16[4,128,2048]{2,1,0:T(8,128)(2,1)}, bf16[128,2048]{1,0:T(8,128)(2,1)S(1)}, ...), branch_computations={%region_40.40_spmd, %region_41.44_spmd} | conditional | flops 1353218048 | bytes 69075104 | solution.py:207
  589.2 15.3 %collective-permute-done.5 = bf16[128,2048]{1,0:T(8,128)(2,1)S(1)} collective-permute-done((bf16[128,2048]{1,0:T(8,128)(2,1)}, bf16[128,2048]{1,0:T(8,128)(2,1)S(1)}, u32[]{:S(2)}, u32[]{:S(2)}) %collective-permute-start.5) | collective-permute-done | bytes 524320 | tf_op jit(solution)/shard_map/while/body/eval_jaxpr/ppermute | solution.py:16
  604.5 16.7 %conditional.23 = (bf16[128,2048]{1,0:T(8,128)(2,1)}, bf16[4,128,2048]{1,2,0:T(8,128)(2,1)}) conditional(s32[]{:T(128)} %convert_element_type.897, bf16[4,128,2048]{1,2,0:T(8,128)(2,1)} %get-tuple-element.4505, (pred[]{:T(512)}, s32[]{:T(128)}, bf16[4,128,2048]{2,1,0:T(8,128)(2,1)}, bf16[128,2048]{1,0:T(8,128)(2,1)S(1)}, ...), branch_computations={%region_40.40_spmd, %region_41.44_spmd} | conditional | flops 1353218048 | bytes 69075104 | solution.py:207
  622.4 10.0 %collective-permute-done.5 = bf16[128,2048]{1,0:T(8,128)(2,1)S(1)} collective-permute-done((bf16[128,2048]{1,0:T(8,128)(2,1)}, bf16[128,2048]{1,0:T(8,128)(2,1)S(1)}, u32[]{:S(2)}, u32[]{:S(2)}) %collective-permute-start.5) | collective-permute-done | bytes 524320 | tf_op jit(solution)/shard_map/while/body/eval_jaxpr/ppermute | solution.py:16
  639.3 10.7 %copy.146 = bf16[4,128,2048]{1,0,2:T(4,128)(2,1)} copy(bf16[4,128,2048]{1,2,0:T(8,128)(2,1)S(1)} %convert_element_type.505) | data formatting | bytes 4194304 | tf_op jit(solution)/shard_map/convert_element_type | solution.py:217
  657.3 7.2 fusion.217
  664.5 6.4 convolution_add_fusion.3
  686.5 40.5 %collective-permute-start.15 = (bf16[256,1024]{1,0:T(8,128)(2,1)S(1)}, bf16[256,1024]{1,0:T(8,128)(2,1)}, u32[]{:S(2)}, u32[]{:S(2)}) collective-permute-start(bf16[256,1024]{1,0:T(8,128)(2,1)S(1)} %get-tuple-element.3486), channel_id=1, source_target_pairs={{0,16},{8,24},{16,0},{24,8},{1,17},{9,25},{17,1},{25,9},{2,18},{10... | collective-permute-start | bytes 1572872 | tf_op jit(solution)/shard_map/ppermute | solution.py:33
  726.9 14.1 %collective-permute-start.16 = (bf16[256,1024]{1,0:T(8,128)(2,1)S(1)}, bf16[256,1024]{1,0:T(8,128)(2,1)S(1)}, u32[]{:S(2)}, u32[]{:S(2)}) collective-permute-start(bf16[256,1024]{1,0:T(8,128)(2,1)S(1)} %get-tuple-element.3485), channel_id=1, source_target_pairs={{0,24},{8,0},{16,8},{24,16},{1,25},{9,1},{17,9},{25,17},{2,26},{10... | collective-permute-start | bytes 1572872 | tf_op jit(solution)/shard_map/ppermute | solution.py:33
  743.2 5.0 collective-permute-start.12
  748.1 19.6 %collective-permute-start.13 = (bf16[64,1024]{1,0:T(8,128)(2,1)S(1)}, bf16[64,1024]{1,0:T(8,128)(2,1)S(1)}, u32[]{:S(2)}, u32[]{:S(2)}) collective-permute-start(bf16[64,1024]{1,0:T(8,128)(2,1)S(1)} %get-tuple-element.3488), channel_id=1, source_target_pairs={{0,24},{8,0},{16,8},{24,16},{1,25},{9,1},{17,9},{25,17},{2,26},{10... | collective-permute-start | bytes 393224 | tf_op jit(solution)/shard_map/ppermute | solution.py:33
  767.8 10.7 %collective-permute-done.15 = bf16[256,1024]{1,0:T(8,128)(2,1)} collective-permute-done((bf16[256,1024]{1,0:T(8,128)(2,1)S(1)}, bf16[256,1024]{1,0:T(8,128)(2,1)}, u32[]{:S(2)}, u32[]{:S(2)}) %collective-permute-start.15) | collective-permute-done | bytes 524320 | tf_op jit(solution)/shard_map/ppermute | solution.py:33
  (283 shorter events, 191.0 us)
Async XLA Ops:
  9.8 3.3 copy-start.6
  9.9 3.3 copy-start.8
  24.7 12.7 %collective-permute-start = (bf16[128,2048]{0,1:T(8,128)(2,1)S(1)}, bf16[128,2048]{0,1:T(8,128)(2,1)S(1)}, u32[]{:S(2)}, u32[]{:S(2)}) collective-permute-start(bf16[128,2048]{0,1:T(8,128)(2,1)S(1)} %get-tuple-element.4027), channel_id=1, source_target_pairs={{0,32},{32,64},{64,96},{1,33},{33,65},{65,97},{2,34},{34,66},{66,9... | collective-permute-start | bytes 1572872 | tf_op jit(solution)/shard_map/while/body/eval_jaxpr/ppermute | solution.py:16
  48.8 15.0 %collective-permute-start = (bf16[128,2048]{0,1:T(8,128)(2,1)S(1)}, bf16[128,2048]{0,1:T(8,128)(2,1)S(1)}, u32[]{:S(2)}, u32[]{:S(2)}) collective-permute-start(bf16[128,2048]{0,1:T(8,128)(2,1)S(1)} %get-tuple-element.4027), channel_id=1, source_target_pairs={{0,32},{32,64},{64,96},{1,33},{33,65},{65,97},{2,34},{34,66},{66,9... | collective-permute-start | bytes 1572872 | tf_op jit(solution)/shard_map/while/body/eval_jaxpr/ppermute | solution.py:16
  75.2 14.1 %collective-permute-start = (bf16[128,2048]{0,1:T(8,128)(2,1)S(1)}, bf16[128,2048]{0,1:T(8,128)(2,1)S(1)}, u32[]{:S(2)}, u32[]{:S(2)}) collective-permute-start(bf16[128,2048]{0,1:T(8,128)(2,1)S(1)} %get-tuple-element.4027), channel_id=1, source_target_pairs={{0,32},{32,64},{64,96},{1,33},{33,65},{65,97},{2,34},{34,66},{66,9... | collective-permute-start | bytes 1572872 | tf_op jit(solution)/shard_map/while/body/eval_jaxpr/ppermute | solution.py:16
  100.8 13.1 %collective-permute-start.1 = (bf16[128,2048]{0,1:T(8,128)(2,1)S(1)}, bf16[128,2048]{0,1:T(8,128)(2,1)S(1)}, u32[]{:S(2)}, u32[]{:S(2)}) collective-permute-start(bf16[128,2048]{0,1:T(8,128)(2,1)S(1)} %get-tuple-element.4051), channel_id=1, source_target_pairs={{0,32},{32,64},{64,96},{96,128},{128,160},{160,192},{192,224},{1,3... | collective-permute-start | bytes 1572872 | tf_op jit(solution)/shard_map/while/body/eval_jaxpr/ppermute | solution.py:16
  114.0 23.6 %collective-permute-start.1 = (bf16[128,2048]{0,1:T(8,128)(2,1)S(1)}, bf16[128,2048]{0,1:T(8,128)(2,1)S(1)}, u32[]{:S(2)}, u32[]{:S(2)}) collective-permute-start(bf16[128,2048]{0,1:T(8,128)(2,1)S(1)} %get-tuple-element.4051), channel_id=1, source_target_pairs={{0,32},{32,64},{64,96},{96,128},{128,160},{160,192},{192,224},{1,3... | collective-permute-start | bytes 1572872 | tf_op jit(solution)/shard_map/while/body/eval_jaxpr/ppermute | solution.py:16
  137.6 11.3 %collective-permute-start.1 = (bf16[128,2048]{0,1:T(8,128)(2,1)S(1)}, bf16[128,2048]{0,1:T(8,128)(2,1)S(1)}, u32[]{:S(2)}, u32[]{:S(2)}) collective-permute-start(bf16[128,2048]{0,1:T(8,128)(2,1)S(1)} %get-tuple-element.4051), channel_id=1, source_target_pairs={{0,32},{32,64},{64,96},{96,128},{128,160},{160,192},{192,224},{1,3... | collective-permute-start | bytes 1572872 | tf_op jit(solution)/shard_map/while/body/eval_jaxpr/ppermute | solution.py:16
  149.0 21.4 %collective-permute-start.1 = (bf16[128,2048]{0,1:T(8,128)(2,1)S(1)}, bf16[128,2048]{0,1:T(8,128)(2,1)S(1)}, u32[]{:S(2)}, u32[]{:S(2)}) collective-permute-start(bf16[128,2048]{0,1:T(8,128)(2,1)S(1)} %get-tuple-element.4051), channel_id=1, source_target_pairs={{0,32},{32,64},{64,96},{96,128},{128,160},{160,192},{192,224},{1,3... | collective-permute-start | bytes 1572872 | tf_op jit(solution)/shard_map/while/body/eval_jaxpr/ppermute | solution.py:16
  170.7 0.7 collective-permute-start.2
  171.6 0.7 collective-permute-start.2
  172.4 0.7 collective-permute-start.2
  173.3 0.7 collective-permute-start.2
  179.4 5.6 copy-start.5
  194.7 0.7 collective-permute-start.3
  196.3 0.7 collective-permute-start.3
  197.8 0.7 collective-permute-start.3
  199.6 14.9 %collective-permute-start.4 = (bf16[128,2048]{1,0:T(8,128)(2,1)}, bf16[128,2048]{1,0:T(8,128)(2,1)S(1)}, u32[]{:S(2)}, u32[]{:S(2)}) collective-permute-start(bf16[128,2048]{1,0:T(8,128)(2,1)} %get-tuple-element.4114), channel_id=1, source_target_pairs={{32,0},{64,32},{96,64},{128,96},{160,128},{192,160},{224,192},{33,... | collective-permute-start | bytes 1572872 | tf_op jit(solution)/shard_map/while/body/eval_jaxpr/ppermute | solution.py:16
  215.3 29.0 %collective-permute-start.4 = (bf16[128,2048]{1,0:T(8,128)(2,1)}, bf16[128,2048]{1,0:T(8,128)(2,1)S(1)}, u32[]{:S(2)}, u32[]{:S(2)}) collective-permute-start(bf16[128,2048]{1,0:T(8,128)(2,1)} %get-tuple-element.4114), channel_id=1, source_target_pairs={{32,0},{64,32},{96,64},{128,96},{160,128},{192,160},{224,192},{33,... | collective-permute-start | bytes 1572872 | tf_op jit(solution)/shard_map/while/body/eval_jaxpr/ppermute | solution.py:16
  245.2 17.7 %collective-permute-start.4 = (bf16[128,2048]{1,0:T(8,128)(2,1)}, bf16[128,2048]{1,0:T(8,128)(2,1)S(1)}, u32[]{:S(2)}, u32[]{:S(2)}) collective-permute-start(bf16[128,2048]{1,0:T(8,128)(2,1)} %get-tuple-element.4114), channel_id=1, source_target_pairs={{32,0},{64,32},{96,64},{128,96},{160,128},{192,160},{224,192},{33,... | collective-permute-start | bytes 1572872 | tf_op jit(solution)/shard_map/while/body/eval_jaxpr/ppermute | solution.py:16
  263.8 239.5 %collective-permute-start.4 = (bf16[128,2048]{1,0:T(8,128)(2,1)}, bf16[128,2048]{1,0:T(8,128)(2,1)S(1)}, u32[]{:S(2)}, u32[]{:S(2)}) collective-permute-start(bf16[128,2048]{1,0:T(8,128)(2,1)} %get-tuple-element.4114), channel_id=1, source_target_pairs={{32,0},{64,32},{96,64},{128,96},{160,128},{192,160},{224,192},{33,... | collective-permute-start | bytes 1572872 | tf_op jit(solution)/shard_map/while/body/eval_jaxpr/ppermute | solution.py:16
  508.3 4.8 slice-start.4
  509.0 4.1 slice-start.5
  519.9 17.3 %collective-permute-start.5 = (bf16[128,2048]{1,0:T(8,128)(2,1)}, bf16[128,2048]{1,0:T(8,128)(2,1)S(1)}, u32[]{:S(2)}, u32[]{:S(2)}) collective-permute-start(bf16[128,2048]{1,0:T(8,128)(2,1)} %get-tuple-element.4131), channel_id=1, source_target_pairs={{32,0},{64,32},{96,64},{33,1},{65,33},{97,65},{34,2},{66,34},{98,6... | collective-permute-start | bytes 1572872 | tf_op jit(solution)/shard_map/while/body/eval_jaxpr/ppermute | solution.py:16
  542.2 4.8 slice-start.4
  542.9 4.1 slice-start.5
  553.8 17.3 %collective-permute-start.5 = (bf16[128,2048]{1,0:T(8,128)(2,1)}, bf16[128,2048]{1,0:T(8,128)(2,1)S(1)}, u32[]{:S(2)}, u32[]{:S(2)}) collective-permute-start(bf16[128,2048]{1,0:T(8,128)(2,1)} %get-tuple-element.4131), channel_id=1, source_target_pairs={{32,0},{64,32},{96,64},{33,1},{65,33},{97,65},{34,2},{66,34},{98,6... | collective-permute-start | bytes 1572872 | tf_op jit(solution)/shard_map/while/body/eval_jaxpr/ppermute | solution.py:16
  576.2 4.8 slice-start.4
  576.9 4.1 slice-start.5
  587.9 16.6 %collective-permute-start.5 = (bf16[128,2048]{1,0:T(8,128)(2,1)}, bf16[128,2048]{1,0:T(8,128)(2,1)S(1)}, u32[]{:S(2)}, u32[]{:S(2)}) collective-permute-start(bf16[128,2048]{1,0:T(8,128)(2,1)} %get-tuple-element.4131), channel_id=1, source_target_pairs={{32,0},{64,32},{96,64},{33,1},{65,33},{97,65},{34,2},{66,34},{98,6... | collective-permute-start | bytes 1572872 | tf_op jit(solution)/shard_map/while/body/eval_jaxpr/ppermute | solution.py:16
  609.5 4.8 slice-start.4
  610.2 4.1 slice-start.5
  621.1 11.3 %collective-permute-start.5 = (bf16[128,2048]{1,0:T(8,128)(2,1)}, bf16[128,2048]{1,0:T(8,128)(2,1)S(1)}, u32[]{:S(2)}, u32[]{:S(2)}) collective-permute-start(bf16[128,2048]{1,0:T(8,128)(2,1)} %get-tuple-element.4131), channel_id=1, source_target_pairs={{32,0},{64,32},{96,64},{33,1},{65,33},{97,65},{34,2},{66,34},{98,6... | collective-permute-start | bytes 1572872 | tf_op jit(solution)/shard_map/while/body/eval_jaxpr/ppermute | solution.py:16
  636.8 27.6 %collective-permute-start.7 = (bf16[512,2048]{1,0:T(8,128)(2,1)}, bf16[512,2048]{1,0:T(8,128)(2,1)}, u32[]{:S(2)}, u32[]{:S(2)}) collective-permute-start(bf16[512,2048]{1,0:T(8,128)(2,1)} %bitcast.93), channel_id=1, source_target_pairs={{0,1},{1,0},{2,3},{3,2},{4,5},{5,4},{6,7},{7,6},{8,9},{9,8},{10,11... | collective-permute-start | bytes 6291464 | tf_op jit(solution)/shard_map/ppermute | solution.py:235
  654.3 3.0 copy-start.7
  656.8 7.7 collective-permute-start.6
  676.3 50.7 %collective-permute-start.10 = (bf16[256,1024]{1,0:T(8,128)(2,1)S(1)}, bf16[256,1024]{1,0:T(8,128)(2,1)}, u32[]{:S(2)}, u32[]{:S(2)}) collective-permute-start(bf16[256,1024]{1,0:T(8,128)(2,1)S(1)} %get-tuple-element.3482), channel_id=1, source_target_pairs={{0,6},{2,0},{4,2},{6,4},{1,7},{3,1},{5,3},{7,5},{8,14},{10,8},{12,... | collective-permute-start | bytes 1572872 | tf_op jit(solution)/shard_map/ppermute | solution.py:33
  679.4 61.6 %collective-permute-start.8 = (bf16[256,1024]{1,0:T(8,128)(2,1)S(1)}, bf16[256,1024]{1,0:T(8,128)(2,1)}, u32[]{:S(2)}, u32[]{:S(2)}) collective-permute-start(bf16[256,1024]{1,0:T(8,128)(2,1)S(1)} %get-tuple-element.3481), channel_id=1, source_target_pairs={{0,2},{2,4},{4,6},{6,0},{1,3},{3,5},{5,7},{7,1},{8,10},{10,12},{12... | collective-permute-start | bytes 1572872 | tf_op jit(solution)/shard_map/ppermute | solution.py:33
  679.4 61.6 %collective-permute-start.9 = (bf16[256,1024]{1,0:T(8,128)(2,1)S(1)}, bf16[256,1024]{1,0:T(8,128)(2,1)}, u32[]{:S(2)}, u32[]{:S(2)}) collective-permute-start(bf16[256,1024]{1,0:T(8,128)(2,1)S(1)} %get-tuple-element.3483), channel_id=1, source_target_pairs={{0,4},{2,6},{4,0},{6,2},{1,5},{3,7},{5,1},{7,3},{8,12},{10,14},{12... | collective-permute-start | bytes 1572872 | tf_op jit(solution)/shard_map/ppermute | solution.py:33
  686.4 61.8 %collective-permute-start.14 = (bf16[256,1024]{1,0:T(8,128)(2,1)S(1)}, bf16[256,1024]{1,0:T(8,128)(2,1)}, u32[]{:S(2)}, u32[]{:S(2)}) collective-permute-start(bf16[256,1024]{1,0:T(8,128)(2,1)S(1)} %get-tuple-element.3484), channel_id=1, source_target_pairs={{0,8},{8,16},{16,24},{24,0},{1,9},{9,17},{17,25},{25,1},{2,10},{10... | collective-permute-start | bytes 1572872 | tf_op jit(solution)/shard_map/ppermute | solution.py:33
  686.5 92.0 %collective-permute-start.15 = (bf16[256,1024]{1,0:T(8,128)(2,1)S(1)}, bf16[256,1024]{1,0:T(8,128)(2,1)}, u32[]{:S(2)}, u32[]{:S(2)}) collective-permute-start(bf16[256,1024]{1,0:T(8,128)(2,1)S(1)} %get-tuple-element.3486), channel_id=1, source_target_pairs={{0,16},{8,24},{16,0},{24,8},{1,17},{9,25},{17,1},{25,9},{2,18},{10... | collective-permute-start | bytes 1572872 | tf_op jit(solution)/shard_map/ppermute | solution.py:33
  726.9 51.5 %collective-permute-start.16 = (bf16[256,1024]{1,0:T(8,128)(2,1)S(1)}, bf16[256,1024]{1,0:T(8,128)(2,1)S(1)}, u32[]{:S(2)}, u32[]{:S(2)}) collective-permute-start(bf16[256,1024]{1,0:T(8,128)(2,1)S(1)} %get-tuple-element.3485), channel_id=1, source_target_pairs={{0,24},{8,0},{16,8},{24,16},{1,25},{9,1},{17,9},{25,17},{2,26},{10... | collective-permute-start | bytes 1572872 | tf_op jit(solution)/shard_map/ppermute | solution.py:33
  743.1 40.1 %collective-permute-start.11 = (bf16[64,1024]{1,0:T(8,128)(2,1)S(1)}, bf16[64,1024]{1,0:T(8,128)(2,1)S(1)}, u32[]{:S(2)}, u32[]{:S(2)}) collective-permute-start(bf16[64,1024]{1,0:T(8,128)(2,1)S(1)} %get-tuple-element.3487), channel_id=1, source_target_pairs={{0,8},{8,16},{16,24},{24,0},{1,9},{9,17},{17,25},{25,1},{2,10},{10... | collective-permute-start | bytes 393224 | tf_op jit(solution)/shard_map/ppermute | solution.py:33
  743.2 41.9 %collective-permute-start.12 = (bf16[64,1024]{1,0:T(8,128)(2,1)S(1)}, bf16[64,1024]{1,0:T(8,128)(2,1)S(1)}, u32[]{:S(2)}, u32[]{:S(2)}) collective-permute-start(bf16[64,1024]{1,0:T(8,128)(2,1)S(1)} %get-tuple-element.3489), channel_id=1, source_target_pairs={{0,16},{8,24},{16,0},{24,8},{1,17},{9,25},{17,1},{25,9},{2,18},{10... | collective-permute-start | bytes 393224 | tf_op jit(solution)/shard_map/ppermute | solution.py:33
  748.1 37.0 %collective-permute-start.13 = (bf16[64,1024]{1,0:T(8,128)(2,1)S(1)}, bf16[64,1024]{1,0:T(8,128)(2,1)S(1)}, u32[]{:S(2)}, u32[]{:S(2)}) collective-permute-start(bf16[64,1024]{1,0:T(8,128)(2,1)S(1)} %get-tuple-element.3488), channel_id=1, source_target_pairs={{0,24},{8,0},{16,8},{24,16},{1,25},{9,1},{17,9},{25,17},{2,26},{10... | collective-permute-start | bytes 393224 | tf_op jit(solution)/shard_map/ppermute | solution.py:33
  780.4 6.6 collective-permute-start.17
  782.3 6.5 collective-permute-start.18
  783.2 5.6 collective-permute-start.19
  (6 other events, 11.6 us)

commit v17 on v12

--- a/solution.py
+++ b/solution.py
@@ -235,7 +235,17 @@
     own = collected.reshape(micro * buses, width)
     right = jnp.concatenate([own, lax.ppermute(own, "core", swap)], axis=0)
     half = jnp.dot(left, right, preferred_element_type=jnp.float32)
-    summed = scatter_sum(scatter_sum(half, "y"), "z")
+    columns = width // 4
+    parts = []
+    for part in range(4):
+        chunk = half[:, part * columns : (part + 1) * columns]
+        if part % 2 == 0:
+            parts.append(scatter_sum(scatter_sum(chunk, "y"), "z"))
+        else:
+            by_z = chunk.reshape(ys, zs, rows_each, columns)
+            by_z = jnp.swapaxes(by_z, 0, 1).reshape(ys * zs * rows_each, columns)
+            parts.append(scatter_sum(scatter_sum(by_z, "z"), "y"))
+    summed = jnp.concatenate(parts, axis=1)
     return summed[None]
 
 

time: 799 us -> 814 us (1.019)
  starting transfers between devices: 111 us -> 180 us
  waiting for transfers between devices: 486 us -> 434 us
    ppermute x6 -> x24, starting transfers between devices: 46 us -> 115 us  [scatter_sum(): received = lax.ppermute(sent.astype(jnp.bfloat16), axis, route)]
    ppermute x6 -> x24, waiting for transfers between devices: 68.8 us -> 16.4 us  [scatter_sum(): received = lax.ppermute(sent.astype(jnp.bfloat16), axis, route)]
    unnamed x13 -> x11, local copies, waits for them, and re-layouts: 24.4 us -> 21.3 us
  transfers between devices with their start and end apart: 30 -> 48, of which waited for: 20 -> 21; matrix products, arithmetic and copies ran while one was open for 3% -> 3% of each run, Pallas kernels for 0% -> 0%
where the time goes in v17:
time: 814 us; the launch traced here: 803 us
  waiting for transfers between devices  434 us (53%)
  starting transfers between devices  180 us (22%)
  local copies, waits for them, and re-layouts  72 us (9%)
  matrix products  69.8 us (9%)
  other arithmetic  44.1 us (5%)
    ppermute x22, waiting for transfers between devices, passed_along(): return lax.ppermute(block, axis, [(i, i + distance) for i in senders])  415 us
    ppermute x24, starting transfers between devices, scatter_sum(): received = lax.ppermute(sent.astype(jnp.bfloat16), axis, route)  115 us
    ppermute x22, starting transfers between devices, passed_along(): return lax.ppermute(block, axis, [(i, i + distance) for i in senders])  64.6 us
    unnamed x11, local copies, waits for them, and re-layouts  21.3 us
    dot_general x4, matrix products, layer_forward(): jnp.dot(normed.reshape(-1, width), weight, preferred_element_type=jnp.flo...  18.8 us
    dot_general x4, matrix products, layer_backward(): lax.dot_general(value_total.reshape(-1, width), weight, (((1,), (1,)), ((...  16.7 us
    ppermute x24, waiting for transfers between devices, scatter_sum(): received = lax.ppermute(sent.astype(jnp.bfloat16), axis, route)  16.4 us
  transfers between devices with their start and end apart: 48, of which 21 were waited for; matrix products, arithmetic and copies ran while one was open for 3% of the time, Pallas kernels for 0%

profile of v17, /device:TPU:96, one launch (start us, length us, event | category | flops | bytes accessed | tf_op | source)
XLA Modules:
  0.0 802.7 jit_solution(10620197194295058016)
XLA Ops:
  13.2 76.2 %while.144 = (s32[]{:T(128)}, bf16[128,2048]{0,1:T(8,128)(2,1)S(1)}, f32[4,128,2048]{1,2,0:T(8,128)}, f32[4,128,1]{1,2,0:T(1,128)S(1)}, bf16[4,128,16,128]{3,2,1...) while((s32[]{:T(128)}, bf16[128,2048]{0,1:T(8,128)(2,1)S(1)}, ...), condition=%wide.region_8.9_spmd.clone, body=%wide.region_1.8_spmd.clone.sunk | while | flops 1216641408 | bytes 26020904 | solution.py:180
  13.3 11.5 %conditional.18 = (bf16[128,2048]{0,1:T(8,128)(2,1)S(1)}, f32[4,128,2048]{1,2,0:T(8,128)}, f32[4,128,1]{1,2,0:T(1,128)S(1)}, bf16[4,128,16,128]{3,2,1,0:T(8,128)...) conditional(s32[]{:T(128)} %convert_element_type.1084, ...), branch_computations={%region_2.2_spmd, %region_3.7_spmd} | conditional | flops 1216641408 | bytes 23923316 | solution.py:171
  13.9 4.7 convolution_convert_fusion
  26.1 11.4 %collective-permute-done = bf16[128,2048]{0,1:T(8,128)(2,1)S(1)} collective-permute-done((bf16[128,2048]{0,1:T(8,128)(2,1)S(1)}, bf16[128,2048]{0,1:T(8,128)(2,1)S(1)}, u32[]{:S(2)}, u32[]{:S(2)}) %collective-permute-start) | collective-permute-done | bytes 524320 | tf_op jit(solution)/shard_map/while/body/eval_jaxpr/ppermute | solution.py:16
  37.5 11.4 %conditional.18 = (bf16[128,2048]{0,1:T(8,128)(2,1)S(1)}, f32[4,128,2048]{1,2,0:T(8,128)}, f32[4,128,1]{1,2,0:T(1,128)S(1)}, bf16[4,128,16,128]{3,2,1,0:T(8,128)...) conditional(s32[]{:T(128)} %convert_element_type.1084, ...), branch_computations={%region_2.2_spmd, %region_3.7_spmd} | conditional | flops 1216641408 | bytes 23923316 | solution.py:171
  38.1 4.7 convolution_convert_fusion
  48.9 4.5 collective-permute-start
  53.4 10.6 %collective-permute-done = bf16[128,2048]{0,1:T(8,128)(2,1)S(1)} collective-permute-done((bf16[128,2048]{0,1:T(8,128)(2,1)S(1)}, bf16[128,2048]{0,1:T(8,128)(2,1)S(1)}, u32[]{:S(2)}, u32[]{:S(2)}) %collective-permute-start) | collective-permute-done | bytes 524320 | tf_op jit(solution)/shard_map/while/body/eval_jaxpr/ppermute | solution.py:16
  64.0 11.3 %conditional.18 = (bf16[128,2048]{0,1:T(8,128)(2,1)S(1)}, f32[4,128,2048]{1,2,0:T(8,128)}, f32[4,128,1]{1,2,0:T(1,128)S(1)}, bf16[4,128,16,128]{3,2,1,0:T(8,128)...) conditional(s32[]{:T(128)} %convert_element_type.1084, ...), branch_computations={%region_2.2_spmd, %region_3.7_spmd} | conditional | flops 1216641408 | bytes 23923316 | solution.py:171
  64.6 4.7 convolution_convert_fusion
  75.3 4.4 collective-permute-start
  79.7 9.7 %collective-permute-done = bf16[128,2048]{0,1:T(8,128)(2,1)S(1)} collective-permute-done((bf16[128,2048]{0,1:T(8,128)(2,1)S(1)}, bf16[128,2048]{0,1:T(8,128)(2,1)S(1)}, u32[]{:S(2)}, u32[]{:S(2)}) %collective-permute-start) | collective-permute-done | bytes 524320 | tf_op jit(solution)/shard_map/while/body/eval_jaxpr/ppermute | solution.py:16
  89.4 81.2 %while.145 = (s32[]{:T(128)}, bf16[128,2048]{0,1:T(8,128)(2,1)S(1)}, f32[4,128,2048]{1,2,0:T(8,128)}, f32[4,128,1]{1,2,0:T(1,128)S(1)}, bf16[4,128,16,128]{3,2,1...) while((s32[]{:T(128)}, bf16[128,2048]{0,1:T(8,128)(2,1)S(1)}, ...), condition=%wide.region_16.17_spmd.clone, body=%wide.region_9.16_spmd.clone.sunk | while | flops 1216641408 | bytes 26020924 | solution.py:180
  89.4 11.5 %conditional.19 = (bf16[128,2048]{0,1:T(8,128)(2,1)S(1)}, f32[4,128,2048]{1,2,0:T(8,128)}, f32[4,128,1]{1,2,0:T(1,128)S(1)}, bf16[4,128,16,128]{3,2,1,0:T(8,128)...) conditional(s32[]{:T(128)} %convert_element_type.1085, ...), branch_computations={%region_10.10_spmd, %region_11.15_spmd} | conditional | flops 1216641408 | bytes 23923316 | solution.py:171
  90.0 4.7 convolution_convert_fusion.1
  100.9 4.3 collective-permute-start.1
  105.2 8.7 %collective-permute-done.1 = bf16[128,2048]{0,1:T(8,128)(2,1)S(1)} collective-permute-done((bf16[128,2048]{0,1:T(8,128)(2,1)S(1)}, bf16[128,2048]{0,1:T(8,128)(2,1)S(1)}, u32[]{:S(2)}, u32[]{:S(2)}) %collective-permute-start.1) | collective-permute-done | bytes 524320 | tf_op jit(solution)/shard_map/while/body/eval_jaxpr/ppermute | solution.py:16
  114.0 15.8 %collective-permute-start.1 = (bf16[128,2048]{0,1:T(8,128)(2,1)S(1)}, bf16[128,2048]{0,1:T(8,128)(2,1)S(1)}, u32[]{:S(2)}, u32[]{:S(2)}) collective-permute-start(bf16[128,2048]{0,1:T(8,128)(2,1)S(1)} %get-tuple-element.4067), channel_id=1, source_target_pairs={{0,32},{32,64},{64,96},{96,128},{128,160},{160,192},{192,224},{1,3... | collective-permute-start | bytes 1572872 | tf_op jit(solution)/shard_map/while/body/eval_jaxpr/ppermute | solution.py:16
  129.8 7.8 collective-permute-done.1
  137.7 4.4 collective-permute-start.1
  142.2 6.9 collective-permute-done.1
  149.2 14.7 %collective-permute-start.1 = (bf16[128,2048]{0,1:T(8,128)(2,1)S(1)}, bf16[128,2048]{0,1:T(8,128)(2,1)S(1)}, u32[]{:S(2)}, u32[]{:S(2)}) collective-permute-start(bf16[128,2048]{0,1:T(8,128)(2,1)S(1)} %get-tuple-element.4067), channel_id=1, source_target_pairs={{0,32},{32,64},{64,96},{96,128},{128,160},{160,192},{192,224},{1,3... | collective-permute-start | bytes 1572872 | tf_op jit(solution)/shard_map/while/body/eval_jaxpr/ppermute | solution.py:16
  163.9 6.6 collective-permute-done.1
  174.2 5.4 copy.150
  179.6 5.6 copy.152
  187.9 4.5 copy.151
  194.1 4.8 while.147
  198.9 305.0 %while.148 = (s32[]{:T(128)}, bf16[128,2048]{1,0:T(8,128)(2,1)S(1)}, bf16[4,128,2048]{1,2,0:T(8,128)(2,1)}, s32[]{:T(128)}, pred[]{:T(512)}, /*index=5*/bf16[4,1...) while((s32[]{:T(128)}, bf16[128,2048]{1,0:T(8,128)(2,1)S(1)}, ...), condition=%wide.region_38.39_spmd.clone, body=%wide.region_32.38_spmd.clone.sunk | while | flops 1353218048 | bytes 71172632 | solution.py:233
  201.5 13.5 %collective-permute-done.4 = bf16[128,2048]{1,0:T(8,128)(2,1)S(1)} collective-permute-done((bf16[128,2048]{1,0:T(8,128)(2,1)}, bf16[128,2048]{1,0:T(8,128)(2,1)S(1)}, u32[]{:S(2)}, u32[]{:S(2)}) %collective-permute-start.4) | collective-permute-done | bytes 524320 | tf_op jit(solution)/shard_map/while/body/eval_jaxpr/ppermute | solution.py:16
  217.1 27.8 %collective-permute-done.4 = bf16[128,2048]{1,0:T(8,128)(2,1)S(1)} collective-permute-done((bf16[128,2048]{1,0:T(8,128)(2,1)}, bf16[128,2048]{1,0:T(8,128)(2,1)S(1)}, u32[]{:S(2)}, u32[]{:S(2)}) %collective-permute-start.4) | collective-permute-done | bytes 524320 | tf_op jit(solution)/shard_map/while/body/eval_jaxpr/ppermute | solution.py:16
  247.0 16.3 %collective-permute-done.4 = bf16[128,2048]{1,0:T(8,128)(2,1)S(1)} collective-permute-done((bf16[128,2048]{1,0:T(8,128)(2,1)}, bf16[128,2048]{1,0:T(8,128)(2,1)S(1)}, u32[]{:S(2)}, u32[]{:S(2)}) %collective-permute-start.4) | collective-permute-done | bytes 524320 | tf_op jit(solution)/shard_map/while/body/eval_jaxpr/ppermute | solution.py:16
  265.5 238.4 %collective-permute-done.4 = bf16[128,2048]{1,0:T(8,128)(2,1)S(1)} collective-permute-done((bf16[128,2048]{1,0:T(8,128)(2,1)}, bf16[128,2048]{1,0:T(8,128)(2,1)S(1)}, u32[]{:S(2)}, u32[]{:S(2)}) %collective-permute-start.4) | collective-permute-done | bytes 524320 | tf_op jit(solution)/shard_map/while/body/eval_jaxpr/ppermute | solution.py:16
  503.9 129.2 %while.149 = (s32[]{:T(128)}, bf16[128,2048]{1,0:T(8,128)(2,1)S(1)}, bf16[4,128,2048]{1,2,0:T(8,128)(2,1)}, s32[]{:T(128)}, pred[]{:T(512)}, /*index=5*/bf16[4,1...) while((s32[]{:T(128)}, bf16[128,2048]{1,0:T(8,128)(2,1)S(1)}, ...), condition=%wide.region_45.46_spmd.clone, body=%wide.region_39.45_spmd.clone.sunk | while | flops 1353218048 | bytes 71172632 | solution.py:233
  503.9 16.7 %conditional.23 = (bf16[128,2048]{1,0:T(8,128)(2,1)}, bf16[4,128,2048]{1,2,0:T(8,128)(2,1)}) conditional(s32[]{:T(128)} %convert_element_type.1089, bf16[4,128,2048]{1,2,0:T(8,128)(2,1)} %get-tuple-element.4521, (pred[]{:T(512)}, s32[]{:T(128)}, bf16[4,128,2048]{2,1,0:T(8,128)(2,1)}, bf16[128,2048]{1,0:T(8,128)(2,1)S(1)}, ...), branch_computations={%region_40.40_spmd, %region_41.44_spmd} | conditional | flops 1353218048 | bytes 69075104 | solution.py:207
  521.9 16.0 %collective-permute-done.5 = bf16[128,2048]{1,0:T(8,128)(2,1)S(1)} collective-permute-done((bf16[128,2048]{1,0:T(8,128)(2,1)}, bf16[128,2048]{1,0:T(8,128)(2,1)S(1)}, u32[]{:S(2)}, u32[]{:S(2)}) %collective-permute-start.5) | collective-permute-done | bytes 524320 | tf_op jit(solution)/shard_map/while/body/eval_jaxpr/ppermute | solution.py:16
  537.9 16.7 %conditional.23 = (bf16[128,2048]{1,0:T(8,128)(2,1)}, bf16[4,128,2048]{1,2,0:T(8,128)(2,1)}) conditional(s32[]{:T(128)} %convert_element_type.1089, bf16[4,128,2048]{1,2,0:T(8,128)(2,1)} %get-tuple-element.4521, (pred[]{:T(512)}, s32[]{:T(128)}, bf16[4,128,2048]{2,1,0:T(8,128)(2,1)}, bf16[128,2048]{1,0:T(8,128)(2,1)S(1)}, ...), branch_computations={%region_40.40_spmd, %region_41.44_spmd} | conditional | flops 1353218048 | bytes 69075104 | solution.py:207
  555.9 16.0 %collective-permute-done.5 = bf16[128,2048]{1,0:T(8,128)(2,1)S(1)} collective-permute-done((bf16[128,2048]{1,0:T(8,128)(2,1)}, bf16[128,2048]{1,0:T(8,128)(2,1)S(1)}, u32[]{:S(2)}, u32[]{:S(2)}) %collective-permute-start.5) | collective-permute-done | bytes 524320 | tf_op jit(solution)/shard_map/while/body/eval_jaxpr/ppermute | solution.py:16
  571.9 16.7 %conditional.23 = (bf16[128,2048]{1,0:T(8,128)(2,1)}, bf16[4,128,2048]{1,2,0:T(8,128)(2,1)}) conditional(s32[]{:T(128)} %convert_element_type.1089, bf16[4,128,2048]{1,2,0:T(8,128)(2,1)} %get-tuple-element.4521, (pred[]{:T(512)}, s32[]{:T(128)}, bf16[4,128,2048]{2,1,0:T(8,128)(2,1)}, bf16[128,2048]{1,0:T(8,128)(2,1)S(1)}, ...), branch_computations={%region_40.40_spmd, %region_41.44_spmd} | conditional | flops 1353218048 | bytes 69075104 | solution.py:207
  589.8 15.3 %collective-permute-done.5 = bf16[128,2048]{1,0:T(8,128)(2,1)S(1)} collective-permute-done((bf16[128,2048]{1,0:T(8,128)(2,1)}, bf16[128,2048]{1,0:T(8,128)(2,1)S(1)}, u32[]{:S(2)}, u32[]{:S(2)}) %collective-permute-start.5) | collective-permute-done | bytes 524320 | tf_op jit(solution)/shard_map/while/body/eval_jaxpr/ppermute | solution.py:16
  605.2 16.7 %conditional.23 = (bf16[128,2048]{1,0:T(8,128)(2,1)}, bf16[4,128,2048]{1,2,0:T(8,128)(2,1)}) conditional(s32[]{:T(128)} %convert_element_type.1089, bf16[4,128,2048]{1,2,0:T(8,128)(2,1)} %get-tuple-element.4521, (pred[]{:T(512)}, s32[]{:T(128)}, bf16[4,128,2048]{2,1,0:T(8,128)(2,1)}, bf16[128,2048]{1,0:T(8,128)(2,1)S(1)}, ...), branch_computations={%region_40.40_spmd, %region_41.44_spmd} | conditional | flops 1353218048 | bytes 69075104 | solution.py:207
  623.1 10.0 %collective-permute-done.5 = bf16[128,2048]{1,0:T(8,128)(2,1)S(1)} collective-permute-done((bf16[128,2048]{1,0:T(8,128)(2,1)}, bf16[128,2048]{1,0:T(8,128)(2,1)S(1)}, u32[]{:S(2)}, u32[]{:S(2)}) %collective-permute-start.5) | collective-permute-done | bytes 524320 | tf_op jit(solution)/shard_map/while/body/eval_jaxpr/ppermute | solution.py:16
  639.7 10.7 %copy.147 = bf16[4,128,2048]{1,0,2:T(4,128)(2,1)} copy(bf16[4,128,2048]{1,2,0:T(8,128)(2,1)S(1)} %convert_element_type.613) | data formatting | bytes 4194304 | tf_op jit(solution)/shard_map/convert_element_type | solution.py:217
  660.5 6.2 fusion.213
  676.6 6.4 collective-permute-done.10
  683.0 52.4 %collective-permute-start.15 = (bf16[256,512]{1,0:T(8,128)(2,1)S(1)}, bf16[256,512]{1,0:T(8,128)(2,1)S(1)}, u32[]{:S(2)}, u32[]{:S(2)}) collective-permute-start(bf16[256,512]{1,0:T(8,128)(2,1)S(1)} %get-tuple-element.3488), channel_id=1, source_target_pairs={{0,16},{8,24},{16,0},{24,8},{1,17},{9,25},{17,1},{25,9},{2,18},{10... | collective-permute-start | bytes 786440 | tf_op jit(solution)/shard_map/ppermute | solution.py:33
  738.2 16.7 %collective-permute-start.16 = (bf16[256,512]{1,0:T(8,128)(2,1)S(1)}, bf16[256,512]{1,0:T(8,128)(2,1)S(1)}, u32[]{:S(2)}, u32[]{:S(2)}) collective-permute-start(bf16[256,512]{1,0:T(8,128)(2,1)S(1)} %get-tuple-element.3487), channel_id=1, source_target_pairs={{0,24},{8,0},{16,8},{24,16},{1,25},{9,1},{17,9},{25,17},{2,26},{10... | collective-permute-start | bytes 786440 | tf_op jit(solution)/shard_map/ppermute | solution.py:33
  761.7 11.6 %collective-permute-start.12 = (bf16[64,512]{1,0:T(8,128)(2,1)S(1)}, bf16[64,512]{1,0:T(8,128)(2,1)S(1)}, u32[]{:S(2)}, u32[]{:S(2)}) collective-permute-start(bf16[64,512]{1,0:T(8,128)(2,1)S(1)} %get-tuple-element.3499), channel_id=1, source_target_pairs={{0,16},{8,24},{16,0},{24,8},{1,17},{9,25},{17,1},{25,9},{2,18},{10... | collective-permute-start | bytes 196616 | tf_op jit(solution)/shard_map/ppermute | solution.py:33
  777.6 5.4 collective-permute-done.27
  (309 shorter events, 203.1 us)
Async XLA Ops:
  24.8 12.7 %collective-permute-start = (bf16[128,2048]{0,1:T(8,128)(2,1)S(1)}, bf16[128,2048]{0,1:T(8,128)(2,1)S(1)}, u32[]{:S(2)}, u32[]{:S(2)}) collective-permute-start(bf16[128,2048]{0,1:T(8,128)(2,1)S(1)} %get-tuple-element.4043), channel_id=1, source_target_pairs={{0,32},{32,64},{64,96},{1,33},{33,65},{65,97},{2,34},{34,66},{66,9... | collective-permute-start | bytes 1572872 | tf_op jit(solution)/shard_map/while/body/eval_jaxpr/ppermute | solution.py:16
  48.9 15.1 %collective-permute-start = (bf16[128,2048]{0,1:T(8,128)(2,1)S(1)}, bf16[128,2048]{0,1:T(8,128)(2,1)S(1)}, u32[]{:S(2)}, u32[]{:S(2)}) collective-permute-start(bf16[128,2048]{0,1:T(8,128)(2,1)S(1)} %get-tuple-element.4043), channel_id=1, source_target_pairs={{0,32},{32,64},{64,96},{1,33},{33,65},{65,97},{2,34},{34,66},{66,9... | collective-permute-start | bytes 1572872 | tf_op jit(solution)/shard_map/while/body/eval_jaxpr/ppermute | solution.py:16
  75.3 14.1 %collective-permute-start = (bf16[128,2048]{0,1:T(8,128)(2,1)S(1)}, bf16[128,2048]{0,1:T(8,128)(2,1)S(1)}, u32[]{:S(2)}, u32[]{:S(2)}) collective-permute-start(bf16[128,2048]{0,1:T(8,128)(2,1)S(1)} %get-tuple-element.4043), channel_id=1, source_target_pairs={{0,32},{32,64},{64,96},{1,33},{33,65},{65,97},{2,34},{34,66},{66,9... | collective-permute-start | bytes 1572872 | tf_op jit(solution)/shard_map/while/body/eval_jaxpr/ppermute | solution.py:16
  100.9 13.0 %collective-permute-start.1 = (bf16[128,2048]{0,1:T(8,128)(2,1)S(1)}, bf16[128,2048]{0,1:T(8,128)(2,1)S(1)}, u32[]{:S(2)}, u32[]{:S(2)}) collective-permute-start(bf16[128,2048]{0,1:T(8,128)(2,1)S(1)} %get-tuple-element.4067), channel_id=1, source_target_pairs={{0,32},{32,64},{64,96},{96,128},{128,160},{160,192},{192,224},{1,3... | collective-permute-start | bytes 1572872 | tf_op jit(solution)/shard_map/while/body/eval_jaxpr/ppermute | solution.py:16
  114.0 23.6 %collective-permute-start.1 = (bf16[128,2048]{0,1:T(8,128)(2,1)S(1)}, bf16[128,2048]{0,1:T(8,128)(2,1)S(1)}, u32[]{:S(2)}, u32[]{:S(2)}) collective-permute-start(bf16[128,2048]{0,1:T(8,128)(2,1)S(1)} %get-tuple-element.4067), channel_id=1, source_target_pairs={{0,32},{32,64},{64,96},{96,128},{128,160},{160,192},{192,224},{1,3... | collective-permute-start | bytes 1572872 | tf_op jit(solution)/shard_map/while/body/eval_jaxpr/ppermute | solution.py:16
  137.7 11.3 %collective-permute-start.1 = (bf16[128,2048]{0,1:T(8,128)(2,1)S(1)}, bf16[128,2048]{0,1:T(8,128)(2,1)S(1)}, u32[]{:S(2)}, u32[]{:S(2)}) collective-permute-start(bf16[128,2048]{0,1:T(8,128)(2,1)S(1)} %get-tuple-element.4067), channel_id=1, source_target_pairs={{0,32},{32,64},{64,96},{96,128},{128,160},{160,192},{192,224},{1,3... | collective-permute-start | bytes 1572872 | tf_op jit(solution)/shard_map/while/body/eval_jaxpr/ppermute | solution.py:16
  149.2 21.4 %collective-permute-start.1 = (bf16[128,2048]{0,1:T(8,128)(2,1)S(1)}, bf16[128,2048]{0,1:T(8,128)(2,1)S(1)}, u32[]{:S(2)}, u32[]{:S(2)}) collective-permute-start(bf16[128,2048]{0,1:T(8,128)(2,1)S(1)} %get-tuple-element.4067), channel_id=1, source_target_pairs={{0,32},{32,64},{64,96},{96,128},{128,160},{160,192},{192,224},{1,3... | collective-permute-start | bytes 1572872 | tf_op jit(solution)/shard_map/while/body/eval_jaxpr/ppermute | solution.py:16
  170.9 0.7 collective-permute-start.2
  171.7 0.7 collective-permute-start.2
  172.6 0.7 collective-permute-start.2
  173.5 0.7 collective-permute-start.2
  195.0 0.7 collective-permute-start.3
  196.6 0.7 collective-permute-start.3
  198.2 0.7 collective-permute-start.3
  200.2 14.8 %collective-permute-start.4 = (bf16[128,2048]{1,0:T(8,128)(2,1)}, bf16[128,2048]{1,0:T(8,128)(2,1)S(1)}, u32[]{:S(2)}, u32[]{:S(2)}) collective-permute-start(bf16[128,2048]{1,0:T(8,128)(2,1)} %get-tuple-element.4130), channel_id=1, source_target_pairs={{32,0},{64,32},{96,64},{128,96},{160,128},{192,160},{224,192},{33,... | collective-permute-start | bytes 1572872 | tf_op jit(solution)/shard_map/while/body/eval_jaxpr/ppermute | solution.py:16
  215.8 29.1 %collective-permute-start.4 = (bf16[128,2048]{1,0:T(8,128)(2,1)}, bf16[128,2048]{1,0:T(8,128)(2,1)S(1)}, u32[]{:S(2)}, u32[]{:S(2)}) collective-permute-start(bf16[128,2048]{1,0:T(8,128)(2,1)} %get-tuple-element.4130), channel_id=1, source_target_pairs={{32,0},{64,32},{96,64},{128,96},{160,128},{192,160},{224,192},{33,... | collective-permute-start | bytes 1572872 | tf_op jit(solution)/shard_map/while/body/eval_jaxpr/ppermute | solution.py:16
  245.7 17.6 %collective-permute-start.4 = (bf16[128,2048]{1,0:T(8,128)(2,1)}, bf16[128,2048]{1,0:T(8,128)(2,1)S(1)}, u32[]{:S(2)}, u32[]{:S(2)}) collective-permute-start(bf16[128,2048]{1,0:T(8,128)(2,1)} %get-tuple-element.4130), channel_id=1, source_target_pairs={{32,0},{64,32},{96,64},{128,96},{160,128},{192,160},{224,192},{33,... | collective-permute-start | bytes 1572872 | tf_op jit(solution)/shard_map/while/body/eval_jaxpr/ppermute | solution.py:16
  264.2 239.7 %collective-permute-start.4 = (bf16[128,2048]{1,0:T(8,128)(2,1)}, bf16[128,2048]{1,0:T(8,128)(2,1)S(1)}, u32[]{:S(2)}, u32[]{:S(2)}) collective-permute-start(bf16[128,2048]{1,0:T(8,128)(2,1)} %get-tuple-element.4130), channel_id=1, source_target_pairs={{32,0},{64,32},{96,64},{128,96},{160,128},{192,160},{224,192},{33,... | collective-permute-start | bytes 1572872 | tf_op jit(solution)/shard_map/while/body/eval_jaxpr/ppermute | solution.py:16
  520.6 17.3 %collective-permute-start.5 = (bf16[128,2048]{1,0:T(8,128)(2,1)}, bf16[128,2048]{1,0:T(8,128)(2,1)S(1)}, u32[]{:S(2)}, u32[]{:S(2)}) collective-permute-start(bf16[128,2048]{1,0:T(8,128)(2,1)} %get-tuple-element.4147), channel_id=1, source_target_pairs={{32,0},{64,32},{96,64},{33,1},{65,33},{97,65},{34,2},{66,34},{98,6... | collective-permute-start | bytes 1572872 | tf_op jit(solution)/shard_map/while/body/eval_jaxpr/ppermute | solution.py:16
  554.6 17.3 %collective-permute-start.5 = (bf16[128,2048]{1,0:T(8,128)(2,1)}, bf16[128,2048]{1,0:T(8,128)(2,1)S(1)}, u32[]{:S(2)}, u32[]{:S(2)}) collective-permute-start(bf16[128,2048]{1,0:T(8,128)(2,1)} %get-tuple-element.4147), channel_id=1, source_target_pairs={{32,0},{64,32},{96,64},{33,1},{65,33},{97,65},{34,2},{66,34},{98,6... | collective-permute-start | bytes 1572872 | tf_op jit(solution)/shard_map/while/body/eval_jaxpr/ppermute | solution.py:16
  588.6 16.6 %collective-permute-start.5 = (bf16[128,2048]{1,0:T(8,128)(2,1)}, bf16[128,2048]{1,0:T(8,128)(2,1)S(1)}, u32[]{:S(2)}, u32[]{:S(2)}) collective-permute-start(bf16[128,2048]{1,0:T(8,128)(2,1)} %get-tuple-element.4147), channel_id=1, source_target_pairs={{32,0},{64,32},{96,64},{33,1},{65,33},{97,65},{34,2},{66,34},{98,6... | collective-permute-start | bytes 1572872 | tf_op jit(solution)/shard_map/while/body/eval_jaxpr/ppermute | solution.py:16
  621.8 11.3 %collective-permute-start.5 = (bf16[128,2048]{1,0:T(8,128)(2,1)}, bf16[128,2048]{1,0:T(8,128)(2,1)S(1)}, u32[]{:S(2)}, u32[]{:S(2)}) collective-permute-start(bf16[128,2048]{1,0:T(8,128)(2,1)} %get-tuple-element.4147), channel_id=1, source_target_pairs={{32,0},{64,32},{96,64},{33,1},{65,33},{97,65},{34,2},{66,34},{98,6... | collective-permute-start | bytes 1572872 | tf_op jit(solution)/shard_map/while/body/eval_jaxpr/ppermute | solution.py:16
  637.2 23.3 %collective-permute-start.7 = (bf16[512,2048]{1,0:T(8,128)(2,1)}, bf16[512,2048]{1,0:T(8,128)(2,1)}, u32[]{:S(2)}, u32[]{:S(2)}) collective-permute-start(bf16[512,2048]{1,0:T(8,128)(2,1)} %bitcast.94), channel_id=1, source_target_pairs={{0,1},{1,0},{2,3},{3,2},{4,5},{5,4},{6,7},{7,6},{8,9},{9,8},{10,11... | collective-permute-start | bytes 6291464 | tf_op jit(solution)/shard_map/ppermute | solution.py:236
  657.5 3.0 collective-permute-start.6
  668.2 14.8 %collective-permute-start.10 = (bf16[256,512]{1,0:T(8,128)(2,1)S(1)}, bf16[256,512]{1,0:T(8,128)(2,1)S(1)}, u32[]{:S(2)}, u32[]{:S(2)}) collective-permute-start(bf16[256,512]{1,0:T(8,128)(2,1)S(1)} %get-tuple-element.3484), channel_id=1, source_target_pairs={{0,6},{2,0},{4,2},{6,4},{1,7},{3,1},{5,3},{7,5},{8,14},{10,8},{12,... | collective-permute-start | bytes 786440 | tf_op jit(solution)/shard_map/ppermute | solution.py:33
  671.3 64.1 %collective-permute-start.8 = (bf16[256,512]{1,0:T(8,128)(2,1)S(1)}, bf16[256,512]{1,0:T(8,128)(2,1)S(1)}, u32[]{:S(2)}, u32[]{:S(2)}) collective-permute-start(bf16[256,512]{1,0:T(8,128)(2,1)S(1)} %get-tuple-element.3483), channel_id=1, source_target_pairs={{0,2},{2,4},{4,6},{6,0},{1,3},{3,5},{5,7},{7,1},{8,10},{10,12},{12... | collective-permute-start | bytes 786440 | tf_op jit(solution)/shard_map/ppermute | solution.py:33
  671.3 64.7 %collective-permute-start.9 = (bf16[256,512]{1,0:T(8,128)(2,1)S(1)}, bf16[256,512]{1,0:T(8,128)(2,1)S(1)}, u32[]{:S(2)}, u32[]{:S(2)}) collective-permute-start(bf16[256,512]{1,0:T(8,128)(2,1)S(1)} %get-tuple-element.3485), channel_id=1, source_target_pairs={{0,4},{2,6},{4,0},{6,2},{1,5},{3,7},{5,1},{7,3},{8,12},{10,14},{12... | collective-permute-start | bytes 786440 | tf_op jit(solution)/shard_map/ppermute | solution.py:33
  674.1 82.6 %collective-permute-start.14 = (bf16[256,512]{1,0:T(8,128)(2,1)S(1)}, bf16[256,512]{1,0:T(8,128)(2,1)S(1)}, u32[]{:S(2)}, u32[]{:S(2)}) collective-permute-start(bf16[256,512]{1,0:T(8,128)(2,1)S(1)} %get-tuple-element.3486), channel_id=1, source_target_pairs={{0,8},{8,16},{16,24},{24,0},{1,9},{9,17},{17,25},{25,1},{2,10},{10... | collective-permute-start | bytes 786440 | tf_op jit(solution)/shard_map/ppermute | solution.py:33
  674.3 63.9 %collective-permute-start.20 = (bf16[256,512]{1,0:T(8,128)(2,1)S(1)}, bf16[256,512]{1,0:T(8,128)(2,1)S(1)}, u32[]{:S(2)}, u32[]{:S(2)}) collective-permute-start(bf16[256,512]{1,0:T(8,128)(2,1)S(1)} %get-tuple-element.3489), channel_id=1, source_target_pairs={{0,2},{2,4},{4,6},{6,0},{1,3},{3,5},{5,7},{7,1},{8,10},{10,12},{12... | collective-permute-start | bytes 786440 | tf_op jit(solution)/shard_map/ppermute | solution.py:33
  683.0 76.1 %collective-permute-start.15 = (bf16[256,512]{1,0:T(8,128)(2,1)S(1)}, bf16[256,512]{1,0:T(8,128)(2,1)S(1)}, u32[]{:S(2)}, u32[]{:S(2)}) collective-permute-start(bf16[256,512]{1,0:T(8,128)(2,1)S(1)} %get-tuple-element.3488), channel_id=1, source_target_pairs={{0,16},{8,24},{16,0},{24,8},{1,17},{9,25},{17,1},{25,9},{2,18},{10... | collective-permute-start | bytes 786440 | tf_op jit(solution)/shard_map/ppermute | solution.py:33
  735.4 19.6 %collective-permute-start.21 = (bf16[256,512]{1,0:T(8,128)(2,1)S(1)}, bf16[256,512]{1,0:T(8,128)(2,1)S(1)}, u32[]{:S(2)}, u32[]{:S(2)}) collective-permute-start(bf16[256,512]{1,0:T(8,128)(2,1)S(1)} %get-tuple-element.3491), channel_id=1, source_target_pairs={{0,4},{2,6},{4,0},{6,2},{1,5},{3,7},{5,1},{7,3},{8,12},{10,14},{12... | collective-permute-start | bytes 786440 | tf_op jit(solution)/shard_map/ppermute | solution.py:33
  736.0 19.1 %collective-permute-start.22 = (bf16[256,512]{1,0:T(8,128)(2,1)S(1)}, bf16[256,512]{1,0:T(8,128)(2,1)S(1)}, u32[]{:S(2)}, u32[]{:S(2)}) collective-permute-start(bf16[256,512]{1,0:T(8,128)(2,1)S(1)} %get-tuple-element.3490), channel_id=1, source_target_pairs={{0,6},{2,0},{4,2},{6,4},{1,7},{3,1},{5,3},{7,5},{8,14},{10,8},{12,... | collective-permute-start | bytes 786440 | tf_op jit(solution)/shard_map/ppermute | solution.py:33
  738.2 23.5 %collective-permute-start.16 = (bf16[256,512]{1,0:T(8,128)(2,1)S(1)}, bf16[256,512]{1,0:T(8,128)(2,1)S(1)}, u32[]{:S(2)}, u32[]{:S(2)}) collective-permute-start(bf16[256,512]{1,0:T(8,128)(2,1)S(1)} %get-tuple-element.3487), channel_id=1, source_target_pairs={{0,24},{8,0},{16,8},{24,16},{1,25},{9,1},{17,9},{25,17},{2,26},{10... | collective-permute-start | bytes 786440 | tf_op jit(solution)/shard_map/ppermute | solution.py:33
  755.0 18.6 %collective-permute-start.26 = (bf16[256,512]{1,0:T(8,128)(2,1)S(1)}, bf16[256,512]{1,0:T(8,128)(2,1)S(1)}, u32[]{:S(2)}, u32[]{:S(2)}) collective-permute-start(bf16[256,512]{1,0:T(8,128)(2,1)S(1)} %get-tuple-element.3492), channel_id=1, source_target_pairs={{0,8},{8,16},{16,24},{24,0},{1,9},{9,17},{17,25},{25,1},{2,10},{10... | collective-permute-start | bytes 786440 | tf_op jit(solution)/shard_map/ppermute | solution.py:33
  755.1 27.9 %collective-permute-start.27 = (bf16[256,512]{1,0:T(8,128)(2,1)S(1)}, bf16[256,512]{1,0:T(8,128)(2,1)S(1)}, u32[]{:S(2)}, u32[]{:S(2)}) collective-permute-start(bf16[256,512]{1,0:T(8,128)(2,1)S(1)} %get-tuple-element.3494), channel_id=1, source_target_pairs={{0,16},{8,24},{16,0},{24,8},{1,17},{9,25},{17,1},{25,9},{2,18},{10... | collective-permute-start | bytes 786440 | tf_op jit(solution)/shard_map/ppermute | solution.py:33
  756.7 27.4 %collective-permute-start.28 = (bf16[256,512]{1,0:T(8,128)(2,1)S(1)}, bf16[256,512]{1,0:T(8,128)(2,1)S(1)}, u32[]{:S(2)}, u32[]{:S(2)}) collective-permute-start(bf16[256,512]{1,0:T(8,128)(2,1)S(1)} %get-tuple-element.3493), channel_id=1, source_target_pairs={{0,24},{8,0},{16,8},{24,16},{1,25},{9,1},{17,9},{25,17},{2,26},{10... | collective-permute-start | bytes 786440 | tf_op jit(solution)/shard_map/ppermute | solution.py:33
  759.1 26.3 %collective-permute-start.11 = (bf16[64,512]{1,0:T(8,128)(2,1)S(1)}, bf16[64,512]{1,0:T(8,128)(2,1)S(1)}, u32[]{:S(2)}, u32[]{:S(2)}) collective-permute-start(bf16[64,512]{1,0:T(8,128)(2,1)S(1)} %get-tuple-element.3497), channel_id=1, source_target_pairs={{0,8},{8,16},{16,24},{24,0},{1,9},{9,17},{17,25},{25,1},{2,10},{10... | collective-permute-start | bytes 196616 | tf_op jit(solution)/shard_map/ppermute | solution.py:33
  761.7 25.3 %collective-permute-start.12 = (bf16[64,512]{1,0:T(8,128)(2,1)S(1)}, bf16[64,512]{1,0:T(8,128)(2,1)S(1)}, u32[]{:S(2)}, u32[]{:S(2)}) collective-permute-start(bf16[64,512]{1,0:T(8,128)(2,1)S(1)} %get-tuple-element.3499), channel_id=1, source_target_pairs={{0,16},{8,24},{16,0},{24,8},{1,17},{9,25},{17,1},{25,9},{2,18},{10... | collective-permute-start | bytes 196616 | tf_op jit(solution)/shard_map/ppermute | solution.py:33
  773.6 17.1 %collective-permute-start.13 = (bf16[64,512]{1,0:T(8,128)(2,1)S(1)}, bf16[64,512]{1,0:T(8,128)(2,1)S(1)}, u32[]{:S(2)}, u32[]{:S(2)}) collective-permute-start(bf16[64,512]{1,0:T(8,128)(2,1)S(1)} %get-tuple-element.3498), channel_id=1, source_target_pairs={{0,24},{8,0},{16,8},{24,16},{1,25},{9,1},{17,9},{25,17},{2,26},{10... | collective-permute-start | bytes 196616 | tf_op jit(solution)/shard_map/ppermute | solution.py:33
  783.0 7.7 collective-permute-start.17
  784.0 7.5 collective-permute-start.18
  785.5 8.0 collective-permute-start.19
  787.0 10.1 %collective-permute-start.23 = (bf16[64,512]{1,0:T(8,128)(2,1)S(1)}, bf16[64,512]{1,0:T(8,128)(2,1)S(1)}, u32[]{:S(2)}, u32[]{:S(2)}) collective-permute-start(bf16[64,512]{1,0:T(8,128)(2,1)S(1)} %get-tuple-element.3503), channel_id=1, source_target_pairs={{0,8},{8,16},{16,24},{24,0},{1,9},{9,17},{17,25},{25,1},{2,10},{10... | collective-permute-start | bytes 196616 | tf_op jit(solution)/shard_map/ppermute | solution.py:33
  790.6 7.2 collective-permute-start.24
  790.7 7.2 collective-permute-start.25
  791.6 6.3 collective-permute-start.29
  793.5 6.5 collective-permute-start.30
  797.1 4.3 collective-permute-start.31
  (15 other events, 55.3 us)

commit v18 on v12

--- a/solution.py
+++ b/solution.py
@@ -234,8 +234,14 @@
     unused_rows, collected = carry
     own = collected.reshape(micro * buses, width)
     right = jnp.concatenate([own, lax.ppermute(own, "core", swap)], axis=0)
-    half = jnp.dot(left, right, preferred_element_type=jnp.float32)
-    summed = scatter_sum(scatter_sum(half, "y"), "z")
+    columns = width // 2
+    first = jnp.dot(left, right[:, :columns], preferred_element_type=jnp.float32)
+    along_y = scatter_sum(scatter_sum(first, "y"), "z")
+    left_z = left.reshape(ys, zs, rows_each, left.shape[1])
+    left_z = jnp.swapaxes(left_z, 0, 1).reshape(left.shape)
+    second = jnp.dot(left_z, right[:, columns:], preferred_element_type=jnp.float32)
+    along_z = scatter_sum(scatter_sum(second, "z"), "y")
+    summed = jnp.concatenate([along_y, along_z], axis=1)
     return summed[None]
 
 

time: 799 us -> 798 us (level); the launches traced: 790 us -> 798 us
  starting transfers between devices: 111 us -> 170 us
  waiting for transfers between devices: 486 us -> 433 us
    ppermute x6 -> x12, starting transfers between devices: 46 us -> 105 us  [scatter_sum(): received = lax.ppermute(sent.astype(jnp.bfloat16), axis, route)]
    ppermute x6 -> x12, waiting for transfers between devices: 68.8 us -> 15.4 us  [scatter_sum(): received = lax.ppermute(sent.astype(jnp.bfloat16), axis, route)]
    unnamed x13 -> x17, local copies, waits for them, and re-layouts: 24.4 us -> 23.9 us
  transfers between devices with their start and end apart: 30 -> 36, of which waited for: 20 -> 20; matrix products, arithmetic and copies ran while one was open for 3% -> 4% of each run, Pallas kernels for 0% -> 0%
where the time goes in v18:
time: 798 us
  waiting for transfers between devices  433 us (54%)
  starting transfers between devices  170 us (21%)
  local copies, waits for them, and re-layouts  73 us (9%)
  matrix products  71.3 us (9%)
  other arithmetic  47.7 us (6%)
    ppermute x22, waiting for transfers between devices, passed_along(): return lax.ppermute(block, axis, [(i, i + distance) for i in senders])  415 us
    ppermute x12, starting transfers between devices, scatter_sum(): received = lax.ppermute(sent.astype(jnp.bfloat16), axis, route)  105 us
    ppermute x22, starting transfers between devices, passed_along(): return lax.ppermute(block, axis, [(i, i + distance) for i in senders])  64.5 us
    unnamed x17, local copies, waits for them, and re-layouts  23.9 us
    dot_general x4, matrix products, layer_forward(): jnp.dot(normed.reshape(-1, width), weight, preferred_element_type=jnp.flo...  18.8 us
    dot_general x4, matrix products, layer_backward(): lax.dot_general(value_total.reshape(-1, width), weight, (((1,), (1,)), ((...  16.7 us
  transfers between devices with their start and end apart: 36, of which 20 were waited for; matrix products, arithmetic and copies ran while one was open for 4% of the time, Pallas kernels for 0%

profile of v18, /device:TPU:96, one launch (start us, length us, event | category | flops | bytes accessed | tf_op | source)
XLA Modules:
  0.0 797.5 jit_solution(18032293711975085591)
XLA Ops:
  13.2 76.1 %while.144 = (s32[]{:T(128)}, bf16[128,2048]{0,1:T(8,128)(2,1)S(1)}, f32[4,128,2048]{1,2,0:T(8,128)}, f32[4,128,1]{1,2,0:T(1,128)S(1)}, bf16[4,128,16,128]{3,2,1...) while((s32[]{:T(128)}, bf16[128,2048]{0,1:T(8,128)(2,1)S(1)}, ...), condition=%wide.region_8.9_spmd.clone, body=%wide.region_1.8_spmd.clone.sunk | while | flops 1216641408 | bytes 26020904 | solution.py:180
  13.2 11.5 %conditional.18 = (bf16[128,2048]{0,1:T(8,128)(2,1)S(1)}, f32[4,128,2048]{1,2,0:T(8,128)}, f32[4,128,1]{1,2,0:T(1,128)S(1)}, bf16[4,128,16,128]{3,2,1,0:T(8,128)...) conditional(s32[]{:T(128)} %convert_element_type.892, ...), branch_computations={%region_2.2_spmd, %region_3.7_spmd} | conditional | flops 1216641408 | bytes 23923316 | solution.py:171
  13.8 4.7 convolution_convert_fusion
  26.0 11.4 %collective-permute-done = bf16[128,2048]{0,1:T(8,128)(2,1)S(1)} collective-permute-done((bf16[128,2048]{0,1:T(8,128)(2,1)S(1)}, bf16[128,2048]{0,1:T(8,128)(2,1)S(1)}, u32[]{:S(2)}, u32[]{:S(2)}) %collective-permute-start) | collective-permute-done | bytes 524320 | tf_op jit(solution)/shard_map/while/body/eval_jaxpr/ppermute | solution.py:16
  37.4 11.4 %conditional.18 = (bf16[128,2048]{0,1:T(8,128)(2,1)S(1)}, f32[4,128,2048]{1,2,0:T(8,128)}, f32[4,128,1]{1,2,0:T(1,128)S(1)}, bf16[4,128,16,128]{3,2,1,0:T(8,128)...) conditional(s32[]{:T(128)} %convert_element_type.892, ...), branch_computations={%region_2.2_spmd, %region_3.7_spmd} | conditional | flops 1216641408 | bytes 23923316 | solution.py:171
  38.0 4.7 convolution_convert_fusion
  48.8 4.5 collective-permute-start
  53.3 10.6 %collective-permute-done = bf16[128,2048]{0,1:T(8,128)(2,1)S(1)} collective-permute-done((bf16[128,2048]{0,1:T(8,128)(2,1)S(1)}, bf16[128,2048]{0,1:T(8,128)(2,1)S(1)}, u32[]{:S(2)}, u32[]{:S(2)}) %collective-permute-start) | collective-permute-done | bytes 524320 | tf_op jit(solution)/shard_map/while/body/eval_jaxpr/ppermute | solution.py:16
  63.9 11.4 %conditional.18 = (bf16[128,2048]{0,1:T(8,128)(2,1)S(1)}, f32[4,128,2048]{1,2,0:T(8,128)}, f32[4,128,1]{1,2,0:T(1,128)S(1)}, bf16[4,128,16,128]{3,2,1,0:T(8,128)...) conditional(s32[]{:T(128)} %convert_element_type.892, ...), branch_computations={%region_2.2_spmd, %region_3.7_spmd} | conditional | flops 1216641408 | bytes 23923316 | solution.py:171
  64.5 4.7 convolution_convert_fusion
  75.2 4.4 collective-permute-start
  79.7 9.6 %collective-permute-done = bf16[128,2048]{0,1:T(8,128)(2,1)S(1)} collective-permute-done((bf16[128,2048]{0,1:T(8,128)(2,1)S(1)}, bf16[128,2048]{0,1:T(8,128)(2,1)S(1)}, u32[]{:S(2)}, u32[]{:S(2)}) %collective-permute-start) | collective-permute-done | bytes 524320 | tf_op jit(solution)/shard_map/while/body/eval_jaxpr/ppermute | solution.py:16
  89.3 81.1 %while.145 = (s32[]{:T(128)}, bf16[128,2048]{0,1:T(8,128)(2,1)S(1)}, f32[4,128,2048]{1,2,0:T(8,128)}, f32[4,128,1]{1,2,0:T(1,128)S(1)}, bf16[4,128,16,128]{3,2,1...) while((s32[]{:T(128)}, bf16[128,2048]{0,1:T(8,128)(2,1)S(1)}, ...), condition=%wide.region_16.17_spmd.clone, body=%wide.region_9.16_spmd.clone.sunk | while | flops 1216641408 | bytes 26020924 | solution.py:180
  89.3 11.4 %conditional.19 = (bf16[128,2048]{0,1:T(8,128)(2,1)S(1)}, f32[4,128,2048]{1,2,0:T(8,128)}, f32[4,128,1]{1,2,0:T(1,128)S(1)}, bf16[4,128,16,128]{3,2,1,0:T(8,128)...) conditional(s32[]{:T(128)} %convert_element_type.893, ...), branch_computations={%region_10.10_spmd, %region_11.15_spmd} | conditional | flops 1216641408 | bytes 23923316 | solution.py:171
  89.9 4.7 convolution_convert_fusion.1
  100.7 4.4 collective-permute-start.1
  105.1 8.7 %collective-permute-done.1 = bf16[128,2048]{0,1:T(8,128)(2,1)S(1)} collective-permute-done((bf16[128,2048]{0,1:T(8,128)(2,1)S(1)}, bf16[128,2048]{0,1:T(8,128)(2,1)S(1)}, u32[]{:S(2)}, u32[]{:S(2)}) %collective-permute-start.1) | collective-permute-done | bytes 524320 | tf_op jit(solution)/shard_map/while/body/eval_jaxpr/ppermute | solution.py:16
  113.9 15.7 %collective-permute-start.1 = (bf16[128,2048]{0,1:T(8,128)(2,1)S(1)}, bf16[128,2048]{0,1:T(8,128)(2,1)S(1)}, u32[]{:S(2)}, u32[]{:S(2)}) collective-permute-start(bf16[128,2048]{0,1:T(8,128)(2,1)S(1)} %get-tuple-element.4051), channel_id=1, source_target_pairs={{0,32},{32,64},{64,96},{96,128},{128,160},{160,192},{192,224},{1,3... | collective-permute-start | bytes 1572872 | tf_op jit(solution)/shard_map/while/body/eval_jaxpr/ppermute | solution.py:16
  129.7 7.8 collective-permute-done.1
  137.6 4.4 collective-permute-start.1
  142.0 6.9 collective-permute-done.1
  149.0 14.7 %collective-permute-start.1 = (bf16[128,2048]{0,1:T(8,128)(2,1)S(1)}, bf16[128,2048]{0,1:T(8,128)(2,1)S(1)}, u32[]{:S(2)}, u32[]{:S(2)}) collective-permute-start(bf16[128,2048]{0,1:T(8,128)(2,1)S(1)} %get-tuple-element.4051), channel_id=1, source_target_pairs={{0,32},{32,64},{64,96},{96,128},{128,160},{160,192},{192,224},{1,3... | collective-permute-start | bytes 1572872 | tf_op jit(solution)/shard_map/while/body/eval_jaxpr/ppermute | solution.py:16
  163.7 6.6 collective-permute-done.1
  174.2 5.4 copy.150
  179.6 5.6 copy.152
  187.8 4.5 copy.151
  194.0 4.8 while.147
  198.8 304.6 %while.148 = (s32[]{:T(128)}, bf16[128,2048]{1,0:T(8,128)(2,1)S(1)}, bf16[4,128,2048]{1,2,0:T(8,128)(2,1)}, s32[]{:T(128)}, pred[]{:T(512)}, /*index=5*/bf16[4,1...) while((s32[]{:T(128)}, bf16[128,2048]{1,0:T(8,128)(2,1)S(1)}, ...), condition=%wide.region_38.39_spmd.clone, body=%wide.region_32.38_spmd.clone.sunk | while | flops 1353218048 | bytes 71172632 | solution.py:233
  201.1 13.5 %collective-permute-done.4 = bf16[128,2048]{1,0:T(8,128)(2,1)S(1)} collective-permute-done((bf16[128,2048]{1,0:T(8,128)(2,1)}, bf16[128,2048]{1,0:T(8,128)(2,1)S(1)}, u32[]{:S(2)}, u32[]{:S(2)}) %collective-permute-start.4) | collective-permute-done | bytes 524320 | tf_op jit(solution)/shard_map/while/body/eval_jaxpr/ppermute | solution.py:16
  216.8 27.7 %collective-permute-done.4 = bf16[128,2048]{1,0:T(8,128)(2,1)S(1)} collective-permute-done((bf16[128,2048]{1,0:T(8,128)(2,1)}, bf16[128,2048]{1,0:T(8,128)(2,1)S(1)}, u32[]{:S(2)}, u32[]{:S(2)}) %collective-permute-start.4) | collective-permute-done | bytes 524320 | tf_op jit(solution)/shard_map/while/body/eval_jaxpr/ppermute | solution.py:16
  246.6 16.4 %collective-permute-done.4 = bf16[128,2048]{1,0:T(8,128)(2,1)S(1)} collective-permute-done((bf16[128,2048]{1,0:T(8,128)(2,1)}, bf16[128,2048]{1,0:T(8,128)(2,1)S(1)}, u32[]{:S(2)}, u32[]{:S(2)}) %collective-permute-start.4) | collective-permute-done | bytes 524320 | tf_op jit(solution)/shard_map/while/body/eval_jaxpr/ppermute | solution.py:16
  265.2 238.2 %collective-permute-done.4 = bf16[128,2048]{1,0:T(8,128)(2,1)S(1)} collective-permute-done((bf16[128,2048]{1,0:T(8,128)(2,1)}, bf16[128,2048]{1,0:T(8,128)(2,1)S(1)}, u32[]{:S(2)}, u32[]{:S(2)}) %collective-permute-start.4) | collective-permute-done | bytes 524320 | tf_op jit(solution)/shard_map/while/body/eval_jaxpr/ppermute | solution.py:16
  503.4 129.2 %while.149 = (s32[]{:T(128)}, bf16[128,2048]{1,0:T(8,128)(2,1)S(1)}, bf16[4,128,2048]{1,2,0:T(8,128)(2,1)}, s32[]{:T(128)}, pred[]{:T(512)}, /*index=5*/bf16[4,1...) while((s32[]{:T(128)}, bf16[128,2048]{1,0:T(8,128)(2,1)S(1)}, ...), condition=%wide.region_45.46_spmd.clone, body=%wide.region_39.45_spmd.clone.sunk | while | flops 1353218048 | bytes 71172632 | solution.py:233
  503.4 16.7 %conditional.23 = (bf16[128,2048]{1,0:T(8,128)(2,1)}, bf16[4,128,2048]{1,2,0:T(8,128)(2,1)}) conditional(s32[]{:T(128)} %convert_element_type.897, bf16[4,128,2048]{1,2,0:T(8,128)(2,1)} %get-tuple-element.4505, (pred[]{:T(512)}, s32[]{:T(128)}, bf16[4,128,2048]{2,1,0:T(8,128)(2,1)}, bf16[128,2048]{1,0:T(8,128)(2,1)S(1)}, ...), branch_computations={%region_40.40_spmd, %region_41.44_spmd} | conditional | flops 1353218048 | bytes 69075104 | solution.py:207
  521.4 16.0 %collective-permute-done.5 = bf16[128,2048]{1,0:T(8,128)(2,1)S(1)} collective-permute-done((bf16[128,2048]{1,0:T(8,128)(2,1)}, bf16[128,2048]{1,0:T(8,128)(2,1)S(1)}, u32[]{:S(2)}, u32[]{:S(2)}) %collective-permute-start.5) | collective-permute-done | bytes 524320 | tf_op jit(solution)/shard_map/while/body/eval_jaxpr/ppermute | solution.py:16
  537.3 16.7 %conditional.23 = (bf16[128,2048]{1,0:T(8,128)(2,1)}, bf16[4,128,2048]{1,2,0:T(8,128)(2,1)}) conditional(s32[]{:T(128)} %convert_element_type.897, bf16[4,128,2048]{1,2,0:T(8,128)(2,1)} %get-tuple-element.4505, (pred[]{:T(512)}, s32[]{:T(128)}, bf16[4,128,2048]{2,1,0:T(8,128)(2,1)}, bf16[128,2048]{1,0:T(8,128)(2,1)S(1)}, ...), branch_computations={%region_40.40_spmd, %region_41.44_spmd} | conditional | flops 1353218048 | bytes 69075104 | solution.py:207
  547.1 4.2 fusion.183
  555.3 16.1 %collective-permute-done.5 = bf16[128,2048]{1,0:T(8,128)(2,1)S(1)} collective-permute-done((bf16[128,2048]{1,0:T(8,128)(2,1)}, bf16[128,2048]{1,0:T(8,128)(2,1)S(1)}, u32[]{:S(2)}, u32[]{:S(2)}) %collective-permute-start.5) | collective-permute-done | bytes 524320 | tf_op jit(solution)/shard_map/while/body/eval_jaxpr/ppermute | solution.py:16
  571.3 16.7 %conditional.23 = (bf16[128,2048]{1,0:T(8,128)(2,1)}, bf16[4,128,2048]{1,2,0:T(8,128)(2,1)}) conditional(s32[]{:T(128)} %convert_element_type.897, bf16[4,128,2048]{1,2,0:T(8,128)(2,1)} %get-tuple-element.4505, (pred[]{:T(512)}, s32[]{:T(128)}, bf16[4,128,2048]{2,1,0:T(8,128)(2,1)}, bf16[128,2048]{1,0:T(8,128)(2,1)S(1)}, ...), branch_computations={%region_40.40_spmd, %region_41.44_spmd} | conditional | flops 1353218048 | bytes 69075104 | solution.py:207
  589.3 15.3 %collective-permute-done.5 = bf16[128,2048]{1,0:T(8,128)(2,1)S(1)} collective-permute-done((bf16[128,2048]{1,0:T(8,128)(2,1)}, bf16[128,2048]{1,0:T(8,128)(2,1)S(1)}, u32[]{:S(2)}, u32[]{:S(2)}) %collective-permute-start.5) | collective-permute-done | bytes 524320 | tf_op jit(solution)/shard_map/while/body/eval_jaxpr/ppermute | solution.py:16
  604.6 16.7 %conditional.23 = (bf16[128,2048]{1,0:T(8,128)(2,1)}, bf16[4,128,2048]{1,2,0:T(8,128)(2,1)}) conditional(s32[]{:T(128)} %convert_element_type.897, bf16[4,128,2048]{1,2,0:T(8,128)(2,1)} %get-tuple-element.4505, (pred[]{:T(512)}, s32[]{:T(128)}, bf16[4,128,2048]{2,1,0:T(8,128)(2,1)}, bf16[128,2048]{1,0:T(8,128)(2,1)S(1)}, ...), branch_computations={%region_40.40_spmd, %region_41.44_spmd} | conditional | flops 1353218048 | bytes 69075104 | solution.py:207
  622.6 10.0 %collective-permute-done.5 = bf16[128,2048]{1,0:T(8,128)(2,1)S(1)} collective-permute-done((bf16[128,2048]{1,0:T(8,128)(2,1)}, bf16[128,2048]{1,0:T(8,128)(2,1)S(1)}, u32[]{:S(2)}, u32[]{:S(2)}) %collective-permute-start.5) | collective-permute-done | bytes 524320 | tf_op jit(solution)/shard_map/while/body/eval_jaxpr/ppermute | solution.py:16
  632.6 4.2 copy.164
  639.3 10.7 %copy.147 = bf16[4,128,2048]{1,0,2:T(4,128)(2,1)} copy(bf16[4,128,2048]{1,2,0:T(8,128)(2,1)S(1)} %convert_element_type.505) | data formatting | bytes 4194304 | tf_op jit(solution)/shard_map/convert_element_type | solution.py:217
  676.5 56.8 %collective-permute-start.15 = (bf16[256,1024]{1,0:T(8,128)(2,1)S(1)}, bf16[256,1024]{1,0:T(8,128)(2,1)}, u32[]{:S(2)}, u32[]{:S(2)}) collective-permute-start(bf16[256,1024]{1,0:T(8,128)(2,1)S(1)} %get-tuple-element.3484), channel_id=1, source_target_pairs={{0,16},{8,24},{16,0},{24,8},{1,17},{9,25},{17,1},{25,9},{2,18},{10... | collective-permute-start | bytes 1572872 | tf_op jit(solution)/shard_map/ppermute | solution.py:33
  740.0 12.4 %collective-permute-start.12 = (bf16[64,1024]{1,0:T(8,128)(2,1)S(1)}, bf16[64,1024]{1,0:T(8,128)(2,1)S(1)}, u32[]{:S(2)}, u32[]{:S(2)}) collective-permute-start(bf16[64,1024]{1,0:T(8,128)(2,1)S(1)} %get-tuple-element.3489), channel_id=1, source_target_pairs={{0,16},{8,24},{16,0},{24,8},{1,17},{9,25},{17,1},{25,9},{2,18},{10... | collective-permute-start | bytes 393224 | tf_op jit(solution)/shard_map/ppermute | solution.py:33
  752.4 22.2 %collective-permute-start.13 = (bf16[64,1024]{1,0:T(8,128)(2,1)S(1)}, bf16[64,1024]{1,0:T(8,128)(2,1)S(1)}, u32[]{:S(2)}, u32[]{:S(2)}) collective-permute-start(bf16[64,1024]{1,0:T(8,128)(2,1)S(1)} %get-tuple-element.3488), channel_id=1, source_target_pairs={{0,24},{8,0},{16,8},{24,16},{1,25},{9,1},{17,9},{25,17},{2,26},{10... | collective-permute-start | bytes 393224 | tf_op jit(solution)/shard_map/ppermute | solution.py:33
  774.6 10.8 %collective-permute-done.15 = bf16[256,1024]{1,0:T(8,128)(2,1)} collective-permute-done((bf16[256,1024]{1,0:T(8,128)(2,1)S(1)}, bf16[256,1024]{1,0:T(8,128)(2,1)}, u32[]{:S(2)}, u32[]{:S(2)}) %collective-permute-start.15) | collective-permute-done | bytes 524320 | tf_op jit(solution)/shard_map/ppermute | solution.py:33
  (283 shorter events, 186.9 us)
Async XLA Ops:
  9.9 3.3 copy-start.4
  9.9 3.3 copy-start.8
  24.7 12.7 %collective-permute-start = (bf16[128,2048]{0,1:T(8,128)(2,1)S(1)}, bf16[128,2048]{0,1:T(8,128)(2,1)S(1)}, u32[]{:S(2)}, u32[]{:S(2)}) collective-permute-start(bf16[128,2048]{0,1:T(8,128)(2,1)S(1)} %get-tuple-element.4027), channel_id=1, source_target_pairs={{0,32},{32,64},{64,96},{1,33},{33,65},{65,97},{2,34},{34,66},{66,9... | collective-permute-start | bytes 1572872 | tf_op jit(solution)/shard_map/while/body/eval_jaxpr/ppermute | solution.py:16
  48.8 15.0 %collective-permute-start = (bf16[128,2048]{0,1:T(8,128)(2,1)S(1)}, bf16[128,2048]{0,1:T(8,128)(2,1)S(1)}, u32[]{:S(2)}, u32[]{:S(2)}) collective-permute-start(bf16[128,2048]{0,1:T(8,128)(2,1)S(1)} %get-tuple-element.4027), channel_id=1, source_target_pairs={{0,32},{32,64},{64,96},{1,33},{33,65},{65,97},{2,34},{34,66},{66,9... | collective-permute-start | bytes 1572872 | tf_op jit(solution)/shard_map/while/body/eval_jaxpr/ppermute | solution.py:16
  75.2 14.1 %collective-permute-start = (bf16[128,2048]{0,1:T(8,128)(2,1)S(1)}, bf16[128,2048]{0,1:T(8,128)(2,1)S(1)}, u32[]{:S(2)}, u32[]{:S(2)}) collective-permute-start(bf16[128,2048]{0,1:T(8,128)(2,1)S(1)} %get-tuple-element.4027), channel_id=1, source_target_pairs={{0,32},{32,64},{64,96},{1,33},{33,65},{65,97},{2,34},{34,66},{66,9... | collective-permute-start | bytes 1572872 | tf_op jit(solution)/shard_map/while/body/eval_jaxpr/ppermute | solution.py:16
  100.7 13.1 %collective-permute-start.1 = (bf16[128,2048]{0,1:T(8,128)(2,1)S(1)}, bf16[128,2048]{0,1:T(8,128)(2,1)S(1)}, u32[]{:S(2)}, u32[]{:S(2)}) collective-permute-start(bf16[128,2048]{0,1:T(8,128)(2,1)S(1)} %get-tuple-element.4051), channel_id=1, source_target_pairs={{0,32},{32,64},{64,96},{96,128},{128,160},{160,192},{192,224},{1,3... | collective-permute-start | bytes 1572872 | tf_op jit(solution)/shard_map/while/body/eval_jaxpr/ppermute | solution.py:16
  113.9 23.6 %collective-permute-start.1 = (bf16[128,2048]{0,1:T(8,128)(2,1)S(1)}, bf16[128,2048]{0,1:T(8,128)(2,1)S(1)}, u32[]{:S(2)}, u32[]{:S(2)}) collective-permute-start(bf16[128,2048]{0,1:T(8,128)(2,1)S(1)} %get-tuple-element.4051), channel_id=1, source_target_pairs={{0,32},{32,64},{64,96},{96,128},{128,160},{160,192},{192,224},{1,3... | collective-permute-start | bytes 1572872 | tf_op jit(solution)/shard_map/while/body/eval_jaxpr/ppermute | solution.py:16
  137.6 11.3 %collective-permute-start.1 = (bf16[128,2048]{0,1:T(8,128)(2,1)S(1)}, bf16[128,2048]{0,1:T(8,128)(2,1)S(1)}, u32[]{:S(2)}, u32[]{:S(2)}) collective-permute-start(bf16[128,2048]{0,1:T(8,128)(2,1)S(1)} %get-tuple-element.4051), channel_id=1, source_target_pairs={{0,32},{32,64},{64,96},{96,128},{128,160},{160,192},{192,224},{1,3... | collective-permute-start | bytes 1572872 | tf_op jit(solution)/shard_map/while/body/eval_jaxpr/ppermute | solution.py:16
  149.0 21.4 %collective-permute-start.1 = (bf16[128,2048]{0,1:T(8,128)(2,1)S(1)}, bf16[128,2048]{0,1:T(8,128)(2,1)S(1)}, u32[]{:S(2)}, u32[]{:S(2)}) collective-permute-start(bf16[128,2048]{0,1:T(8,128)(2,1)S(1)} %get-tuple-element.4051), channel_id=1, source_target_pairs={{0,32},{32,64},{64,96},{96,128},{128,160},{160,192},{192,224},{1,3... | collective-permute-start | bytes 1572872 | tf_op jit(solution)/shard_map/while/body/eval_jaxpr/ppermute | solution.py:16
  171.0 0.7 collective-permute-start.2
  171.8 0.7 collective-permute-start.2
  172.7 0.7 collective-permute-start.2
  173.5 0.7 collective-permute-start.2
  179.6 5.6 copy-start.3
  194.9 0.7 collective-permute-start.3
  196.5 0.7 collective-permute-start.3
  198.1 0.7 collective-permute-start.3
  199.8 14.8 %collective-permute-start.4 = (bf16[128,2048]{1,0:T(8,128)(2,1)}, bf16[128,2048]{1,0:T(8,128)(2,1)S(1)}, u32[]{:S(2)}, u32[]{:S(2)}) collective-permute-start(bf16[128,2048]{1,0:T(8,128)(2,1)} %get-tuple-element.4114), channel_id=1, source_target_pairs={{32,0},{64,32},{96,64},{128,96},{160,128},{192,160},{224,192},{33,... | collective-permute-start | bytes 1572872 | tf_op jit(solution)/shard_map/while/body/eval_jaxpr/ppermute | solution.py:16
  215.5 29.0 %collective-permute-start.4 = (bf16[128,2048]{1,0:T(8,128)(2,1)}, bf16[128,2048]{1,0:T(8,128)(2,1)S(1)}, u32[]{:S(2)}, u32[]{:S(2)}) collective-permute-start(bf16[128,2048]{1,0:T(8,128)(2,1)} %get-tuple-element.4114), channel_id=1, source_target_pairs={{32,0},{64,32},{96,64},{128,96},{160,128},{192,160},{224,192},{33,... | collective-permute-start | bytes 1572872 | tf_op jit(solution)/shard_map/while/body/eval_jaxpr/ppermute | solution.py:16
  245.3 17.7 %collective-permute-start.4 = (bf16[128,2048]{1,0:T(8,128)(2,1)}, bf16[128,2048]{1,0:T(8,128)(2,1)S(1)}, u32[]{:S(2)}, u32[]{:S(2)}) collective-permute-start(bf16[128,2048]{1,0:T(8,128)(2,1)} %get-tuple-element.4114), channel_id=1, source_target_pairs={{32,0},{64,32},{96,64},{128,96},{160,128},{192,160},{224,192},{33,... | collective-permute-start | bytes 1572872 | tf_op jit(solution)/shard_map/while/body/eval_jaxpr/ppermute | solution.py:16
  263.9 239.5 %collective-permute-start.4 = (bf16[128,2048]{1,0:T(8,128)(2,1)}, bf16[128,2048]{1,0:T(8,128)(2,1)S(1)}, u32[]{:S(2)}, u32[]{:S(2)}) collective-permute-start(bf16[128,2048]{1,0:T(8,128)(2,1)} %get-tuple-element.4114), channel_id=1, source_target_pairs={{32,0},{64,32},{96,64},{128,96},{160,128},{192,160},{224,192},{33,... | collective-permute-start | bytes 1572872 | tf_op jit(solution)/shard_map/while/body/eval_jaxpr/ppermute | solution.py:16
  508.4 4.8 slice-start.4
  509.1 4.1 slice-start.5
  520.1 17.3 %collective-permute-start.5 = (bf16[128,2048]{1,0:T(8,128)(2,1)}, bf16[128,2048]{1,0:T(8,128)(2,1)S(1)}, u32[]{:S(2)}, u32[]{:S(2)}) collective-permute-start(bf16[128,2048]{1,0:T(8,128)(2,1)} %get-tuple-element.4131), channel_id=1, source_target_pairs={{32,0},{64,32},{96,64},{33,1},{65,33},{97,65},{34,2},{66,34},{98,6... | collective-permute-start | bytes 1572872 | tf_op jit(solution)/shard_map/while/body/eval_jaxpr/ppermute | solution.py:16
  542.4 4.8 slice-start.4
  543.1 4.1 slice-start.5
  554.0 17.3 %collective-permute-start.5 = (bf16[128,2048]{1,0:T(8,128)(2,1)}, bf16[128,2048]{1,0:T(8,128)(2,1)S(1)}, u32[]{:S(2)}, u32[]{:S(2)}) collective-permute-start(bf16[128,2048]{1,0:T(8,128)(2,1)} %get-tuple-element.4131), channel_id=1, source_target_pairs={{32,0},{64,32},{96,64},{33,1},{65,33},{97,65},{34,2},{66,34},{98,6... | collective-permute-start | bytes 1572872 | tf_op jit(solution)/shard_map/while/body/eval_jaxpr/ppermute | solution.py:16
  576.4 4.8 slice-start.4
  577.1 4.1 slice-start.5
  588.0 16.6 %collective-permute-start.5 = (bf16[128,2048]{1,0:T(8,128)(2,1)}, bf16[128,2048]{1,0:T(8,128)(2,1)S(1)}, u32[]{:S(2)}, u32[]{:S(2)}) collective-permute-start(bf16[128,2048]{1,0:T(8,128)(2,1)} %get-tuple-element.4131), channel_id=1, source_target_pairs={{32,0},{64,32},{96,64},{33,1},{65,33},{97,65},{34,2},{66,34},{98,6... | collective-permute-start | bytes 1572872 | tf_op jit(solution)/shard_map/while/body/eval_jaxpr/ppermute | solution.py:16
  609.7 4.8 slice-start.4
  610.4 4.1 slice-start.5
  621.3 11.3 %collective-permute-start.5 = (bf16[128,2048]{1,0:T(8,128)(2,1)}, bf16[128,2048]{1,0:T(8,128)(2,1)S(1)}, u32[]{:S(2)}, u32[]{:S(2)}) collective-permute-start(bf16[128,2048]{1,0:T(8,128)(2,1)} %get-tuple-element.4131), channel_id=1, source_target_pairs={{32,0},{64,32},{96,64},{33,1},{65,33},{97,65},{34,2},{66,34},{98,6... | collective-permute-start | bytes 1572872 | tf_op jit(solution)/shard_map/while/body/eval_jaxpr/ppermute | solution.py:16
  636.8 23.7 %collective-permute-start.7 = (bf16[512,2048]{1,0:T(8,128)(2,1)}, bf16[512,2048]{1,0:T(8,128)(2,1)}, u32[]{:S(2)}, u32[]{:S(2)}) collective-permute-start(bf16[512,2048]{1,0:T(8,128)(2,1)} %bitcast.94), channel_id=1, source_target_pairs={{0,1},{1,0},{2,3},{3,2},{4,5},{5,4},{6,7},{7,6},{8,9},{9,8},{10,11... | collective-permute-start | bytes 6291464 | tf_op jit(solution)/shard_map/ppermute | solution.py:236
  657.0 3.0 collective-permute-start.6
  664.4 9.7 %copy-start.6 = (f32[1024,1024]{1,0:T(8,128)}, f32[1024,1024]{1,0:T(8,128)S(1)}, u32[]{:S(2)}) copy-start(f32[1024,1024]{1,0:T(8,128)S(1)} %fusion.214) | copy-start | bytes 12582916
  664.6 68.6 %collective-permute-start.10 = (bf16[256,1024]{1,0:T(8,128)(2,1)S(1)}, bf16[256,1024]{1,0:T(8,128)(2,1)S(1)}, u32[]{:S(2)}, u32[]{:S(2)}) collective-permute-start(bf16[256,1024]{1,0:T(8,128)(2,1)S(1)} %get-tuple-element.3480), channel_id=1, source_target_pairs={{0,6},{2,0},{4,2},{6,4},{1,7},{3,1},{5,3},{7,5},{8,14},{10,8},{12,... | collective-permute-start | bytes 1572872 | tf_op jit(solution)/shard_map/ppermute | solution.py:33
  667.8 69.0 %collective-permute-start.8 = (bf16[256,1024]{1,0:T(8,128)(2,1)S(1)}, bf16[256,1024]{1,0:T(8,128)(2,1)}, u32[]{:S(2)}, u32[]{:S(2)}) collective-permute-start(bf16[256,1024]{1,0:T(8,128)(2,1)S(1)} %get-tuple-element.3479), channel_id=1, source_target_pairs={{0,2},{2,4},{4,6},{6,0},{1,3},{3,5},{5,7},{7,1},{8,10},{10,12},{12... | collective-permute-start | bytes 1572872 | tf_op jit(solution)/shard_map/ppermute | solution.py:33
  667.8 69.0 %collective-permute-start.9 = (bf16[256,1024]{1,0:T(8,128)(2,1)S(1)}, bf16[256,1024]{1,0:T(8,128)(2,1)}, u32[]{:S(2)}, u32[]{:S(2)}) collective-permute-start(bf16[256,1024]{1,0:T(8,128)(2,1)S(1)} %get-tuple-element.3481), channel_id=1, source_target_pairs={{0,4},{2,6},{4,0},{6,2},{1,5},{3,7},{5,1},{7,3},{8,12},{10,14},{12... | collective-permute-start | bytes 1572872 | tf_op jit(solution)/shard_map/ppermute | solution.py:33
  676.4 76.1 %collective-permute-start.14 = (bf16[256,1024]{1,0:T(8,128)(2,1)S(1)}, bf16[256,1024]{1,0:T(8,128)(2,1)S(1)}, u32[]{:S(2)}, u32[]{:S(2)}) collective-permute-start(bf16[256,1024]{1,0:T(8,128)(2,1)S(1)} %get-tuple-element.3482), channel_id=1, source_target_pairs={{0,8},{8,16},{16,24},{24,0},{1,9},{9,17},{17,25},{25,1},{2,10},{10... | collective-permute-start | bytes 1572872 | tf_op jit(solution)/shard_map/ppermute | solution.py:33
  676.5 108.9 %collective-permute-start.15 = (bf16[256,1024]{1,0:T(8,128)(2,1)S(1)}, bf16[256,1024]{1,0:T(8,128)(2,1)}, u32[]{:S(2)}, u32[]{:S(2)}) collective-permute-start(bf16[256,1024]{1,0:T(8,128)(2,1)S(1)} %get-tuple-element.3484), channel_id=1, source_target_pairs={{0,16},{8,24},{16,0},{24,8},{1,17},{9,25},{17,1},{25,9},{2,18},{10... | collective-permute-start | bytes 1572872 | tf_op jit(solution)/shard_map/ppermute | solution.py:33
  734.0 51.4 %collective-permute-start.16 = (bf16[256,1024]{1,0:T(8,128)(2,1)S(1)}, bf16[256,1024]{1,0:T(8,128)(2,1)}, u32[]{:S(2)}, u32[]{:S(2)}) collective-permute-start(bf16[256,1024]{1,0:T(8,128)(2,1)S(1)} %get-tuple-element.3483), channel_id=1, source_target_pairs={{0,24},{8,0},{16,8},{24,16},{1,25},{9,1},{17,9},{25,17},{2,26},{10... | collective-permute-start | bytes 1572872 | tf_op jit(solution)/shard_map/ppermute | solution.py:33
  738.9 52.3 %collective-permute-start.11 = (bf16[64,1024]{1,0:T(8,128)(2,1)S(1)}, bf16[64,1024]{1,0:T(8,128)(2,1)S(1)}, u32[]{:S(2)}, u32[]{:S(2)}) collective-permute-start(bf16[64,1024]{1,0:T(8,128)(2,1)S(1)} %get-tuple-element.3487), channel_id=1, source_target_pairs={{0,8},{8,16},{16,24},{24,0},{1,9},{9,17},{17,25},{25,1},{2,10},{10... | collective-permute-start | bytes 393224 | tf_op jit(solution)/shard_map/ppermute | solution.py:33
  740.0 51.5 %collective-permute-start.12 = (bf16[64,1024]{1,0:T(8,128)(2,1)S(1)}, bf16[64,1024]{1,0:T(8,128)(2,1)S(1)}, u32[]{:S(2)}, u32[]{:S(2)}) collective-permute-start(bf16[64,1024]{1,0:T(8,128)(2,1)S(1)} %get-tuple-element.3489), channel_id=1, source_target_pairs={{0,16},{8,24},{16,0},{24,8},{1,17},{9,25},{17,1},{25,9},{2,18},{10... | collective-permute-start | bytes 393224 | tf_op jit(solution)/shard_map/ppermute | solution.py:33
  752.4 39.1 %collective-permute-start.13 = (bf16[64,1024]{1,0:T(8,128)(2,1)S(1)}, bf16[64,1024]{1,0:T(8,128)(2,1)S(1)}, u32[]{:S(2)}, u32[]{:S(2)}) collective-permute-start(bf16[64,1024]{1,0:T(8,128)(2,1)S(1)} %get-tuple-element.3488), channel_id=1, source_target_pairs={{0,24},{8,0},{16,8},{24,16},{1,25},{9,1},{17,9},{25,17},{2,26},{10... | collective-permute-start | bytes 393224 | tf_op jit(solution)/shard_map/ppermute | solution.py:33
  787.3 6.5 collective-permute-start.17
  787.4 8.2 %collective-permute-start.18 = (bf16[64,1024]{1,0:T(8,128)(2,1)S(1)}, bf16[64,1024]{1,0:T(8,128)(2,1)S(1)}, u32[]{:S(2)}, u32[]{:S(2)}) collective-permute-start(bf16[64,1024]{1,0:T(8,128)(2,1)S(1)} %get-tuple-element.3492), channel_id=1, source_target_pairs={{0,4},{2,6},{4,0},{6,2},{1,5},{3,7},{5,1},{7,3},{8,12},{10,14},{12... | collective-permute-start | bytes 393224 | tf_op jit(solution)/shard_map/ppermute | solution.py:33
  791.2 5.0 collective-permute-start.19
  (6 other events, 10.4 us)
